TPU v7x, 32 devices: a whole 2x2x4 slice. The times are simulated.
32 devices in a mesh: dp: 2 (over x), seq: 4 (over y, core), heads: 4 (over z).
Axes of the slice: x: 2, y: 2, z: 4, core: 2. Of those that a mesh axis runs over, the one named last changes fastest.
Arguments:
- frames: bfloat16 [4, 2048, 1024], P('dp', 'seq'), may hold values from -6 to 6
- segment_ids: int32 [4, 2048], P('dp'), may hold values from 0 to 3, never falling along the last dimension, each value on 1 to 1024 neighbouring positions
- bucket_of: int32 [4095], replicated, may hold values from 0 to 31
- ffn1_gain: bfloat16 [1024], replicated, may hold values from 0.25 to 1.75
- ffn1_in: bfloat16 [1024, 4096], P(None, 'heads'), may hold values from -0.1875 to 0.1875
- ffn1_out: bfloat16 [4096, 1024], P('heads'), may hold values from -0.09375 to 0.09375
- attn_gain: bfloat16 [1024], replicated, may hold values from 0.25 to 1.75
- query_weight: bfloat16 [1024, 1024], P(None, 'heads'), may hold values from -0.1875 to 0.1875
- key_weight: bfloat16 [1024, 1024], P(None, 'heads'), may hold values from -0.1875 to 0.1875
- value_weight: bfloat16 [1024, 1024], P(None, 'heads'), may hold values from -0.1875 to 0.1875
- output_weight: bfloat16 [1024, 1024], P('heads'), may hold values from -1.5 to 1.5
- position_table: float32 [8, 32], P('heads'), may hold values from -4 to 4
- conv_gain: bfloat16 [1024], P(('dp', 'seq', 'heads')), may hold values from 0.25 to 1.75
- pointwise_in: bfloat16 [1024, 2048], P(('dp', 'seq', 'heads')), may hold values from -0.1875 to 0.1875
- depthwise: bfloat16 [5, 1024], P(None, ('dp', 'seq', 'heads')), may hold values from -2.5 to 2.5
- depth_gain: bfloat16 [1024], P(('dp', 'seq', 'heads')), may hold values from 0.25 to 1.75
- pointwise_out: bfloat16 [1024, 1024], P(('dp', 'seq', 'heads')), may hold values from -0.1875 to 0.1875
- ffn2_gain: bfloat16 [1024], replicated, may hold values from 0.25 to 1.75
- ffn2_in: bfloat16 [1024, 4096], P(None, 'heads'), may hold values from -0.1875 to 0.1875
- ffn2_out: bfloat16 [4096, 1024], P('heads'), may hold values from -0.09375 to 0.09375
- final_gain: bfloat16 [1024], replicated, may hold values from 0.25 to 1.75
- cotangent: bfloat16 [4, 2048, 1024], P('dp', 'seq'), may hold values from -6 to 6
Outputs:
- layer_out: bfloat16 [4, 2048, 1024], P('dp', 'seq')
- input_grad: float32 [4, 2048, 1024], P('dp', 'seq')
- ffn1_gain_grad: float32 [1024], P(('dp', 'seq'))
- ffn1_in_grad: float32 [1024, 4096], P(('dp', 'seq'), 'heads')
- ffn1_out_grad: float32 [4096, 1024], P('heads', ('dp', 'seq'))
- attn_gain_grad: float32 [1024], P(('dp', 'seq'))
- query_grad: float32 [1024, 1024], P(('dp', 'seq'), 'heads')
- key_grad: float32 [1024, 1024], P(('dp', 'seq'), 'heads')
- value_grad: float32 [1024, 1024], P(('dp', 'seq'), 'heads')
- output_grad: float32 [1024, 1024], P('heads', ('dp', 'seq'))
- table_grad: float32 [8, 32], P('heads', ('dp', 'seq'))
- conv_gain_grad: float32 [1024], P(('dp', 'seq', 'heads'))
- pointwise_in_grad: float32 [1024, 2048], P(('dp', 'seq', 'heads'))
- depthwise_grad: float32 [5, 1024], P(None, ('dp', 'seq', 'heads'))
- depth_gain_grad: float32 [1024], P(('dp', 'seq', 'heads'))
- pointwise_out_grad: float32 [1024, 1024], P(('dp', 'seq', 'heads'))
- ffn2_gain_grad: float32 [1024], P(('dp', 'seq'))
- ffn2_in_grad: float32 [1024, 4096], P(('dp', 'seq'), 'heads')
- ffn2_out_grad: float32 [4096, 1024], P('heads', ('dp', 'seq'))
- final_gain_grad: float32 [1024], P(('dp', 'seq'))
Inputs may be any that keep to these rules, and one draw needn't show every extreme that they name: `segment_ids`: in each row, ids never fall along the frames; each utterance has at most 1024 frames and one has exactly that many.
All inputs are finite; a program needn't handle non-finite values.
Results may differ from a plain program's by a relative error of at most 0.029.
Values may be sent and summed in bfloat16 or wider, within the bound.
No kernel may reach another device: no remote copies, remote signals or barrier semaphores. Data moves between devices by JAX's collectives and lax.ppermute only.
A program may use at most 192 MiB of HBM per device.

v0:
```python
import jax
import jax.numpy as jnp
from jax import lax
from jax.sharding import PartitionSpec as P

HEAD_DIM = 128
KERNEL = 5


EPSILON = 1e-05
NEGATIVE = -1e30
HIGHEST = lax.Precision.HIGHEST


def extended(array, sides, width):
    for axis, dim in sides:
        peers, length = (lax.axis_size(axis), array.shape[dim])
        up = [(i, (i + 1) % peers) for i in range(peers - 1)]
        down = [(j, i) for i, j in up]
        last = lax.slice_in_dim(array, length - width, length, axis=dim)
        leading = lax.slice_in_dim(array, 0, width, axis=dim)
        before = lax.ppermute(last, axis, up)
        after = lax.ppermute(leading, axis, down)
        array = jnp.concatenate([before, array, after], axis=dim)
    return array


def matmul_plain(left, right):
    return jnp.dot(left, right, preferred_element_type=jnp.float32)


def matmul_against(left, right):
    return lax.dot_general(
        left, right, (((1,), (1,)), ((), ())), preferred_element_type=jnp.float32
    )


def matmul_outer(left, right):
    return lax.dot_general(
        left, right, (((0,), (0,)), ((), ())), preferred_element_type=jnp.float32
    )


def norm_forward(values, gain_vec):
    centred = values - jnp.mean(values, axis=-1, keepdims=True)
    inverse = lax.rsqrt(jnp.mean(centred * centred, axis=-1, keepdims=True) + EPSILON)
    normed = centred * inverse
    return (normed * gain_vec.astype(jnp.float32), normed, inverse)


def norm_backward(gradient, normed, inverse, gain_vec):
    scaled = gradient * gain_vec.astype(jnp.float32)
    mean_grad = jnp.mean(scaled, axis=-1, keepdims=True)
    second = jnp.mean(scaled * normed, axis=-1, keepdims=True)
    gain_grad = jnp.sum((gradient * normed).reshape(-1, gradient.shape[-1]), axis=0)
    return (inverse * (scaled - mean_grad - normed * second), gain_grad)


def silu_slope(values):
    sigmoid = jax.nn.sigmoid(values)
    return sigmoid * (1.0 + values * (1.0 - sigmoid))


def reduce_branch(partial_out):
    return lax.psum(partial_out, "heads")


def reduce_normed(partial_grad):
    return lax.psum(partial_grad.astype(jnp.bfloat16), "heads").astype(jnp.float32)


def ffn_forward(stream, gain_vec, weight_in, weight_out):
    normed_out, normed, inverse = norm_forward(stream, gain_vec)
    whole_low = normed_out.astype(jnp.bfloat16)
    row_count, frame_count, width = whole_low.shape
    flat_low = whole_low.reshape(row_count * frame_count, width)
    hidden_pre = matmul_plain(flat_low, weight_in)
    active_low = jax.nn.silu(hidden_pre).astype(jnp.bfloat16)
    branch = reduce_branch(
        matmul_plain(active_low, weight_out).reshape(row_count, frame_count, width)
    )
    return (stream + 0.5 * branch, (normed, inverse, flat_low, hidden_pre, active_low))


def ffn_backward(gradient, saved_state, gain_vec, weight_in, weight_out):
    normed, inverse, flat_low, hidden_pre, active_low = saved_state
    whole_grad = (0.5 * gradient).astype(jnp.bfloat16)
    row_count, frame_count, width = whole_grad.shape
    branch_low = whole_grad.reshape(row_count * frame_count, width)
    active_grad = matmul_against(branch_low, weight_out)
    out_grad = matmul_outer(active_low, branch_low)
    pre_low = (active_grad * silu_slope(hidden_pre)).astype(jnp.bfloat16)
    in_grad = matmul_outer(flat_low, pre_low)
    normed_grad = reduce_normed(
        matmul_against(pre_low, weight_in).reshape(row_count, frame_count, width)
    )
    stream_part, gain_grad = norm_backward(normed_grad, normed, inverse, gain_vec)
    return (gradient + stream_part, (gain_grad, in_grad, out_grad))


def bucket_onehot(bias_table, bucket_of):
    levels = lax.broadcasted_iota(jnp.int32, (bias_table.shape[1], bucket_of.shape[0]), 0)
    return (levels == bucket_of[None, :]).astype(jnp.float32)


def offset_bias(bias_table, onehot, query_start, local_len, length):
    by_offset = jnp.dot(bias_table, onehot, precision=HIGHEST)
    span_width = length + local_len - 1
    head_count = bias_table.shape[0]
    window = lax.dynamic_slice_in_dim(by_offset, length - local_len - query_start, span_width, 1)
    spread = jnp.broadcast_to(window[:, None, :], (head_count, local_len, span_width)).reshape(
        head_count, local_len * span_width
    )
    spread = jnp.pad(spread, ((0, 0), (0, local_len)))
    return spread.reshape(head_count, local_len, length + local_len)[:, ::-1, :length]


def offset_gradient(score_sum, onehot, query_start, local_len, length):
    head_count = score_sum.shape[0]
    span_width = length + local_len - 1
    flipped = jnp.pad(score_sum[:, ::-1, :], ((0, 0), (0, 0), (0, local_len)))
    skewed = flipped.reshape(head_count, -1)[:, : local_len * span_width].reshape(
        head_count, local_len, span_width
    )
    window_grad = jnp.sum(skewed, axis=1)
    by_offset = jnp.zeros((head_count, onehot.shape[1]), jnp.float32)
    by_offset = lax.dynamic_update_slice_in_dim(
        by_offset, window_grad, length - local_len - query_start, 1
    )
    return lax.dot_general(by_offset, onehot, (((1,), (1,)), ((), ())), precision=HIGHEST)


def score_block(query_low, key_all, bias_block, allowed):
    scaling = query_low.shape[-1] ** (-0.5)
    scores = (
        jnp.einsum("rihd,rjhd->rhij", query_low, key_all, preferred_element_type=jnp.float32)
        * scaling
    )
    return jnp.where(allowed[:, None], scores + bias_block[None], NEGATIVE)


def attention_forward(
    stream, gain_vec, query_weight, key_weight, value_weight, output_weight, bias_block, allowed
):
    normed_out, normed, inverse = norm_forward(stream, gain_vec)
    whole_low = normed_out.astype(jnp.bfloat16)
    row_count, local_len, width = whole_low.shape
    normed_low = whole_low.reshape(row_count * local_len, width)
    head_count = query_weight.shape[1] // HEAD_DIM
    query_low = (
        matmul_plain(normed_low, query_weight)
        .astype(jnp.bfloat16)
        .reshape(row_count, local_len, head_count, HEAD_DIM)
    )
    key_low = (
        matmul_plain(normed_low, key_weight)
        .astype(jnp.bfloat16)
        .reshape(row_count, local_len, head_count * HEAD_DIM)
    )
    value_low = (
        matmul_plain(normed_low, value_weight)
        .astype(jnp.bfloat16)
        .reshape(row_count, local_len, head_count * HEAD_DIM)
    )
    key_all, value_all = (
        lax.all_gather(key_low, "seq", axis=1, tiled=True),
        lax.all_gather(value_low, "seq", axis=1, tiled=True),
    )
    length = key_all.shape[1]
    key_all = key_all.reshape(row_count, length, head_count, HEAD_DIM)
    value_all = value_all.reshape(row_count, length, head_count, HEAD_DIM)
    scores = score_block(query_low, key_all, bias_block, allowed)
    row_max = jnp.max(scores, axis=-1, keepdims=True)
    exponent = jnp.exp(scores - row_max)
    row_total = jnp.sum(exponent, axis=-1, keepdims=True)
    probs_low = (exponent / row_total).astype(jnp.bfloat16)
    mixture = jnp.einsum(
        "rhij,rjhd->rihd", probs_low, value_all, preferred_element_type=jnp.float32
    )
    mixture_low = mixture.astype(jnp.bfloat16).reshape(row_count * local_len, head_count * HEAD_DIM)
    branch = reduce_branch(
        matmul_plain(mixture_low, output_weight).reshape(row_count, local_len, width)
    )
    saved_state = (
        normed,
        inverse,
        normed_low,
        query_low,
        key_all,
        value_all,
        row_max + jnp.log(row_total),
        mixture_low,
    )
    return (stream + branch, saved_state)


def attention_backward(
    gradient,
    saved_state,
    gain_vec,
    query_weight,
    key_weight,
    value_weight,
    output_weight,
    bias_block,
    allowed,
    onehot,
    query_start,
):
    normed, inverse, normed_low, query_low, key_all, value_all, log_total, mixture_low = saved_state
    row_count, local_len, head_count = (query_low.shape[0], query_low.shape[1], query_low.shape[2])
    length = key_all.shape[1]
    width = gradient.shape[-1]
    scaling = HEAD_DIM ** (-0.5)
    branch_low = gradient.astype(jnp.bfloat16).reshape(row_count * local_len, width)
    output_grad = matmul_outer(mixture_low, branch_low)
    mixture_grad = (
        matmul_against(branch_low, output_weight)
        .astype(jnp.bfloat16)
        .reshape(row_count, local_len, head_count, HEAD_DIM)
    )
    probs = jnp.exp(score_block(query_low, key_all, bias_block, allowed) - log_total)
    probs_grad = jnp.einsum(
        "rihd,rjhd->rhij", mixture_grad, value_all, preferred_element_type=jnp.float32
    )
    value_part = jnp.einsum(
        "rhij,rihd->rjhd",
        probs.astype(jnp.bfloat16),
        mixture_grad,
        preferred_element_type=jnp.float32,
    )
    score_low = (probs * (probs_grad - jnp.sum(probs * probs_grad, axis=-1, keepdims=True))).astype(
        jnp.bfloat16
    )
    query_grad = (
        jnp.einsum("rhij,rjhd->rihd", score_low, key_all, preferred_element_type=jnp.float32)
        * scaling
    ).astype(jnp.bfloat16)
    key_part = (
        jnp.einsum("rhij,rihd->rjhd", score_low, query_low, preferred_element_type=jnp.float32)
        * scaling
    )
    flat_shape = (row_count, length, head_count * HEAD_DIM)
    key_sum, value_sum = (
        lax.psum_scatter(
            key_part.reshape(flat_shape).astype(jnp.bfloat16),
            "seq",
            scatter_dimension=1,
            tiled=True,
        ).astype(jnp.float32),
        lax.psum_scatter(
            value_part.reshape(flat_shape).astype(jnp.bfloat16),
            "seq",
            scatter_dimension=1,
            tiled=True,
        ).astype(jnp.float32),
    )
    token_count = row_count * local_len
    query_flat = query_grad.reshape(token_count, head_count * HEAD_DIM)
    key_flat = key_sum.astype(jnp.bfloat16).reshape(token_count, head_count * HEAD_DIM)
    value_flat = value_sum.astype(jnp.bfloat16).reshape(token_count, head_count * HEAD_DIM)
    normed_part = (
        matmul_against(query_flat, query_weight)
        + matmul_against(key_flat, key_weight)
        + matmul_against(value_flat, value_weight)
    )
    normed_grad = reduce_normed(normed_part.reshape(row_count, local_len, width))
    stream_part, gain_grad = norm_backward(normed_grad, normed, inverse, gain_vec)
    table_grad = offset_gradient(
        jnp.sum(score_low.astype(jnp.float32), axis=0), onehot, query_start, local_len, length
    )
    weight_grads = (
        gain_grad,
        matmul_outer(normed_low, query_flat),
        matmul_outer(normed_low, key_flat),
        matmul_outer(normed_low, value_flat),
        output_grad,
        table_grad,
    )
    return (gradient + stream_part, weight_grads)


def conv_forward(piece, start, local_len, conv_weights, segment_ids):
    in_weight, out_weight, depth_weight, gain_one, gain_two = conv_weights
    row_count, slice_len, width = piece.shape
    normed_out, normed, inverse = norm_forward(piece, gain_one)
    normed_low = normed_out.astype(jnp.bfloat16).reshape(row_count * slice_len, width)
    doubled = matmul_plain(normed_low, in_weight).reshape(row_count, slice_len, 2 * width)
    gate_sig = jax.nn.sigmoid(doubled[..., width:])
    glu_low = (doubled[..., :width] * gate_sig).astype(jnp.bfloat16)
    reach = KERNEL // 2
    padded = extended(glu_low, ((("seq", "heads"), 1),), reach)
    frame_start = lax.axis_index("seq") * local_len + start
    ids_pad = jnp.pad(segment_ids, ((0, 0), (reach, reach)), constant_values=-1)
    window_ids = lax.dynamic_slice_in_dim(ids_pad, frame_start, slice_len + 2 * reach, 1)
    centre = window_ids[:, reach : reach + slice_len]
    depth_float = depth_weight.astype(jnp.float32)
    depth_out = jnp.zeros((row_count, slice_len, width), jnp.float32)
    for offset in range(KERNEL):
        same = (window_ids[:, offset : offset + slice_len] == centre).astype(jnp.float32)[..., None]
        depth_out = (
            depth_out
            + padded[:, offset : offset + slice_len].astype(jnp.float32)
            * depth_float[offset]
            * same
        )
    norm_two, hat_two, inverse_two = norm_forward(depth_out, gain_two)
    swish_low = jax.nn.silu(norm_two).astype(jnp.bfloat16).reshape(row_count * slice_len, width)
    branch = matmul_plain(swish_low, out_weight).reshape(row_count, slice_len, width)
    saved_state = (
        window_ids,
        normed,
        inverse,
        normed_low,
        doubled,
        gate_sig,
        padded,
        hat_two,
        inverse_two,
        norm_two,
        swish_low,
    )
    return (branch, saved_state)


def conv_backward(grad_piece, saved_state, conv_weights):
    in_weight, out_weight, depth_weight, gain_one, gain_two = conv_weights
    (
        window_ids,
        normed,
        inverse,
        normed_low,
        doubled,
        gate_sig,
        padded,
        hat_two,
        inverse_two,
        norm_two,
        swish_low,
    ) = saved_state
    row_count, slice_len, width = norm_two.shape
    reach = KERNEL // 2
    piece_low = grad_piece.astype(jnp.bfloat16).reshape(row_count * slice_len, width)
    out_grad = matmul_outer(swish_low, piece_low)
    swish_grad = matmul_against(piece_low, out_weight).reshape(row_count, slice_len, width)
    depth_grad, gain_two_grad = norm_backward(
        swish_grad * silu_slope(norm_two), hat_two, inverse_two, gain_two
    )
    depth_low = depth_grad.astype(jnp.bfloat16)
    beside_all = extended(depth_low, ((("seq", "heads"), 1),), reach)
    centre = window_ids[:, reach : reach + slice_len]
    depth_float = depth_weight.astype(jnp.float32)
    depth_low_float = depth_low.astype(jnp.float32)
    glu_grad = jnp.zeros((row_count, slice_len, width), jnp.float32)
    tap_grads = []
    for offset in range(KERNEL):
        same = (window_ids[:, offset : offset + slice_len] == centre).astype(jnp.float32)[..., None]
        tap_terms = (
            depth_low_float * padded[:, offset : offset + slice_len].astype(jnp.float32) * same
        )
        tap_grads.append(jnp.sum(tap_terms.reshape(row_count * slice_len, width), axis=0))
        mirror = 2 * reach - offset
        back_same = (window_ids[:, mirror : mirror + slice_len] == centre).astype(jnp.float32)[
            ..., None
        ]
        glu_grad = (
            glu_grad
            + beside_all[:, mirror : mirror + slice_len].astype(jnp.float32)
            * depth_float[offset]
            * back_same
        )
    depth_weight_grad = jnp.stack(tap_grads)
    gate_in = doubled[..., :width]
    doubled_low = (
        jnp.concatenate(
            [glu_grad * gate_sig, glu_grad * gate_in * gate_sig * (1.0 - gate_sig)], axis=-1
        )
        .astype(jnp.bfloat16)
        .reshape(row_count * slice_len, 2 * width)
    )
    in_grad = matmul_outer(normed_low, doubled_low)
    normed_grad = matmul_against(doubled_low, in_weight).reshape(row_count, slice_len, width)
    piece_grad, gain_one_grad = norm_backward(normed_grad, normed, inverse, gain_one)
    return (piece_grad, (in_grad, out_grad, depth_weight_grad, gain_one_grad, gain_two_grad))


def on_device(
    frames,
    segment_ids,
    bucket_of,
    ffn1_gain,
    ffn1_in,
    ffn1_out,
    attn_gain,
    query_weight,
    key_weight,
    value_weight,
    output_weight,
    position_table,
    conv_gain,
    pointwise_in,
    depthwise,
    depth_gain,
    pointwise_out,
    ffn2_gain,
    ffn2_in,
    ffn2_out,
    final_gain,
    cotangent,
):
    row_count, local_len, width = frames.shape
    length = segment_ids.shape[1]
    conv_weights = (
        lax.all_gather(pointwise_in, ("dp", "seq", "heads"), axis=0, tiled=True),
        lax.all_gather(pointwise_out, ("dp", "seq", "heads"), axis=0, tiled=True),
        lax.all_gather(depthwise, ("dp", "seq", "heads"), axis=1, tiled=True),
        lax.all_gather(conv_gain, ("dp", "seq", "heads"), axis=0, tiled=True),
        lax.all_gather(depth_gain, ("dp", "seq", "heads"), axis=0, tiled=True),
    )
    query_start = lax.axis_index("seq") * local_len
    query_ids = lax.dynamic_slice_in_dim(segment_ids, query_start, local_len, 1)
    allowed = query_ids[:, :, None] == segment_ids[:, None, :]
    onehot = bucket_onehot(position_table, bucket_of)
    bias_block = offset_bias(position_table, onehot, query_start, local_len, length)
    slice_len = local_len // lax.axis_size("heads")
    start = lax.axis_index("heads") * slice_len
    stream_zero = frames.astype(jnp.float32)
    cotangent_float = cotangent.astype(jnp.float32)
    stream_one, ffn1_state = ffn_forward(stream_zero, ffn1_gain, ffn1_in, ffn1_out)
    stream_two, attn_state = attention_forward(
        stream_one,
        attn_gain,
        query_weight,
        key_weight,
        value_weight,
        output_weight,
        bias_block,
        allowed,
    )
    conv_piece = lax.dynamic_slice_in_dim(stream_two, start, slice_len, 1)
    conv_branch, conv_state = conv_forward(conv_piece, start, local_len, conv_weights, segment_ids)
    stream_three = stream_two + lax.all_gather(
        conv_branch.astype(jnp.bfloat16), "heads", axis=1, tiled=True
    ).astype(conv_branch.dtype)
    stream_four, ffn2_state = ffn_forward(stream_three, ffn2_gain, ffn2_in, ffn2_out)
    final_out, final_hat, final_inverse = norm_forward(stream_four, final_gain)
    layer_low = final_out.astype(jnp.bfloat16)
    grad_four, final_gain_grad = norm_backward(
        cotangent_float, final_hat, final_inverse, final_gain
    )
    grad_three, ffn2_grads = ffn_backward(grad_four, ffn2_state, ffn2_gain, ffn2_in, ffn2_out)
    grad_slice = lax.dynamic_slice_in_dim(grad_three, start, slice_len, 1)
    piece_grad, conv_grads = conv_backward(grad_slice, conv_state, conv_weights)
    grad_two = grad_three + lax.all_gather(
        piece_grad.astype(jnp.bfloat16), "heads", axis=1, tiled=True
    ).astype(piece_grad.dtype)
    grad_one, attn_grads = attention_backward(
        grad_two,
        attn_state,
        attn_gain,
        query_weight,
        key_weight,
        value_weight,
        output_weight,
        bias_block,
        allowed,
        onehot,
        query_start,
    )
    grad_zero, ffn1_grads = ffn_backward(grad_one, ffn1_state, ffn1_gain, ffn1_in, ffn1_out)
    f1_gain_g, f1_in_g, f1_out_g = ffn1_grads
    at_gain_g, query_g, key_g, value_g, output_g, table_g = attn_grads
    f2_gain_g, f2_in_g, f2_out_g = ffn2_grads
    pw_in_g, pw_out_g, depth_g, cv_gain_g, dp_gain_g = conv_grads
    reduced = (
        lax.psum_scatter(
            f1_gain_g.astype(jnp.bfloat16), ("dp", "seq"), scatter_dimension=0, tiled=True
        ).astype(jnp.float32),
        lax.psum_scatter(
            f1_in_g.astype(jnp.bfloat16), ("dp", "seq"), scatter_dimension=0, tiled=True
        ).astype(jnp.float32),
        lax.psum_scatter(
            f1_out_g.astype(jnp.bfloat16), ("dp", "seq"), scatter_dimension=1, tiled=True
        ).astype(jnp.float32),
        lax.psum_scatter(
            at_gain_g.astype(jnp.bfloat16), ("dp", "seq"), scatter_dimension=0, tiled=True
        ).astype(jnp.float32),
        lax.psum_scatter(
            query_g.astype(jnp.bfloat16), ("dp", "seq"), scatter_dimension=0, tiled=True
        ).astype(jnp.float32),
        lax.psum_scatter(
            key_g.astype(jnp.bfloat16), ("dp", "seq"), scatter_dimension=0, tiled=True
        ).astype(jnp.float32),
        lax.psum_scatter(
            value_g.astype(jnp.bfloat16), ("dp", "seq"), scatter_dimension=0, tiled=True
        ).astype(jnp.float32),
        lax.psum_scatter(
            output_g.astype(jnp.bfloat16), ("dp", "seq"), scatter_dimension=1, tiled=True
        ).astype(jnp.float32),
        lax.psum_scatter(
            table_g.astype(jnp.bfloat16), ("dp", "seq"), scatter_dimension=1, tiled=True
        ).astype(jnp.float32),
        lax.psum_scatter(
            f2_gain_g.astype(jnp.bfloat16), ("dp", "seq"), scatter_dimension=0, tiled=True
        ).astype(jnp.float32),
        lax.psum_scatter(
            f2_in_g.astype(jnp.bfloat16), ("dp", "seq"), scatter_dimension=0, tiled=True
        ).astype(jnp.float32),
        lax.psum_scatter(
            f2_out_g.astype(jnp.bfloat16), ("dp", "seq"), scatter_dimension=1, tiled=True
        ).astype(jnp.float32),
        lax.psum_scatter(
            final_gain_grad.astype(jnp.bfloat16), ("dp", "seq"), scatter_dimension=0, tiled=True
        ).astype(jnp.float32),
    )
    conv_reduced = (
        lax.psum_scatter(pw_in_g, ("dp", "seq", "heads"), scatter_dimension=0, tiled=True),
        lax.psum_scatter(pw_out_g, ("dp", "seq", "heads"), scatter_dimension=0, tiled=True),
        lax.psum_scatter(depth_g, ("dp", "seq", "heads"), scatter_dimension=1, tiled=True),
        lax.psum_scatter(cv_gain_g, ("dp", "seq", "heads"), scatter_dimension=0, tiled=True),
        lax.psum_scatter(dp_gain_g, ("dp", "seq", "heads"), scatter_dimension=0, tiled=True),
    )
    return (
        layer_low,
        grad_zero,
        reduced[0],
        reduced[1],
        reduced[2],
        reduced[3],
        reduced[4],
        reduced[5],
        reduced[6],
        reduced[7],
        reduced[8],
        conv_reduced[3],
        conv_reduced[0],
        conv_reduced[2],
        conv_reduced[4],
        conv_reduced[1],
        reduced[9],
        reduced[10],
        reduced[11],
        reduced[12],
    )


def solution(mesh):
    return jax.shard_map(
        on_device,
        mesh=mesh,
        in_specs=(
            P("dp", "seq", None),
            P("dp", None),
            P(),
            P(),
            P(None, "heads"),
            P("heads", None),
            P(),
            P(None, "heads"),
            P(None, "heads"),
            P(None, "heads"),
            P("heads", None),
            P("heads", None),
            P(("dp", "seq", "heads")),
            P(("dp", "seq", "heads"), None),
            P(None, ("dp", "seq", "heads")),
            P(("dp", "seq", "heads")),
            P(("dp", "seq", "heads"), None),
            P(),
            P(None, "heads"),
            P("heads", None),
            P(),
            P("dp", "seq", None),
        ),
        out_specs=(
            P("dp", "seq", None),
            P("dp", "seq", None),
            P(("dp", "seq")),
            P(("dp", "seq"), "heads"),
            P("heads", ("dp", "seq")),
            P(("dp", "seq")),
            P(("dp", "seq"), "heads"),
            P(("dp", "seq"), "heads"),
            P(("dp", "seq"), "heads"),
            P("heads", ("dp", "seq")),
            P("heads", ("dp", "seq")),
            P(("dp", "seq", "heads")),
            P(("dp", "seq", "heads"), None),
            P(None, ("dp", "seq", "heads")),
            P(("dp", "seq", "heads")),
            P(("dp", "seq", "heads"), None),
            P(("dp", "seq")),
            P(("dp", "seq"), "heads"),
            P("heads", ("dp", "seq")),
            P(("dp", "seq")),
        ),
        check_vma=False,
    )
```

profile of v0, /device:TPU:0, one launch (start us, length us, event | category | flops | bytes accessed | tf_op | source)
XLA Modules:
  0.0 1998.3 jit_solution(4291674310678749992)
XLA Ops:
  21.6 157.2 %all-reduce.22.cloned.1.call-done = f32[2,512,1024]{2,1,0:T(8,128)} async-done(((f32[2,512,1024]{2,1,0:T(8,128)}), f32[2,512,1024]{2,1,0:T(8,128)}) %all-reduce.22.cloned.1.call-update) | async-done | bytes 4194320 | tf_op jit(solution)/shard_map/psum | solution.py:65
  191.2 5.3 broadcast_in_dim.17
  196.5 14.9 reshape.354
  211.4 16.8 reshape.311
  228.2 6.7 pad.12
  234.9 5.9 copy.144
  240.7 7.8 slice.134
  248.6 64.3 %rev.6 = f32[2,512,2048]{2,1,0:T(8,128)} reverse(f32[2,512,2048]{2,1,0:T(8,128)} %slice.134), dimensions={1} | reverse | bytes 16777216 | tf_op jit(solution)/shard_map/rev | solution.py:115
  319.9 11.6 fusion.123
  331.5 8.1 fusion
  343.7 8.3 fusion.64
  357.3 45.5 %all-reduce.13 = (bf16[1024]{0:T(1024)(128)(2,1)S(1)}, bf16[1024]{0:T(1024)(128)(2,1)S(1)}) all-reduce(bf16[1024]{0:T(1024)(128)(2,1)S(1)} %dynamic-update-slice, bf16[1024]{0:T(1024)(128)(2,1)S(1)} %dynamic-update-slice.1), channel_id=1, replica_groups=mesh['dp'=2,'seq'=4,'heads'=4] {'dp','seq','heads'}, use_global_device_ids=true, to_apply=%add.3 | all-reduce | flops 2048 | bytes 8192
  402.8 69.5 %all-gather = bf16[32,32,5]{1,2,0:T(8,128)(2,1)S(1)} all-gather(bf16[1,32,5]{1,2,0:T(8,128)(2,1)S(1)} %bitcast.222), channel_id=1, replica_groups=mesh['dp'=2,'seq'=4,'heads'=4] {'dp','seq','heads'}, dimensions={0}, use_global_device_ids=true | all-gather | bytes 10560 | tf_op jit(solution)/shard_map/all_gather | solution.py:416
  472.5 46.5 %all-reduce.24.cloned.1.call-done = f32[2,512,1024]{2,1,0:T(8,128)} async-done(((f32[2,512,1024]{2,1,0:T(8,128)}), f32[2,512,1024]{2,1,0:T(8,128)}) %all-reduce.24.cloned.1.call-update) | async-done | bytes 4194320 | tf_op jit(solution)/shard_map/psum | solution.py:65
  525.7 5.5 all-gather.12.cloned.1.call-done
  546.4 43.2 %all-gather.14.cloned.1.call-done = bf16[1024,1024]{1,0:T(8,128)(2,1)} async-done(((bf16[32,1024]{1,0:T(8,128)(2,1)}), bf16[1024,1024]{1,0:T(8,128)(2,1)}) %all-gather.14.cloned.1.call-update) | async-done | bytes 2097168 | tf_op jit(solution)/shard_map/all_gather | solution.py:415
  592.9 44.6 %all-gather.16.cloned.1.call-done = bf16[2,512,1024]{2,1,0:T(8,128)(2,1)} async-done(((bf16[2,128,1024]{2,1,0:T(8,128)(2,1)}), bf16[2,512,1024]{2,1,0:T(8,128)(2,1)}) %all-gather.16.cloned.1.call-update) | async-done | bytes 2097168 | tf_op jit(solution)/shard_map/all_gather | solution.py:442
  651.5 153.3 %all-reduce.26.cloned.1.call-done = f32[2,512,1024]{2,1,0:T(8,128)} async-done(((f32[2,512,1024]{2,1,0:T(8,128)}), f32[2,512,1024]{2,1,0:T(8,128)}) %all-reduce.26.cloned.1.call-update) | async-done | bytes 4194320 | tf_op jit(solution)/shard_map/psum | solution.py:65
  823.9 85.2 %all-reduce.28.cloned.1.call-done = bf16[2,512,1024]{2,1,0:T(8,128)(2,1)} async-done(((bf16[2,512,1024]{2,1,0:T(8,128)(2,1)}), bf16[2,512,1024]{2,1,0:T(8,128)(2,1)}) %all-reduce.28.cloned.1.call-update) | async-done | bytes 2097168 | tf_op jit(solution)/shard_map/psum | solution.py:69
  913.9 6.0 fusion.33
  935.6 47.2 %all-gather.18.cloned.1.call-done = bf16[2,512,1024]{2,1,0:T(8,128)(2,1)} async-done(((bf16[2,128,1024]{2,1,0:T(8,128)(2,1)}), bf16[2,512,1024]{2,1,0:T(8,128)(2,1)}) %all-gather.18.cloned.1.call-update) | async-done | bytes 2097168 | tf_op jit(solution)/shard_map/all_gather | solution.py:454
  993.3 11.2 multiply_reduce_fusion
  1004.5 15.7 convert_reduce_fusion
  1026.1 9.5 fusion.47
  1038.3 7.3 fusion.65
  1048.8 7.3 reduce-scatter.23.cloned.1.call-done
  1059.8 29.8 %reduce-scatter.25.cloned.1.call-done = bf16[2,512,256]{2,1,0:T(8,128)(2,1)} async-done(((bf16[2,2048,256]{2,1,0:T(8,128)(2,1)}), bf16[2,512,256]{2,1,0:T(8,128)(2,1)}) %reduce-scatter.25.cloned.1.call-update) | async-done | bytes 524304 | tf_op jit(solution)/shard_map/reduce_scatter | solution.py:251
  1089.6 5.7 add_convert_fusion
  1096.6 5.3 convolution_convert_fusion
  1104.6 6.1 convolution_convert_fusion.1
  1126.7 57.0 %all-reduce.30.cloned.1.call-done = bf16[2,512,1024]{2,1,0:T(8,128)(2,1)} async-done(((bf16[2,512,1024]{2,1,0:T(8,128)(2,1)}), bf16[2,512,1024]{2,1,0:T(8,128)(2,1)}) %all-reduce.30.cloned.1.call-update) | async-done | bytes 2097168 | tf_op jit(solution)/shard_map/psum | solution.py:69
  1201.7 6.7 convolution_convert_fusion.2
  1212.5 5.3 convolution_convert_fusion.3
  1223.4 5.9 convolution_bitcast_fusion
  1231.9 41.5 %all-reduce.12 = (f32[1024]{0:T(1024)S(1)}, f32[1024]{0:T(1024)S(1)}) all-reduce(f32[1024]{0:T(1024)S(1)} %get-tuple-element.26, f32[1024]{0:T(1024)S(1)} %get-tuple-element.34), channel_id=13, replica_groups=mesh['dp'=2,'seq'=4,'heads'=4] {'dp','seq','heads'}, use_global_device_ids=true, to_apply=%region_49.50.clone | all-reduce | flops 2048 | bytes 16384
  1274.5 50.6 %reduce-scatter.45.cloned.1.call-done = f32[32,5]{1,0:T(8,128)} async-done(((f32[1024,5]{1,0:T(8,128)}), f32[32,5]{1,0:T(8,128)}) %reduce-scatter.45.cloned.1.call-update) | async-done | bytes 656
  1326.5 43.0 %reduce-scatter.47.cloned.1.call-done = bf16[128,1024]{1,0:T(8,128)(2,1)} async-done(((bf16[1024,1024]{1,0:T(8,128)(2,1)}), bf16[128,1024]{1,0:T(8,128)(2,1)}) %reduce-scatter.47.cloned.1.call-update) | async-done | bytes 262160
  1371.5 42.4 %reduce-scatter.39.cloned.1.call-done = bf16[128,1024]{1,0:T(8,128)(2,1)} async-done(((bf16[1024,1024]{1,0:T(8,128)(2,1)}), bf16[128,1024]{1,0:T(8,128)(2,1)}) %reduce-scatter.39.cloned.1.call-update) | async-done | bytes 262160 | tf_op jit(solution)/shard_map/reduce_scatter | solution.py:506
  1415.7 64.3 %rev.7 = f32[2,512,2048]{2,1,0:T(8,128)} reverse(f32[2,512,2048]{2,1,0:T(8,128)} %get-tuple-element.55), dimensions={1} | reverse | bytes 16777216 | tf_op jit(solution)/shard_map/rev | solution.py:121
  1484.2 24.2 %copy.129 = f32[1,2,512,2560]{3,1,2,0:T(2,128)S(1)} copy(f32[1,2,512,2560]{3,2,1,0:T(8,128)S(1)} %pad_bitcast_fusion) | data formatting | bytes 20971520
  1512.7 24.2 %reshape.356 = f32[2620416]{0:T(1024)} reshape(f32[2,1310208]{1,0:T(2,128)} %slice.154) | data formatting | bytes 20963328
  1537.0 15.2 reshape.324
  1568.5 12.6 all-reduce.14
  1584.1 5.6 fusion.25
  1589.7 18.1 reduce-scatter.41.cloned.1.call-done
  1609.8 42.2 %reduce-scatter.27.cloned.1.call-done = bf16[128,1024]{1,0:T(8,128)(2,1)} async-done(((bf16[1024,1024]{1,0:T(8,128)(2,1)}), bf16[128,1024]{1,0:T(8,128)(2,1)}) %reduce-scatter.27.cloned.1.call-update) | async-done | bytes 262160 | tf_op jit(solution)/shard_map/reduce_scatter | solution.py:479
  1653.8 150.0 %reduce-scatter.37.cloned.1.call-done = f32[32,1024]{1,0:T(8,128)} async-done(((f32[1024,1024]{1,0:T(8,128)}), f32[32,1024]{1,0:T(8,128)}) %reduce-scatter.37.cloned.1.call-update) | async-done | bytes 131088 | tf_op jit(solution)/shard_map/reduce_scatter | solution.py:518
  1803.7 186.8 %reduce-scatter.35.cloned.1.call-done = f32[32,2048]{1,0:T(8,128)} async-done(((f32[1024,2048]{1,0:T(8,128)}), f32[32,2048]{1,0:T(8,128)}) %reduce-scatter.35.cloned.1.call-update) | async-done | bytes 262160 | tf_op jit(solution)/shard_map/reduce_scatter | solution.py:517
  (376 shorter events, 232.6 us)
Async XLA Ops:
  8.0 638.4 %copy-start = (bf16[1024,1024]{1,0:T(8,128)(2,1)S(1)}, bf16[1024,1024]{1,0:T(8,128)(2,1)}, u32[]{:S(2)}) copy-start(bf16[1024,1024]{1,0:T(8,128)(2,1)} %param.41) | copy-start | bytes 6291460
  8.0 170.7 %all-reduce.22.cloned.1.call-start = ((), (), s32[]{:S(2)}) async-start(), calls=%async_computation.13 | async-start | bytes 8388608 | tf_op jit(solution)/shard_map/psum | solution.py:65
  20.9 299.0 %all-gather.10.cloned.1.call-start = ((), (), s32[]{:S(2)}) async-start(), calls=%async_computation.15 | async-start | bytes 2621440 | tf_op jit(solution)/shard_map/all_gather | solution.py:166
  21.6 161.3 %copy-start.57 = (f32[1024]{0:T(1024)}, f32[1024]{0:T(1024)S(1)}, u32[]{:S(2)}) copy-start(f32[1024]{0:T(1024)S(1)} %convert_element_type.330) | copy-start | bytes 12292
  187.4 152.3 %all-gather.8.cloned.1.call-start = ((), (), s32[]{:S(2)}) async-start(), calls=%async_computation.14 | async-start | bytes 2621440 | tf_op jit(solution)/shard_map/all_gather | solution.py:167
  190.9 328.1 %all-reduce.24.cloned.1.call-start = ((), (), s32[]{:S(2)}) async-start(), calls=%async_computation.16 | async-start | bytes 8388608 | tf_op jit(solution)/shard_map/psum | solution.py:65
  248.6 66.6 %copy-start.42 = (bf16[1024,256]{1,0:T(8,128)(2,1)S(1)}, bf16[1024,256]{1,0:T(8,128)(2,1)}, u32[]{:S(2)}) copy-start(bf16[1024,256]{1,0:T(8,128)(2,1)} %param.29) | copy-start | bytes 1572868
  319.8 11.7 copy-start.24
  352.8 50.0 %copy-start.64 = (bf16[5,32]{1,0:T(8,128)(2,1)S(1)}, bf16[5,32]{1,0:T(8,128)(2,1)}, u32[]{:S(2)}) copy-start(bf16[5,32]{1,0:T(8,128)(2,1)} %param.36) | copy-start | bytes 964
  355.5 175.7 %all-gather.12.cloned.1.call-start = ((), (), s32[]{:S(2)}) async-start(), calls=%async_computation.17 | async-start | bytes 4325376 | tf_op jit(solution)/shard_map/all_gather | solution.py:414
  356.1 233.5 %all-gather.14.cloned.1.call-start = ((), (), s32[]{:S(2)}) async-start(), calls=%async_computation.18 | async-start | bytes 2162688 | tf_op jit(solution)/shard_map/all_gather | solution.py:415
  356.7 280.8 %all-gather.16.cloned.1.call-start = ((), (), s32[]{:S(2)}) async-start(), calls=%async_computation.19 | async-start | bytes 2621440 | tf_op jit(solution)/shard_map/all_gather | solution.py:442
  536.7 4.2 collective-permute-start
  539.4 5.6 collective-permute-start.1
  546.4 46.5 %copy-start.65 = (bf16[1024]{0:T(1024)(128)(2,1)S(1)}, bf16[1024]{0:T(1024)(128)(2,1)}, u32[]{:S(2)}) copy-start(bf16[1024]{0:T(1024)(128)(2,1)} %param.39) | copy-start | bytes 6148
  592.9 211.9 %all-reduce.26.cloned.1.call-start = ((), (), s32[]{:S(2)}) async-start(), calls=%async_computation.20 | async-start | bytes 8388608 | tf_op jit(solution)/shard_map/psum | solution.py:65
  650.8 258.3 %all-reduce.28.cloned.1.call-start = ((), (), s32[]{:S(2)}) async-start(), calls=%async_computation.21 | async-start | bytes 4194304 | tf_op jit(solution)/shard_map/psum | solution.py:69
  823.8 90.1 %copy-start.16 = (bf16[2,512,1024]{2,1,0:T(8,128)(2,1)S(1)}, bf16[2,512,1024]{2,1,0:T(8,128)(2,1)}, u32[]{:S(2)}) copy-start(bf16[2,512,1024]{2,1,0:T(8,128)(2,1)} %param.43) | copy-start | bytes 6291460
  823.8 159.0 %all-gather.18.cloned.1.call-start = ((), (), s32[]{:S(2)}) async-start(), calls=%async_computation.22 | async-start | bytes 2621440 | tf_op jit(solution)/shard_map/all_gather | solution.py:454
  923.6 6.6 collective-permute-start.2
  925.1 5.9 collective-permute-start.3
  935.5 120.5 %reduce-scatter.23.cloned.1.call-start = ((), (), s32[]{:S(2)}) async-start(), calls=%async_computation.23 | async-start | bytes 2621440 | tf_op jit(solution)/shard_map/reduce_scatter | solution.py:245
  1004.5 15.7 copy-start.25
  1025.9 63.7 %reduce-scatter.25.cloned.1.call-start = ((), (), s32[]{:S(2)}) async-start(), calls=%async_computation.24 | async-start | bytes 2621440 | tf_op jit(solution)/shard_map/reduce_scatter | solution.py:251
  1038.2 145.4 %all-reduce.30.cloned.1.call-start = ((), (), s32[]{:S(2)}) async-start(), calls=%async_computation.25 | async-start | bytes 4194304 | tf_op jit(solution)/shard_map/psum | solution.py:69
  1046.1 13.8 copy-start.35
  1046.1 43.5 %copy-start.47 = (bf16[1024,256]{1,0:T(8,128)(2,1)S(1)}, bf16[1024,256]{1,0:T(8,128)(2,1)}, u32[]{:S(2)}) copy-start(bf16[1024,256]{1,0:T(8,128)(2,1)} %param.31) | copy-start | bytes 1572868
  1095.4 229.7 %reduce-scatter.45.cloned.1.call-start = ((), (), s32[]{:S(2)}) async-start(), calls=%async_computation.36 | async-start | bytes 540672
  1096.5 273.0 %reduce-scatter.47.cloned.1.call-start = ((), (), s32[]{:S(2)}) async-start(), calls=%async_computation.37 | async-start | bytes 2359296
  1104.5 309.3 %reduce-scatter.39.cloned.1.call-start = ((), (), s32[]{:S(2)}) async-start(), calls=%async_computation.33 | async-start | bytes 2359296 | tf_op jit(solution)/shard_map/reduce_scatter | solution.py:506
  1110.7 447.0 %reduce-scatter.43.cloned.1.call-start = ((), (), s32[]{:S(2)}) async-start(), calls=%async_computation.35 | async-start | bytes 589824
  1117.4 441.9 %reduce-scatter.29.cloned.1.call-start = ((), (), s32[]{:S(2)}) async-start(), calls=%async_computation.28 | async-start | bytes 589824 | tf_op jit(solution)/shard_map/reduce_scatter | solution.py:488
  1120.9 439.9 %reduce-scatter.33.cloned.1.call-start = ((), (), s32[]{:S(2)}) async-start(), calls=%async_computation.30 | async-start | bytes 589824 | tf_op jit(solution)/shard_map/reduce_scatter | solution.py:494
  1123.6 60.1 %copy-start.52 = (f32[2,512]{1,0:T(2,128)S(1)}, f32[2,512]{1,0:T(2,128)}, u32[]{:S(2)}) copy-start(f32[2,512]{1,0:T(2,128)} %copy-done.51) | copy-start | bytes 12292
  1123.6 60.1 %copy-start.58 = (f32[1024]{0:T(1024)S(1)}, f32[1024]{0:T(1024)}, u32[]{:S(2)}) copy-start(f32[1024]{0:T(1024)} %copy-done.57) | copy-start | bytes 12292
  1123.6 60.1 %copy-start.60 = (f32[2,512]{1,0:T(2,128)S(1)}, f32[2,512]{1,0:T(2,128)}, u32[]{:S(2)}) copy-start(f32[2,512]{1,0:T(2,128)} %copy-done.59) | copy-start | bytes 12292
  1123.6 439.9 %reduce-scatter.31.cloned.1.call-start = ((), (), s32[]{:S(2)}) async-start(), calls=%async_computation.29 | async-start | bytes 589824 | tf_op jit(solution)/shard_map/reduce_scatter | solution.py:491
  1126.3 438.7 %all-reduce.32.cloned.1.call-start = ((), (), s32[]{:S(2)}) async-start(), calls=%async_computation.26 | async-start | bytes 4194304 | tf_op jit(solution)/shard_map/psum | solution.py:69
  1201.6 406.2 %reduce-scatter.41.cloned.1.call-start = ((), (), s32[]{:S(2)}) async-start(), calls=%async_computation.34 | async-start | bytes 2359296
  1212.5 439.5 %reduce-scatter.27.cloned.1.call-start = ((), (), s32[]{:S(2)}) async-start(), calls=%async_computation.27 | async-start | bytes 2359296 | tf_op jit(solution)/shard_map/reduce_scatter | solution.py:479
  1217.9 585.8 %reduce-scatter.37.cloned.1.call-start = ((), (), s32[]{:S(2)}) async-start(), calls=%async_computation.32 | async-start | bytes 4325376 | tf_op jit(solution)/shard_map/reduce_scatter | solution.py:518
  1222.3 768.3 %reduce-scatter.35.cloned.1.call-start = ((), (), s32[]{:S(2)}) async-start(), calls=%async_computation.31 | async-start | bytes 8650752 | tf_op jit(solution)/shard_map/reduce_scatter | solution.py:517
  1552.2 12.8 copy-start.8
  1552.2 12.8 copy-start.50
  1552.2 12.8 copy-start.54
  1552.2 12.8 copy-start.56
  1556.9 11.6 copy-start.61
  1584.1 406.4 %copy-start.1 = (bf16[1024,1024]{1,0:T(8,128)(2,1)S(1)}, bf16[1024,1024]{1,0:T(8,128)(2,1)}, u32[]{:S(2)}) copy-start(bf16[1024,1024]{1,0:T(8,128)(2,1)} %param.41) | copy-start | bytes 6291460
  (67 other events, 281.4 us)
Sparse Core Ops, SparseCore 0:
  21.0 157.7 all-reduce.21
  187.5 21.5 all-gather.9
  211.2 22.5 all-gather.7
  355.7 163.3 all-reduce.23
  593.0 44.4 all-gather.15
  650.9 153.7 all-reduce.25
  824.0 85.0 all-reduce.27
  935.6 47.1 all-gather.17
  1026.0 29.9 reduce-scatter.22
  1058.4 31.1 reduce-scatter.24
  1095.5 88.1 all-reduce.29
  1201.7 87.7 all-reduce.31
Sparse Core Ops, SparseCore 1:
  359.0 172.1 all-gather.11
  534.0 55.5 all-gather.13
  1098.1 227.0 reduce-scatter.44
  1328.4 41.1 reduce-scatter.46
  1372.8 41.0 reduce-scatter.38
  1417.0 34.1 reduce-scatter.42
  1454.7 34.0 reduce-scatter.28
  1491.7 34.0 reduce-scatter.32
  1529.3 34.1 reduce-scatter.30
  1566.8 41.0 reduce-scatter.40
  1611.0 41.0 reduce-scatter.26
  1654.8 148.8 reduce-scatter.36
  1806.5 184.0 reduce-scatter.34
where the time goes:
time: 2020 us; the launch traced here: 2000 us
  waiting for transfers between devices  1220 us (60%)
  local copies, waits for them, and re-layouts  313 us (15%)
  blocking collectives  169 us (8%)
  matrix products  155 us (8%)
  other arithmetic  112 us (6%)
    psum x3, waiting for transfers between devices, reduce_branch(): return lax.psum(partial_out, 'heads')  357 us
    reduce_scatter x1, waiting for transfers between devices, on_device(): lax.psum_scatter(pw_in_g, ('dp', 'seq', 'heads'), scatter_dimension=0, ti...  187 us
    reduce_scatter x1, waiting for transfers between devices, on_device(): lax.psum_scatter(pw_out_g, ('dp', 'seq', 'heads'), scatter_dimension=0, t...  150 us
    psum x3, waiting for transfers between devices, reduce_normed(): lax.psum(partial_grad.astype(jnp.bfloat16), 'heads').astype(jnp.float32)  142 us
    unnamed x29, waiting for transfers between devices  113 us
    unnamed x192, local copies, waits for them, and re-layouts  110 us
    unnamed x3, blocking collectives  99.6 us
    all_gather x1, blocking collectives, on_device(): lax.all_gather(depthwise, ('dp', 'seq', 'heads'), axis=1, tiled=True)  69.5 us
  transfers between devices with their start and end apart: 29, of which 21 were waited for; matrix products, arithmetic and copies ran while one was open for 22% of the time, Pallas kernels for 0%

commit v1 on v0

v1 whole, which is shorter than its diff:
```python
import functools
import math
import jax
import jax.numpy as jnp
from jax import lax
from jax.experimental import pallas as pl
from jax.experimental.pallas import tpu as pltpu
from jax.sharding import PartitionSpec as P

HEAD_DIM=128
NEGATIVE=-1e30
LOG2E=math.log2(math.e)
TILE=256

def bias_tiles_kernel(win_ref, out_ref):
    width = win_ref.shape[2]
    rows = jnp.broadcast_to(win_ref[0], (8, width))
    rows = pltpu.roll(rows, width - (TILE - 1), 1, stride=1, stride_axis=0)
    step = 8
    while step < TILE:
        rows = jnp.concatenate([rows, pltpu.roll(rows, step, 1)], axis=0)
        step *= 2
    for t in range(out_ref.shape[1]):
        out_ref[0, t] = rows[:, t * TILE : (t + 1) * TILE]

def bias_tiles(window):
    heads, width = window.shape
    tiles = width // TILE - 1
    return pl.pallas_call(
        bias_tiles_kernel,
        grid=(heads,),
        in_specs=[pl.BlockSpec((1, 1, width), lambda h: (h, 0, 0))],
        out_specs=pl.BlockSpec((1, tiles, TILE, TILE), lambda h: (h, 0, 0, 0)),
        out_shape=jax.ShapeDtypeStruct((heads, tiles, TILE, TILE), jnp.float32),
        cost_estimate=pl.CostEstimate(flops=heads*tiles*TILE*TILE*4, transcendentals=0, bytes_accessed=heads*tiles*TILE*TILE*4),
    )(window[:, None])

def offset_sums_kernel(tiles_ref, out_ref, wide):
    tiles = tiles_ref.shape[1]
    for t in range(tiles):
        wide[:, t * TILE : (t + 1) * TILE] = tiles_ref[0, t]
    wide[:, tiles * TILE :] = jnp.zeros((TILE, TILE), jnp.float32)
    rows = wide[...]
    half = TILE // 2
    while half >= 1:
        rows = pltpu.roll(rows[:half], half, 1) + rows[half:]
        half //= 2
    out_ref[0] = rows

def offset_sums(tile_grads):
    heads, tiles = tile_grads.shape[:2]
    width = (tiles + 1) * TILE
    return pl.pallas_call(
        offset_sums_kernel,
        grid=(heads,),
        in_specs=[pl.BlockSpec((1, tiles, TILE, TILE), lambda h: (h, 0, 0, 0))],
        out_specs=pl.BlockSpec((1, 1, width), lambda h: (h, 0, 0)),
        out_shape=jax.ShapeDtypeStruct((heads, 1, width), jnp.float32),
        scratch_shapes=[pltpu.VMEM((TILE, width), jnp.float32)],
        cost_estimate=pl.CostEstimate(flops=heads*tiles*TILE*TILE*4, transcendentals=0, bytes_accessed=heads*tiles*TILE*TILE*4),
    )(tile_grads)[:, 0]

def columns_of(head, per_shard):
    shard, at = head // per_shard, head % per_shard
    key = (shard * 2 * per_shard + at) * HEAD_DIM
    value = key + per_shard * HEAD_DIM
    return pl.multiple_of(key, HEAD_DIM), pl.multiple_of(value, HEAD_DIM)

def load_pieces(scal, pieces, whole, sems):
    local = pieces[0].shape[1]
    copies = []
    count = sum(p.shape[0] for p in pieces)
    nbits = count.bit_length() - 1
    rel = [0]
    n = 0
    for p in pieces:
        ids = [0] if p is pieces[0] else None
        if ids is None:
            bit = nbits - 1 - (n.bit_length() - 1)
            ids = [r ^ (1 << bit) for r in rel]
            rel = rel + ids
        for k, r in enumerate(ids):
            at = pl.multiple_of((scal[0] ^ r) * local, local)
            copies.append(pltpu.make_async_copy(p.at[k], whole.at[pl.ds(at, local)], sems.at[n]))
            n += 1
    for c in copies: c.start()
    for c in copies: c.wait()

def forward_kernel(scal, per_shard, pieces_n, *refs):
    q_ref, bias_ref, qid_ref, kid_ref = refs[:4]
    pieces = refs[4 : 4 + pieces_n]
    out_ref, lse_ref, whole, sems = refs[4 + pieces_n :]
    head = pl.program_id(0)
    @pl.when(head == 0)
    def _(): load_pieces(scal, pieces, whole, sems)
    kcol, vcol = columns_of(head, per_shard)
    scale = LOG2E * HEAD_DIM ** -0.5
    nk = whole.shape[0] // TILE
    for qb in range(q_ref.shape[0] // TILE):
        q = q_ref[qb * TILE : (qb + 1) * TILE, :]
        qid = qid_ref[:, qb * TILE : (qb + 1) * TILE]
        def body(kb, carry):
            top, total, acc = carry
            at = pl.multiple_of(kb * TILE, TILE)
            k = whole[pl.ds(at, TILE), pl.ds(kcol, HEAD_DIM)]
            v = whole[pl.ds(at, TILE), pl.ds(vcol, HEAD_DIM)]
            s = lax.dot_general(k, q, (((1,), (1,)), ((), ())), preferred_element_type=jnp.float32)
            s = s * scale + bias_ref[0, qb - kb + nk - 1]
            s = jnp.where(kid_ref[pl.ds(at, TILE), :] == qid, s, NEGATIVE)
            new_top = jnp.maximum(top, jnp.max(s, axis=0, keepdims=True))
            p = jnp.exp2(s - new_top)
            fade = jnp.exp2(top - new_top)
            total = total * fade + jnp.sum(p, axis=0, keepdims=True)
            acc = acc * fade + lax.dot_general(v, p.astype(jnp.bfloat16), (((0,), (0,)), ((), ())), preferred_element_type=jnp.float32)
            return new_top, total, acc
        top, total, acc = lax.fori_loop(scal[1 + 2 * qb], scal[2 + 2 * qb], body, (
            jnp.full((1, TILE), NEGATIVE, jnp.float32), jnp.zeros((1, TILE), jnp.float32), jnp.zeros((HEAD_DIM, TILE), jnp.float32)))
        out_ref[qb * TILE : (qb + 1) * TILE, :] = (acc / total).T.astype(jnp.bfloat16)
        lse_ref[0, :, qb * TILE : (qb + 1) * TILE] = top + jnp.log2(total)

def attend(scalars, q, tiles, qid, kid, pieces, per_shard):
    tokens, width = q.shape
    heads = width // HEAD_DIM
    length = kid.shape[0]
    count = sum(p.shape[0] for p in pieces)
    n_tiles = tiles.shape[1]
    fn = lambda scal, *refs: forward_kernel(scal, per_shard, len(pieces), *refs)
    flops = 4 * heads * tokens * length * HEAD_DIM
    return pl.pallas_call(
        fn,
        grid_spec=pltpu.PrefetchScalarGridSpec(
            num_scalar_prefetch=1, grid=(heads,),
            in_specs=[
                pl.BlockSpec((tokens, HEAD_DIM), lambda h, s: (0, h)),
                pl.BlockSpec((1, n_tiles, TILE, TILE), lambda h, s: (h, 0, 0, 0)),
                pl.BlockSpec((1, tokens), lambda h, s: (0, 0)),
                pl.BlockSpec((length, 1), lambda h, s: (0, 0)),
            ] + [pl.BlockSpec(memory_space=pl.ANY)] * len(pieces),
            out_specs=[
                pl.BlockSpec((tokens, HEAD_DIM), lambda h, s: (0, h)),
                pl.BlockSpec((1, 1, tokens), lambda h, s: (h, 0, 0)),
            ],
            scratch_shapes=[pltpu.VMEM((length, pieces[0].shape[-1]), jnp.bfloat16), pltpu.SemaphoreType.DMA((count,))],
        ),
        out_shape=[jax.ShapeDtypeStruct((tokens, width), jnp.bfloat16), jax.ShapeDtypeStruct((heads, 1, tokens), jnp.float32)],
        cost_estimate=pl.CostEstimate(flops=flops, transcendentals=heads*tokens*length, bytes_accessed=heads*n_tiles*TILE*TILE*4),
    )(scalars, q, tiles, qid, kid, *pieces)

def backward_kernel(scal, per_shard, pieces_n, *refs):
    q_ref, bias_ref, qid_ref, kid_ref, mix_ref, dmix_ref, lse_ref = refs[:7]
    pieces = refs[7 : 7 + pieces_n]
    dq_ref, dkv_ref, dtile_ref, whole, dk_acc, dv_acc, sems = refs[7 + pieces_n :]
    head = pl.program_id(0)
    @pl.when(head == 0)
    def _(): load_pieces(scal, pieces, whole, sems)
    kcol, vcol = columns_of(head, per_shard)
    scale = HEAD_DIM ** -0.5
    nk = whole.shape[0] // TILE
    dk_acc[...] = jnp.zeros_like(dk_acc)
    dv_acc[...] = jnp.zeros_like(dv_acc)
    dtile_ref[...] = jnp.zeros_like(dtile_ref)
    for qb in range(q_ref.shape[0] // TILE):
        rows = slice(qb * TILE, (qb + 1) * TILE)
        q = q_ref[rows, :]
        qid = qid_ref[:, rows]
        dmix = dmix_ref[rows, :]
        lse = lse_ref[0, :, rows]
        delta = jnp.sum((dmix.astype(jnp.float32) * mix_ref[rows, :].astype(jnp.float32)).T, axis=0, keepdims=True)
        def body(kb, dq):
            at = pl.multiple_of(kb * TILE, TILE)
            k = whole[pl.ds(at, TILE), pl.ds(kcol, HEAD_DIM)]
            v = whole[pl.ds(at, TILE), pl.ds(vcol, HEAD_DIM)]
            s = lax.dot_general(k, q, (((1,), (1,)), ((), ())), preferred_element_type=jnp.float32)
            s = s * (scale * LOG2E) + bias_ref[0, qb - kb + nk - 1]
            s = jnp.where(kid_ref[pl.ds(at, TILE), :] == qid, s, NEGATIVE)
            p = jnp.exp2(s - lse)
            dp = lax.dot_general(v, dmix, (((1,), (1,)), ((), ())), preferred_element_type=jnp.float32)
            ds = p * (dp - delta)
            dtile_ref[0, qb - kb + nk - 1] += ds
            low = ds.astype(jnp.bfloat16)
            dv_acc[pl.ds(at, TILE), :] += jnp.dot(p.astype(jnp.bfloat16), dmix, preferred_element_type=jnp.float32)
            dk_acc[pl.ds(at, TILE), :] += jnp.dot(low, q, preferred_element_type=jnp.float32)
            return dq + lax.dot_general(k, low, (((0,), (0,)), ((), ())), preferred_element_type=jnp.float32)
        dq = lax.fori_loop(scal[1 + 2 * qb], scal[2 + 2 * qb], body, jnp.zeros((HEAD_DIM, TILE), jnp.float32))
        dq_ref[rows, :] = (dq * scale).T.astype(jnp.bfloat16)
    count, local = dkv_ref.shape[:2]
    nbits = count.bit_length() - 1
    for block in range(count):
        diff = scal[0] ^ block
        slot = 0
        for bit in range(nbits):
            slot = slot | (((diff >> bit) & 1) << (nbits - 1 - bit))
        rows = slice(block * local, (block + 1) * local)
        dkv_ref[slot, :, pl.ds(kcol, HEAD_DIM)] = (dk_acc[rows, :] * scale).astype(jnp.bfloat16)
        dkv_ref[slot, :, pl.ds(vcol, HEAD_DIM)] = dv_acc[rows, :].astype(jnp.bfloat16)

def attend_back(scalars, q, tiles, qid, kid, mixture, mix_grad, lse, pieces, per_shard):
    tokens, width = q.shape
    heads = width // HEAD_DIM
    length = kid.shape[0]
    count = sum(p.shape[0] for p in pieces)
    n_tiles = tiles.shape[1]
    kvw = pieces[0].shape[-1]
    fn = lambda scal, *refs: backward_kernel(scal, per_shard, len(pieces), *refs)
    head_block = pl.BlockSpec((tokens, HEAD_DIM), lambda h, s: (0, h))
    tile_block = pl.BlockSpec((1, n_tiles, TILE, TILE), lambda h, s: (h, 0, 0, 0))
    return pl.pallas_call(
        fn,
        grid_spec=pltpu.PrefetchScalarGridSpec(
            num_scalar_prefetch=1, grid=(heads,),
            in_specs=[head_block, tile_block,
                pl.BlockSpec((1, tokens), lambda h, s: (0, 0)),
                pl.BlockSpec((length, 1), lambda h, s: (0, 0)),
                head_block, head_block,
                pl.BlockSpec((1, 1, tokens), lambda h, s: (h, 0, 0)),
            ] + [pl.BlockSpec(memory_space=pl.ANY)] * len(pieces),
            out_specs=[head_block,
                pl.BlockSpec((count, length // count, kvw), lambda h, s: (0, 0, 0)),
                tile_block],
            scratch_shapes=[pltpu.VMEM((length, kvw), jnp.bfloat16), pltpu.VMEM((length, HEAD_DIM), jnp.float32), pltpu.VMEM((length, HEAD_DIM), jnp.float32), pltpu.SemaphoreType.DMA((count,))],
        ),
        out_shape=[jax.ShapeDtypeStruct((tokens, width), jnp.bfloat16),
                   jax.ShapeDtypeStruct((count, length // count, kvw), jnp.bfloat16),
                   jax.ShapeDtypeStruct(tiles.shape, jnp.float32)],
        compiler_params=pltpu.CompilerParams(vmem_limit_bytes=50 * 1024 * 1024),
        cost_estimate=pl.CostEstimate(flops=10 * heads * tokens * length * HEAD_DIM, transcendentals=heads*tokens*length, bytes_accessed=2*heads*n_tiles*TILE*TILE*4),
    )(scalars, q, tiles, qid, kid, mixture, mix_grad, lse, *pieces)


EPSILON = 1e-05
KERNEL = 5
HIGHEST = lax.Precision.HIGHEST


def bits(count):
    return list(range(count.bit_length() - 1))


def swap(array, axis, bit):
    count = lax.axis_size(axis)
    return lax.ppermute(array, axis, [(i, i ^ (1 << bit)) for i in range(count)])


def bit_of(axis, bit):
    return (lax.axis_index(axis) >> bit) & 1


def row_dims(axes):
    return [(axis, bit) for axis in axes for bit in reversed(bits(lax.axis_size(axis)))]


def orders():
    seq = [("seq", bit) for bit in reversed(bits(lax.axis_size("seq")))]
    dp = [("dp", bit) for bit in reversed(bits(lax.axis_size("dp")))]
    near, far = seq[-1:], seq[:-1]
    return dp + far + near, far + dp + near


def gather_rows(piece, order, axes=("dp", "seq")):
    dims = row_dims(axes)
    array = piece.reshape((1,) * len(dims) + piece.shape)
    for axis, bit in order:
        dim = dims.index((axis, bit))
        other = swap(array, axis, bit)
        lower = bit_of(axis, bit) == 0
        array = jnp.concatenate(
            [jnp.where(lower, array, other), jnp.where(lower, other, array)], axis=dim
        )
    return array.reshape(-1, piece.shape[-1])


def own_rows(array, axes=("dp", "seq")):
    count = math.prod(lax.axis_size(axis) for axis in axes)
    part = array.shape[0] // count
    return lax.dynamic_slice_in_dim(array, lax.axis_index(axes) * part, part, 0)


def outer(left, right):
    return lax.dot_general(
        left, right, (((0,), (0,)), ((), ())), preferred_element_type=jnp.float32
    )


def plain(left, right):
    return jnp.dot(left, right, preferred_element_type=jnp.float32)


def against(left, right):
    return lax.dot_general(
        left, right, (((1,), (1,)), ((), ())), preferred_element_type=jnp.float32
    )


def scatter_rows(low, right, order, axes=("dp", "seq")):
    dims = row_dims(axes)
    tokens, rows = low.shape
    part = rows >> len(dims)
    (axis, bit), later = order[0], order[1:]
    dim = dims.index((axis, bit))
    stride = part << (len(dims) - 1 - dim)
    pairs = rows // (2 * stride)
    lower = bit_of(axis, bit) == 0
    first = [low[:, (2 * i) * stride : (2 * i + 1) * stride] for i in range(pairs)]
    second = [low[:, (2 * i + 1) * stride : (2 * i + 2) * stride] for i in range(pairs)]
    first, second = jnp.concatenate(first, 1), jnp.concatenate(second, 1)
    sent = outer(jnp.where(lower, second, first), right).astype(jnp.bfloat16)
    came = swap(sent, axis, bit)
    array = outer(jnp.where(lower, first, second), right) + came.astype(jnp.float32)
    shape = [2] * len(dims) + [part, right.shape[1]]
    shape[dim] = 1
    array = array.reshape(shape)
    for axis, bit in later:
        array = array.astype(jnp.bfloat16)
        dim = dims.index((axis, bit))
        here = bit_of(axis, bit)
        kept = lax.dynamic_index_in_dim(array, here, dim)
        sent = lax.dynamic_index_in_dim(array, 1 - here, dim)
        array = kept.astype(jnp.float32) + swap(sent, axis, bit).astype(jnp.float32)
    return array.reshape(part, right.shape[1])


def norm_forward(values, gain_vec):
    centred = values - jnp.mean(values, axis=-1, keepdims=True)
    inverse = lax.rsqrt(jnp.mean(centred * centred, axis=-1, keepdims=True) + EPSILON)
    normed = centred * inverse
    return (normed * gain_vec.astype(jnp.float32), normed, inverse)


def norm_backward(gradient, normed, inverse, gain_vec):
    scaled = gradient * gain_vec.astype(jnp.float32)
    mean_grad = jnp.mean(scaled, axis=-1, keepdims=True)
    second = jnp.mean(scaled * normed, axis=-1, keepdims=True)
    gain_grad = jnp.sum((gradient * normed).reshape(-1, gradient.shape[-1]), axis=0)
    return (inverse * (scaled - mean_grad - normed * second), gain_grad)


def silu_slope(values):
    sigmoid = jax.nn.sigmoid(values)
    return sigmoid * (1.0 + values * (1.0 - sigmoid))


def team_sum(partial):
    for bit in bits(lax.axis_size("heads"))[:-1]:
        partial = partial + swap(partial.astype(jnp.bfloat16), "heads", bit).astype(jnp.float32)
    return partial


def sum_everyone(array):
    for axis in ("seq", "dp", "heads"):
        for bit in bits(lax.axis_size(axis)):
            array = array + swap(array, axis, bit)
    return array


def far_swap(array):
    return swap(array, "heads", bits(lax.axis_size("heads"))[-1])


def ffn_forward(stream, gain_vec, weights):
    normed_out, normed, inverse = norm_forward(stream, gain_vec)
    low = normed_out.astype(jnp.bfloat16)
    pres, acts, partial = [], [], 0.0
    for weight_in, weight_out in weights:
        pre = plain(low, weight_in)
        act = jax.nn.silu(pre).astype(jnp.bfloat16)
        partial = partial + plain(act, weight_out)
        pres.append(pre)
        acts.append(act)
    return (stream + 0.5 * team_sum(partial), (normed, inverse, low, pres, acts))


def ffn_backward(gradient, saved_state, gain_vec, weights):
    normed, inverse, low, pres, acts = saved_state
    order_a, order_b = orders()
    branch_low = (0.5 * gradient).astype(jnp.bfloat16)
    partial, pre_lows = 0.0, []
    for (weight_in, weight_out), pre in zip(weights, pres):
        pre_low = (against(branch_low, weight_out) * silu_slope(pre)).astype(jnp.bfloat16)
        partial = partial + against(pre_low, weight_in)
        pre_lows.append(pre_low)
    normed_grad = team_sum(partial)
    out_grad = scatter_rows(branch_low, jnp.concatenate(acts, 1), order_b[::-1])
    in_grad = scatter_rows(low, jnp.concatenate(pre_lows, 1), order_a[::-1])
    stream_part, gain_grad = norm_backward(normed_grad, normed, inverse, gain_vec)
    hidden = in_grad.shape[1] // 2
    came = far_swap(
        jnp.concatenate([in_grad[:, hidden:], out_grad[:, hidden:]], 1).astype(jnp.bfloat16)
    ).astype(jnp.float32)
    in_grad = in_grad[:, :hidden] + came[:, :hidden]
    out_grad = (out_grad[:, :hidden] + came[:, hidden:]).T
    return (gradient + stream_part, gain_grad, in_grad, out_grad)


def halo(array, reach):
    peers, length = lax.axis_size("seq"), array.shape[0]
    up = [(i, i + 1) for i in range(peers - 1)]
    down = [(j, i) for i, j in up]
    before = lax.ppermute(array[length - reach :], "seq", up)
    after = lax.ppermute(array[:reach], "seq", down)
    return jnp.concatenate([before, array, after], axis=0)


def conv_forward(stream, window_ids, weights):
    in_weight, out_weight, taps, gain_one, gain_two = weights
    tokens, width = stream.shape
    reach = KERNEL // 2
    normed_out, normed, inverse = norm_forward(stream, gain_one)
    low = normed_out.astype(jnp.bfloat16)
    doubled = plain(low, in_weight)
    gate = jax.nn.sigmoid(doubled[:, width:])
    glu_low = (doubled[:, :width] * gate).astype(jnp.bfloat16)
    padded = halo(glu_low, reach)
    centre = window_ids[reach : reach + tokens]
    taps_float = taps.astype(jnp.float32)
    depth = jnp.zeros((tokens, width), jnp.float32)
    for k in range(KERNEL):
        same = (window_ids[k : k + tokens] == centre).astype(jnp.float32)[:, None]
        depth = depth + padded[k : k + tokens].astype(jnp.float32) * taps_float[k] * same
    norm_two, hat_two, inverse_two = norm_forward(depth, gain_two)
    swish_low = jax.nn.silu(norm_two).astype(jnp.bfloat16)
    branch = plain(swish_low, out_weight)
    saved = (normed, inverse, low, doubled, gate, padded, hat_two, inverse_two, norm_two, swish_low)
    return (stream + branch, saved)


def conv_backward(gradient, saved, window_ids, weights):
    in_weight, out_weight, taps, gain_one, gain_two = weights
    normed, inverse, low, doubled, gate, padded, hat_two, inverse_two, norm_two, swish_low = saved
    tokens, width = gradient.shape
    reach = KERNEL // 2
    branch_low = gradient.astype(jnp.bfloat16)
    swish_grad = against(branch_low, out_weight)
    depth_grad, gain_two_grad = norm_backward(
        swish_grad * silu_slope(norm_two), hat_two, inverse_two, gain_two
    )
    depth_low = depth_grad.astype(jnp.bfloat16)
    beside = halo(depth_low, reach)
    centre = window_ids[reach : reach + tokens]
    taps_float = taps.astype(jnp.float32)
    depth_float = depth_low.astype(jnp.float32)
    glu_grad = jnp.zeros((tokens, width), jnp.float32)
    tap_grads = []
    for k in range(KERNEL):
        same = (window_ids[k : k + tokens] == centre).astype(jnp.float32)[:, None]
        tap_grads.append(
            jnp.sum(depth_float * padded[k : k + tokens].astype(jnp.float32) * same, axis=0)
        )
        mirror = 2 * reach - k
        back = (window_ids[mirror : mirror + tokens] == centre).astype(jnp.float32)[:, None]
        glu_grad = (
            glu_grad + beside[mirror : mirror + tokens].astype(jnp.float32) * taps_float[k] * back
        )
    gate_in = doubled[:, :width]
    doubled_low = jnp.concatenate(
        [glu_grad * gate, glu_grad * gate_in * gate * (1.0 - gate)], axis=-1
    ).astype(jnp.bfloat16)
    normed_grad = against(doubled_low, in_weight)
    team = lax.axis_size("heads") // 2
    share = tokens // team
    mine = (lax.axis_index("heads") % team) * share
    cut = lambda array: lax.dynamic_slice_in_dim(array, mine, share, 0)
    order_a, order_b = orders()
    axes = ("dp", "seq", "heads")
    heads = [("heads", bit) for bit in reversed(bits(lax.axis_size("heads")))]
    out_grad = scatter_rows(cut(swish_low), cut(branch_low), order_b[::-1] + heads, axes)
    in_grad = scatter_rows(cut(low), cut(doubled_low), order_a[::-1] + heads, axes)
    part, gain_one_grad = norm_backward(normed_grad, normed, inverse, gain_one)
    small = [gain_one_grad, gain_two_grad] + tap_grads
    return (gradient + part, in_grad, out_grad, small)


def on_device(
    frames,
    segment_ids,
    bucket_of,
    ffn1_gain,
    ffn1_in,
    ffn1_out,
    attn_gain,
    query_weight,
    key_weight,
    value_weight,
    output_weight,
    position_table,
    conv_gain,
    pointwise_in,
    depthwise,
    depth_gain,
    pointwise_out,
    ffn2_gain,
    ffn2_in,
    ffn2_out,
    final_gain,
    cotangent,
):
    row_count, local, width = frames.shape
    length = segment_ids.shape[1]
    n_heads = lax.axis_size("heads")
    team = n_heads // 2
    place = lax.axis_index("heads")
    seq_at = lax.axis_index("seq")
    rows_mine = row_count // 2
    my_row = place // team
    order_a, order_b = orders()
    bf16 = jnp.bfloat16

    far_in = gather_rows(far_swap(own_rows(ffn1_in)), order_a)
    far_out = gather_rows(far_swap(own_rows(ffn1_out)), order_b)
    ffn1_weights = [(ffn1_in, ffn1_out), (far_in, far_out)]
    qkv = jnp.concatenate([query_weight, key_weight, value_weight], axis=1)
    out_cols = output_weight.shape[0]
    groups = lax.axis_size("dp") * lax.axis_size("seq")
    group_at = lax.axis_index(("dp", "seq"))
    part = width // groups
    out_piece = lax.dynamic_slice_in_dim(output_weight, group_at * part, part, 1).T
    attn_piece = far_swap(jnp.concatenate([own_rows(qkv), out_piece], axis=1))
    small_piece = jnp.concatenate([depthwise, conv_gain[None], depth_gain[None]], axis=0).T
    small_piece = jnp.pad(small_piece, ((0, 0), (0, 128 - small_piece.shape[1])))
    conv_piece = jnp.concatenate([pointwise_in, pointwise_out, small_piece], axis=1)
    for bit in bits(n_heads):
        other = swap(conv_piece, "heads", bit)
        lower = bit_of("heads", bit) == 0
        conv_piece = jnp.concatenate(
            [jnp.where(lower, conv_piece, other), jnp.where(lower, other, conv_piece)], axis=0
        )
    group_a = gather_rows(
        jnp.concatenate([attn_piece, conv_piece[:, 2 * width :]], axis=1), order_a
    )
    pw_in = gather_rows(conv_piece[:, : 2 * width], order_b)
    n_qkv = qkv.shape[1]
    far_qkv = group_a[:, :n_qkv]
    far_output = group_a[:, n_qkv : n_qkv + out_cols]
    pw_out = group_a[:, n_qkv + out_cols : n_qkv + out_cols + width]
    small_all = group_a[:, n_qkv + out_cols + width :][:, : KERNEL + 2].T
    far_in2 = gather_rows(far_swap(own_rows(ffn2_in)), order_a)
    far_out2 = gather_rows(far_swap(own_rows(ffn2_out)), order_b)
    ffn2_weights = [(ffn2_in, ffn2_out), (far_in2, far_out2)]
    taps, conv_gain_all, depth_gain_all = (
        small_all[:KERNEL],
        small_all[KERNEL],
        small_all[KERNEL + 1],
    )
    conv_weights = (pw_in, pw_out, taps, conv_gain_all, depth_gain_all)

    table = jnp.concatenate([position_table, far_swap(position_table)], axis=0)
    n_q, n_k = local // TILE, length // TILE
    reversed_buckets = jnp.pad(bucket_of[::-1], (0, 1))
    window = lax.dynamic_slice_in_dim(reversed_buckets, seq_at * local, (n_q + n_k) * TILE, 0)
    levels = lax.broadcasted_iota(jnp.int32, (position_table.shape[1], window.shape[0]), 0)
    onehot = (levels == window[None, :]).astype(jnp.float32)
    tiles = bias_tiles(jnp.dot(table, onehot, precision=HIGHEST) * LOG2E)

    outs = []
    for at in range(rows_mine):
        row = my_row * rows_mine + at
        pick = lambda array: lax.dynamic_index_in_dim(array, row, 0, keepdims=False)
        ids = pick(segment_ids)
        reach = KERNEL // 2
        ids_pad = jnp.pad(ids, (reach, reach), constant_values=-1)
        window_ids = lax.dynamic_slice_in_dim(ids_pad, seq_at * local, local + 2 * reach, 0)
        query_ids = window_ids[reach : reach + local]
        scalars = [seq_at.astype(jnp.int32)]
        for block in range(n_q):
            low_id = query_ids[block * TILE]
            top_id = query_ids[(block + 1) * TILE - 1]
            scalars.append(jnp.sum((ids < low_id).astype(jnp.int32)) // TILE)
            scalars.append((jnp.sum((ids <= top_id).astype(jnp.int32)) + TILE - 1) // TILE)
        scalars = jnp.stack(scalars)

        stream_zero = pick(frames).astype(jnp.float32)
        stream_one, ffn1_state = ffn_forward(stream_zero, ffn1_gain, ffn1_weights)

        normed_out, normed, inverse = norm_forward(stream_one, attn_gain)
        low = normed_out.astype(bf16)
        q_cols = query_weight.shape[1]
        kv = jnp.concatenate(
            [plain(low, qkv[:, q_cols:]).astype(bf16), plain(low, far_qkv[:, q_cols:]).astype(bf16)],
            axis=1,
        )[None]
        pieces = [kv]
        for bit in reversed(bits(lax.axis_size("seq"))):
            held = pieces[0] if len(pieces) == 1 else jnp.concatenate(pieces, axis=0)
            pieces.append(swap(held, "seq", bit))
        query = jnp.concatenate(
            [plain(low, qkv[:, :q_cols]).astype(bf16), plain(low, far_qkv[:, :q_cols]).astype(bf16)],
            axis=1,
        )
        per_shard = q_cols // HEAD_DIM
        mixture, log_total = attend(
            scalars, query, tiles, query_ids[None], ids[:, None], pieces, per_shard
        )
        branch = team_sum(
            plain(mixture[:, :out_cols], output_weight)
            + against(mixture[:, out_cols:], far_output)
        )
        stream_two = stream_one + branch

        stream_three, conv_state = conv_forward(stream_two, window_ids, conv_weights)
        stream_four, ffn2_state = ffn_forward(stream_three, ffn2_gain, ffn2_weights)
        final_out, final_hat, final_inverse = norm_forward(stream_four, final_gain)
        layer_low = final_out.astype(bf16)
        grad_four, final_gain_grad = norm_backward(
            pick(cotangent).astype(jnp.float32), final_hat, final_inverse, final_gain
        )
        grad_three, ffn2_gain_grad, f2_in_g, f2_out_g = ffn_backward(
            grad_four, ffn2_state, ffn2_gain, ffn2_weights
        )
        grad_two, pw_in_g, pw_out_g, conv_small = conv_backward(
            grad_three, conv_state, window_ids, conv_weights
        )

        branch_low = grad_two.astype(bf16)
        mix_grad = jnp.concatenate(
            [
                against(branch_low, output_weight).astype(bf16),
                plain(branch_low, far_output).astype(bf16),
            ],
            axis=1,
        )
        q_grad, kv_grad, tile_grads = attend_back(
            scalars, query, tiles, query_ids[None], ids[:, None], mixture, mix_grad, log_total, pieces, per_shard
        )
        for bit in bits(lax.axis_size("seq")):
            half = kv_grad.shape[0] // 2
            kv_grad = (
                kv_grad[:half].astype(jnp.float32)
                + swap(kv_grad[half:], "seq", bit).astype(jnp.float32)
            ).astype(bf16)
        kv_grad = kv_grad[0]
        kv_cols = 2 * q_cols
        own_grads = jnp.concatenate([q_grad[:, :q_cols], kv_grad[:, :kv_cols]], axis=1)
        far_grads = jnp.concatenate([q_grad[:, q_cols:], kv_grad[:, kv_cols:]], axis=1)
        normed_grad = team_sum(against(own_grads, qkv) + against(far_grads, far_qkv))
        o_g = scatter_rows(branch_low, mixture, order_b[::-1])
        qkv_g = scatter_rows(low, jnp.concatenate([own_grads, far_grads], 1), order_a[::-1])
        came = far_swap(
            jnp.concatenate([qkv_g[:, n_qkv:], o_g[:, out_cols:]], 1).astype(bf16)
        ).astype(jnp.float32)
        qkv_g = qkv_g[:, :n_qkv] + came[:, :n_qkv]
        o_g = (o_g[:, :out_cols] + came[:, n_qkv:]).T
        table_grad = lax.dot_general(
            offset_sums(tile_grads), onehot, (((1,), (1,)), ((), ())), precision=HIGHEST
        )
        stream_part, attn_gain_grad = norm_backward(normed_grad, normed, inverse, attn_gain)
        grad_one = grad_two + stream_part
        grad_zero, ffn1_gain_grad, f1_in_g, f1_out_g = ffn_backward(
            grad_one, ffn1_state, ffn1_gain, ffn1_weights
        )
        big = (f1_in_g, f1_out_g, qkv_g, o_g, pw_in_g, pw_out_g, f2_in_g, f2_out_g)
        gains = [ffn2_gain_grad, final_gain_grad] + conv_small
        outs.append((layer_low, grad_zero, big, gains, table_grad, ffn1_gain_grad, attn_gain_grad))

    total = lambda items: functools.reduce(lambda one, two: one + two, items)
    big = [total([out[2][i] for out in outs]) for i in range(8)]
    f1_in_g, f1_out_g, qkv_g, o_g, pw_in_g, pw_out_g, f2_in_g, f2_out_g = big
    gains = [total([out[3][i] for out in outs]) for i in range(len(outs[0][3]))]
    table_grad = total([out[4] for out in outs])
    per_shard = position_table.shape[0]
    all_heads = jnp.zeros((n_heads * per_shard, position_table.shape[1]), jnp.float32)
    all_heads = lax.dynamic_update_slice_in_dim(
        all_heads, team * table_grad[:per_shard], place * per_shard, 0
    )
    all_heads = lax.dynamic_update_slice_in_dim(
        all_heads, team * table_grad[per_shard:], (place ^ team) * per_shard, 0
    )
    small = jnp.concatenate([jnp.stack(gains).reshape(-1), all_heads.reshape(-1)])
    small = small.reshape(-1, 128) * (1.0 / team)
    everyone = ("dp", "seq", "heads")
    small = sum_everyone(small).reshape(-1)
    gains_all = small[: len(gains) * width].reshape(len(gains), width)
    table_all = small[len(gains) * width :].reshape(all_heads.shape)
    table_mine = lax.dynamic_slice_in_dim(table_all, place * per_shard, per_shard, 0)
    table_cols = table_mine.shape[1] // groups
    table_mine = lax.dynamic_slice_in_dim(table_mine, group_at * table_cols, table_cols, 1)
    group_part = lax.dynamic_slice_in_dim(gains_all[:2], group_at * part, part, 1)
    every = width // (groups * n_heads)
    conv_part = lax.dynamic_slice_in_dim(
        gains_all[2:], lax.axis_index(everyone) * every, every, 1
    )
    last = jnp.stack([total([out[5] for out in outs]), total([out[6] for out in outs])])
    last = last.reshape(-1, 128) * (1.0 / team)
    last = sum_everyone(last).reshape(2, width)
    last_part = lax.dynamic_slice_in_dim(last, group_at * part, part, 1)

    def both_rows(pieces):
        mine = jnp.stack(pieces)
        other = far_swap(mine.astype(bf16)).astype(mine.dtype)
        first = my_row == 0
        return jnp.concatenate([jnp.where(first, mine, other), jnp.where(first, other, mine)], 0)

    layer_out = both_rows([out[0] for out in outs])
    input_grad = both_rows([out[1] for out in outs])
    q_cols = query_weight.shape[1]
    return (
        layer_out,
        input_grad,
        last_part[0],
        f1_in_g,
        f1_out_g,
        last_part[1],
        qkv_g[:, :q_cols],
        qkv_g[:, q_cols : 2 * q_cols],
        qkv_g[:, 2 * q_cols :],
        o_g,
        table_mine,
        conv_part[0],
        pw_in_g,
        conv_part[2:],
        conv_part[1],
        pw_out_g,
        group_part[0],
        f2_in_g,
        f2_out_g,
        group_part[1],
    )


def solution(mesh):
    return jax.shard_map(
        on_device,
        mesh=mesh,
        in_specs=(
            P("dp", "seq", None),
            P("dp", None),
            P(),
            P(),
            P(None, "heads"),
            P("heads", None),
            P(),
            P(None, "heads"),
            P(None, "heads"),
            P(None, "heads"),
            P("heads", None),
            P("heads", None),
            P(("dp", "seq", "heads")),
            P(("dp", "seq", "heads"), None),
            P(None, ("dp", "seq", "heads")),
            P(("dp", "seq", "heads")),
            P(("dp", "seq", "heads"), None),
            P(),
            P(None, "heads"),
            P("heads", None),
            P(),
            P("dp", "seq", None),
        ),
        out_specs=(
            P("dp", "seq", None),
            P("dp", "seq", None),
            P(("dp", "seq")),
            P(("dp", "seq"), "heads"),
            P("heads", ("dp", "seq")),
            P(("dp", "seq")),
            P(("dp", "seq"), "heads"),
            P(("dp", "seq"), "heads"),
            P(("dp", "seq"), "heads"),
            P("heads", ("dp", "seq")),
            P("heads", ("dp", "seq")),
            P(("dp", "seq", "heads")),
            P(("dp", "seq", "heads"), None),
            P(None, ("dp", "seq", "heads")),
            P(("dp", "seq", "heads")),
            P(("dp", "seq", "heads"), None),
            P(("dp", "seq")),
            P(("dp", "seq"), "heads"),
            P("heads", ("dp", "seq")),
            P(("dp", "seq")),
        ),
        check_vma=False,
    )
```

time: 2020 us -> 882 us (0.44)
  waiting for transfers between devices: 1220 us -> 420 us
  local copies, waits for them, and re-layouts: 313 us -> 89.3 us
  blocking collectives: 169 us -> 0 us
  starting transfers between devices: 12.8 us -> 81.4 us
  Pallas kernels: 0 us -> 58.3 us
  matrix products: 155 us -> 98.5 us
    psum x6 -> x0, waiting for transfers between devices: 499 us -> none  [the longest x3 357 us: reduce_branch(): return lax.psum(partial_out, 'heads')]
    reduce_scatter x9 -> x0, waiting for transfers between devices: 460 us -> none  [the longest x1 187 us: on_device(): lax.psum_scatter(pw_in_g, ('dp', 'seq', 'heads'), scatter_dimension=0, ti...]
    ppermute x4 -> x83, waiting for transfers between devices: 5.08 us -> 420 us  [the longest x79 418 us: swap(): return lax.ppermute(array, axis, [(i, i ^ 1 << bit) for i in range(count)])]
    all_gather x6 -> x0, waiting for transfers between devices: 141 us -> none  [the longest x1 47.2 us: on_device(): lax.all_gather(piece_grad.astype(jnp.bfloat16), 'heads', axis=1, tiled=True)]
    rev x2 -> x0, local copies, waits for them, and re-layouts: 129 us -> none  [the longest x1 64.3 us: offset_bias(): spread.reshape(head_count, local_len, length + local_len)[:, ::-1, :length]]
    unnamed x29 -> x0, waiting for transfers between devices: 113 us -> none
    unnamed x3 -> x0, blocking collectives: 99.6 us -> none
    ppermute x4 -> x83, starting transfers between devices: 10.6 us -> 81.4 us  [the longest x79 74.5 us: swap(): return lax.ppermute(array, axis, [(i, i ^ 1 << bit) for i in range(count)])]
  transfers between devices with their start and end apart: 29 -> 83, of which waited for: 21 -> 40; matrix products, arithmetic and copies ran while one was open for 22% -> 26% of each run, Pallas kernels for 0% -> 7%
where the time goes in v1:
time: 882 us; the launch traced here: 867 us
  waiting for transfers between devices  420 us (48%)
  other arithmetic  108 us (12%)
  matrix products  98.5 us (11%)
  local copies, waits for them, and re-layouts  89.3 us (10%)
  starting transfers between devices  81.4 us (9%)
  Pallas kernels  58.3 us (7%)
  between operations  11.3 us (1%)
    ppermute x79, waiting for transfers between devices, swap(): return lax.ppermute(array, axis, [(i, i ^ 1 << bit) for i in range(count)])  418 us
    ppermute x79, starting transfers between devices, swap(): return lax.ppermute(array, axis, [(i, i ^ 1 << bit) for i in range(count)])  74.5 us
    unnamed x512, local copies, waits for them, and re-layouts  53.7 us
    dot_general x16, matrix products, outer(): lax.dot_general(left, right, (((0,), (0,)), ((), ())), preferred_element_...  39.8 us
    dot_general x16, matrix products, plain(): return jnp.dot(left, right, preferred_element_type=jnp.float32)  31.1 us
    dot_general x14, matrix products, against(): lax.dot_general(left, right, (((1,), (1,)), ((), ())), preferred_element_...  25.7 us
    pallas_call x1, Pallas kernels, attend_back(): pl.pallas_call(fn, grid_spec=pltpu.PrefetchScalarGridSpec(num_scalar_pref...  25.5 us
    pallas_call x1, Pallas kernels, attend(): pl.pallas_call(fn, grid_spec=pltpu.PrefetchScalarGridSpec(num_scalar_pref...  20.8 us
  transfers between devices with their start and end apart: 83, of which 40 were waited for; matrix products, arithmetic and copies ran while one was open for 26% of the time, Pallas kernels for 7%

profile of v1, /device:TPU:0, one launch (start us, length us, event | category | flops | bytes accessed | tf_op | source)
XLA Modules:
  0.0 866.6 jit_solution(9089392487000135557)
XLA Ops:
  3.3 3.1 collective-permute-start.10
  21.0 3.3 convert_reduce_fusion.1
  54.5 13.5 %collective-permute-done.24 = bf16[128,1024]{1,0:T(8,128)(2,1)S(1)} collective-permute-done((bf16[128,1024]{1,0:T(8,128)(2,1)}, bf16[128,1024]{1,0:T(8,128)(2,1)S(1)}, u32[]{:S(2)}, u32[]{:S(2)}) %collective-permute-start.24) | collective-permute-done | bytes 262176 | tf_op jit(solution)/shard_map/ppermute | solution.py:241
  73.6 3.9 collective-permute-done.1
  86.3 7.3 collective-permute-done.11
  98.0 23.1 %collective-permute-done.12 = bf16[1,1,1,128,2176]{4,3,2,1,0:T(8,128)(2,1)S(1)} collective-permute-done((bf16[1,1,1,128,2176]{4,3,2,1,0:T(8,128)(2,1)S(1)}, bf16[1,1,1,128,2176]{4,3,2,1,0:T(8,128)(2,1)S(1)}, u32[]{:S(2)}, u32[]{:S(2)}) %collective-permute-start.12) | collective-permute-done | bytes 557088 | tf_op jit(solution)/shard_map/ppermute | solution.py:241
  131.0 28.7 %collective-permute-done.13 = bf16[2,1,1,128,2176]{4,3,2,1,0:T(8,128)(2,1)S(1)} collective-permute-done((bf16[2,1,1,128,2176]{4,3,2,1,0:T(8,128)(2,1)S(1)}, bf16[2,1,1,128,2176]{4,3,2,1,0:T(8,128)(2,1)S(1)}, u32[]{:S(2)}, u32[]{:S(2)}) %collective-permute-start.13) | collective-permute-done | bytes 1114144 | tf_op jit(solution)/shard_map/ppermute | solution.py:241
  162.1 22.3 %collective-permute-done.8 = bf16[512,1024]{1,0:T(8,128)(2,1)S(1)} collective-permute-done((bf16[512,1024]{1,0:T(8,128)(2,1)S(1)}, bf16[512,1024]{1,0:T(8,128)(2,1)S(1)}, u32[]{:S(2)}, u32[]{:S(2)}) %collective-permute-start.8) | collective-permute-done | bytes 1048608 | tf_op jit(solution)/shard_map/ppermute | solution.py:241
  195.2 5.5 shard_map.365.refs_1_
  203.5 10.9 %collective-permute-done.16.refs_5_.refs_8_ = bf16[1,512,1024]{2,1,0:T(8,128)(2,1)} collective-permute-done((bf16[1,512,1024]{2,1,0:T(8,128)(2,1)S(1)}, bf16[1,512,1024]{2,1,0:T(8,128)(2,1)}, u32[]{:S(2)}, u32[]{:S(2)}) %collective-permute-start.16) | collective-permute-done | bytes 1048608 | tf_op jit(solution)/shard_map/ppermute | solution.py:241
  226.3 20.8 %shard_map.366 = (bf16[512,512]{1,0:T(8,128)(2,1)}, f32[4,1,512]{2,1,0:T(1,128)}) custom-call(s32[5]{0:T(128)} %stack.68.scal, bf16[512,512]{1,0:T(8,128)(2,1)} %pad_maximum_fusion.47.refs_0_, f32[4,9,256,256]{3,2,1,0:T(8,128)} %shard_map.365.refs_1_, s32[1,512]{1,0:T(1,128)} %bitcast.226, s32[2048,1]{1,0:T(8,128)} %copy.77.refs_3_, ...), custom_call_target="tpu_custom_call" | custom-call | flops 2147483648 | bytes 9437184 | tf_op jit(solution)/shard_map/pallas_call | solution.py:129
  257.2 19.2 %collective-permute-done.18 = bf16[512,1024]{1,0:T(8,128)(2,1)} collective-permute-done((bf16[512,1024]{1,0:T(8,128)(2,1)}, bf16[512,1024]{1,0:T(8,128)(2,1)}, u32[]{:S(2)}, u32[]{:S(2)}) %collective-permute-start.18) | collective-permute-done | bytes 1048608 | tf_op jit(solution)/shard_map/ppermute | solution.py:241
  291.3 3.2 fusion.194
  296.6 3.3 fusion.214
  308.9 3.0 fusion.215
  314.9 22.6 %collective-permute-done.32 = bf16[512,1024]{1,0:T(8,128)(2,1)} collective-permute-done((bf16[512,1024]{1,0:T(8,128)(2,1)}, bf16[512,1024]{1,0:T(8,128)(2,1)}, u32[]{:S(2)}, u32[]{:S(2)}) %collective-permute-start.32) | collective-permute-done | bytes 1048608 | tf_op jit(solution)/shard_map/ppermute | solution.py:241
  359.6 18.7 %collective-permute-done.34 = bf16[512,1024]{1,0:T(8,128)(2,1)S(1)} collective-permute-done((bf16[512,1024]{1,0:T(8,128)(2,1)S(1)}, bf16[512,1024]{1,0:T(8,128)(2,1)S(1)}, u32[]{:S(2)}, u32[]{:S(2)}) %collective-permute-start.34) | collective-permute-done | bytes 1048608 | tf_op jit(solution)/shard_map/ppermute | solution.py:241
  385.1 4.4 fusion.45
  397.6 3.8 multiply_convert_fusion.4
  413.2 25.5 %shard_map.367 = (bf16[512,512]{1,0:T(8,128)(2,1)S(1)}, bf16[4,512,1024]{2,1,0:T(8,128)(2,1)}, f32[4,9,256,256]{3,2,1,0:T(8,128)}) custom-call(s32[5]{0:T(128)S(1)} %copy-done.6, bf16[512,512]{1,0:T(8,128)(2,1)S(1)} %copy-done.3, f32[4,9,256,256]{3,2,1,0:T(8,128)} %shard_map.365.refs_1_, s32[1,512]{1,0:T(1,128)S(1)} %bitcast.227, s32[2048,1]{1,0:T(8,128)S(1)} %copy-done.2, ...), custom_call_target="tpu_custom_call" | custom-call | flops 5368709120 | bytes 18874368 | tf_op jit(solution)/shard_map/pallas_call | solution.py:207
  438.8 6.5 shard_map.368
  448.6 3.2 collective-permute-done.62
  463.5 3.4 convolution_convert_fusion
  477.3 3.2 collective-permute-done.59
  481.2 4.2 collective-permute-done.72
  485.7 28.2 %collective-permute-done.33 = bf16[1,512,1024]{2,1,0:T(8,128)(2,1)S(1)} collective-permute-done((bf16[1,512,1024]{2,1,0:T(8,128)(2,1)S(1)}, bf16[1,512,1024]{2,1,0:T(8,128)(2,1)S(1)}, u32[]{:S(2)}, u32[]{:S(2)}) %collective-permute-start.33) | collective-permute-done | bytes 1048608 | tf_op jit(solution)/shard_map/ppermute | solution.py:241
  522.7 4.4 add_convert_fusion.1
  534.5 4.3 add_convert_fusion
  539.5 17.0 %collective-permute-done.38 = bf16[1,512,1024]{2,1,0:T(8,128)(2,1)S(1)} collective-permute-done((bf16[1,512,1024]{2,1,0:T(8,128)(2,1)S(1)}, bf16[1,512,1024]{2,1,0:T(8,128)(2,1)S(1)}, u32[]{:S(2)}, u32[]{:S(2)}) %collective-permute-start.38) | collective-permute-done | bytes 1048608 | tf_op jit(solution)/shard_map/ppermute | solution.py:241
  557.0 19.8 %collective-permute-done.67 = bf16[2,1,1,2,2,32,2048]{6,5,4,3,2,1,0:T(8,128)(2,1)S(1)} collective-permute-done((bf16[2,1,1,2,2,32,2048]{6,5,4,3,2,1,0:T(8,128)(2,1)S(1)}, bf16[2,1,1,2,2,32,2048]{6,5,4,3,2,1,0:T(8,128)(2,1)S(1)}, u32[]{:S(2)}, u32[]{:S(2)}) %collective-permute-start.67) | collective-permute-done | bytes 1048608 | tf_op jit(solution)/shard_map/ppermute | solution.py:241
  584.8 4.9 collective-permute-done.68
  593.6 17.2 %collective-permute-done.69 = bf16[1,1,1,1,2,32,2048]{6,5,4,3,2,1,0:T(8,128)(2,1)S(1)} collective-permute-done((bf16[1,1,1,1,2,32,2048]{6,5,4,3,2,1,0:T(8,128)(2,1)S(1)}, bf16[1,1,1,1,2,32,2048]{6,5,4,3,2,1,0:T(8,128)(2,1)S(1)}, u32[]{:S(2)}, u32[]{:S(2)}) %collective-permute-start.69) | collective-permute-done | bytes 262176 | tf_op jit(solution)/shard_map/ppermute | solution.py:241
  610.9 3.7 collective-permute-start.70
  634.8 14.4 %collective-permute-done.40 = bf16[512,1024]{1,0:T(8,128)(2,1)S(1)} collective-permute-done((bf16[512,1024]{1,0:T(8,128)(2,1)}, bf16[512,1024]{1,0:T(8,128)(2,1)S(1)}, u32[]{:S(2)}, u32[]{:S(2)}) %collective-permute-start.40) | collective-permute-done | bytes 1048608 | tf_op jit(solution)/shard_map/ppermute | solution.py:241
  649.3 3.2 fusion.17
  654.5 5.0 convolution_convert_fusion.5
  669.3 3.3 collective-permute-done.45
  677.8 4.2 convert_bitcast_fusion.1
  692.2 48.5 %collective-permute-done.60 = bf16[128,1024]{0,1:T(8,128)(2,1)S(1)} collective-permute-done((bf16[128,1024]{0,1:T(8,128)(2,1)S(1)}, bf16[128,1024]{0,1:T(8,128)(2,1)S(1)}, u32[]{:S(2)}, u32[]{:S(2)}) %collective-permute-start.60) | collective-permute-done | bytes 262176 | tf_op jit(solution)/shard_map/ppermute | solution.py:241
  740.9 3.1 add_convert_fusion.4
  748.8 4.0 add_convert_fusion.3
  778.6 5.0 collective-permute-done.80
  786.3 9.9 %collective-permute-done.48 = bf16[2,1,1,128,2048]{3,4,2,1,0:T(8,128)(2,1)} collective-permute-done((bf16[2,1,1,128,2048]{3,4,2,1,0:T(8,128)(2,1)}, bf16[2,1,1,128,2048]{3,4,2,1,0:T(8,128)(2,1)}, u32[]{:S(2)}, u32[]{:S(2)}) %collective-permute-start.48) | collective-permute-done | bytes 1048608 | tf_op jit(solution)/shard_map/ppermute | solution.py:241
  799.5 6.6 collective-permute-done.51
  808.7 8.5 collective-permute-done.78
  817.6 8.4 collective-permute-done.49
  832.4 17.3 %collective-permute-done.82 = bf16[128,2048]{0,1:T(8,128)(2,1)S(1)} collective-permute-done((bf16[128,2048]{0,1:T(8,128)(2,1)S(1)}, bf16[128,2048]{0,1:T(8,128)(2,1)S(1)}, u32[]{:S(2)}, u32[]{:S(2)}) %collective-permute-start.82) | collective-permute-done | bytes 524320 | tf_op jit(solution)/shard_map/ppermute | solution.py:241
  851.7 9.3 %collective-permute-done.53 = bf16[128,2048]{0,1:T(8,128)(2,1)} collective-permute-done((bf16[128,2048]{0,1:T(8,128)(2,1)}, bf16[128,2048]{0,1:T(8,128)(2,1)}, u32[]{:S(2)}, u32[]{:S(2)}) %collective-permute-start.53) | collective-permute-done | bytes 524320 | tf_op jit(solution)/shard_map/ppermute | solution.py:241
  (917 shorter events, 338.6 us)
Async XLA Ops:
  3.3 45.8 %collective-permute-start.10 = (bf16[32,3200]{1,0:T(8,128)(2,1)}, bf16[32,3200]{1,0:T(8,128)(2,1)S(1)}, u32[]{:S(2)}, u32[]{:S(2)}) collective-permute-start(bf16[32,3200]{1,0:T(8,128)(2,1)} %fusion.147), channel_id=1, source_target_pairs={{0,1},{1,0},{2,3},{3,2},{4,5},{5,4},{6,7},{7,6},{8,9},{9,8},{10,11... | collective-permute-start | bytes 614408 | tf_op jit(solution)/shard_map/ppermute | solution.py:241
  8.0 44.5 %collective-permute-start.4 = (bf16[128,1024]{1,0:T(8,128)(2,1)}, bf16[128,1024]{1,0:T(8,128)(2,1)}, u32[]{:S(2)}, u32[]{:S(2)}) collective-permute-start(bf16[128,1024]{1,0:T(8,128)(2,1)} %constant_dynamic-slice_fusion.36), channel_id=1, source_target_pairs={{0,2},{1,3},{2,0},{3,1},{4,6},{5,7},{6,4},{7,5},{8,10},{9,11},{10,... | collective-permute-start | bytes 786440 | tf_op jit(solution)/shard_map/ppermute | solution.py:241
  12.3 41.8 %collective-permute-start = (bf16[128,1024]{1,0:T(8,128)(2,1)}, bf16[128,1024]{1,0:T(8,128)(2,1)}, u32[]{:S(2)}, u32[]{:S(2)}) collective-permute-start(bf16[128,1024]{1,0:T(8,128)(2,1)} %constant_dynamic-slice_fusion.37), channel_id=1, source_target_pairs={{0,2},{1,3},{2,0},{3,1},{4,6},{5,7},{6,4},{7,5},{8,10},{9,11},{10,... | collective-permute-start | bytes 786440 | tf_op jit(solution)/shard_map/ppermute | solution.py:241
  16.7 78.6 %collective-permute-start.9 = (bf16[128,1024]{1,0:T(8,128)(2,1)}, bf16[128,1024]{1,0:T(8,128)(2,1)S(1)}, u32[]{:S(2)}, u32[]{:S(2)}) collective-permute-start(bf16[128,1024]{1,0:T(8,128)(2,1)} %pad_maximum_fusion.68), channel_id=1, source_target_pairs={{0,2},{1,3},{2,0},{3,1},{4,6},{5,7},{6,4},{7,5},{8,10},{9,11},{10,... | collective-permute-start | bytes 786440 | tf_op jit(solution)/shard_map/ppermute | solution.py:241
  19.3 174.3 %collective-permute-start.15 = (f32[2,32]{1,0:T(2,128)}, f32[2,32]{1,0:T(2,128)}, u32[]{:S(2)}, u32[]{:S(2)}) collective-permute-start(f32[2,32]{1,0:T(2,128)} %param.33), channel_id=1, source_target_pairs={{0,2},{1,3},{2,0},{3,1},{4,6},{5,7},{6,4},{7,5},{8,10},{9,11},{10,... | collective-permute-start | bytes 776 | tf_op jit(solution)/shard_map/ppermute | solution.py:241
  54.1 19.5 %collective-permute-start.28 = (bf16[128,1024]{1,0:T(8,128)(2,1)S(1)}, bf16[128,1024]{1,0:T(8,128)(2,1)S(1)}, u32[]{:S(2)}, u32[]{:S(2)}) collective-permute-start(bf16[128,1024]{1,0:T(8,128)(2,1)S(1)} %constant_dynamic-slice_fusion.31), channel_id=1, source_target_pairs={{0,2},{1,3},{2,0},{3,1},{4,6},{5,7},{6,4},{7,5},{8,10},{9,11},{10,... | collective-permute-start | bytes 786440 | tf_op jit(solution)/shard_map/ppermute | solution.py:241
  73.6 20.0 %collective-permute-start.11 = (bf16[64,3200]{1,0:T(8,128)(2,1)S(1)}, bf16[64,3200]{1,0:T(8,128)(2,1)S(1)}, u32[]{:S(2)}, u32[]{:S(2)}) collective-permute-start(bf16[64,3200]{1,0:T(8,128)(2,1)S(1)} %pad_maximum_fusion.65), channel_id=1, source_target_pairs={{0,2},{1,3},{2,0},{3,1},{4,6},{5,7},{6,4},{7,5},{8,10},{9,11},{10,... | collective-permute-start | bytes 1228808 | tf_op jit(solution)/shard_map/ppermute | solution.py:241
  93.6 66.5 %collective-permute-start.26 = (bf16[2,1,1,128,1024]{4,3,2,1,0:T(8,128)(2,1)S(1)}, bf16[2,1,1,128,1024]{4,3,2,1,0:T(8,128)(2,1)S(1)}, u32[]{:S(2)}, u32[]{:S(2)}) collective-permute-start(bf16[2,1,1,128,1024]{4,3,2,1,0:T(8,128)(2,1)S(1)} %pad_maximum_fusion.48), channel_id=1, source_target_pairs={{0,8},{4,12},{8,0},{12,4},{1,9},{5,13},{9,1},{13,5},{2,10},{6,14},... | collective-permute-start | bytes 1572872 | tf_op jit(solution)/shard_map/ppermute | solution.py:241
  95.3 105.3 %collective-permute-start.30 = (bf16[1,2,1,128,1024]{4,3,2,1,0:T(8,128)(2,1)}, bf16[1,2,1,128,1024]{4,3,2,1,0:T(8,128)(2,1)}, u32[]{:S(2)}, u32[]{:S(2)}) collective-permute-start(bf16[1,2,1,128,1024]{4,3,2,1,0:T(8,128)(2,1)} %pad_maximum_fusion.49), channel_id=1, source_target_pairs={{0,16},{16,0},{1,17},{17,1},{2,18},{18,2},{3,19},{19,3},{4,20},{20... | collective-permute-start | bytes 1572872 | tf_op jit(solution)/shard_map/ppermute | solution.py:241
  97.0 24.1 %collective-permute-start.12 = (bf16[1,1,1,128,2176]{4,3,2,1,0:T(8,128)(2,1)S(1)}, bf16[1,1,1,128,2176]{4,3,2,1,0:T(8,128)(2,1)S(1)}, u32[]{:S(2)}, u32[]{:S(2)}) collective-permute-start(bf16[1,1,1,128,2176]{4,3,2,1,0:T(8,128)(2,1)S(1)} %fusion.92), channel_id=1, source_target_pairs={{0,16},{16,0},{1,17},{17,1},{2,18},{18,2},{3,19},{19,3},{4,20},{20... | collective-permute-start | bytes 1671176 | tf_op jit(solution)/shard_map/ppermute | solution.py:241
  97.8 23.6 %collective-permute-start.7 = (bf16[2,2,1,128,1024]{4,3,2,1,0:T(8,128)(2,1)S(1)}, bf16[2,2,1,128,1024]{4,3,2,1,0:T(8,128)(2,1)S(1)}, u32[]{:S(2)}, u32[]{:S(2)}) collective-permute-start(bf16[2,2,1,128,1024]{4,3,2,1,0:T(8,128)(2,1)S(1)} %pad_maximum_fusion.40), channel_id=1, source_target_pairs={{0,4},{4,0},{8,12},{12,8},{1,5},{5,1},{9,13},{13,9},{2,6},{6,2},{1... | collective-permute-start | bytes 3145736 | tf_op jit(solution)/shard_map/ppermute | solution.py:241
  121.4 40.1 %collective-permute-start.19 = (bf16[1,1,1,128,2048]{4,3,2,1,0:T(8,128)(2,1)S(1)}, bf16[1,1,1,128,2048]{4,3,2,1,0:T(8,128)(2,1)S(1)}, u32[]{:S(2)}, u32[]{:S(2)}) collective-permute-start(bf16[1,1,1,128,2048]{4,3,2,1,0:T(8,128)(2,1)S(1)} %fusion.95), channel_id=1, source_target_pairs={{0,8},{4,12},{8,0},{12,4},{1,9},{5,13},{9,1},{13,5},{2,10},{6,14},... | collective-permute-start | bytes 1572872 | tf_op jit(solution)/shard_map/ppermute | solution.py:241
  123.8 35.9 %collective-permute-start.13 = (bf16[2,1,1,128,2176]{4,3,2,1,0:T(8,128)(2,1)S(1)}, bf16[2,1,1,128,2176]{4,3,2,1,0:T(8,128)(2,1)S(1)}, u32[]{:S(2)}, u32[]{:S(2)}) collective-permute-start(bf16[2,1,1,128,2176]{4,3,2,1,0:T(8,128)(2,1)S(1)} %pad_maximum_fusion.34), channel_id=1, source_target_pairs={{0,8},{4,12},{8,0},{12,4},{1,9},{5,13},{9,1},{13,5},{2,10},{6,14},... | collective-permute-start | bytes 3342344 | tf_op jit(solution)/shard_map/ppermute | solution.py:241
  159.6 24.7 %collective-permute-start.8 = (bf16[512,1024]{1,0:T(8,128)(2,1)S(1)}, bf16[512,1024]{1,0:T(8,128)(2,1)S(1)}, u32[]{:S(2)}, u32[]{:S(2)}) collective-permute-start(bf16[512,1024]{1,0:T(8,128)(2,1)S(1)} %get-tuple-element.279), channel_id=1, source_target_pairs={{0,1},{1,0},{2,3},{3,2},{4,5},{5,4},{6,7},{7,6},{8,9},{9,8},{10,11... | collective-permute-start | bytes 3145736 | tf_op jit(solution)/shard_map/ppermute | solution.py:241
  160.1 27.4 %collective-permute-start.14 = (bf16[2,2,1,128,2176]{4,3,2,1,0:T(8,128)(2,1)S(1)}, bf16[2,2,1,128,2176]{4,3,2,1,0:T(8,128)(2,1)S(1)}, u32[]{:S(2)}, u32[]{:S(2)}) collective-permute-start(bf16[2,2,1,128,2176]{4,3,2,1,0:T(8,128)(2,1)S(1)} %pad_maximum_fusion.4), channel_id=1, source_target_pairs={{0,4},{4,0},{8,12},{12,8},{1,5},{5,1},{9,13},{13,9},{2,6},{6,2},{1... | collective-permute-start | bytes 6684680 | tf_op jit(solution)/shard_map/ppermute | solution.py:241
  161.5 40.7 %collective-permute-start.27 = (bf16[2,2,1,128,1024]{4,3,2,1,0:T(8,128)(2,1)}, bf16[2,2,1,128,1024]{4,3,2,1,0:T(8,128)(2,1)}, u32[]{:S(2)}, u32[]{:S(2)}) collective-permute-start(bf16[2,2,1,128,1024]{4,3,2,1,0:T(8,128)(2,1)} %pad_maximum_fusion.42), channel_id=1, source_target_pairs={{0,4},{4,0},{8,12},{12,8},{1,5},{5,1},{9,13},{13,9},{2,6},{6,2},{1... | collective-permute-start | bytes 3145736 | tf_op jit(solution)/shard_map/ppermute | solution.py:241
  190.5 24.0 %collective-permute-start.16 = (bf16[1,512,1024]{2,1,0:T(8,128)(2,1)S(1)}, bf16[1,512,1024]{2,1,0:T(8,128)(2,1)}, u32[]{:S(2)}, u32[]{:S(2)}) collective-permute-start(bf16[1,512,1024]{2,1,0:T(8,128)(2,1)S(1)} %maximum_bitcast_fusion.refs_4_.refs_7_), channel_id=1, source_target_pairs={{0,8},{4,12},{8,0},{12,4},{1,9},{5,13},{9,1},{13,5},{2,10},{6,14},... | collective-permute-start | bytes 3145736 | tf_op jit(solution)/shard_map/ppermute | solution.py:241
  192.1 23.9 %collective-permute-start.20 = (bf16[1,2,1,128,2048]{4,3,2,1,0:T(8,128)(2,1)}, bf16[1,2,1,128,2048]{4,3,2,1,0:T(8,128)(2,1)}, u32[]{:S(2)}, u32[]{:S(2)}) collective-permute-start(bf16[1,2,1,128,2048]{4,3,2,1,0:T(8,128)(2,1)} %pad_maximum_fusion.41), channel_id=1, source_target_pairs={{0,16},{16,0},{1,17},{17,1},{2,18},{18,2},{3,19},{19,3},{4,20},{20... | collective-permute-start | bytes 3145736 | tf_op jit(solution)/shard_map/ppermute | solution.py:241
  202.0 19.3 %collective-permute-start.31 = (bf16[2,2,1,128,1024]{4,3,2,1,0:T(8,128)(2,1)S(1)}, bf16[2,2,1,128,1024]{4,3,2,1,0:T(8,128)(2,1)S(1)}, u32[]{:S(2)}, u32[]{:S(2)}) collective-permute-start(bf16[2,2,1,128,1024]{4,3,2,1,0:T(8,128)(2,1)S(1)} %pad_maximum_fusion.43), channel_id=1, source_target_pairs={{0,4},{4,0},{8,12},{12,8},{1,5},{5,1},{9,13},{13,9},{2,6},{6,2},{1... | collective-permute-start | bytes 3145736 | tf_op jit(solution)/shard_map/ppermute | solution.py:241
  219.3 32.2 %collective-permute-start.21 = (bf16[2,2,1,128,2048]{4,3,2,1,0:T(8,128)(2,1)}, bf16[2,2,1,128,2048]{4,3,2,1,0:T(8,128)(2,1)}, u32[]{:S(2)}, u32[]{:S(2)}) collective-permute-start(bf16[2,2,1,128,2048]{4,3,2,1,0:T(8,128)(2,1)} %pad_maximum_fusion.9), channel_id=1, source_target_pairs={{0,4},{4,0},{8,12},{12,8},{1,5},{5,1},{9,13},{13,9},{2,6},{6,2},{1... | collective-permute-start | bytes 6291464 | tf_op jit(solution)/shard_map/ppermute | solution.py:241
  251.0 25.4 %collective-permute-start.18 = (bf16[512,1024]{1,0:T(8,128)(2,1)}, bf16[512,1024]{1,0:T(8,128)(2,1)}, u32[]{:S(2)}, u32[]{:S(2)}) collective-permute-start(bf16[512,1024]{1,0:T(8,128)(2,1)} %get-tuple-element.281), channel_id=1, source_target_pairs={{0,1},{1,0},{2,3},{3,2},{4,5},{5,4},{6,7},{7,6},{8,9},{9,8},{10,11... | collective-permute-start | bytes 3145736 | tf_op jit(solution)/shard_map/ppermute | solution.py:241
  311.9 25.6 %collective-permute-start.32 = (bf16[512,1024]{1,0:T(8,128)(2,1)}, bf16[512,1024]{1,0:T(8,128)(2,1)}, u32[]{:S(2)}, u32[]{:S(2)}) collective-permute-start(bf16[512,1024]{1,0:T(8,128)(2,1)} %get-tuple-element.289), channel_id=1, source_target_pairs={{0,1},{1,0},{2,3},{3,2},{4,5},{5,4},{6,7},{7,6},{8,9},{9,8},{10,11... | collective-permute-start | bytes 3145736 | tf_op jit(solution)/shard_map/ppermute | solution.py:241
  352.6 25.7 %collective-permute-start.34 = (bf16[512,1024]{1,0:T(8,128)(2,1)S(1)}, bf16[512,1024]{1,0:T(8,128)(2,1)S(1)}, u32[]{:S(2)}, u32[]{:S(2)}) collective-permute-start(bf16[512,1024]{1,0:T(8,128)(2,1)S(1)} %get-tuple-element.291), channel_id=1, source_target_pairs={{0,1},{1,0},{2,3},{3,2},{4,5},{5,4},{6,7},{7,6},{8,9},{9,8},{10,11... | collective-permute-start | bytes 3145736 | tf_op jit(solution)/shard_map/ppermute | solution.py:241
  359.0 163.6 %collective-permute-start.76 = (bf16[512,2048]{1,0:T(8,128)(2,1)}, bf16[512,2048]{1,0:T(8,128)(2,1)}, u32[]{:S(2)}, u32[]{:S(2)}) collective-permute-start(bf16[512,2048]{1,0:T(8,128)(2,1)} %convolution_convert_fusion.3), channel_id=1, source_target_pairs={{0,4},{4,0},{8,12},{12,8},{1,5},{5,1},{9,13},{13,9},{2,6},{6,2},{1... | collective-permute-start | bytes 6291464 | tf_op jit(solution)/shard_map/ppermute | solution.py:241
  396.7 137.7 %collective-permute-start.79 = (bf16[512,2048]{1,0:T(8,128)(2,1)}, bf16[512,2048]{1,0:T(8,128)(2,1)}, u32[]{:S(2)}, u32[]{:S(2)}) collective-permute-start(bf16[512,2048]{1,0:T(8,128)(2,1)} %convolution_convert_fusion.2), channel_id=1, source_target_pairs={{0,4},{4,0},{8,12},{12,8},{1,5},{5,1},{9,13},{13,9},{2,6},{6,2},{1... | collective-permute-start | bytes 6291464 | tf_op jit(solution)/shard_map/ppermute | solution.py:241
  468.5 45.4 %collective-permute-start.33 = (bf16[1,512,1024]{2,1,0:T(8,128)(2,1)S(1)}, bf16[1,512,1024]{2,1,0:T(8,128)(2,1)S(1)}, u32[]{:S(2)}, u32[]{:S(2)}) collective-permute-start(bf16[1,512,1024]{2,1,0:T(8,128)(2,1)S(1)} %copy-done.61), channel_id=1, source_target_pairs={{0,2},{1,3},{2,0},{3,1},{4,6},{5,7},{6,4},{7,5},{8,10},{9,11},{10,... | collective-permute-start | bytes 3145736 | tf_op jit(solution)/shard_map/ppermute | solution.py:241
  480.5 48.7 %collective-permute-start.37 = (bf16[2,512,1024]{2,1,0:T(8,128)(2,1)}, bf16[2,512,1024]{2,1,0:T(8,128)(2,1)S(1)}, u32[]{:S(2)}, u32[]{:S(2)}) collective-permute-start(bf16[2,512,1024]{2,1,0:T(8,128)(2,1)} %slice.538), channel_id=1, source_target_pairs={{0,4},{4,0},{8,12},{12,8},{1,5},{5,1},{9,13},{13,9},{2,6},{6,2},{1... | collective-permute-start | bytes 6291464 | tf_op jit(solution)/shard_map/ppermute | solution.py:241
  485.5 46.5 %collective-permute-start.66 = (bf16[512,2048]{1,0:T(8,128)(2,1)S(1)}, bf16[512,2048]{1,0:T(8,128)(2,1)S(1)}, u32[]{:S(2)}, u32[]{:S(2)}) collective-permute-start(bf16[512,2048]{1,0:T(8,128)(2,1)S(1)} %copy-done.222), channel_id=1, source_target_pairs={{0,4},{4,0},{8,12},{12,8},{1,5},{5,1},{9,13},{13,9},{2,6},{6,2},{1... | collective-permute-start | bytes 6291464 | tf_op jit(solution)/shard_map/ppermute | solution.py:241
  530.4 26.1 %collective-permute-start.38 = (bf16[1,512,1024]{2,1,0:T(8,128)(2,1)S(1)}, bf16[1,512,1024]{2,1,0:T(8,128)(2,1)S(1)}, u32[]{:S(2)}, u32[]{:S(2)}) collective-permute-start(bf16[1,512,1024]{2,1,0:T(8,128)(2,1)S(1)} %slice.672), channel_id=1, source_target_pairs={{0,8},{4,12},{8,0},{12,4},{1,9},{5,13},{9,1},{13,5},{2,10},{6,14},... | collective-permute-start | bytes 3145736 | tf_op jit(solution)/shard_map/ppermute | solution.py:241
  533.0 43.7 %collective-permute-start.67 = (bf16[2,1,1,2,2,32,2048]{6,5,4,3,2,1,0:T(8,128)(2,1)S(1)}, bf16[2,1,1,2,2,32,2048]{6,5,4,3,2,1,0:T(8,128)(2,1)S(1)}, u32[]{:S(2)}, u32[]{:S(2)}) collective-permute-start(bf16[2,1,1,2,2,32,2048]{6,5,4,3,2,1,0:T(8,128)(2,1)S(1)} %constant_dynamic-slice_fusion.16), channel_id=1, source_target_pairs={{0,8},{4,12},{8,0},{12,4},{1,9},{5,13},{9,1},{13,5},{2,10},{6,14},... | collective-permute-start | bytes 3145736 | tf_op jit(solution)/shard_map/ppermute | solution.py:241
  583.0 31.5 %collective-permute-start.39 = (bf16[512,1024]{1,0:T(8,128)(2,1)S(1)}, bf16[512,1024]{1,0:T(8,128)(2,1)S(1)}, u32[]{:S(2)}, u32[]{:S(2)}) collective-permute-start(bf16[512,1024]{1,0:T(8,128)(2,1)S(1)} %get-tuple-element.295), channel_id=1, source_target_pairs={{0,1},{1,0},{2,3},{3,2},{4,5},{5,4},{6,7},{7,6},{8,9},{9,8},{10,11... | collective-permute-start | bytes 3145736 | tf_op jit(solution)/shard_map/ppermute | solution.py:241
  589.9 20.9 %collective-permute-start.69 = (bf16[1,1,1,1,2,32,2048]{6,5,4,3,2,1,0:T(8,128)(2,1)S(1)}, bf16[1,1,1,1,2,32,2048]{6,5,4,3,2,1,0:T(8,128)(2,1)S(1)}, u32[]{:S(2)}, u32[]{:S(2)}) collective-permute-start(bf16[1,1,1,1,2,32,2048]{6,5,4,3,2,1,0:T(8,128)(2,1)S(1)} %constant_dynamic-slice_fusion.14), channel_id=1, source_target_pairs={{0,2},{1,3},{2,0},{3,1},{4,6},{5,7},{6,4},{7,5},{8,10},{9,11},{10,... | collective-permute-start | bytes 786440 | tf_op jit(solution)/shard_map/ppermute | solution.py:241
  593.5 35.4 %collective-permute-start.54 = (bf16[512,1536]{1,0:T(8,128)(2,1)S(1)}, bf16[512,1536]{1,0:T(8,128)(2,1)S(1)}, u32[]{:S(2)}, u32[]{:S(2)}) collective-permute-start(bf16[512,1536]{1,0:T(8,128)(2,1)S(1)} %convolution_convert_fusion.1), channel_id=1, source_target_pairs={{0,4},{4,0},{8,12},{12,8},{1,5},{5,1},{9,13},{13,9},{2,6},{6,2},{1... | collective-permute-start | bytes 4718600 | tf_op jit(solution)/shard_map/ppermute | solution.py:241
  628.1 21.2 %collective-permute-start.40 = (bf16[512,1024]{1,0:T(8,128)(2,1)}, bf16[512,1024]{1,0:T(8,128)(2,1)S(1)}, u32[]{:S(2)}, u32[]{:S(2)}) collective-permute-start(bf16[512,1024]{1,0:T(8,128)(2,1)} %get-tuple-element.297), channel_id=1, source_target_pairs={{0,1},{1,0},{2,3},{3,2},{4,5},{5,4},{6,7},{7,6},{8,9},{9,8},{10,11... | collective-permute-start | bytes 3145736 | tf_op jit(solution)/shard_map/ppermute | solution.py:241
  633.5 39.5 %collective-permute-start.55 = (bf16[2,1,1,128,1536]{3,4,2,1,0:T(8,128)(2,1)}, bf16[2,1,1,128,1536]{3,4,2,1,0:T(8,128)(2,1)}, u32[]{:S(2)}, u32[]{:S(2)}) collective-permute-start(bf16[2,1,1,128,1536]{3,4,2,1,0:T(8,128)(2,1)} %copy.117), channel_id=1, source_target_pairs={{0,8},{4,12},{8,0},{12,4},{1,9},{5,13},{9,1},{13,5},{2,10},{6,14},... | collective-permute-start | bytes 2359304 | tf_op jit(solution)/shard_map/ppermute | solution.py:241
  660.8 80.0 %collective-permute-start.47 = (bf16[512,2048]{1,0:T(8,128)(2,1)}, bf16[512,2048]{1,0:T(8,128)(2,1)}, u32[]{:S(2)}, u32[]{:S(2)}) collective-permute-start(bf16[512,2048]{1,0:T(8,128)(2,1)} %convolution_convert_fusion.5), channel_id=1, source_target_pairs={{0,4},{4,0},{8,12},{12,8},{1,5},{5,1},{9,13},{13,9},{2,6},{6,2},{1... | collective-permute-start | bytes 6291464 | tf_op jit(solution)/shard_map/ppermute | solution.py:241
  666.5 82.3 %collective-permute-start.50 = (bf16[512,2048]{1,0:T(8,128)(2,1)}, bf16[512,2048]{1,0:T(8,128)(2,1)}, u32[]{:S(2)}, u32[]{:S(2)}) collective-permute-start(bf16[512,2048]{1,0:T(8,128)(2,1)} %convolution_convert_fusion.4), channel_id=1, source_target_pairs={{0,4},{4,0},{8,12},{12,8},{1,5},{5,1},{9,13},{13,9},{2,6},{6,2},{1... | collective-permute-start | bytes 6291464 | tf_op jit(solution)/shard_map/ppermute | solution.py:241
  682.0 145.2 %collective-permute-start.41 = (bf16[1,512,1024]{2,1,0:T(8,128)(2,1)}, bf16[1,512,1024]{2,1,0:T(8,128)(2,1)}, u32[]{:S(2)}, u32[]{:S(2)}) collective-permute-start(bf16[1,512,1024]{2,1,0:T(8,128)(2,1)} %get-tuple-element.100), channel_id=1, source_target_pairs={{0,2},{1,3},{2,0},{3,1},{4,6},{5,7},{6,4},{7,5},{8,10},{9,11},{10,... | collective-permute-start | bytes 3145736 | tf_op jit(solution)/shard_map/ppermute | solution.py:241
  688.6 52.1 %collective-permute-start.60 = (bf16[128,1024]{0,1:T(8,128)(2,1)S(1)}, bf16[128,1024]{0,1:T(8,128)(2,1)S(1)}, u32[]{:S(2)}, u32[]{:S(2)}) collective-permute-start(bf16[128,1024]{0,1:T(8,128)(2,1)S(1)} %pad_maximum_fusion.69), channel_id=1, source_target_pairs={{0,2},{1,3},{2,0},{3,1},{4,6},{5,7},{6,4},{7,5},{8,10},{9,11},{10,... | collective-permute-start | bytes 786440 | tf_op jit(solution)/shard_map/ppermute | solution.py:241
  747.8 28.2 %collective-permute-start.77 = (bf16[2,1,1,128,2048]{3,4,2,1,0:T(8,128)(2,1)}, bf16[2,1,1,128,2048]{3,4,2,1,0:T(8,128)(2,1)}, u32[]{:S(2)}, u32[]{:S(2)}) collective-permute-start(bf16[2,1,1,128,2048]{3,4,2,1,0:T(8,128)(2,1)} %copy.121), channel_id=1, source_target_pairs={{0,8},{4,12},{8,0},{12,4},{1,9},{5,13},{9,1},{13,5},{2,10},{6,14},... | collective-permute-start | bytes 3145736 | tf_op jit(solution)/shard_map/ppermute | solution.py:241
  757.2 26.3 %collective-permute-start.80 = (bf16[1,2,1,128,2048]{3,4,2,1,0:T(8,128)(2,1)}, bf16[1,2,1,128,2048]{3,4,2,1,0:T(8,128)(2,1)}, u32[]{:S(2)}, u32[]{:S(2)}) collective-permute-start(bf16[1,2,1,128,2048]{3,4,2,1,0:T(8,128)(2,1)} %copy.123), channel_id=1, source_target_pairs={{0,16},{16,0},{1,17},{17,1},{2,18},{18,2},{3,19},{19,3},{4,20},{20... | collective-permute-start | bytes 3145736 | tf_op jit(solution)/shard_map/ppermute | solution.py:241
  769.8 26.3 %collective-permute-start.48 = (bf16[2,1,1,128,2048]{3,4,2,1,0:T(8,128)(2,1)}, bf16[2,1,1,128,2048]{3,4,2,1,0:T(8,128)(2,1)}, u32[]{:S(2)}, u32[]{:S(2)}) collective-permute-start(bf16[2,1,1,128,2048]{3,4,2,1,0:T(8,128)(2,1)} %copy.113), channel_id=1, source_target_pairs={{0,8},{4,12},{8,0},{12,4},{1,9},{5,13},{9,1},{13,5},{2,10},{6,14},... | collective-permute-start | bytes 3145736 | tf_op jit(solution)/shard_map/ppermute | solution.py:241
  773.6 32.4 %collective-permute-start.51 = (bf16[1,2,1,128,2048]{3,4,2,1,0:T(8,128)(2,1)}, bf16[1,2,1,128,2048]{3,4,2,1,0:T(8,128)(2,1)}, u32[]{:S(2)}, u32[]{:S(2)}) collective-permute-start(bf16[1,2,1,128,2048]{3,4,2,1,0:T(8,128)(2,1)} %copy.115), channel_id=1, source_target_pairs={{0,16},{16,0},{1,17},{17,1},{2,18},{18,2},{3,19},{19,3},{4,20},{20... | collective-permute-start | bytes 3145736 | tf_op jit(solution)/shard_map/ppermute | solution.py:241
  778.0 39.2 %collective-permute-start.78 = (bf16[1,1,1,128,2048]{3,4,2,1,0:T(8,128)(2,1)S(1)}, bf16[1,1,1,128,2048]{3,4,2,1,0:T(8,128)(2,1)S(1)}, u32[]{:S(2)}, u32[]{:S(2)}) collective-permute-start(bf16[1,1,1,128,2048]{3,4,2,1,0:T(8,128)(2,1)S(1)} %constant_dynamic-slice_fusion.4), channel_id=1, source_target_pairs={{0,16},{16,0},{1,17},{17,1},{2,18},{18,2},{3,19},{19,3},{4,20},{20... | collective-permute-start | bytes 1572872 | tf_op jit(solution)/shard_map/ppermute | solution.py:241
  785.1 32.2 %collective-permute-start.81 = (bf16[1,1,1,128,2048]{3,4,2,1,0:T(8,128)(2,1)S(1)}, bf16[1,1,1,128,2048]{3,4,2,1,0:T(8,128)(2,1)S(1)}, u32[]{:S(2)}, u32[]{:S(2)}) collective-permute-start(bf16[1,1,1,128,2048]{3,4,2,1,0:T(8,128)(2,1)S(1)} %constant_dynamic-slice_fusion.1), channel_id=1, source_target_pairs={{0,8},{4,12},{8,0},{12,4},{1,9},{5,13},{9,1},{13,5},{2,10},{6,14},... | collective-permute-start | bytes 1572872 | tf_op jit(solution)/shard_map/ppermute | solution.py:241
  797.7 28.3 %collective-permute-start.49 = (bf16[1,1,1,128,2048]{3,4,2,1,0:T(8,128)(2,1)S(1)}, bf16[1,1,1,128,2048]{3,4,2,1,0:T(8,128)(2,1)S(1)}, u32[]{:S(2)}, u32[]{:S(2)}) collective-permute-start(bf16[1,1,1,128,2048]{3,4,2,1,0:T(8,128)(2,1)S(1)} %constant_dynamic-slice_fusion.27), channel_id=1, source_target_pairs={{0,16},{16,0},{1,17},{17,1},{2,18},{18,2},{3,19},{19,3},{4,20},{20... | collective-permute-start | bytes 1572872 | tf_op jit(solution)/shard_map/ppermute | solution.py:241
  817.5 32.2 %collective-permute-start.82 = (bf16[128,2048]{0,1:T(8,128)(2,1)S(1)}, bf16[128,2048]{0,1:T(8,128)(2,1)S(1)}, u32[]{:S(2)}, u32[]{:S(2)}) collective-permute-start(bf16[128,2048]{0,1:T(8,128)(2,1)S(1)} %pad_maximum_fusion.64), channel_id=1, source_target_pairs={{0,2},{1,3},{2,0},{3,1},{4,6},{5,7},{6,4},{7,5},{8,10},{9,11},{10,... | collective-permute-start | bytes 1572872 | tf_op jit(solution)/shard_map/ppermute | solution.py:241
  827.2 33.8 %collective-permute-start.53 = (bf16[128,2048]{0,1:T(8,128)(2,1)}, bf16[128,2048]{0,1:T(8,128)(2,1)}, u32[]{:S(2)}, u32[]{:S(2)}) collective-permute-start(bf16[128,2048]{0,1:T(8,128)(2,1)} %pad_maximum_fusion.55), channel_id=1, source_target_pairs={{0,2},{1,3},{2,0},{3,1},{4,6},{5,7},{6,4},{7,5},{8,10},{9,11},{10,... | collective-permute-start | bytes 1572872 | tf_op jit(solution)/shard_map/ppermute | solution.py:241
  (279 other events, 2510.9 us)

commit v2 on v1

--- a/solution.py
+++ b/solution.py
@@ -1,4 +1,3 @@
-import functools
 import math
 import jax
 import jax.numpy as jnp
@@ -245,28 +244,8 @@
     return (lax.axis_index(axis) >> bit) & 1
 
 
-def row_dims(axes):
-    return [(axis, bit) for axis in axes for bit in reversed(bits(lax.axis_size(axis)))]
-
-
-def orders():
-    seq = [("seq", bit) for bit in reversed(bits(lax.axis_size("seq")))]
-    dp = [("dp", bit) for bit in reversed(bits(lax.axis_size("dp")))]
-    near, far = seq[-1:], seq[:-1]
-    return dp + far + near, far + dp + near
-
-
-def gather_rows(piece, order, axes=("dp", "seq")):
-    dims = row_dims(axes)
-    array = piece.reshape((1,) * len(dims) + piece.shape)
-    for axis, bit in order:
-        dim = dims.index((axis, bit))
-        other = swap(array, axis, bit)
-        lower = bit_of(axis, bit) == 0
-        array = jnp.concatenate(
-            [jnp.where(lower, array, other), jnp.where(lower, other, array)], axis=dim
-        )
-    return array.reshape(-1, piece.shape[-1])
+def gather_all(piece):
+    return lax.all_gather(piece, ("dp", "seq"), axis=0, tiled=True)
 
 
 def own_rows(array, axes=("dp", "seq")):
@@ -289,34 +268,6 @@
     return lax.dot_general(
         left, right, (((1,), (1,)), ((), ())), preferred_element_type=jnp.float32
     )
-
-
-def scatter_rows(low, right, order, axes=("dp", "seq")):
-    dims = row_dims(axes)
-    tokens, rows = low.shape
-    part = rows >> len(dims)
-    (axis, bit), later = order[0], order[1:]
-    dim = dims.index((axis, bit))
-    stride = part << (len(dims) - 1 - dim)
-    pairs = rows // (2 * stride)
-    lower = bit_of(axis, bit) == 0
-    first = [low[:, (2 * i) * stride : (2 * i + 1) * stride] for i in range(pairs)]
-    second = [low[:, (2 * i + 1) * stride : (2 * i + 2) * stride] for i in range(pairs)]
-    first, second = jnp.concatenate(first, 1), jnp.concatenate(second, 1)
-    sent = outer(jnp.where(lower, second, first), right).astype(jnp.bfloat16)
-    came = swap(sent, axis, bit)
-    array = outer(jnp.where(lower, first, second), right) + came.astype(jnp.float32)
-    shape = [2] * len(dims) + [part, right.shape[1]]
-    shape[dim] = 1
-    array = array.reshape(shape)
-    for axis, bit in later:
-        array = array.astype(jnp.bfloat16)
-        dim = dims.index((axis, bit))
-        here = bit_of(axis, bit)
-        kept = lax.dynamic_index_in_dim(array, here, dim)
-        sent = lax.dynamic_index_in_dim(array, 1 - here, dim)
-        array = kept.astype(jnp.float32) + swap(sent, axis, bit).astype(jnp.float32)
-    return array.reshape(part, right.shape[1])
 
 
 def norm_forward(values, gain_vec):
@@ -339,12 +290,6 @@
     return sigmoid * (1.0 + values * (1.0 - sigmoid))
 
 
-def team_sum(partial):
-    for bit in bits(lax.axis_size("heads"))[:-1]:
-        partial = partial + swap(partial.astype(jnp.bfloat16), "heads", bit).astype(jnp.float32)
-    return partial
-
-
 def sum_everyone(array):
     for axis in ("seq", "dp", "heads"):
         for bit in bits(lax.axis_size(axis)):
@@ -352,52 +297,134 @@
     return array
 
 
+def after(array, *events):
+    return lax.optimization_barrier((array,) + events)[0]
+
+
 def far_swap(array):
     return swap(array, "heads", bits(lax.axis_size("heads"))[-1])
 
 
-def ffn_forward(stream, gain_vec, weights):
-    normed_out, normed, inverse = norm_forward(stream, gain_vec)
-    low = normed_out.astype(jnp.bfloat16)
-    pres, acts, partial = [], [], 0.0
-    for weight_in, weight_out in weights:
-        pre = plain(low, weight_in)
-        act = jax.nn.silu(pre).astype(jnp.bfloat16)
-        partial = partial + plain(act, weight_out)
-        pres.append(pre)
-        acts.append(act)
-    return (stream + 0.5 * team_sum(partial), (normed, inverse, low, pres, acts))
-
-
-def ffn_backward(gradient, saved_state, gain_vec, weights):
-    normed, inverse, low, pres, acts = saved_state
-    order_a, order_b = orders()
-    branch_low = (0.5 * gradient).astype(jnp.bfloat16)
-    partial, pre_lows = 0.0, []
-    for (weight_in, weight_out), pre in zip(weights, pres):
-        pre_low = (against(branch_low, weight_out) * silu_slope(pre)).astype(jnp.bfloat16)
-        partial = partial + against(pre_low, weight_in)
-        pre_lows.append(pre_low)
-    normed_grad = team_sum(partial)
-    out_grad = scatter_rows(branch_low, jnp.concatenate(acts, 1), order_b[::-1])
-    in_grad = scatter_rows(low, jnp.concatenate(pre_lows, 1), order_a[::-1])
-    stream_part, gain_grad = norm_backward(normed_grad, normed, inverse, gain_vec)
-    hidden = in_grad.shape[1] // 2
-    came = far_swap(
-        jnp.concatenate([in_grad[:, hidden:], out_grad[:, hidden:]], 1).astype(jnp.bfloat16)
-    ).astype(jnp.float32)
-    in_grad = in_grad[:, :hidden] + came[:, :hidden]
-    out_grad = (out_grad[:, :hidden] + came[:, hidden:]).T
-    return (gradient + stream_part, gain_grad, in_grad, out_grad)
+def team_bits():
+    return bits(lax.axis_size("heads"))[:-1]
+
+
+def gather_parts(own):
+    parts = [own]
+    for bit in team_bits():
+        held = parts[0] if len(parts) == 1 else jnp.concatenate(parts, axis=0)
+        parts.append(swap(held, "heads", bit))
+    return parts
+
+
+def reduce_parts(partials):
+    partials = list(partials)
+    for bit in reversed(team_bits()):
+        came = swap(partials.pop().astype(jnp.bfloat16), "heads", bit).astype(jnp.float32)
+        at, kept = 0, []
+        for item in partials:
+            kept.append(item + came[at : at + item.shape[0]])
+            at += item.shape[0]
+        partials = kept
+    return partials[0]
+
+
+def reorder(parts):
+    team = lax.axis_size("heads") // 2
+    mine = lax.axis_index("heads") % team
+    whole = join(parts)
+    block = whole.shape[0] // team
+    if team == 2:
+        first, second = parts
+        lower = mine == 0
+        return jnp.concatenate(
+            [jnp.where(lower, first, second), jnp.where(lower, second, first)], axis=0
+        )
+    return jnp.concatenate(
+        [lax.dynamic_slice_in_dim(whole, (at ^ mine) * block, block, 0) for at in range(team)],
+        axis=0,
+    )
+
+
+def cut_parts(array):
+    team = lax.axis_size("heads") // 2
+    mine = lax.axis_index("heads") % team
+    block = array.shape[0] // team
+    take = lambda at: lax.dynamic_slice_in_dim(array, (at ^ mine) * block, block, 0)
+    parts = [take(0)]
+    for bit in team_bits():
+        parts.append(join([take(at) for at in range(1 << bit, 2 << bit)]))
+    return parts
+
+
+def join(parts):
+    return parts[0] if len(parts) == 1 else jnp.concatenate(parts, axis=0)
+
+
+def scatter_groups(array):
+    return lax.psum_scatter(array, ("dp", "seq"), scatter_dimension=0, tiled=True)
+
+
+def grad_of(left, right):
+    return outer(left, right).astype(jnp.bfloat16)
+
+
+def ffn_forward(low_own, weights):
+    lows = gather_parts(low_own)
+    pres = [[plain(low, weight_in) for weight_in, _ in weights] for low in lows]
+    acts = [[jax.nn.silu(pre).astype(jnp.bfloat16) for pre in pair] for pair in pres]
+    partials = [
+        sum(plain(act, weight_out) for act, (_, weight_out) in zip(pair, weights))
+        for pair in acts
+    ]
+    return reduce_parts(partials), (lows, pres, acts)
+
+
+def ffn_backward(gradient, saved, weights):
+    lows, pres, acts = saved
+    branches = gather_parts((0.5 * gradient).astype(jnp.bfloat16))
+    pre_lows = [
+        [
+            (against(branch, weight_out) * silu_slope(pre)).astype(jnp.bfloat16)
+            for (_, weight_out), pre in zip(weights, pair)
+        ]
+        for branch, pair in zip(branches, pres)
+    ]
+    partials = [
+        sum(against(pre_low, weight_in) for pre_low, (weight_in, _) in zip(pair, weights))
+        for pair in pre_lows
+    ]
+    normed_grad = reduce_parts(partials)
+    low, branch = join(lows), join(branches)
+    wide = lambda items: join([jnp.concatenate(pair, axis=1) for pair in items])
+    grads = jnp.concatenate(
+        [grad_of(branch, wide(acts)), grad_of(low, wide(pre_lows))], axis=1
+    )
+    return normed_grad, scatter_groups(grads)
+
+
+def fold_far(array, far_cols, own_cols):
+    came = far_swap(jnp.concatenate([array[:, a:b] for a, b in far_cols], axis=1))
+    came, outs, at = came.astype(jnp.float32), [], 0
+    for a, b in own_cols:
+        outs.append(array[:, a:b].astype(jnp.float32) + came[:, at : at + b - a])
+        at += b - a
+    return outs
 
 
 def halo(array, reach):
-    peers, length = lax.axis_size("seq"), array.shape[0]
-    up = [(i, i + 1) for i in range(peers - 1)]
+    peers, n_heads = lax.axis_size("seq"), lax.axis_size("heads")
+    team = n_heads // 2
+    spot = lambda row, at: (at // team) * n_heads + row * team + at % team
+    up = [
+        (spot(row, at), spot(row, at + 1))
+        for row in range(2)
+        for at in range(peers * team - 1)
+    ]
     down = [(j, i) for i, j in up]
-    before = lax.ppermute(array[length - reach :], "seq", up)
-    after = lax.ppermute(array[:reach], "seq", down)
-    return jnp.concatenate([before, array, after], axis=0)
+    before = lax.ppermute(array[array.shape[0] - reach :], ("seq", "heads"), up)
+    after_it = lax.ppermute(array[:reach], ("seq", "heads"), down)
+    return jnp.concatenate([before, array, after_it], axis=0)
 
 
 def conv_forward(stream, window_ids, weights):
@@ -455,18 +482,23 @@
         [glu_grad * gate, glu_grad * gate_in * gate * (1.0 - gate)], axis=-1
     ).astype(jnp.bfloat16)
     normed_grad = against(doubled_low, in_weight)
-    team = lax.axis_size("heads") // 2
-    share = tokens // team
-    mine = (lax.axis_index("heads") % team) * share
-    cut = lambda array: lax.dynamic_slice_in_dim(array, mine, share, 0)
-    order_a, order_b = orders()
-    axes = ("dp", "seq", "heads")
-    heads = [("heads", bit) for bit in reversed(bits(lax.axis_size("heads")))]
-    out_grad = scatter_rows(cut(swish_low), cut(branch_low), order_b[::-1] + heads, axes)
-    in_grad = scatter_rows(cut(low), cut(doubled_low), order_a[::-1] + heads, axes)
+    grads = scatter_groups(
+        jnp.concatenate([grad_of(low, doubled_low), grad_of(swish_low, branch_low)], axis=1)
+    )
     part, gain_one_grad = norm_backward(normed_grad, normed, inverse, gain_one)
     small = [gain_one_grad, gain_two_grad] + tap_grads
-    return (gradient + part, in_grad, out_grad, small)
+    return (gradient + part, grads, small)
+
+
+def fold_heads(both):
+    for bit in reversed(bits(lax.axis_size("heads"))):
+        both = both.astype(jnp.bfloat16)
+        half = both.shape[0] // 2
+        here = bit_of("heads", bit) * half
+        kept = lax.dynamic_slice_in_dim(both, here, half, 0)
+        sent = lax.dynamic_slice_in_dim(both, half - here, half, 0)
+        both = kept.astype(jnp.float32) + swap(sent, "heads", bit).astype(jnp.float32)
+    return both
 
 
 def on_device(
@@ -499,174 +531,223 @@
     team = n_heads // 2
     place = lax.axis_index("heads")
     seq_at = lax.axis_index("seq")
-    rows_mine = row_count // 2
-    my_row = place // team
-    order_a, order_b = orders()
+    assert row_count == 2
+    my_row, mine = place // team, place % team
+    block = local // team
     bf16 = jnp.bfloat16
-
-    far_in = gather_rows(far_swap(own_rows(ffn1_in)), order_a)
-    far_out = gather_rows(far_swap(own_rows(ffn1_out)), order_b)
-    ffn1_weights = [(ffn1_in, ffn1_out), (far_in, far_out)]
-    qkv = jnp.concatenate([query_weight, key_weight, value_weight], axis=1)
-    out_cols = output_weight.shape[0]
     groups = lax.axis_size("dp") * lax.axis_size("seq")
     group_at = lax.axis_index(("dp", "seq"))
     part = width // groups
-    out_piece = lax.dynamic_slice_in_dim(output_weight, group_at * part, part, 1).T
-    attn_piece = far_swap(jnp.concatenate([own_rows(qkv), out_piece], axis=1))
+
+    own_qkv = jnp.concatenate([query_weight, key_weight, value_weight], axis=1)
+    q_cols, out_cols, n_qkv = query_weight.shape[1], output_weight.shape[0], own_qkv.shape[1]
+    output_piece = lax.dynamic_slice_in_dim(output_weight, group_at * part, part, 1).T
+    attn_piece = far_swap(jnp.concatenate([own_rows(own_qkv), output_piece], axis=1))
+    far_attn = gather_all(attn_piece)
+    far_qkv, far_output = far_attn[:, :n_qkv], far_attn[:, n_qkv:]
     small_piece = jnp.concatenate([depthwise, conv_gain[None], depth_gain[None]], axis=0).T
     small_piece = jnp.pad(small_piece, ((0, 0), (0, 128 - small_piece.shape[1])))
     conv_piece = jnp.concatenate([pointwise_in, pointwise_out, small_piece], axis=1)
+    conv_piece = after(conv_piece, attn_piece)
     for bit in bits(n_heads):
         other = swap(conv_piece, "heads", bit)
         lower = bit_of("heads", bit) == 0
         conv_piece = jnp.concatenate(
             [jnp.where(lower, conv_piece, other), jnp.where(lower, other, conv_piece)], axis=0
         )
-    group_a = gather_rows(
-        jnp.concatenate([attn_piece, conv_piece[:, 2 * width :]], axis=1), order_a
-    )
-    pw_in = gather_rows(conv_piece[:, : 2 * width], order_b)
-    n_qkv = qkv.shape[1]
-    far_qkv = group_a[:, :n_qkv]
-    far_output = group_a[:, n_qkv : n_qkv + out_cols]
-    pw_out = group_a[:, n_qkv + out_cols : n_qkv + out_cols + width]
-    small_all = group_a[:, n_qkv + out_cols + width :][:, : KERNEL + 2].T
-    far_in2 = gather_rows(far_swap(own_rows(ffn2_in)), order_a)
-    far_out2 = gather_rows(far_swap(own_rows(ffn2_out)), order_b)
-    ffn2_weights = [(ffn2_in, ffn2_out), (far_in2, far_out2)]
-    taps, conv_gain_all, depth_gain_all = (
-        small_all[:KERNEL],
-        small_all[KERNEL],
-        small_all[KERNEL + 1],
-    )
-    conv_weights = (pw_in, pw_out, taps, conv_gain_all, depth_gain_all)
-
-    table = jnp.concatenate([position_table, far_swap(position_table)], axis=0)
+    conv_all = gather_all(conv_piece)
+    pw_in, pw_out = conv_all[:, : 2 * width], conv_all[:, 2 * width : 3 * width]
+    small_all = conv_all[:, 3 * width : 3 * width + KERNEL + 2].T
+    conv_weights = (pw_in, pw_out, small_all[:KERNEL], small_all[KERNEL], small_all[KERNEL + 1])
+
+    rows = [lax.dynamic_index_in_dim(frames, my_row ^ f, 0, keepdims=False) for f in (0, 1)]
+    units = [cut_parts(row) for row in rows]
+    stream_zero = units[0][0].astype(jnp.float32)
+    ffn1_low, ffn1_pre, ffn1_act, ffn1_partial = [], [], [], []
+    ffn1_norm = None
+    for f in (0, 1):
+        lows, pres, acts, partials = [], [], [], []
+        for unit in units[f]:
+            normed_out, normed, inverse = norm_forward(unit.astype(jnp.float32), ffn1_gain)
+            if ffn1_norm is None:
+                ffn1_norm = (normed, inverse)
+            low = normed_out.astype(bf16)
+            pre = plain(low, ffn1_in)
+            act = jax.nn.silu(pre).astype(bf16)
+            lows.append(low)
+            pres.append(pre)
+            acts.append(act)
+            partials.append(plain(act, ffn1_out))
+        ffn1_low.append(lows)
+        ffn1_pre.append(pres)
+        ffn1_act.append(acts)
+        ffn1_partial.append(partials)
+    summed = reduce_parts(ffn1_partial[1])
+    far_part = far_swap(summed.astype(bf16)).astype(jnp.float32)
+    stream_one = stream_zero + 0.5 * (reduce_parts(ffn1_partial[0]) + far_part)
+
     n_q, n_k = local // TILE, length // TILE
-    reversed_buckets = jnp.pad(bucket_of[::-1], (0, 1))
+    early = ffn1_act[0][0]
+    my_ids = lax.dynamic_index_in_dim(after(segment_ids, early), my_row, 0, keepdims=False)
+    reach = KERNEL // 2
+    ids_pad = jnp.pad(my_ids, (reach, reach), constant_values=-1)
+    query_ids = lax.dynamic_slice_in_dim(my_ids, seq_at * local, local, 0)
+    window_ids = lax.dynamic_slice_in_dim(
+        ids_pad, seq_at * local + mine * block, block + 2 * reach, 0
+    )
+    low_ids = query_ids.reshape(n_q, TILE)[:, 0]
+    top_ids = query_ids.reshape(n_q, TILE)[:, TILE - 1]
+    starts = jnp.sum((my_ids[None] < low_ids[:, None]).astype(jnp.int32), axis=1) // TILE
+    ends = jnp.sum((my_ids[None] <= top_ids[:, None]).astype(jnp.int32), axis=1)
+    ends = (ends + TILE - 1) // TILE
+    scalars = jnp.concatenate(
+        [seq_at.astype(jnp.int32)[None], jnp.stack([starts, ends], axis=1).reshape(-1)]
+    )
+    reversed_buckets = jnp.pad(after(bucket_of, early)[::-1], (0, 1))
     window = lax.dynamic_slice_in_dim(reversed_buckets, seq_at * local, (n_q + n_k) * TILE, 0)
     levels = lax.broadcasted_iota(jnp.int32, (position_table.shape[1], window.shape[0]), 0)
     onehot = (levels == window[None, :]).astype(jnp.float32)
-    tiles = bias_tiles(jnp.dot(table, onehot, precision=HIGHEST) * LOG2E)
-
-    outs = []
-    for at in range(rows_mine):
-        row = my_row * rows_mine + at
-        pick = lambda array: lax.dynamic_index_in_dim(array, row, 0, keepdims=False)
-        ids = pick(segment_ids)
-        reach = KERNEL // 2
-        ids_pad = jnp.pad(ids, (reach, reach), constant_values=-1)
-        window_ids = lax.dynamic_slice_in_dim(ids_pad, seq_at * local, local + 2 * reach, 0)
-        query_ids = window_ids[reach : reach + local]
-        scalars = [seq_at.astype(jnp.int32)]
-        for block in range(n_q):
-            low_id = query_ids[block * TILE]
-            top_id = query_ids[(block + 1) * TILE - 1]
-            scalars.append(jnp.sum((ids < low_id).astype(jnp.int32)) // TILE)
-            scalars.append((jnp.sum((ids <= top_id).astype(jnp.int32)) + TILE - 1) // TILE)
-        scalars = jnp.stack(scalars)
-
-        stream_zero = pick(frames).astype(jnp.float32)
-        stream_one, ffn1_state = ffn_forward(stream_zero, ffn1_gain, ffn1_weights)
-
-        normed_out, normed, inverse = norm_forward(stream_one, attn_gain)
-        low = normed_out.astype(bf16)
-        q_cols = query_weight.shape[1]
-        kv = jnp.concatenate(
-            [plain(low, qkv[:, q_cols:]).astype(bf16), plain(low, far_qkv[:, q_cols:]).astype(bf16)],
-            axis=1,
-        )[None]
-        pieces = [kv]
-        for bit in reversed(bits(lax.axis_size("seq"))):
-            held = pieces[0] if len(pieces) == 1 else jnp.concatenate(pieces, axis=0)
-            pieces.append(swap(held, "seq", bit))
-        query = jnp.concatenate(
-            [plain(low, qkv[:, :q_cols]).astype(bf16), plain(low, far_qkv[:, :q_cols]).astype(bf16)],
-            axis=1,
+    tables = jnp.concatenate([position_table, far_swap(position_table)], axis=0)
+    biases = jnp.dot(tables, onehot, precision=HIGHEST) * LOG2E
+    per_shard = q_cols // HEAD_DIM
+    tiles = [bias_tiles(biases[:per_shard]), bias_tiles(biases[per_shard:])]
+
+    attn_out, attn_hat, attn_inverse = norm_forward(stream_one, attn_gain)
+    low = reorder(gather_parts(attn_out.astype(bf16)))
+    hidden = ffn2_in.shape[1]
+    ffn2_pieces = [own_rows(ffn2_in), own_rows(ffn2_out)]
+    if hidden == width:
+        ffn2_piece = jnp.concatenate(ffn2_pieces, axis=1)
+        far_ffn2 = gather_all(far_swap(after(ffn2_piece, low)))
+        far_ffn2 = (far_ffn2[:, :hidden], far_ffn2[:, hidden:])
+    else:
+        far_ffn2 = tuple(gather_all(far_swap(after(piece, low))) for piece in ffn2_pieces)
+    ffn2_weights = [(ffn2_in, ffn2_out), far_ffn2]
+    seq_bits = bits(lax.axis_size("seq"))
+    pieces, queries, mixtures, log_totals = [], [], [], []
+    for qkv in (own_qkv, far_qkv):
+        held = [plain(low, qkv[:, q_cols:]).astype(bf16)[None]]
+        for bit in reversed(seq_bits):
+            held.append(swap(join(held), "seq", bit))
+        pieces.append(held)
+        queries.append(plain(low, qkv[:, :q_cols]).astype(bf16))
+    for shard in (0, 1):
+        mixture, log_total = attend(
+            scalars, queries[shard], tiles[shard], query_ids[None], my_ids[:, None],
+            pieces[shard], per_shard,
         )
-        per_shard = q_cols // HEAD_DIM
-        mixture, log_total = attend(
-            scalars, query, tiles, query_ids[None], ids[:, None], pieces, per_shard
+        mixtures.append(mixture)
+        log_totals.append(log_total)
+    mix_parts = [cut_parts(mixture) for mixture in mixtures]
+    branch = reduce_parts(
+        [
+            plain(own, output_weight) + against(far, far_output)
+            for own, far in zip(*mix_parts)
+        ]
+    )
+    stream_two = stream_one + branch
+
+    stream_three, conv_state = conv_forward(stream_two, window_ids, conv_weights)
+    ffn2_out_norm, ffn2_hat, ffn2_inverse = norm_forward(stream_three, ffn2_gain)
+    branch, ffn2_state = ffn_forward(ffn2_out_norm.astype(bf16), ffn2_weights)
+    stream_four = stream_three + 0.5 * branch
+    final_out, final_hat, final_inverse = norm_forward(stream_four, final_gain)
+    layer_low = final_out.astype(bf16)
+    cot = lax.dynamic_index_in_dim(cotangent, my_row, 0, keepdims=False)
+    cot = lax.dynamic_slice_in_dim(cot, mine * block, block, 0).astype(jnp.float32)
+    grad_four, final_gain_grad = norm_backward(cot, final_hat, final_inverse, final_gain)
+
+    normed_grad, ffn2_grads = ffn_backward(grad_four, ffn2_state, ffn2_weights)
+    stream_part, ffn2_gain_grad = norm_backward(normed_grad, ffn2_hat, ffn2_inverse, ffn2_gain)
+    grad_three = grad_four + stream_part
+    grad_two, conv_grads, conv_small = conv_backward(
+        grad_three, conv_state, window_ids, conv_weights
+    )
+    branch_low = reorder(gather_parts(grad_two.astype(bf16)))
+    mix_grads = [
+        against(branch_low, output_weight).astype(bf16),
+        plain(branch_low, far_output).astype(bf16),
+    ]
+    q_grads, kv_grads, table_grads = [], [], []
+    for shard in (0, 1):
+        q_grad, kv_grad, tile_grads = attend_back(
+            scalars, queries[shard], tiles[shard], query_ids[None], my_ids[:, None],
+            mixtures[shard], mix_grads[shard], log_totals[shard], pieces[shard], per_shard,
         )
-        branch = team_sum(
-            plain(mixture[:, :out_cols], output_weight)
-            + against(mixture[:, out_cols:], far_output)
-        )
-        stream_two = stream_one + branch
-
-        stream_three, conv_state = conv_forward(stream_two, window_ids, conv_weights)
-        stream_four, ffn2_state = ffn_forward(stream_three, ffn2_gain, ffn2_weights)
-        final_out, final_hat, final_inverse = norm_forward(stream_four, final_gain)
-        layer_low = final_out.astype(bf16)
-        grad_four, final_gain_grad = norm_backward(
-            pick(cotangent).astype(jnp.float32), final_hat, final_inverse, final_gain
-        )
-        grad_three, ffn2_gain_grad, f2_in_g, f2_out_g = ffn_backward(
-            grad_four, ffn2_state, ffn2_gain, ffn2_weights
-        )
-        grad_two, pw_in_g, pw_out_g, conv_small = conv_backward(
-            grad_three, conv_state, window_ids, conv_weights
-        )
-
-        branch_low = grad_two.astype(bf16)
-        mix_grad = jnp.concatenate(
-            [
-                against(branch_low, output_weight).astype(bf16),
-                plain(branch_low, far_output).astype(bf16),
-            ],
-            axis=1,
-        )
-        q_grad, kv_grad, tile_grads = attend_back(
-            scalars, query, tiles, query_ids[None], ids[:, None], mixture, mix_grad, log_total, pieces, per_shard
-        )
-        for bit in bits(lax.axis_size("seq")):
+        for bit in seq_bits:
             half = kv_grad.shape[0] // 2
             kv_grad = (
                 kv_grad[:half].astype(jnp.float32)
                 + swap(kv_grad[half:], "seq", bit).astype(jnp.float32)
             ).astype(bf16)
-        kv_grad = kv_grad[0]
-        kv_cols = 2 * q_cols
-        own_grads = jnp.concatenate([q_grad[:, :q_cols], kv_grad[:, :kv_cols]], axis=1)
-        far_grads = jnp.concatenate([q_grad[:, q_cols:], kv_grad[:, kv_cols:]], axis=1)
-        normed_grad = team_sum(against(own_grads, qkv) + against(far_grads, far_qkv))
-        o_g = scatter_rows(branch_low, mixture, order_b[::-1])
-        qkv_g = scatter_rows(low, jnp.concatenate([own_grads, far_grads], 1), order_a[::-1])
-        came = far_swap(
-            jnp.concatenate([qkv_g[:, n_qkv:], o_g[:, out_cols:]], 1).astype(bf16)
-        ).astype(jnp.float32)
-        qkv_g = qkv_g[:, :n_qkv] + came[:, :n_qkv]
-        o_g = (o_g[:, :out_cols] + came[:, n_qkv:]).T
-        table_grad = lax.dot_general(
-            offset_sums(tile_grads), onehot, (((1,), (1,)), ((), ())), precision=HIGHEST
+        q_grads.append(q_grad)
+        kv_grads.append(kv_grad[0])
+        table_grads.append(
+            lax.dot_general(
+                offset_sums(tile_grads), onehot, (((1,), (1,)), ((), ())), precision=HIGHEST
+            )
         )
-        stream_part, attn_gain_grad = norm_backward(normed_grad, normed, inverse, attn_gain)
-        grad_one = grad_two + stream_part
-        grad_zero, ffn1_gain_grad, f1_in_g, f1_out_g = ffn_backward(
-            grad_one, ffn1_state, ffn1_gain, ffn1_weights
+    qkv_grads = [jnp.concatenate(pair, axis=1) for pair in zip(q_grads, kv_grads)]
+    grad_parts = [cut_parts(grads) for grads in qkv_grads]
+    normed_grad = reduce_parts(
+        [against(own, own_qkv) + against(far, far_qkv) for own, far in zip(*grad_parts)]
+    )
+    attn_grads = scatter_groups(
+        jnp.concatenate(
+            [
+                grad_of(branch_low, jnp.concatenate(mixtures, axis=1)),
+                grad_of(low, jnp.concatenate(qkv_grads, axis=1)),
+            ],
+            axis=1,
         )
-        big = (f1_in_g, f1_out_g, qkv_g, o_g, pw_in_g, pw_out_g, f2_in_g, f2_out_g)
-        gains = [ffn2_gain_grad, final_gain_grad] + conv_small
-        outs.append((layer_low, grad_zero, big, gains, table_grad, ffn1_gain_grad, attn_gain_grad))
-
-    total = lambda items: functools.reduce(lambda one, two: one + two, items)
-    big = [total([out[2][i] for out in outs]) for i in range(8)]
-    f1_in_g, f1_out_g, qkv_g, o_g, pw_in_g, pw_out_g, f2_in_g, f2_out_g = big
-    gains = [total([out[3][i] for out in outs]) for i in range(len(outs[0][3]))]
-    table_grad = total([out[4] for out in outs])
-    per_shard = position_table.shape[0]
+    )
+    stream_part, attn_gain_grad = norm_backward(normed_grad, attn_hat, attn_inverse, attn_gain)
+    grad_one = grad_two + stream_part
+
+    own_branch = (0.5 * grad_one).astype(bf16)
+    branches = [gather_parts(own_branch), gather_parts(far_swap(own_branch))]
+    pre_lows, partials = [], []
+    for f in (0, 1):
+        pre_lows.append(
+            [
+                (against(branch, ffn1_out) * silu_slope(pre)).astype(bf16)
+                for branch, pre in zip(branches[f], ffn1_pre[f])
+            ]
+        )
+        partials.append([against(pre_low, ffn1_in) for pre_low in pre_lows[f]])
+    every_frame = lambda lists: join(lists[0] + lists[1])
+    f1_out_g = scatter_groups(grad_of(every_frame(branches), every_frame(ffn1_act)))
+    f1_in_g = scatter_groups(grad_of(every_frame(ffn1_low), every_frame(pre_lows)))
+    far_part = far_swap(reduce_parts(partials[1]).astype(bf16)).astype(jnp.float32)
+    normed_grad = reduce_parts(partials[0]) + far_part
+    stream_part, ffn1_gain_grad = norm_backward(normed_grad, *ffn1_norm, ffn1_gain)
+    grad_zero = grad_one + stream_part
+
+    ffn2_grads = after(ffn2_grads, kv_grads[0])
+    n_hid = 2 * hidden
+    f2_out_g, f2_in_g = fold_far(
+        ffn2_grads,
+        [(hidden, n_hid), (n_hid + hidden, 2 * n_hid)],
+        [(0, hidden), (n_hid, n_hid + hidden)],
+    )
+    conv_grads = fold_heads(after(conv_grads, kv_grads[1]))
+    attn_grads = after(attn_grads, branches[0][-1])
+    n_out = 2 * out_cols
+    o_g, qkv_g = fold_far(
+        attn_grads,
+        [(out_cols, n_out), (n_out + n_qkv, n_out + 2 * n_qkv)],
+        [(0, out_cols), (n_out, n_out + n_qkv)],
+    )
+
+    gains = [ffn2_gain_grad, final_gain_grad] + conv_small
     all_heads = jnp.zeros((n_heads * per_shard, position_table.shape[1]), jnp.float32)
+    all_heads = lax.dynamic_update_slice_in_dim(all_heads, table_grads[0], place * per_shard, 0)
     all_heads = lax.dynamic_update_slice_in_dim(
-        all_heads, team * table_grad[:per_shard], place * per_shard, 0
-    )
-    all_heads = lax.dynamic_update_slice_in_dim(
-        all_heads, team * table_grad[per_shard:], (place ^ team) * per_shard, 0
+        all_heads, table_grads[1], (place ^ team) * per_shard, 0
     )
     small = jnp.concatenate([jnp.stack(gains).reshape(-1), all_heads.reshape(-1)])
-    small = small.reshape(-1, 128) * (1.0 / team)
     everyone = ("dp", "seq", "heads")
-    small = sum_everyone(small).reshape(-1)
+    small = sum_everyone(small.reshape(-1, 128)).reshape(-1)
     gains_all = small[: len(gains) * width].reshape(len(gains), width)
     table_all = small[len(gains) * width :].reshape(all_heads.shape)
     table_mine = lax.dynamic_slice_in_dim(table_all, place * per_shard, per_shard, 0)
@@ -677,40 +758,36 @@
     conv_part = lax.dynamic_slice_in_dim(
         gains_all[2:], lax.axis_index(everyone) * every, every, 1
     )
-    last = jnp.stack([total([out[5] for out in outs]), total([out[6] for out in outs])])
-    last = last.reshape(-1, 128) * (1.0 / team)
+    last = jnp.stack([ffn1_gain_grad, attn_gain_grad]).reshape(-1, 128)
     last = sum_everyone(last).reshape(2, width)
     last_part = lax.dynamic_slice_in_dim(last, group_at * part, part, 1)
 
-    def both_rows(pieces):
-        mine = jnp.stack(pieces)
-        other = far_swap(mine.astype(bf16)).astype(mine.dtype)
+    def everywhere(own):
+        near, far = gather_parts(own), gather_parts(far_swap(own))
+        near, far = reorder(near), reorder(far)
         first = my_row == 0
-        return jnp.concatenate([jnp.where(first, mine, other), jnp.where(first, other, mine)], 0)
-
-    layer_out = both_rows([out[0] for out in outs])
-    input_grad = both_rows([out[1] for out in outs])
-    q_cols = query_weight.shape[1]
+        return jnp.stack([jnp.where(first, near, far), jnp.where(first, far, near)])
+
     return (
-        layer_out,
-        input_grad,
+        everywhere(after(layer_low, branch_low)),
+        everywhere(grad_zero.astype(bf16)).astype(jnp.float32),
         last_part[0],
-        f1_in_g,
-        f1_out_g,
+        f1_in_g.astype(jnp.float32),
+        f1_out_g.T.astype(jnp.float32),
         last_part[1],
         qkv_g[:, :q_cols],
         qkv_g[:, q_cols : 2 * q_cols],
         qkv_g[:, 2 * q_cols :],
-        o_g,
+        o_g.T,
         table_mine,
         conv_part[0],
-        pw_in_g,
+        conv_grads[:, : 2 * width],
         conv_part[2:],
         conv_part[1],
-        pw_out_g,
+        conv_grads[:, 2 * width :],
         group_part[0],
         f2_in_g,
-        f2_out_g,
+        f2_out_g.T,
         group_part[1],
     )
 

time: 882 us -> 762 us (0.86); the launches traced: 867 us -> 758 us
  local copies, waits for them, and re-layouts: 89.3 us -> 42.7 us
  waiting for transfers between devices: 420 us -> 377 us
  other arithmetic: 108 us -> 80.3 us
    ppermute x79 -> x50, waiting for transfers between devices: 418 us -> 369 us  [swap(): return lax.ppermute(array, axis, [(i, i ^ 1 << bit) for i in range(count)])]
    unnamed x512 -> x296, local copies, waits for them, and re-layouts: 53.7 us -> 17 us
    concatenate x27 -> x14, other arithmetic: 21.3 us -> 37.4 us  [the longest x2 16.2 us: join(): return parts[0] if len(parts) == 1 else jnp.concatenate(parts, axis=0)]
    dot_general x16 -> x8, matrix products: 39.8 us -> 27.3 us  [outer(): lax.dot_general(left, right, (((0,), (0,)), ((), ())), preferred_element_...]
    convert_element_type x24 -> x12, other arithmetic: 23.9 us -> 13.9 us  [the longest x1 3.51 us: on_device(): everywhere(grad_zero.astype(bf16)).astype(jnp.float32)]
    dot_general x16 -> x25, matrix products: 31.1 us -> 40.9 us  [plain(): return jnp.dot(left, right, preferred_element_type=jnp.float32)]
    select_n x20 -> x5, other arithmetic: 12.9 us -> 3.73 us  [the longest x2 2.21 us: everywhere(): return jnp.stack([jnp.where(first, near, far), jnp.where(first, far, near)])]
    ppermute x79 -> x50, starting transfers between devices: 74.5 us -> 69.9 us  [swap(): return lax.ppermute(array, axis, [(i, i ^ 1 << bit) for i in range(count)])]
  transfers between devices with their start and end apart: 83 -> 62, of which waited for: 40 -> 39; matrix products, arithmetic and copies ran while one was open for 26% -> 23% of each run, Pallas kernels for 7% -> 7%
where the time goes in v2:
time: 762 us; the launch traced here: 758 us
  waiting for transfers between devices  377 us (49%)
  matrix products  97 us (13%)
  starting transfers between devices  81.5 us (11%)
  other arithmetic  80.3 us (11%)
  Pallas kernels  62.5 us (8%)
  local copies, waits for them, and re-layouts  42.7 us (6%)
  between operations  16.7 us (2%)
    ppermute x50, waiting for transfers between devices, swap(): return lax.ppermute(array, axis, [(i, i ^ 1 << bit) for i in range(count)])  369 us
    ppermute x50, starting transfers between devices, swap(): return lax.ppermute(array, axis, [(i, i ^ 1 << bit) for i in range(count)])  69.9 us
    dot_general x25, matrix products, plain(): return jnp.dot(left, right, preferred_element_type=jnp.float32)  40.9 us
    dot_general x25, matrix products, against(): lax.dot_general(left, right, (((1,), (1,)), ((), ())), preferred_element_...  27.5 us
    dot_general x8, matrix products, outer(): lax.dot_general(left, right, (((0,), (0,)), ((), ())), preferred_element_...  27.3 us
    pallas_call x2, Pallas kernels, attend_back(): pl.pallas_call(fn, grid_spec=pltpu.PrefetchScalarGridSpec(num_scalar_pref...  25.7 us
    pallas_call x2, Pallas kernels, attend(): pl.pallas_call(fn, grid_spec=pltpu.PrefetchScalarGridSpec(num_scalar_pref...  22.1 us
    unnamed x296, local copies, waits for them, and re-layouts  17 us
  transfers between devices with their start and end apart: 62, of which 39 were waited for; matrix products, arithmetic and copies ran while one was open for 23% of the time, Pallas kernels for 7%

profile of v2, /device:TPU:0, one launch (start us, length us, event | category | flops | bytes accessed | tf_op | source)
XLA Modules:
  0.0 758.1 jit_solution(657876099390339646)
XLA Ops:
  11.9 4.1 collective-permute-start.7
  16.2 11.8 %collective-permute-done.7 = bf16[128,1024]{1,0:T(8,128)(2,1)S(1)} collective-permute-done((bf16[128,1024]{1,0:T(8,128)(2,1)S(1)}, bf16[128,1024]{1,0:T(8,128)(2,1)S(1)}, u32[]{:S(2)}, u32[]{:S(2)}) %collective-permute-start.7) | collective-permute-done | bytes 262176 | tf_op jit(solution)/shard_map/ppermute | solution.py:240
  29.6 5.5 collective-permute-done.11
  38.4 17.8 %collective-permute-done.12 = bf16[64,3200]{1,0:T(8,128)(2,1)S(1)} collective-permute-done((bf16[64,3200]{1,0:T(8,128)(2,1)S(1)}, bf16[64,3200]{1,0:T(8,128)(2,1)S(1)}, u32[]{:S(2)}, u32[]{:S(2)}) %collective-permute-start.12) | collective-permute-done | bytes 409632 | tf_op jit(solution)/shard_map/ppermute | solution.py:240
  82.4 10.8 %collective-permute-done.1 = bf16[256,1024]{1,0:T(8,128)(2,1)} collective-permute-done((bf16[256,1024]{1,0:T(8,128)(2,1)}, bf16[256,1024]{1,0:T(8,128)(2,1)}, u32[]{:S(2)}, u32[]{:S(2)}) %collective-permute-start.1) | collective-permute-done | bytes 524320 | tf_op jit(solution)/shard_map/ppermute | solution.py:240
  97.8 4.8 collective-permute-done
  102.7 25.0 %collective-permute-done.2 = bf16[256,1024]{1,0:T(8,128)(2,1)S(1)} collective-permute-done((bf16[256,1024]{1,0:T(8,128)(2,1)S(1)}, bf16[256,1024]{1,0:T(8,128)(2,1)S(1)}, u32[]{:S(2)}, u32[]{:S(2)}) %collective-permute-start.2) | collective-permute-done | bytes 524320 | tf_op jit(solution)/shard_map/ppermute | solution.py:240
  130.8 13.9 %collective-permute-done.3 = bf16[256,1024]{1,0:T(8,128)(2,1)} collective-permute-done((bf16[256,1024]{1,0:T(8,128)(2,1)}, bf16[256,1024]{1,0:T(8,128)(2,1)}, u32[]{:S(2)}, u32[]{:S(2)}) %collective-permute-start.3) | collective-permute-done | bytes 524320 | tf_op jit(solution)/shard_map/ppermute | solution.py:240
  154.4 8.4 %collective-permute-done.5.refs_5_.refs_8_ = bf16[1,512,512]{2,1,0:T(8,128)(2,1)} collective-permute-done((bf16[1,512,512]{2,1,0:T(8,128)(2,1)}, bf16[1,512,512]{2,1,0:T(8,128)(2,1)}, u32[]{:S(2)}, u32[]{:S(2)}) %collective-permute-start.5) | collective-permute-done | bytes 524320 | tf_op jit(solution)/shard_map/ppermute | solution.py:240
  165.1 7.0 collective-permute-done.8.refs_5_.refs_8_
  172.1 13.9 %pad_maximum_fusion.6 = bf16[2,512,512]{2,1,0:T(8,128)(2,1)} fusion(bf16[1,512,512]{2,1,0:T(8,128)(2,1)S(1)} %collective-permute-done.8.refs_5_.refs_8_, bf16[1,512,512]{2,1,0:T(8,128)(2,1)S(1)} %fusion.138.refs_4_.refs_7_), kind=kLoop, calls=%fused_computation.232 | loop fusion | flops 524288 | bytes 2097152 | tf_op jit(solution)/shard_map/concatenate | solution.py:361
  196.7 11.2 %shard_map.366 = (bf16[512,256]{1,0:T(8,128)(2,1)}, f32[2,1,512]{2,1,0:T(1,128)}) custom-call(s32[5]{0:T(128)} %pad_add_fusion.1.scal, bf16[512,256]{1,0:T(8,128)(2,1)} %convolution_convert_fusion.15.refs_0_, f32[2,9,256,256]{3,2,1,0:T(8,128)} %shard_map.365.refs_1_, s32[1,512]{1,0:T(1,128)} %get-tuple-element.193.refs_2_, s32[2048,1]{1,0:T(8,128)} %copy.79.refs_3_, ...), custom_call_target="tpu_custom_call" | custom-call | flops 1073741824 | bytes 4718592 | tf_op jit(solution)/shard_map/pallas_call | solution.py:128
  210.1 11.0 %shard_map.368 = (bf16[512,256]{1,0:T(8,128)(2,1)}, f32[2,1,512]{2,1,0:T(1,128)}) custom-call(s32[5]{0:T(128)} %pad_add_fusion.1.scal, bf16[512,256]{1,0:T(8,128)(2,1)} %convolution_convert_fusion.14.refs_0_, f32[2,9,256,256]{3,2,1,0:T(8,128)} %shard_map.367.refs_1_, s32[1,512]{1,0:T(1,128)} %get-tuple-element.193.refs_2_, s32[2048,1]{1,0:T(8,128)} %copy.79.refs_3_, ...), custom_call_target="tpu_custom_call" | custom-call | flops 1073741824 | bytes 4718592 | tf_op jit(solution)/shard_map/pallas_call | solution.py:128
  225.0 12.2 %collective-permute-done.10 = bf16[256,1024]{1,0:T(8,128)(2,1)S(1)} collective-permute-done((bf16[256,1024]{1,0:T(8,128)(2,1)S(1)}, bf16[256,1024]{1,0:T(8,128)(2,1)S(1)}, u32[]{:S(2)}, u32[]{:S(2)}) %collective-permute-start.10) | collective-permute-done | bytes 524320 | tf_op jit(solution)/shard_map/ppermute | solution.py:240
  240.4 3.9 fusion.2
  245.8 4.5 collective-permute-start.13
  260.5 8.8 %collective-permute-done.16 = bf16[256,1024]{1,0:T(8,128)(2,1)S(1)} collective-permute-done((bf16[256,1024]{1,0:T(8,128)(2,1)S(1)}, bf16[256,1024]{1,0:T(8,128)(2,1)S(1)}, u32[]{:S(2)}, u32[]{:S(2)}) %collective-permute-start.16) | collective-permute-done | bytes 524320 | tf_op jit(solution)/shard_map/ppermute | solution.py:240
  281.6 10.3 %collective-permute-done.17 = bf16[256,1024]{1,0:T(8,128)(2,1)S(1)} collective-permute-done((bf16[256,1024]{1,0:T(8,128)(2,1)S(1)}, bf16[256,1024]{1,0:T(8,128)(2,1)S(1)}, u32[]{:S(2)}, u32[]{:S(2)}) %collective-permute-start.17) | collective-permute-done | bytes 524320 | tf_op jit(solution)/shard_map/ppermute | solution.py:240
  297.8 11.6 %collective-permute-done.18 = bf16[256,1024]{1,0:T(8,128)(2,1)S(1)} collective-permute-done((bf16[256,1024]{1,0:T(8,128)(2,1)S(1)}, bf16[256,1024]{1,0:T(8,128)(2,1)S(1)}, u32[]{:S(2)}, u32[]{:S(2)}) %collective-permute-start.18) | collective-permute-done | bytes 524320 | tf_op jit(solution)/shard_map/ppermute | solution.py:240
  317.6 10.3 %collective-permute-done.19 = bf16[256,1024]{1,0:T(8,128)(2,1)S(1)} collective-permute-done((bf16[256,1024]{1,0:T(8,128)(2,1)S(1)}, bf16[256,1024]{1,0:T(8,128)(2,1)S(1)}, u32[]{:S(2)}, u32[]{:S(2)}) %collective-permute-start.19) | collective-permute-done | bytes 524320 | tf_op jit(solution)/shard_map/ppermute | solution.py:240
  338.7 4.0 collective-permute-done.20
  349.2 13.4 %collective-permute-done.22 = bf16[256,1024]{1,0:T(8,128)(2,1)S(1)} collective-permute-done((bf16[256,1024]{1,0:T(8,128)(2,1)S(1)}, bf16[256,1024]{1,0:T(8,128)(2,1)S(1)}, u32[]{:S(2)}, u32[]{:S(2)}) %collective-permute-start.22) | collective-permute-done | bytes 524320 | tf_op jit(solution)/shard_map/ppermute | solution.py:240
  363.3 13.0 %shard_map.369 = (bf16[512,256]{1,0:T(8,128)(2,1)S(1)}, bf16[4,512,512]{2,1,0:T(8,128)(2,1)}, f32[2,9,256,256]{3,2,1,0:T(8,128)}) custom-call(s32[5]{0:T(128)S(1)} %copy-done.11, bf16[512,256]{1,0:T(8,128)(2,1)S(1)} %copy-done.9, f32[2,9,256,256]{3,2,1,0:T(8,128)} %shard_map.365.refs_1_, s32[1,512]{1,0:T(1,128)S(1)} %copy-done.10, s32[2048,1]{1,0:T(8,128)S(1)} %copy-done.1, ...), custom_call_target="tpu_custom_call" | custom-call | flops 2684354560 | bytes 9437184 | tf_op jit(solution)/shard_map/pallas_call | solution.py:206
  379.3 12.7 %shard_map.370 = (bf16[512,256]{1,0:T(8,128)(2,1)S(1)}, bf16[4,512,512]{2,1,0:T(8,128)(2,1)}, f32[2,9,256,256]{3,2,1,0:T(8,128)}) custom-call(s32[5]{0:T(128)S(1)} %copy-done.11, bf16[512,256]{1,0:T(8,128)(2,1)S(1)} %copy-done.8, f32[2,9,256,256]{3,2,1,0:T(8,128)} %shard_map.367.refs_1_, s32[1,512]{1,0:T(1,128)S(1)} %copy-done.10, s32[2048,1]{1,0:T(8,128)S(1)} %copy-done.1, ...), custom_call_target="tpu_custom_call" | custom-call | flops 2684354560 | bytes 9437184 | tf_op jit(solution)/shard_map/pallas_call | solution.py:206
  402.8 7.6 %collective-permute-done.27 = bf16[1,512,512]{2,1,0:T(8,128)(2,1)} collective-permute-done((bf16[1,512,512]{2,1,0:T(8,128)(2,1)}, bf16[1,512,512]{2,1,0:T(8,128)(2,1)}, u32[]{:S(2)}, u32[]{:S(2)}) %collective-permute-start.27) | collective-permute-done | bytes 524320 | tf_op jit(solution)/shard_map/ppermute | solution.py:240
  411.7 9.3 %collective-permute-done.29 = bf16[1,512,512]{2,1,0:T(8,128)(2,1)} collective-permute-done((bf16[1,512,512]{2,1,0:T(8,128)(2,1)}, bf16[1,512,512]{2,1,0:T(8,128)(2,1)}, u32[]{:S(2)}, u32[]{:S(2)}) %collective-permute-start.29) | collective-permute-done | bytes 524320 | tf_op jit(solution)/shard_map/ppermute | solution.py:240
  432.4 11.7 %collective-permute-done.30 = bf16[256,1024]{1,0:T(8,128)(2,1)S(1)} collective-permute-done((bf16[256,1024]{1,0:T(8,128)(2,1)S(1)}, bf16[256,1024]{1,0:T(8,128)(2,1)S(1)}, u32[]{:S(2)}, u32[]{:S(2)}) %collective-permute-start.30) | collective-permute-done | bytes 524320 | tf_op jit(solution)/shard_map/ppermute | solution.py:240
  448.7 22.6 %collective-permute-done.33 = bf16[256,1024]{1,0:T(8,128)(2,1)S(1)} collective-permute-done((bf16[256,1024]{1,0:T(8,128)(2,1)S(1)}, bf16[256,1024]{1,0:T(8,128)(2,1)S(1)}, u32[]{:S(2)}, u32[]{:S(2)}) %collective-permute-start.33) | collective-permute-done | bytes 524320 | tf_op jit(solution)/shard_map/ppermute | solution.py:240
  471.9 13.1 %collective-permute-done.34 = bf16[256,1024]{1,0:T(8,128)(2,1)S(1)} collective-permute-done((bf16[256,1024]{1,0:T(8,128)(2,1)S(1)}, bf16[256,1024]{1,0:T(8,128)(2,1)S(1)}, u32[]{:S(2)}, u32[]{:S(2)}) %collective-permute-start.34) | collective-permute-done | bytes 524320 | tf_op jit(solution)/shard_map/ppermute | solution.py:240
  485.8 3.8 fusion.48
  501.6 3.9 convolution_convert_fusion.4
  507.0 4.9 pad_maximum_fusion.1
  512.0 6.4 convolution_convert_fusion
  518.4 4.4 convolution_convert_fusion.1
  522.8 8.0 %pad_maximum_fusion = bf16[1024,4096]{1,0:T(8,128)(2,1)} fusion(bf16[1024,2048]{1,0:T(8,128)(2,1)} %convolution_convert_fusion, bf16[1024,2048]{1,0:T(8,128)(2,1)} %convolution_convert_fusion.1), kind=kLoop, calls=%fused_computation | loop fusion | flops 16777216 | bytes 16777216 | tf_op jit(solution)/shard_map/concatenate | solution.py:400
  530.9 3.9 shard_map.371
  534.9 3.8 shard_map.372
  545.5 10.5 %collective-permute-start.48 = (f32[74,128]{1,0:T(8,128)S(1)}, f32[74,128]{1,0:T(8,128)S(1)}, u32[]{:S(2)}, u32[]{:S(2)}) collective-permute-start(f32[74,128]{1,0:T(8,128)S(1)} %fusion.354), channel_id=1, source_target_pairs={{0,16},{16,0},{1,17},{17,1},{2,18},{18,2},{3,19},{19,3},{4,20},{20... | collective-permute-start | bytes 113672 | tf_op jit(solution)/shard_map/ppermute | solution.py:240
  558.3 8.3 %collective-permute-done.24 = bf16[256,1024]{1,0:T(8,128)(2,1)} collective-permute-done((bf16[256,1024]{1,0:T(8,128)(2,1)S(1)}, bf16[256,1024]{1,0:T(8,128)(2,1)}, u32[]{:S(2)}, u32[]{:S(2)}) %collective-permute-start.24) | collective-permute-done | bytes 524320 | tf_op jit(solution)/shard_map/ppermute | solution.py:240
  569.2 10.1 %collective-permute-done.50 = f32[74,128]{1,0:T(8,128)S(1)} collective-permute-done((f32[74,128]{1,0:T(8,128)S(1)}, f32[74,128]{1,0:T(8,128)S(1)}, u32[]{:S(2)}, u32[]{:S(2)}) %collective-permute-start.50) | collective-permute-done | bytes 37920 | tf_op jit(solution)/shard_map/ppermute | solution.py:240
  586.0 11.4 %collective-permute-done.35 = bf16[256,1024]{1,0:T(8,128)(2,1)S(1)} collective-permute-done((bf16[256,1024]{1,0:T(8,128)(2,1)S(1)}, bf16[256,1024]{1,0:T(8,128)(2,1)S(1)}, u32[]{:S(2)}, u32[]{:S(2)}) %collective-permute-start.35) | collective-permute-done | bytes 524320 | tf_op jit(solution)/shard_map/ppermute | solution.py:240
  602.9 14.9 %collective-permute-done.32 = bf16[256,1024]{1,0:T(8,128)(2,1)S(1)} collective-permute-done((bf16[256,1024]{1,0:T(8,128)(2,1)S(1)}, bf16[256,1024]{1,0:T(8,128)(2,1)S(1)}, u32[]{:S(2)}, u32[]{:S(2)}) %collective-permute-start.32) | collective-permute-done | bytes 524320 | tf_op jit(solution)/shard_map/ppermute | solution.py:240
  628.3 9.7 %collective-permute-start.42 = (f32[16,128]{1,0:T(8,128)S(1)}, f32[16,128]{1,0:T(8,128)S(1)}, u32[]{:S(2)}, u32[]{:S(2)}) collective-permute-start(f32[16,128]{1,0:T(8,128)S(1)} %add.546), channel_id=1, source_target_pairs={{0,16},{16,0},{1,17},{17,1},{2,18},{18,2},{3,19},{19,3},{4,20},{20... | collective-permute-start | bytes 24584 | tf_op jit(solution)/shard_map/ppermute | solution.py:240
  642.2 22.0 %collective-permute-done.43 = f32[16,128]{1,0:T(8,128)S(1)} collective-permute-done((f32[16,128]{1,0:T(8,128)S(1)}, f32[16,128]{1,0:T(8,128)S(1)}, u32[]{:S(2)}, u32[]{:S(2)}) %collective-permute-start.43) | collective-permute-done | bytes 8224 | tf_op jit(solution)/shard_map/ppermute | solution.py:240
  670.6 9.8 %collective-permute-done.39 = bf16[256,1024]{1,0:T(8,128)(2,1)S(1)} collective-permute-done((bf16[256,1024]{1,0:T(8,128)(2,1)S(1)}, bf16[256,1024]{1,0:T(8,128)(2,1)S(1)}, u32[]{:S(2)}, u32[]{:S(2)}) %collective-permute-start.39) | collective-permute-done | bytes 524320 | tf_op jit(solution)/shard_map/ppermute | solution.py:240
  700.1 17.5 %collective-permute-done.51 = bf16[64,3072]{1,0:T(8,128)(2,1)S(1)} collective-permute-done((bf16[64,3072]{1,0:T(8,128)(2,1)S(1)}, bf16[64,3072]{1,0:T(8,128)(2,1)S(1)}, u32[]{:S(2)}, u32[]{:S(2)}) %collective-permute-start.51) | collective-permute-done | bytes 393248 | tf_op jit(solution)/shard_map/ppermute | solution.py:240
  717.8 4.3 reduce-scatter.14.cloned.1.call-done
  727.2 21.8 %collective-permute-done.53 = bf16[128,2048]{1,0:T(8,128)(2,1)S(1)} collective-permute-done((bf16[128,2048]{1,0:T(8,128)(2,1)S(1)}, bf16[128,2048]{1,0:T(8,128)(2,1)S(1)}, u32[]{:S(2)}, u32[]{:S(2)}) %collective-permute-start.53) | collective-permute-done | bytes 524320 | tf_op jit(solution)/shard_map/ppermute | solution.py:240
  (620 shorter events, 247.4 us)
Async XLA Ops:
  7.2 142.0 %all-gather.4.cloned.1.call-start = ((), (), s32[]{:S(2)}) async-start(), calls=%async_computation.5 | async-start | bytes 2359296 | tf_op jit(solution)/shard_map/all_gather | solution.py:248
  11.9 16.1 %collective-permute-start.7 = (bf16[128,1024]{1,0:T(8,128)(2,1)S(1)}, bf16[128,1024]{1,0:T(8,128)(2,1)S(1)}, u32[]{:S(2)}, u32[]{:S(2)}) collective-permute-start(bf16[128,1024]{1,0:T(8,128)(2,1)S(1)} %pad_maximum_fusion.23), channel_id=1, source_target_pairs={{0,2},{1,3},{2,0},{3,1},{4,6},{5,7},{6,4},{7,5},{8,10},{9,11},{10,... | collective-permute-start | bytes 786440 | tf_op jit(solution)/shard_map/ppermute | solution.py:240
  28.7 210.3 %all-gather.6.cloned.1.call-start = ((), (), s32[]{:S(2)}) async-start(), calls=%async_computation.6 | async-start | bytes 7372800 | tf_op jit(solution)/shard_map/all_gather | solution.py:248
  35.2 21.0 %collective-permute-start.12 = (bf16[64,3200]{1,0:T(8,128)(2,1)S(1)}, bf16[64,3200]{1,0:T(8,128)(2,1)S(1)}, u32[]{:S(2)}, u32[]{:S(2)}) collective-permute-start(bf16[64,3200]{1,0:T(8,128)(2,1)S(1)} %pad_maximum_fusion.22), channel_id=1, source_target_pairs={{0,2},{1,3},{2,0},{3,1},{4,6},{5,7},{6,4},{7,5},{8,10},{9,11},{10,... | collective-permute-start | bytes 1228808 | tf_op jit(solution)/shard_map/ppermute | solution.py:240
  57.4 216.1 %all-gather.8.cloned.1.call-start = ((), (), s32[]{:S(2)}) async-start(), calls=%async_computation.7 | async-start | bytes 4718592 | tf_op jit(solution)/shard_map/all_gather | solution.py:248
  66.8 26.4 %collective-permute-start.1 = (bf16[256,1024]{1,0:T(8,128)(2,1)}, bf16[256,1024]{1,0:T(8,128)(2,1)}, u32[]{:S(2)}, u32[]{:S(2)}) collective-permute-start(bf16[256,1024]{1,0:T(8,128)(2,1)} %convolution_convert_fusion.8), channel_id=1, source_target_pairs={{0,1},{1,0},{2,3},{3,2},{4,5},{5,4},{6,7},{7,6},{8,9},{9,8},{10,11... | collective-permute-start | bytes 1572872 | tf_op jit(solution)/shard_map/ppermute | solution.py:240
  70.7 31.9 %collective-permute-start = (bf16[256,1024]{1,0:T(8,128)(2,1)}, bf16[256,1024]{1,0:T(8,128)(2,1)}, u32[]{:S(2)}, u32[]{:S(2)}) collective-permute-start(bf16[256,1024]{1,0:T(8,128)(2,1)} %convolution_convert_fusion.9), channel_id=1, source_target_pairs={{0,1},{1,0},{2,3},{3,2},{4,5},{5,4},{6,7},{7,6},{8,9},{9,8},{10,11... | collective-permute-start | bytes 1572872 | tf_op jit(solution)/shard_map/ppermute | solution.py:240
  72.1 82.1 %collective-permute-start.4 = (f32[2,32]{1,0:T(2,128)S(1)}, f32[2,32]{1,0:T(2,128)S(1)}, u32[]{:S(2)}, u32[]{:S(2)}) collective-permute-start(f32[2,32]{1,0:T(2,128)S(1)} %copy-done.121), channel_id=1, source_target_pairs={{0,2},{1,3},{2,0},{3,1},{4,6},{5,7},{6,4},{7,5},{8,10},{9,11},{10,... | collective-permute-start | bytes 776 | tf_op jit(solution)/shard_map/ppermute | solution.py:240
  76.0 118.2 %collective-permute-start.15 = (bf16[128,2048]{1,0:T(8,128)(2,1)}, bf16[128,2048]{1,0:T(8,128)(2,1)}, u32[]{:S(2)}, u32[]{:S(2)}) collective-permute-start(bf16[128,2048]{1,0:T(8,128)(2,1)} %pad_maximum_fusion.20), channel_id=1, source_target_pairs={{0,2},{1,3},{2,0},{3,1},{4,6},{5,7},{6,4},{7,5},{8,10},{9,11},{10,... | collective-permute-start | bytes 1572872 | tf_op jit(solution)/shard_map/ppermute | solution.py:240
  95.0 32.6 %collective-permute-start.2 = (bf16[256,1024]{1,0:T(8,128)(2,1)S(1)}, bf16[256,1024]{1,0:T(8,128)(2,1)S(1)}, u32[]{:S(2)}, u32[]{:S(2)}) collective-permute-start(bf16[256,1024]{1,0:T(8,128)(2,1)S(1)} %add_convert_fusion.5), channel_id=1, source_target_pairs={{0,2},{1,3},{2,0},{3,1},{4,6},{5,7},{6,4},{7,5},{8,10},{9,11},{10,... | collective-permute-start | bytes 1572872 | tf_op jit(solution)/shard_map/ppermute | solution.py:240
  130.6 14.2 %collective-permute-start.3 = (bf16[256,1024]{1,0:T(8,128)(2,1)}, bf16[256,1024]{1,0:T(8,128)(2,1)}, u32[]{:S(2)}, u32[]{:S(2)}) collective-permute-start(bf16[256,1024]{1,0:T(8,128)(2,1)} %multiply_convert_fusion.14), channel_id=1, source_target_pairs={{0,1},{1,0},{2,3},{3,2},{4,5},{5,4},{6,7},{7,6},{8,9},{9,8},{10,11... | collective-permute-start | bytes 1572872 | tf_op jit(solution)/shard_map/ppermute | solution.py:240
  147.7 15.1 %collective-permute-start.5 = (bf16[1,512,512]{2,1,0:T(8,128)(2,1)}, bf16[1,512,512]{2,1,0:T(8,128)(2,1)}, u32[]{:S(2)}, u32[]{:S(2)}) collective-permute-start(bf16[1,512,512]{2,1,0:T(8,128)(2,1)} %fusion.137.refs_4_.refs_7_), channel_id=1, source_target_pairs={{0,8},{4,12},{8,0},{12,4},{1,9},{5,13},{9,1},{13,5},{2,10},{6,14},... | collective-permute-start | bytes 1572872 | tf_op jit(solution)/shard_map/ppermute | solution.py:240
  151.5 20.6 %collective-permute-start.8 = (bf16[1,512,512]{2,1,0:T(8,128)(2,1)S(1)}, bf16[1,512,512]{2,1,0:T(8,128)(2,1)S(1)}, u32[]{:S(2)}, u32[]{:S(2)}) collective-permute-start(bf16[1,512,512]{2,1,0:T(8,128)(2,1)S(1)} %fusion.138.refs_4_.refs_7_), channel_id=1, source_target_pairs={{0,8},{4,12},{8,0},{12,4},{1,9},{5,13},{9,1},{13,5},{2,10},{6,14},... | collective-permute-start | bytes 1572872 | tf_op jit(solution)/shard_map/ppermute | solution.py:240
  165.1 31.6 %collective-permute-start.6 = (bf16[2,512,512]{2,1,0:T(8,128)(2,1)}, bf16[2,512,512]{2,1,0:T(8,128)(2,1)}, u32[]{:S(2)}, u32[]{:S(2)}) collective-permute-start(bf16[2,512,512]{2,1,0:T(8,128)(2,1)} %pad_maximum_fusion.5), channel_id=1, source_target_pairs={{0,4},{4,0},{8,12},{12,8},{1,5},{5,1},{9,13},{13,9},{2,6},{6,2},{1... | collective-permute-start | bytes 3145736 | tf_op jit(solution)/shard_map/ppermute | solution.py:240
  186.0 24.0 %collective-permute-start.9 = (bf16[2,512,512]{2,1,0:T(8,128)(2,1)}, bf16[2,512,512]{2,1,0:T(8,128)(2,1)}, u32[]{:S(2)}, u32[]{:S(2)}) collective-permute-start(bf16[2,512,512]{2,1,0:T(8,128)(2,1)} %pad_maximum_fusion.6), channel_id=1, source_target_pairs={{0,4},{4,0},{8,12},{12,8},{1,5},{5,1},{9,13},{13,9},{2,6},{6,2},{1... | collective-permute-start | bytes 3145736 | tf_op jit(solution)/shard_map/ppermute | solution.py:240
  194.2 487.8 %reduce-scatter.10.cloned.1.call-start = ((), (), s32[]{:S(2)}) async-start(), calls=%async_computation.10 | async-start | bytes 4718592 | tf_op jit(solution)/shard_map/reduce_scatter | solution.py:365
  222.9 14.4 %collective-permute-start.10 = (bf16[256,1024]{1,0:T(8,128)(2,1)S(1)}, bf16[256,1024]{1,0:T(8,128)(2,1)S(1)}, u32[]{:S(2)}, u32[]{:S(2)}) collective-permute-start(bf16[256,1024]{1,0:T(8,128)(2,1)S(1)} %fusion.130), channel_id=1, source_target_pairs={{0,1},{1,0},{2,3},{3,2},{4,5},{5,4},{6,7},{7,6},{8,9},{9,8},{10,11... | collective-permute-start | bytes 1572872 | tf_op jit(solution)/shard_map/ppermute | solution.py:240
  256.3 13.0 %collective-permute-start.16 = (bf16[256,1024]{1,0:T(8,128)(2,1)S(1)}, bf16[256,1024]{1,0:T(8,128)(2,1)S(1)}, u32[]{:S(2)}, u32[]{:S(2)}) collective-permute-start(bf16[256,1024]{1,0:T(8,128)(2,1)S(1)} %multiply_convert_fusion.10), channel_id=1, source_target_pairs={{0,1},{1,0},{2,3},{3,2},{4,5},{5,4},{6,7},{7,6},{8,9},{9,8},{10,11... | collective-permute-start | bytes 1572872 | tf_op jit(solution)/shard_map/ppermute | solution.py:240
  277.6 14.2 %collective-permute-start.17 = (bf16[256,1024]{1,0:T(8,128)(2,1)S(1)}, bf16[256,1024]{1,0:T(8,128)(2,1)S(1)}, u32[]{:S(2)}, u32[]{:S(2)}) collective-permute-start(bf16[256,1024]{1,0:T(8,128)(2,1)S(1)} %fusion.112), channel_id=1, source_target_pairs={{0,1},{1,0},{2,3},{3,2},{4,5},{5,4},{6,7},{7,6},{8,9},{9,8},{10,11... | collective-permute-start | bytes 1572872 | tf_op jit(solution)/shard_map/ppermute | solution.py:240
  294.5 14.9 %collective-permute-start.18 = (bf16[256,1024]{1,0:T(8,128)(2,1)S(1)}, bf16[256,1024]{1,0:T(8,128)(2,1)S(1)}, u32[]{:S(2)}, u32[]{:S(2)}) collective-permute-start(bf16[256,1024]{1,0:T(8,128)(2,1)S(1)} %multiply_convert_fusion.4), channel_id=1, source_target_pairs={{0,1},{1,0},{2,3},{3,2},{4,5},{5,4},{6,7},{7,6},{8,9},{9,8},{10,11... | collective-permute-start | bytes 1572872 | tf_op jit(solution)/shard_map/ppermute | solution.py:240
  314.1 13.7 %collective-permute-start.19 = (bf16[256,1024]{1,0:T(8,128)(2,1)S(1)}, bf16[256,1024]{1,0:T(8,128)(2,1)S(1)}, u32[]{:S(2)}, u32[]{:S(2)}) collective-permute-start(bf16[256,1024]{1,0:T(8,128)(2,1)S(1)} %fusion.123), channel_id=1, source_target_pairs={{0,1},{1,0},{2,3},{3,2},{4,5},{5,4},{6,7},{7,6},{8,9},{9,8},{10,11... | collective-permute-start | bytes 1572872 | tf_op jit(solution)/shard_map/ppermute | solution.py:240
  349.1 13.5 %collective-permute-start.22 = (bf16[256,1024]{1,0:T(8,128)(2,1)S(1)}, bf16[256,1024]{1,0:T(8,128)(2,1)S(1)}, u32[]{:S(2)}, u32[]{:S(2)}) collective-permute-start(bf16[256,1024]{1,0:T(8,128)(2,1)S(1)} %get-tuple-element.184), channel_id=1, source_target_pairs={{0,1},{1,0},{2,3},{3,2},{4,5},{5,4},{6,7},{7,6},{8,9},{9,8},{10,11... | collective-permute-start | bytes 1572872 | tf_op jit(solution)/shard_map/ppermute | solution.py:240
  377.6 16.3 %collective-permute-start.26 = (bf16[2,512,512]{2,1,0:T(8,128)(2,1)S(1)}, bf16[2,512,512]{2,1,0:T(8,128)(2,1)S(1)}, u32[]{:S(2)}, u32[]{:S(2)}) collective-permute-start(bf16[2,512,512]{2,1,0:T(8,128)(2,1)S(1)} %slice.310), channel_id=1, source_target_pairs={{0,4},{4,0},{8,12},{12,8},{1,5},{5,1},{9,13},{13,9},{2,6},{6,2},{1... | collective-permute-start | bytes 3145736 | tf_op jit(solution)/shard_map/ppermute | solution.py:240
  395.3 15.1 %collective-permute-start.27 = (bf16[1,512,512]{2,1,0:T(8,128)(2,1)}, bf16[1,512,512]{2,1,0:T(8,128)(2,1)}, u32[]{:S(2)}, u32[]{:S(2)}) collective-permute-start(bf16[1,512,512]{2,1,0:T(8,128)(2,1)} %slice.382), channel_id=1, source_target_pairs={{0,8},{4,12},{8,0},{12,4},{1,9},{5,13},{9,1},{13,5},{2,10},{6,14},... | collective-permute-start | bytes 1572872 | tf_op jit(solution)/shard_map/ppermute | solution.py:240
  397.7 23.3 %collective-permute-start.29 = (bf16[1,512,512]{2,1,0:T(8,128)(2,1)}, bf16[1,512,512]{2,1,0:T(8,128)(2,1)}, u32[]{:S(2)}, u32[]{:S(2)}) collective-permute-start(bf16[1,512,512]{2,1,0:T(8,128)(2,1)} %slice.384), channel_id=1, source_target_pairs={{0,8},{4,12},{8,0},{12,4},{1,9},{5,13},{9,1},{13,5},{2,10},{6,14},... | collective-permute-start | bytes 1572872 | tf_op jit(solution)/shard_map/ppermute | solution.py:240
  427.6 262.7 %reduce-scatter.8.cloned.1.call-start = ((), (), s32[]{:S(2)}) async-start(), calls=%async_computation.9 | async-start | bytes 2359296 | tf_op jit(solution)/shard_map/reduce_scatter | solution.py:365
  430.7 13.4 %collective-permute-start.30 = (bf16[256,1024]{1,0:T(8,128)(2,1)S(1)}, bf16[256,1024]{1,0:T(8,128)(2,1)S(1)}, u32[]{:S(2)}, u32[]{:S(2)}) collective-permute-start(bf16[256,1024]{1,0:T(8,128)(2,1)S(1)} %fusion.109), channel_id=1, source_target_pairs={{0,1},{1,0},{2,3},{3,2},{4,5},{5,4},{6,7},{7,6},{8,9},{9,8},{10,11... | collective-permute-start | bytes 1572872 | tf_op jit(solution)/shard_map/ppermute | solution.py:240
  446.6 24.7 %collective-permute-start.33 = (bf16[256,1024]{1,0:T(8,128)(2,1)S(1)}, bf16[256,1024]{1,0:T(8,128)(2,1)S(1)}, u32[]{:S(2)}, u32[]{:S(2)}) collective-permute-start(bf16[256,1024]{1,0:T(8,128)(2,1)S(1)} %get-tuple-element.182), channel_id=1, source_target_pairs={{0,2},{1,3},{2,0},{3,1},{4,6},{5,7},{6,4},{7,5},{8,10},{9,11},{10,... | collective-permute-start | bytes 1572872 | tf_op jit(solution)/shard_map/ppermute | solution.py:240
  448.4 23.5 %collective-permute-start.31 = (bf16[256,1024]{1,0:T(8,128)(2,1)S(1)}, bf16[256,1024]{1,0:T(8,128)(2,1)S(1)}, u32[]{:S(2)}, u32[]{:S(2)}) collective-permute-start(bf16[256,1024]{1,0:T(8,128)(2,1)S(1)} %get-tuple-element.182), channel_id=1, source_target_pairs={{0,1},{1,0},{2,3},{3,2},{4,5},{5,4},{6,7},{7,6},{8,9},{9,8},{10,11... | collective-permute-start | bytes 1572872 | tf_op jit(solution)/shard_map/ppermute | solution.py:240
  471.3 13.7 %collective-permute-start.34 = (bf16[256,1024]{1,0:T(8,128)(2,1)S(1)}, bf16[256,1024]{1,0:T(8,128)(2,1)S(1)}, u32[]{:S(2)}, u32[]{:S(2)}) collective-permute-start(bf16[256,1024]{1,0:T(8,128)(2,1)S(1)} %collective-permute-done.33), channel_id=1, source_target_pairs={{0,1},{1,0},{2,3},{3,2},{4,5},{5,4},{6,7},{7,6},{8,9},{9,8},{10,11... | collective-permute-start | bytes 1572872 | tf_op jit(solution)/shard_map/ppermute | solution.py:240
  489.6 202.7 %reduce-scatter.6.cloned.1.call-start = ((), (), s32[]{:S(2)}) async-start(), calls=%async_computation.8 | async-start | bytes 2359296 | tf_op jit(solution)/shard_map/reduce_scatter | solution.py:365
  501.2 197.0 %reduce-scatter.12.cloned.1.call-start = ((), (), s32[]{:S(2)}) async-start(), calls=%async_computation.11 | async-start | bytes 7077888 | tf_op jit(solution)/shard_map/reduce_scatter | solution.py:365
  511.9 210.3 %reduce-scatter.14.cloned.1.call-start = ((), (), s32[]{:S(2)}) async-start(), calls=%async_computation.12 | async-start | bytes 9437184 | tf_op jit(solution)/shard_map/reduce_scatter | solution.py:365
  540.1 26.4 %collective-permute-start.24 = (bf16[256,1024]{1,0:T(8,128)(2,1)S(1)}, bf16[256,1024]{1,0:T(8,128)(2,1)}, u32[]{:S(2)}, u32[]{:S(2)}) collective-permute-start(bf16[256,1024]{1,0:T(8,128)(2,1)S(1)} %copy-done.41), channel_id=1, source_target_pairs={{0,2},{1,3},{2,0},{3,1},{4,6},{5,7},{6,4},{7,5},{8,10},{9,11},{10,... | collective-permute-start | bytes 1572872 | tf_op jit(solution)/shard_map/ppermute | solution.py:240
  540.2 27.8 %collective-permute-start.23 = (bf16[256,1024]{1,0:T(8,128)(2,1)S(1)}, bf16[256,1024]{1,0:T(8,128)(2,1)S(1)}, u32[]{:S(2)}, u32[]{:S(2)}) collective-permute-start(bf16[256,1024]{1,0:T(8,128)(2,1)S(1)} %copy-done.41), channel_id=1, source_target_pairs={{0,1},{1,0},{2,3},{3,2},{4,5},{5,4},{6,7},{7,6},{8,9},{9,8},{10,11... | collective-permute-start | bytes 1572872 | tf_op jit(solution)/shard_map/ppermute | solution.py:240
  545.5 12.5 %collective-permute-start.48 = (f32[74,128]{1,0:T(8,128)S(1)}, f32[74,128]{1,0:T(8,128)S(1)}, u32[]{:S(2)}, u32[]{:S(2)}) collective-permute-start(f32[74,128]{1,0:T(8,128)S(1)} %fusion.354), channel_id=1, source_target_pairs={{0,16},{16,0},{1,17},{17,1},{2,18},{18,2},{3,19},{19,3},{4,20},{20... | collective-permute-start | bytes 113672 | tf_op jit(solution)/shard_map/ppermute | solution.py:240
  566.5 71.5 %collective-permute-start.25 = (bf16[256,1024]{1,0:T(8,128)(2,1)}, bf16[256,1024]{1,0:T(8,128)(2,1)}, u32[]{:S(2)}, u32[]{:S(2)}) collective-permute-start(bf16[256,1024]{1,0:T(8,128)(2,1)} %collective-permute-done.24), channel_id=1, source_target_pairs={{0,1},{1,0},{2,3},{3,2},{4,5},{5,4},{6,7},{7,6},{8,9},{9,8},{10,11... | collective-permute-start | bytes 1572872 | tf_op jit(solution)/shard_map/ppermute | solution.py:240
  567.2 12.0 %collective-permute-start.50 = (f32[74,128]{1,0:T(8,128)S(1)}, f32[74,128]{1,0:T(8,128)S(1)}, u32[]{:S(2)}, u32[]{:S(2)}) collective-permute-start(f32[74,128]{1,0:T(8,128)S(1)} %add.557), channel_id=1, source_target_pairs={{0,2},{1,3},{2,0},{3,1},{4,6},{5,7},{6,4},{7,5},{8,10},{9,11},{10,... | collective-permute-start | bytes 113672 | tf_op jit(solution)/shard_map/ppermute | solution.py:240
  582.5 14.9 %collective-permute-start.35 = (bf16[256,1024]{1,0:T(8,128)(2,1)S(1)}, bf16[256,1024]{1,0:T(8,128)(2,1)S(1)}, u32[]{:S(2)}, u32[]{:S(2)}) collective-permute-start(bf16[256,1024]{1,0:T(8,128)(2,1)S(1)} %convolution_convert_fusion.6), channel_id=1, source_target_pairs={{0,1},{1,0},{2,3},{3,2},{4,5},{5,4},{6,7},{7,6},{8,9},{9,8},{10,11... | collective-permute-start | bytes 1572872 | tf_op jit(solution)/shard_map/ppermute | solution.py:240
  585.5 32.3 %collective-permute-start.32 = (bf16[256,1024]{1,0:T(8,128)(2,1)S(1)}, bf16[256,1024]{1,0:T(8,128)(2,1)S(1)}, u32[]{:S(2)}, u32[]{:S(2)}) collective-permute-start(bf16[256,1024]{1,0:T(8,128)(2,1)S(1)} %convolution_convert_fusion.7), channel_id=1, source_target_pairs={{0,1},{1,0},{2,3},{3,2},{4,5},{5,4},{6,7},{7,6},{8,9},{9,8},{10,11... | collective-permute-start | bytes 1572872 | tf_op jit(solution)/shard_map/ppermute | solution.py:240
  598.2 23.4 %collective-permute-start.36 = (bf16[256,1024]{1,0:T(8,128)(2,1)S(1)}, bf16[256,1024]{1,0:T(8,128)(2,1)S(1)}, u32[]{:S(2)}, u32[]{:S(2)}) collective-permute-start(bf16[256,1024]{1,0:T(8,128)(2,1)S(1)} %add_convert_fusion.2), channel_id=1, source_target_pairs={{0,2},{1,3},{2,0},{3,1},{4,6},{5,7},{6,4},{7,5},{8,10},{9,11},{10,... | collective-permute-start | bytes 1572872 | tf_op jit(solution)/shard_map/ppermute | solution.py:240
  628.2 40.7 %collective-permute-start.38 = (bf16[256,1024]{1,0:T(8,128)(2,1)}, bf16[256,1024]{1,0:T(8,128)(2,1)S(1)}, u32[]{:S(2)}, u32[]{:S(2)}) collective-permute-start(bf16[256,1024]{1,0:T(8,128)(2,1)} %fusion.144), channel_id=1, source_target_pairs={{0,2},{1,3},{2,0},{3,1},{4,6},{5,7},{6,4},{7,5},{8,10},{9,11},{10,... | collective-permute-start | bytes 1572872 | tf_op jit(solution)/shard_map/ppermute | solution.py:240
  628.3 12.7 %collective-permute-start.42 = (f32[16,128]{1,0:T(8,128)S(1)}, f32[16,128]{1,0:T(8,128)S(1)}, u32[]{:S(2)}, u32[]{:S(2)}) collective-permute-start(f32[16,128]{1,0:T(8,128)S(1)} %add.546), channel_id=1, source_target_pairs={{0,16},{16,0},{1,17},{17,1},{2,18},{18,2},{3,19},{19,3},{4,20},{20... | collective-permute-start | bytes 24584 | tf_op jit(solution)/shard_map/ppermute | solution.py:240
  639.3 30.1 %collective-permute-start.37 = (bf16[256,1024]{1,0:T(8,128)(2,1)}, bf16[256,1024]{1,0:T(8,128)(2,1)S(1)}, u32[]{:S(2)}, u32[]{:S(2)}) collective-permute-start(bf16[256,1024]{1,0:T(8,128)(2,1)} %fusion.144), channel_id=1, source_target_pairs={{0,1},{1,0},{2,3},{3,2},{4,5},{5,4},{6,7},{7,6},{8,9},{9,8},{10,11... | collective-permute-start | bytes 1572872 | tf_op jit(solution)/shard_map/ppermute | solution.py:240
  641.0 23.3 %collective-permute-start.43 = (f32[16,128]{1,0:T(8,128)S(1)}, f32[16,128]{1,0:T(8,128)S(1)}, u32[]{:S(2)}, u32[]{:S(2)}) collective-permute-start(f32[16,128]{1,0:T(8,128)S(1)} %add.547), channel_id=1, source_target_pairs={{0,1},{1,0},{2,3},{3,2},{4,5},{5,4},{6,7},{7,6},{8,9},{9,8},{10,11... | collective-permute-start | bytes 24584 | tf_op jit(solution)/shard_map/ppermute | solution.py:240
  684.6 12.7 %collective-permute-start.45 = (bf16[128,1024]{1,0:T(8,128)(2,1)}, bf16[128,1024]{1,0:T(8,128)(2,1)S(1)}, u32[]{:S(2)}, u32[]{:S(2)}) collective-permute-start(bf16[128,1024]{1,0:T(8,128)(2,1)} %pad_maximum_fusion.24), channel_id=1, source_target_pairs={{0,2},{1,3},{2,0},{3,1},{4,6},{5,7},{6,4},{7,5},{8,10},{9,11},{10,... | collective-permute-start | bytes 786440 | tf_op jit(solution)/shard_map/ppermute | solution.py:240
  699.2 18.4 %collective-permute-start.51 = (bf16[64,3072]{1,0:T(8,128)(2,1)S(1)}, bf16[64,3072]{1,0:T(8,128)(2,1)S(1)}, u32[]{:S(2)}, u32[]{:S(2)}) collective-permute-start(bf16[64,3072]{1,0:T(8,128)(2,1)S(1)} %constant_dynamic-slice_fusion.2), channel_id=1, source_target_pairs={{0,2},{1,3},{2,0},{3,1},{4,6},{5,7},{6,4},{7,5},{8,10},{9,11},{10,... | collective-permute-start | bytes 1179656 | tf_op jit(solution)/shard_map/ppermute | solution.py:240
  723.3 25.7 %collective-permute-start.53 = (bf16[128,2048]{1,0:T(8,128)(2,1)S(1)}, bf16[128,2048]{1,0:T(8,128)(2,1)S(1)}, u32[]{:S(2)}, u32[]{:S(2)}) collective-permute-start(bf16[128,2048]{1,0:T(8,128)(2,1)S(1)} %pad_maximum_fusion.21), channel_id=1, source_target_pairs={{0,2},{1,3},{2,0},{3,1},{4,6},{5,7},{6,4},{7,5},{8,10},{9,11},{10,... | collective-permute-start | bytes 1572872 | tf_op jit(solution)/shard_map/ppermute | solution.py:240
  (158 other events, 1369.7 us)
Sparse Core Ops, SparseCore 0:
  28.8 28.9 all-gather.3
  59.7 46.4 all-gather.5
  194.4 35.1 all-gather.7
  427.7 57.4 reduce-scatter.9
  489.8 47.7 reduce-scatter.7
  540.7 41.1 reduce-scatter.5
  585.3 61.8 reduce-scatter.11
  650.6 71.4 reduce-scatter.13

commit v3 on v2

--- a/solution.py
+++ b/solution.py
@@ -31,10 +31,10 @@
         in_specs=[pl.BlockSpec((1, 1, width), lambda h: (h, 0, 0))],
         out_specs=pl.BlockSpec((1, tiles, TILE, TILE), lambda h: (h, 0, 0, 0)),
         out_shape=jax.ShapeDtypeStruct((heads, tiles, TILE, TILE), jnp.float32),
-        cost_estimate=pl.CostEstimate(flops=heads*tiles*TILE*TILE*4, transcendentals=0, bytes_accessed=heads*tiles*TILE*TILE*4),
+        cost_estimate=pl.CostEstimate(flops=heads*TILE*TILE, transcendentals=0, bytes_accessed=heads*TILE*TILE),
     )(window[:, None])
 
-def offset_sums_kernel(tiles_ref, out_ref, wide):
+def offset_sums_kernel(when_ref, tiles_ref, out_ref, wide):
     tiles = tiles_ref.shape[1]
     for t in range(tiles):
         wide[:, t * TILE : (t + 1) * TILE] = tiles_ref[0, t]
@@ -46,18 +46,21 @@
         half //= 2
     out_ref[0] = rows
 
-def offset_sums(tile_grads):
+def offset_sums(tile_grads, when):
     heads, tiles = tile_grads.shape[:2]
     width = (tiles + 1) * TILE
     return pl.pallas_call(
         offset_sums_kernel,
         grid=(heads,),
-        in_specs=[pl.BlockSpec((1, tiles, TILE, TILE), lambda h: (h, 0, 0, 0))],
+        in_specs=[
+            pl.BlockSpec(memory_space=pltpu.SMEM),
+            pl.BlockSpec((1, tiles, TILE, TILE), lambda h: (h, 0, 0, 0)),
+        ],
         out_specs=pl.BlockSpec((1, 1, width), lambda h: (h, 0, 0)),
         out_shape=jax.ShapeDtypeStruct((heads, 1, width), jnp.float32),
         scratch_shapes=[pltpu.VMEM((TILE, width), jnp.float32)],
-        cost_estimate=pl.CostEstimate(flops=heads*tiles*TILE*TILE*4, transcendentals=0, bytes_accessed=heads*tiles*TILE*TILE*4),
-    )(tile_grads)[:, 0]
+        cost_estimate=pl.CostEstimate(flops=heads*TILE*TILE, transcendentals=0, bytes_accessed=heads*TILE*TILE),
+    )(mark(when)[None], tile_grads)[:, 0]
 
 def columns_of(head, per_shard):
     shard, at = head // per_shard, head % per_shard
@@ -248,10 +251,11 @@
     return lax.all_gather(piece, ("dp", "seq"), axis=0, tiled=True)
 
 
-def own_rows(array, axes=("dp", "seq")):
+def own_rows(array, shift=0):
+    axes = ("dp", "seq")
     count = math.prod(lax.axis_size(axis) for axis in axes)
     part = array.shape[0] // count
-    return lax.dynamic_slice_in_dim(array, lax.axis_index(axes) * part, part, 0)
+    return lax.dynamic_slice_in_dim(array, lax.axis_index(axes) * part + shift, part, 0)
 
 
 def outer(left, right):
@@ -297,8 +301,17 @@
     return array
 
 
-def after(array, *events):
-    return lax.optimization_barrier((array,) + events)[0]
+def tie(*arrays):
+    return lax.optimization_barrier(arrays)
+
+
+def mark(value):
+    first = value[(0,) * value.ndim]
+    return (first != first).astype(jnp.int32)
+
+
+def later(array, value):
+    return array + mark(value).astype(array.dtype)
 
 
 def far_swap(array):
@@ -327,6 +340,10 @@
             at += item.shape[0]
         partials = kept
     return partials[0]
+
+
+def spread(own):
+    return gather_parts(own), gather_parts(far_swap(own))
 
 
 def reorder(parts):
@@ -400,14 +417,17 @@
     grads = jnp.concatenate(
         [grad_of(branch, wide(acts)), grad_of(low, wide(pre_lows))], axis=1
     )
-    return normed_grad, scatter_groups(grads)
-
-
-def fold_far(array, far_cols, own_cols):
-    came = far_swap(jnp.concatenate([array[:, a:b] for a, b in far_cols], axis=1))
-    came, outs, at = came.astype(jnp.float32), [], 0
-    for a, b in own_cols:
-        outs.append(array[:, a:b].astype(jnp.float32) + came[:, at : at + b - a])
+    return tie(normed_grad, grads)
+
+
+def far_columns(array, ranges):
+    return far_swap(jnp.concatenate([array[:, a:b] for a, b in ranges], axis=1))
+
+
+def add_far(array, came, ranges):
+    outs, at = [], 0
+    for a, b in ranges:
+        outs.append(array[:, a:b].astype(jnp.float32) + came[:, at : at + b - a].astype(jnp.float32))
         at += b - a
     return outs
 
@@ -482,9 +502,7 @@
         [glu_grad * gate, glu_grad * gate_in * gate * (1.0 - gate)], axis=-1
     ).astype(jnp.bfloat16)
     normed_grad = against(doubled_low, in_weight)
-    grads = scatter_groups(
-        jnp.concatenate([grad_of(low, doubled_low), grad_of(swish_low, branch_low)], axis=1)
-    )
+    grads = jnp.concatenate([grad_of(low, doubled_low), grad_of(swish_low, branch_low)], axis=1)
     part, gain_one_grad = norm_backward(normed_grad, normed, inverse, gain_one)
     small = [gain_one_grad, gain_two_grad] + tap_grads
     return (gradient + part, grads, small)
@@ -543,26 +561,13 @@
     q_cols, out_cols, n_qkv = query_weight.shape[1], output_weight.shape[0], own_qkv.shape[1]
     output_piece = lax.dynamic_slice_in_dim(output_weight, group_at * part, part, 1).T
     attn_piece = far_swap(jnp.concatenate([own_rows(own_qkv), output_piece], axis=1))
-    far_attn = gather_all(attn_piece)
-    far_qkv, far_output = far_attn[:, :n_qkv], far_attn[:, n_qkv:]
     small_piece = jnp.concatenate([depthwise, conv_gain[None], depth_gain[None]], axis=0).T
     small_piece = jnp.pad(small_piece, ((0, 0), (0, 128 - small_piece.shape[1])))
     conv_piece = jnp.concatenate([pointwise_in, pointwise_out, small_piece], axis=1)
-    conv_piece = after(conv_piece, attn_piece)
-    for bit in bits(n_heads):
-        other = swap(conv_piece, "heads", bit)
-        lower = bit_of("heads", bit) == 0
-        conv_piece = jnp.concatenate(
-            [jnp.where(lower, conv_piece, other), jnp.where(lower, other, conv_piece)], axis=0
-        )
-    conv_all = gather_all(conv_piece)
-    pw_in, pw_out = conv_all[:, : 2 * width], conv_all[:, 2 * width : 3 * width]
-    small_all = conv_all[:, 3 * width : 3 * width + KERNEL + 2].T
-    conv_weights = (pw_in, pw_out, small_all[:KERNEL], small_all[KERNEL], small_all[KERNEL + 1])
-
     rows = [lax.dynamic_index_in_dim(frames, my_row ^ f, 0, keepdims=False) for f in (0, 1)]
     units = [cut_parts(row) for row in rows]
     stream_zero = units[0][0].astype(jnp.float32)
+    hidden1 = ffn1_in.shape[1]
     ffn1_low, ffn1_pre, ffn1_act, ffn1_partial = [], [], [], []
     ffn1_norm = None
     for f in (0, 1):
@@ -582,13 +587,24 @@
         ffn1_pre.append(pres)
         ffn1_act.append(acts)
         ffn1_partial.append(partials)
+    attn_piece = later(attn_piece, ffn1_act[0][0])
+    far_attn = gather_all(attn_piece)
+    far_qkv, far_output = far_attn[:, :n_qkv], far_attn[:, n_qkv:]
+    for bit in bits(n_heads):
+        other = swap(conv_piece, "heads", bit)
+        lower = bit_of("heads", bit) == 0
+        conv_piece = jnp.concatenate(
+            [jnp.where(lower, conv_piece, other), jnp.where(lower, other, conv_piece)], axis=0
+        )
+        if bit < len(bits(n_heads)) - 1:
+            conv_piece = later(conv_piece, ffn1_act[1][-1])
     summed = reduce_parts(ffn1_partial[1])
-    far_part = far_swap(summed.astype(bf16)).astype(jnp.float32)
-    stream_one = stream_zero + 0.5 * (reduce_parts(ffn1_partial[0]) + far_part)
-
+    conv_all = gather_all(later(conv_piece, summed))
+    pw_in, pw_out = conv_all[:, : 2 * width], conv_all[:, 2 * width : 3 * width]
+    small_all = conv_all[:, 3 * width : 3 * width + KERNEL + 2].T
+    conv_weights = (pw_in, pw_out, small_all[:KERNEL], small_all[KERNEL], small_all[KERNEL + 1])
     n_q, n_k = local // TILE, length // TILE
-    early = ffn1_act[0][0]
-    my_ids = lax.dynamic_index_in_dim(after(segment_ids, early), my_row, 0, keepdims=False)
+    my_ids = lax.dynamic_index_in_dim(segment_ids, my_row, 0, keepdims=False)
     reach = KERNEL // 2
     ids_pad = jnp.pad(my_ids, (reach, reach), constant_values=-1)
     query_ids = lax.dynamic_slice_in_dim(my_ids, seq_at * local, local, 0)
@@ -603,7 +619,7 @@
     scalars = jnp.concatenate(
         [seq_at.astype(jnp.int32)[None], jnp.stack([starts, ends], axis=1).reshape(-1)]
     )
-    reversed_buckets = jnp.pad(after(bucket_of, early)[::-1], (0, 1))
+    reversed_buckets = jnp.pad(bucket_of[::-1], (0, 1))
     window = lax.dynamic_slice_in_dim(reversed_buckets, seq_at * local, (n_q + n_k) * TILE, 0)
     levels = lax.broadcasted_iota(jnp.int32, (position_table.shape[1], window.shape[0]), 0)
     onehot = (levels == window[None, :]).astype(jnp.float32)
@@ -611,33 +627,43 @@
     biases = jnp.dot(tables, onehot, precision=HIGHEST) * LOG2E
     per_shard = q_cols // HEAD_DIM
     tiles = [bias_tiles(biases[:per_shard]), bias_tiles(biases[per_shard:])]
+    far_part = far_swap(summed.astype(bf16))
+    far_part, tiles[0], tiles[1], scalars = tie(far_part, tiles[0], tiles[1], scalars)
+    stream_one = stream_zero + 0.5 * (
+        reduce_parts(ffn1_partial[0]) + far_part.astype(jnp.float32)
+    )
 
     attn_out, attn_hat, attn_inverse = norm_forward(stream_one, attn_gain)
     low = reorder(gather_parts(attn_out.astype(bf16)))
     hidden = ffn2_in.shape[1]
-    ffn2_pieces = [own_rows(ffn2_in), own_rows(ffn2_out)]
+    ffn2_pieces = [own_rows(ffn2_in, mark(low)), own_rows(ffn2_out, mark(low))]
     if hidden == width:
-        ffn2_piece = jnp.concatenate(ffn2_pieces, axis=1)
-        far_ffn2 = gather_all(far_swap(after(ffn2_piece, low)))
-        far_ffn2 = (far_ffn2[:, :hidden], far_ffn2[:, hidden:])
-    else:
-        far_ffn2 = tuple(gather_all(far_swap(after(piece, low))) for piece in ffn2_pieces)
-    ffn2_weights = [(ffn2_in, ffn2_out), far_ffn2]
+        ffn2_pieces = [jnp.concatenate(ffn2_pieces, axis=1)]
+    ffn2_pieces = [far_swap(piece) for piece in ffn2_pieces]
     seq_bits = bits(lax.axis_size("seq"))
+    both_kv = [plain(low, qkv[:, q_cols:]).astype(bf16)[None] for qkv in (own_qkv, far_qkv)]
     pieces, queries, mixtures, log_totals = [], [], [], []
-    for qkv in (own_qkv, far_qkv):
-        held = [plain(low, qkv[:, q_cols:]).astype(bf16)[None]]
+    for shard in (0, 1):
+        held = [both_kv[shard]]
+        first = both_kv[1] if shard == 0 else mixtures[0]
         for bit in reversed(seq_bits):
-            held.append(swap(join(held), "seq", bit))
+            whole = join(held)
+            if len(held) == len(seq_bits):
+                whole = later(whole, first)
+            held.append(swap(whole, "seq", bit))
         pieces.append(held)
-        queries.append(plain(low, qkv[:, :q_cols]).astype(bf16))
-    for shard in (0, 1):
+        queries.append(plain(low, (own_qkv, far_qkv)[shard][:, :q_cols]).astype(bf16))
         mixture, log_total = attend(
             scalars, queries[shard], tiles[shard], query_ids[None], my_ids[:, None],
             pieces[shard], per_shard,
         )
         mixtures.append(mixture)
         log_totals.append(log_total)
+    mixtures[1], ffn2_pieces = tie(mixtures[1], ffn2_pieces)
+    far_ffn2 = [gather_all(piece) for piece in ffn2_pieces]
+    if hidden == width:
+        far_ffn2 = [far_ffn2[0][:, :hidden], far_ffn2[0][:, hidden:]]
+    ffn2_weights = [(ffn2_in, ffn2_out), tuple(far_ffn2)]
     mix_parts = [cut_parts(mixture) for mixture in mixtures]
     branch = reduce_parts(
         [
@@ -658,54 +684,72 @@
     grad_four, final_gain_grad = norm_backward(cot, final_hat, final_inverse, final_gain)
 
     normed_grad, ffn2_grads = ffn_backward(grad_four, ffn2_state, ffn2_weights)
+    ffn2_grads = scatter_groups(ffn2_grads)
     stream_part, ffn2_gain_grad = norm_backward(normed_grad, ffn2_hat, ffn2_inverse, ffn2_gain)
     grad_three = grad_four + stream_part
     grad_two, conv_grads, conv_small = conv_backward(
         grad_three, conv_state, window_ids, conv_weights
     )
     branch_low = reorder(gather_parts(grad_two.astype(bf16)))
+    branch_low, conv_grads = tie(branch_low, conv_grads)
     mix_grads = [
         against(branch_low, output_weight).astype(bf16),
         plain(branch_low, far_output).astype(bf16),
     ]
-    q_grads, kv_grads, table_grads = [], [], []
+    layer_low = later(layer_low, branch_low)
+    layer_near, layer_far = gather_parts(layer_low), far_swap(layer_low)
+    q_grads, kv_grads, all_tile_grads = [], [], []
+    turn = scalars
     for shard in (0, 1):
         q_grad, kv_grad, tile_grads = attend_back(
-            scalars, queries[shard], tiles[shard], query_ids[None], my_ids[:, None],
+            turn, queries[shard], tiles[shard], query_ids[None], my_ids[:, None],
             mixtures[shard], mix_grads[shard], log_totals[shard], pieces[shard], per_shard,
         )
+        if shard == 1:
+            kv_grad, kv_grads[0], layer_near, layer_far = tie(
+                kv_grad, kv_grads[0], layer_near, layer_far
+            )
         for bit in seq_bits:
             half = kv_grad.shape[0] // 2
             kv_grad = (
                 kv_grad[:half].astype(jnp.float32)
                 + swap(kv_grad[half:], "seq", bit).astype(jnp.float32)
             ).astype(bf16)
+            if shard == 0 and bit == 0:
+                turn = scalars + mark(kv_grad)
         q_grads.append(q_grad)
         kv_grads.append(kv_grad[0])
-        table_grads.append(
-            lax.dot_general(
-                offset_sums(tile_grads), onehot, (((1,), (1,)), ((), ())), precision=HIGHEST
-            )
-        )
+        all_tile_grads.append(tile_grads)
+    layer_far = gather_parts(layer_far)
+    ffn2_grads, conv_grads, kv_grads[1] = tie(ffn2_grads, conv_grads, kv_grads[1])
+    conv_grads = scatter_groups(conv_grads)
+    n_hid = 2 * hidden
+    ffn2_out_came = far_columns(ffn2_grads, [(hidden, n_hid)])
     qkv_grads = [jnp.concatenate(pair, axis=1) for pair in zip(q_grads, kv_grads)]
     grad_parts = [cut_parts(grads) for grads in qkv_grads]
-    normed_grad = reduce_parts(
-        [against(own, own_qkv) + against(far, far_qkv) for own, far in zip(*grad_parts)]
-    )
-    attn_grads = scatter_groups(
-        jnp.concatenate(
-            [
-                grad_of(branch_low, jnp.concatenate(mixtures, axis=1)),
-                grad_of(low, jnp.concatenate(qkv_grads, axis=1)),
-            ],
-            axis=1,
-        )
+    partials = [against(own, own_qkv) + against(far, far_qkv) for own, far in zip(*grad_parts)]
+    normed_grad = reduce_parts(partials)
+    low = later(low, partials[0])
+    attn_grads = jnp.concatenate(
+        [
+            grad_of(later(branch_low, partials[0]), jnp.concatenate(mixtures, axis=1)),
+            grad_of(low, jnp.concatenate(qkv_grads, axis=1)),
+        ],
+        axis=1,
+    )
+    normed_grad, attn_grads, ffn2_out_came, layer_far = tie(
+        normed_grad, attn_grads, ffn2_out_came, layer_far
     )
     stream_part, attn_gain_grad = norm_backward(normed_grad, attn_hat, attn_inverse, attn_gain)
     grad_one = grad_two + stream_part
 
     own_branch = (0.5 * grad_one).astype(bf16)
-    branches = [gather_parts(own_branch), gather_parts(far_swap(own_branch))]
+    near, far = tie(gather_parts(own_branch), far_swap(own_branch))
+    branches = [near, gather_parts(far)]
+    attn_grads, conv_grads, branches[0][-1] = tie(attn_grads, conv_grads, branches[0][-1])
+    attn_grads = scatter_groups(attn_grads)
+    conv_grads = fold_heads(conv_grads)
+    branches[1][-1], conv_grads = tie(branches[1][-1], conv_grads)
     pre_lows, partials = [], []
     for f in (0, 1):
         pre_lows.append(
@@ -716,65 +760,72 @@
         )
         partials.append([against(pre_low, ffn1_in) for pre_low in pre_lows[f]])
     every_frame = lambda lists: join(lists[0] + lists[1])
-    f1_out_g = scatter_groups(grad_of(every_frame(branches), every_frame(ffn1_act)))
-    f1_in_g = scatter_groups(grad_of(every_frame(ffn1_low), every_frame(pre_lows)))
+    table_grads = [
+        lax.dot_general(
+            offset_sums(tile_grads, branches[0][-1]), onehot, (((1,), (1,)), ((), ())),
+            precision=HIGHEST,
+        )
+        for tile_grads in all_tile_grads
+    ]
+    last_sent = partials[1][-1]
+    ffn1_grads = jnp.concatenate(
+        [
+            grad_of(later(every_frame(branches), last_sent), every_frame(ffn1_act)),
+            grad_of(later(every_frame(ffn1_low), last_sent), every_frame(pre_lows)),
+        ],
+        axis=1,
+    )
+    ffn1_grads, attn_grads = tie(ffn1_grads, attn_grads)
+    ffn1_grads = scatter_groups(ffn1_grads).astype(jnp.float32)
     far_part = far_swap(reduce_parts(partials[1]).astype(bf16)).astype(jnp.float32)
-    normed_grad = reduce_parts(partials[0]) + far_part
+    near_sum = reduce_parts(partials[0])
+    normed_grad = near_sum + far_part
     stream_part, ffn1_gain_grad = norm_backward(normed_grad, *ffn1_norm, ffn1_gain)
     grad_zero = grad_one + stream_part
 
-    ffn2_grads = after(ffn2_grads, kv_grads[0])
-    n_hid = 2 * hidden
-    f2_out_g, f2_in_g = fold_far(
-        ffn2_grads,
-        [(hidden, n_hid), (n_hid + hidden, 2 * n_hid)],
-        [(0, hidden), (n_hid, n_hid + hidden)],
-    )
-    conv_grads = fold_heads(after(conv_grads, kv_grads[1]))
-    attn_grads = after(attn_grads, branches[0][-1])
+    low = grad_zero.astype(bf16)
+    near, far = tie(gather_parts(low), far_swap(low))
+    spread_grad = near, gather_parts(far)
+
+    (f2_out_g,) = add_far(ffn2_grads, ffn2_out_came, [(0, hidden)])
+    ffn2_in_came = far_columns(later(ffn2_grads, spread_grad[1][0]), [(n_hid + hidden, 2 * n_hid)])
+    (f2_in_g,) = add_far(ffn2_grads, ffn2_in_came, [(n_hid, n_hid + hidden)])
     n_out = 2 * out_cols
-    o_g, qkv_g = fold_far(
-        attn_grads,
-        [(out_cols, n_out), (n_out + n_qkv, n_out + 2 * n_qkv)],
-        [(0, out_cols), (n_out, n_out + n_qkv)],
-    )
-
-    gains = [ffn2_gain_grad, final_gain_grad] + conv_small
+    attn_came = far_columns(later(attn_grads, spread_grad[1][0]), [(out_cols, n_out), (n_out + n_qkv, n_out + 2 * n_qkv)])
+    o_g, qkv_g = add_far(attn_grads, attn_came, [(0, out_cols), (n_out, n_out + n_qkv)])
+
     all_heads = jnp.zeros((n_heads * per_shard, position_table.shape[1]), jnp.float32)
     all_heads = lax.dynamic_update_slice_in_dim(all_heads, table_grads[0], place * per_shard, 0)
     all_heads = lax.dynamic_update_slice_in_dim(
         all_heads, table_grads[1], (place ^ team) * per_shard, 0
     )
+    gains = [ffn1_gain_grad, attn_gain_grad, ffn2_gain_grad, final_gain_grad] + conv_small
     small = jnp.concatenate([jnp.stack(gains).reshape(-1), all_heads.reshape(-1)])
-    everyone = ("dp", "seq", "heads")
-    small = sum_everyone(small.reshape(-1, 128)).reshape(-1)
+    small = later(small.reshape(-1, 128), spread_grad[1][0])
+    small = sum_everyone(small).reshape(-1)
     gains_all = small[: len(gains) * width].reshape(len(gains), width)
     table_all = small[len(gains) * width :].reshape(all_heads.shape)
     table_mine = lax.dynamic_slice_in_dim(table_all, place * per_shard, per_shard, 0)
     table_cols = table_mine.shape[1] // groups
     table_mine = lax.dynamic_slice_in_dim(table_mine, group_at * table_cols, table_cols, 1)
-    group_part = lax.dynamic_slice_in_dim(gains_all[:2], group_at * part, part, 1)
+    group_part = lax.dynamic_slice_in_dim(gains_all[:4], group_at * part, part, 1)
     every = width // (groups * n_heads)
     conv_part = lax.dynamic_slice_in_dim(
-        gains_all[2:], lax.axis_index(everyone) * every, every, 1
-    )
-    last = jnp.stack([ffn1_gain_grad, attn_gain_grad]).reshape(-1, 128)
-    last = sum_everyone(last).reshape(2, width)
-    last_part = lax.dynamic_slice_in_dim(last, group_at * part, part, 1)
-
-    def everywhere(own):
-        near, far = gather_parts(own), gather_parts(far_swap(own))
-        near, far = reorder(near), reorder(far)
+        gains_all[4:], lax.axis_index(("dp", "seq", "heads")) * every, every, 1
+    )
+
+    def everywhere(parts):
+        near, far = reorder(parts[0]), reorder(parts[1])
         first = my_row == 0
         return jnp.stack([jnp.where(first, near, far), jnp.where(first, far, near)])
 
     return (
-        everywhere(after(layer_low, branch_low)),
-        everywhere(grad_zero.astype(bf16)).astype(jnp.float32),
-        last_part[0],
-        f1_in_g.astype(jnp.float32),
-        f1_out_g.T.astype(jnp.float32),
-        last_part[1],
+        everywhere((layer_near, layer_far)),
+        everywhere(spread_grad).astype(jnp.float32),
+        group_part[0],
+        ffn1_grads[:, hidden1:],
+        ffn1_grads[:, :hidden1].T,
+        group_part[1],
         qkv_g[:, :q_cols],
         qkv_g[:, q_cols : 2 * q_cols],
         qkv_g[:, 2 * q_cols :],
@@ -785,10 +836,10 @@
         conv_part[2:],
         conv_part[1],
         conv_grads[:, 2 * width :],
-        group_part[0],
+        group_part[2],
         f2_in_g,
         f2_out_g.T,
-        group_part[1],
+        group_part[3],
     )
 
 

time: 762 us -> 671 us (0.88)
  waiting for transfers between devices: 377 us -> 231 us
  local copies, waits for them, and re-layouts: 42.7 us -> 69.6 us
  starting transfers between devices: 81.5 us -> 65 us
  between operations: 16.7 us -> 32.3 us
  matrix products: 97 us -> 111 us
    ppermute x50 -> x46, waiting for transfers between devices: 369 us -> 229 us  [swap(): return lax.ppermute(array, axis, [(i, i ^ 1 << bit) for i in range(count)])]
    ppermute x50 -> x46, starting transfers between devices: 69.9 us -> 52.8 us  [swap(): return lax.ppermute(array, axis, [(i, i ^ 1 << bit) for i in range(count)])]
    concatenate x8 -> x4, other arithmetic: 21.4 us -> 6.29 us  [the longest x1 2.96 us: on_device(): jnp.concatenate([grad_of(later(branch_low, partials[0]), jnp.concatenate(...]
    unnamed x296 -> x274, local copies, waits for them, and re-layouts: 17 us -> 27.6 us
    add x1 -> x12, other arithmetic: 0.04 us -> 9.6 us  [the longest x9 7.12 us: later(): return array + mark(value).astype(array.dtype)]
    dot_general x25, matrix products: 27.5 us -> 36.6 us  [against(): lax.dot_general(left, right, (((1,), (1,)), ((), ())), preferred_element_...]
    slice x7 -> x21, local copies, waits for them, and re-layouts: 2.91 us -> 10.6 us  [the longest x12 9.5 us: mark(): first = value[(0,) * value.ndim]]
  transfers between devices with their start and end apart: 62 -> 57, of which waited for: 39 -> 28; matrix products, arithmetic and copies ran while one was open for 23% -> 34% of each run, Pallas kernels for 7% -> 10%
where the time goes in v3:
time: 671 us; the launch traced here: 661 us
  waiting for transfers between devices  231 us (34%)
  matrix products  111 us (17%)
  other arithmetic  83.8 us (12%)
  local copies, waits for them, and re-layouts  69.6 us (10%)
  Pallas kernels  68.7 us (10%)
  starting transfers between devices  65 us (10%)
  between operations  32.3 us (5%)
    ppermute x46, waiting for transfers between devices, swap(): return lax.ppermute(array, axis, [(i, i ^ 1 << bit) for i in range(count)])  229 us
    ppermute x46, starting transfers between devices, swap(): return lax.ppermute(array, axis, [(i, i ^ 1 << bit) for i in range(count)])  52.8 us
    dot_general x25, matrix products, plain(): return jnp.dot(left, right, preferred_element_type=jnp.float32)  47.3 us
    dot_general x25, matrix products, against(): lax.dot_general(left, right, (((1,), (1,)), ((), ())), preferred_element_...  36.6 us
    pallas_call x2, Pallas kernels, attend_back(): pl.pallas_call(fn, grid_spec=pltpu.PrefetchScalarGridSpec(num_scalar_pref...  29.2 us
    unnamed x274, local copies, waits for them, and re-layouts  27.6 us
    pallas_call x2, Pallas kernels, attend(): pl.pallas_call(fn, grid_spec=pltpu.PrefetchScalarGridSpec(num_scalar_pref...  25.1 us
    dot_general x8, matrix products, outer(): lax.dot_general(left, right, (((0,), (0,)), ((), ())), preferred_element_...  23.7 us
  transfers between devices with their start and end apart: 57, of which 28 were waited for; matrix products, arithmetic and copies ran while one was open for 34% of the time, Pallas kernels for 10%

profile of v3, /device:TPU:0, one launch (start us, length us, event | category | flops | bytes accessed | tf_op | source)
XLA Modules:
  0.0 660.9 jit_solution(272772109201486232)
XLA Ops:
  14.8 4.1 collective-permute-start.6
  33.1 3.3 convolution_convert_fusion.8
  45.8 11.6 %collective-permute-done = bf16[256,1024]{1,0:T(8,128)(2,1)} collective-permute-done((bf16[256,1024]{1,0:T(8,128)(2,1)}, bf16[256,1024]{1,0:T(8,128)(2,1)}, u32[]{:S(2)}, u32[]{:S(2)}) %collective-permute-start) | collective-permute-done | bytes 524320 | tf_op jit(solution)/shard_map/ppermute | solution.py:243
  57.3 3.3 fusion.276
  73.7 3.3 fusion.285
  81.2 3.4 shard_map.365.refs_1_
  84.7 3.4 shard_map.366.refs_1_
  88.0 14.5 %collective-permute-done.1 = bf16[256,1024]{1,0:T(8,128)(2,1)S(1)} collective-permute-done((bf16[256,1024]{1,0:T(8,128)(2,1)S(1)}, bf16[256,1024]{1,0:T(8,128)(2,1)S(1)}, u32[]{:S(2)}, u32[]{:S(2)}) %collective-permute-start.1) | collective-permute-done | bytes 524320 | tf_op jit(solution)/shard_map/ppermute | solution.py:243
  106.8 13.2 %collective-permute-done.4 = bf16[256,1024]{1,0:T(8,128)(2,1)} collective-permute-done((bf16[256,1024]{1,0:T(8,128)(2,1)}, bf16[256,1024]{1,0:T(8,128)(2,1)}, u32[]{:S(2)}, u32[]{:S(2)}) %collective-permute-start.4) | collective-permute-done | bytes 524320 | tf_op jit(solution)/shard_map/ppermute | solution.py:243
  127.9 6.6 collective-permute-done.5.refs_5_.refs_8_
  141.7 12.6 %shard_map.367 = (bf16[512,256]{1,0:T(8,128)(2,1)}, f32[2,1,512]{2,1,0:T(1,128)}) custom-call(s32[5]{0:T(128)} %pad_add_fusion.1.scal, bf16[512,256]{1,0:T(8,128)(2,1)} %convolution_convert_fusion.14.refs_0_, f32[2,9,256,256]{3,2,1,0:T(8,128)} %shard_map.365.refs_1_, s32[1,512]{1,0:T(1,128)} %get-tuple-element.269.refs_2_, s32[2048,1]{1,0:T(8,128)} %copy.97.refs_3_, ...), custom_call_target="tpu_custom_call" | custom-call | flops 1073741824 | bytes 4718592 | tf_op jit(solution)/shard_map/pallas_call | solution.py:131
  166.6 12.6 %shard_map.368 = (bf16[512,256]{1,0:T(8,128)(2,1)}, f32[2,1,512]{2,1,0:T(1,128)}) custom-call(s32[5]{0:T(128)} %pad_add_fusion.1.scal, bf16[512,256]{1,0:T(8,128)(2,1)} %convolution_convert_fusion.13.refs_0_, f32[2,9,256,256]{3,2,1,0:T(8,128)} %shard_map.366.refs_1_, s32[1,512]{1,0:T(1,128)} %get-tuple-element.269.refs_2_, s32[2048,1]{1,0:T(8,128)} %copy.97.refs_3_, ...), custom_call_target="tpu_custom_call" | custom-call | flops 1073741824 | bytes 4718592 | tf_op jit(solution)/shard_map/pallas_call | solution.py:131
  179.2 11.0 %collective-permute-done.10 = bf16[128,2048]{1,0:T(8,128)(2,1)} collective-permute-done((bf16[128,2048]{1,0:T(8,128)(2,1)}, bf16[128,2048]{1,0:T(8,128)(2,1)}, u32[]{:S(2)}, u32[]{:S(2)}) %collective-permute-start.10) | collective-permute-done | bytes 524320 | tf_op jit(solution)/shard_map/ppermute | solution.py:243
  193.8 12.3 %collective-permute-done.11 = bf16[256,1024]{1,0:T(8,128)(2,1)S(1)} collective-permute-done((bf16[256,1024]{1,0:T(8,128)(2,1)S(1)}, bf16[256,1024]{1,0:T(8,128)(2,1)S(1)}, u32[]{:S(2)}, u32[]{:S(2)}) %collective-permute-start.11) | collective-permute-done | bytes 524320 | tf_op jit(solution)/shard_map/ppermute | solution.py:243
  209.2 3.9 fusion.2
  214.7 5.0 collective-permute-start.14
  229.4 10.7 %collective-permute-done.16 = bf16[256,1024]{1,0:T(8,128)(2,1)S(1)} collective-permute-done((bf16[256,1024]{1,0:T(8,128)(2,1)S(1)}, bf16[256,1024]{1,0:T(8,128)(2,1)S(1)}, u32[]{:S(2)}, u32[]{:S(2)}) %collective-permute-start.16) | collective-permute-done | bytes 524320 | tf_op jit(solution)/shard_map/ppermute | solution.py:243
  250.8 11.1 %collective-permute-done.17 = bf16[256,1024]{1,0:T(8,128)(2,1)S(1)} collective-permute-done((bf16[256,1024]{1,0:T(8,128)(2,1)S(1)}, bf16[256,1024]{1,0:T(8,128)(2,1)S(1)}, u32[]{:S(2)}, u32[]{:S(2)}) %collective-permute-start.17) | collective-permute-done | bytes 524320 | tf_op jit(solution)/shard_map/ppermute | solution.py:243
  269.4 7.9 %collective-permute-done.18 = bf16[256,1024]{1,0:T(8,128)(2,1)S(1)} collective-permute-done((bf16[256,1024]{1,0:T(8,128)(2,1)S(1)}, bf16[256,1024]{1,0:T(8,128)(2,1)S(1)}, u32[]{:S(2)}, u32[]{:S(2)}) %collective-permute-start.18) | collective-permute-done | bytes 524320 | tf_op jit(solution)/shard_map/ppermute | solution.py:243
  281.8 4.4 convolution_convert_fusion.3
  286.2 4.4 convolution_convert_fusion.2
  290.6 7.9 %pad_maximum_fusion = bf16[1024,4096]{1,0:T(8,128)(2,1)} fusion(bf16[1024,2048]{1,0:T(8,128)(2,1)} %convolution_convert_fusion.2, bf16[1024,2048]{1,0:T(8,128)(2,1)} %convolution_convert_fusion.3), kind=kLoop, calls=%fused_computation | loop fusion | flops 16777216 | bytes 16777216 | tf_op jit(solution)/shard_map/concatenate | solution.py:417
  298.5 3.9 fusion.100
  307.3 3.8 multiply_reduce_fusion
  313.7 3.4 collective-permute-start.21
  331.8 5.0 pad_maximum_fusion.1
  336.9 5.6 collective-permute-done.22
  345.4 14.7 %shard_map.369 = (bf16[512,256]{1,0:T(8,128)(2,1)S(1)}, bf16[4,512,512]{2,1,0:T(8,128)(2,1)}, f32[2,9,256,256]{3,2,1,0:T(8,128)}) custom-call(s32[5]{0:T(128)S(1)} %copy-done.13, bf16[512,256]{1,0:T(8,128)(2,1)S(1)} %copy-done.11, f32[2,9,256,256]{3,2,1,0:T(8,128)} %shard_map.365.refs_1_, s32[1,512]{1,0:T(1,128)S(1)} %copy-done.12, s32[2048,1]{1,0:T(8,128)S(1)} %copy-done.1, ...), custom_call_target="tpu_custom_call" | custom-call | flops 2684354560 | bytes 9437184 | tf_op jit(solution)/shard_map/pallas_call | solution.py:209
  370.9 14.6 %shard_map.370 = (bf16[512,256]{1,0:T(8,128)(2,1)S(1)}, bf16[4,512,512]{2,1,0:T(8,128)(2,1)}, f32[2,9,256,256]{3,2,1,0:T(8,128)}) custom-call(s32[5]{0:T(128)S(1)} %broadcast_add_fusion.2.scal, bf16[512,256]{1,0:T(8,128)(2,1)S(1)} %copy-done.10, f32[2,9,256,256]{3,2,1,0:T(8,128)} %shard_map.366.refs_1_, s32[1,512]{1,0:T(1,128)S(1)} %copy-done.12, ...), custom_call_target="tpu_custom_call" | custom-call | flops 2684354560 | bytes 9437184 | tf_op jit(solution)/shard_map/pallas_call | solution.py:209
  394.2 14.0 %collective-permute-done.28 = bf16[1,512,512]{2,1,0:T(8,128)(2,1)S(1)} collective-permute-done((bf16[1,512,512]{2,1,0:T(8,128)(2,1)S(1)}, bf16[1,512,512]{2,1,0:T(8,128)(2,1)S(1)}, u32[]{:S(2)}, u32[]{:S(2)}) %collective-permute-start.28) | collective-permute-done | bytes 524320 | tf_op jit(solution)/shard_map/ppermute | solution.py:243
  428.3 3.2 convolution_convert_fusion
  434.5 5.7 collective-permute-done.29
  445.5 3.4 collective-permute-start.33
  448.9 19.2 %collective-permute-done.32 = bf16[256,1024]{1,0:T(8,128)(2,1)S(1)} collective-permute-done((bf16[256,1024]{1,0:T(8,128)(2,1)}, bf16[256,1024]{1,0:T(8,128)(2,1)S(1)}, u32[]{:S(2)}, u32[]{:S(2)}) %collective-permute-start.32) | collective-permute-done | bytes 524320 | tf_op jit(solution)/shard_map/ppermute | solution.py:243
  481.6 16.6 %collective-permute-done.36 = bf16[64,3072]{1,0:T(8,128)(2,1)S(1)} collective-permute-done((bf16[64,3072]{1,0:T(8,128)(2,1)S(1)}, bf16[64,3072]{1,0:T(8,128)(2,1)S(1)}, u32[]{:S(2)}, u32[]{:S(2)}) %collective-permute-start.36) | collective-permute-done | bytes 393248 | tf_op jit(solution)/shard_map/ppermute | solution.py:243
  502.0 3.6 collective-permute-done.37
  514.0 12.8 %collective-permute-done.38 = bf16[256,1024]{1,0:T(8,128)(2,1)S(1)} collective-permute-done((bf16[256,1024]{1,0:T(8,128)(2,1)S(1)}, bf16[256,1024]{1,0:T(8,128)(2,1)S(1)}, u32[]{:S(2)}, u32[]{:S(2)}) %collective-permute-start.38) | collective-permute-done | bytes 524320 | tf_op jit(solution)/shard_map/ppermute | solution.py:243
  528.4 3.0 collective-permute-start.39
  531.4 3.8 fusion.49
  537.7 6.7 %copy.104 = bf16[1024,2048]{1,0:T(8,128)(2,1)} copy(bf16[1024,2048]{0,1:T(8,128)(2,1)} %pad_maximum_fusion.3) | data formatting | bytes 8388608
  544.4 10.1 %collective-permute-done.39 = bf16[256,1024]{1,0:T(8,128)(2,1)} collective-permute-done((bf16[256,1024]{1,0:T(8,128)(2,1)}, bf16[256,1024]{1,0:T(8,128)(2,1)}, u32[]{:S(2)}, u32[]{:S(2)}) %collective-permute-start.39) | collective-permute-done | bytes 524320 | tf_op jit(solution)/shard_map/ppermute | solution.py:243
  560.5 3.4 collective-permute-start.41
  566.5 3.7 shard_map.371
  570.2 3.8 shard_map.372
  584.1 3.3 collective-permute-done.41
  604.7 16.0 %collective-permute-done.46 = f32[90,128]{1,0:T(8,128)S(1)} collective-permute-done((f32[90,128]{1,0:T(8,128)S(1)}, f32[90,128]{1,0:T(8,128)S(1)}, u32[]{:S(2)}, u32[]{:S(2)}) %collective-permute-start.46) | collective-permute-done | bytes 46112 | tf_op jit(solution)/shard_map/ppermute | solution.py:243
  622.4 3.3 collective-permute-done.47
  637.4 8.7 %collective-permute-done.48 = bf16[128,1024]{1,0:T(8,128)(2,1)S(1)} collective-permute-done((bf16[128,1024]{1,0:T(8,128)(2,1)S(1)}, bf16[128,1024]{1,0:T(8,128)(2,1)S(1)}, u32[]{:S(2)}, u32[]{:S(2)}) %collective-permute-start.48) | collective-permute-done | bytes 262176 | tf_op jit(solution)/shard_map/ppermute | solution.py:243
  (598 shorter events, 263.1 us)
Async XLA Ops:
  7.2 116.5 %all-gather.4.cloned.1.call-start = ((), (), s32[]{:S(2)}) async-start(), calls=%async_computation.4 | async-start | bytes 2359296 | tf_op jit(solution)/shard_map/all_gather | solution.py:251
  14.8 17.5 %collective-permute-start.6 = (bf16[128,1024]{1,0:T(8,128)(2,1)}, bf16[128,1024]{1,0:T(8,128)(2,1)S(1)}, u32[]{:S(2)}, u32[]{:S(2)}) collective-permute-start(bf16[128,1024]{1,0:T(8,128)(2,1)} %pad_maximum_fusion.19), channel_id=1, source_target_pairs={{0,2},{1,3},{2,0},{3,1},{4,6},{5,7},{6,4},{7,5},{8,10},{9,11},{10,... | collective-permute-start | bytes 786440 | tf_op jit(solution)/shard_map/ppermute | solution.py:243
  19.7 19.6 %collective-permute-start.12 = (bf16[32,3200]{1,0:T(8,128)(2,1)}, bf16[32,3200]{1,0:T(8,128)(2,1)}, u32[]{:S(2)}, u32[]{:S(2)}) collective-permute-start(bf16[32,3200]{1,0:T(8,128)(2,1)} %fusion.232), channel_id=1, source_target_pairs={{0,1},{1,0},{2,3},{3,2},{4,5},{5,4},{6,7},{7,6},{8,9},{9,8},{10,11... | collective-permute-start | bytes 614408 | tf_op jit(solution)/shard_map/ppermute | solution.py:243
  33.0 174.8 %all-gather.6.cloned.1.call-start = ((), (), s32[]{:S(2)}) async-start(), calls=%async_computation.5 | async-start | bytes 7372800 | tf_op jit(solution)/shard_map/all_gather | solution.py:251
  36.4 20.9 %collective-permute-start = (bf16[256,1024]{1,0:T(8,128)(2,1)}, bf16[256,1024]{1,0:T(8,128)(2,1)}, u32[]{:S(2)}, u32[]{:S(2)}) collective-permute-start(bf16[256,1024]{1,0:T(8,128)(2,1)} %convolution_convert_fusion.8), channel_id=1, source_target_pairs={{0,1},{1,0},{2,3},{3,2},{4,5},{5,4},{6,7},{7,6},{8,9},{9,8},{10,11... | collective-permute-start | bytes 1572872 | tf_op jit(solution)/shard_map/ppermute | solution.py:243
  40.5 22.0 %collective-permute-start.13 = (bf16[64,3200]{1,0:T(8,128)(2,1)S(1)}, bf16[64,3200]{1,0:T(8,128)(2,1)}, u32[]{:S(2)}, u32[]{:S(2)}) collective-permute-start(bf16[64,3200]{1,0:T(8,128)(2,1)S(1)} %maximum_add_fusion.11), channel_id=1, source_target_pairs={{0,2},{1,3},{2,0},{3,1},{4,6},{5,7},{6,4},{7,5},{8,10},{9,11},{10,... | collective-permute-start | bytes 1228808 | tf_op jit(solution)/shard_map/ppermute | solution.py:243
  64.6 179.7 %all-gather.8.cloned.1.call-start = ((), (), s32[]{:S(2)}) async-start(), calls=%async_computation.6 | async-start | bytes 4718592 | tf_op jit(solution)/shard_map/all_gather | solution.py:251
  64.9 12.7 %collective-permute-start.2 = (f32[2,32]{1,0:T(2,128)}, f32[2,32]{1,0:T(2,128)S(1)}, u32[]{:S(2)}, u32[]{:S(2)}) collective-permute-start(f32[2,32]{1,0:T(2,128)} %param.33), channel_id=1, source_target_pairs={{0,2},{1,3},{2,0},{3,1},{4,6},{5,7},{6,4},{7,5},{8,10},{9,11},{10,... | collective-permute-start | bytes 776 | tf_op jit(solution)/shard_map/ppermute | solution.py:243
  68.2 35.1 %collective-permute-start.3 = (bf16[256,1024]{1,0:T(8,128)(2,1)}, bf16[256,1024]{1,0:T(8,128)(2,1)}, u32[]{:S(2)}, u32[]{:S(2)}) collective-permute-start(bf16[256,1024]{1,0:T(8,128)(2,1)} %convolution_convert_fusion.7), channel_id=1, source_target_pairs={{0,1},{1,0},{2,3},{3,2},{4,5},{5,4},{6,7},{7,6},{8,9},{9,8},{10,11... | collective-permute-start | bytes 1572872 | tf_op jit(solution)/shard_map/ppermute | solution.py:243
  77.8 24.7 %collective-permute-start.1 = (bf16[256,1024]{1,0:T(8,128)(2,1)S(1)}, bf16[256,1024]{1,0:T(8,128)(2,1)S(1)}, u32[]{:S(2)}, u32[]{:S(2)}) collective-permute-start(bf16[256,1024]{1,0:T(8,128)(2,1)S(1)} %copy-done.78), channel_id=1, source_target_pairs={{0,2},{1,3},{2,0},{3,1},{4,6},{5,7},{6,4},{7,5},{8,10},{9,11},{10,... | collective-permute-start | bytes 1572872 | tf_op jit(solution)/shard_map/ppermute | solution.py:243
  106.8 13.2 %collective-permute-start.4 = (bf16[256,1024]{1,0:T(8,128)(2,1)}, bf16[256,1024]{1,0:T(8,128)(2,1)}, u32[]{:S(2)}, u32[]{:S(2)}) collective-permute-start(bf16[256,1024]{1,0:T(8,128)(2,1)} %multiply_convert_fusion.14), channel_id=1, source_target_pairs={{0,1},{1,0},{2,3},{3,2},{4,5},{5,4},{6,7},{7,6},{8,9},{9,8},{10,11... | collective-permute-start | bytes 1572872 | tf_op jit(solution)/shard_map/ppermute | solution.py:243
  122.3 12.1 %collective-permute-start.5 = (bf16[1,512,512]{2,1,0:T(8,128)(2,1)S(1)}, bf16[1,512,512]{2,1,0:T(8,128)(2,1)}, u32[]{:S(2)}, u32[]{:S(2)}) collective-permute-start(bf16[1,512,512]{2,1,0:T(8,128)(2,1)S(1)} %fusion.136.refs_4_.refs_7_), channel_id=1, source_target_pairs={{0,8},{4,12},{8,0},{12,4},{1,9},{5,13},{9,1},{13,5},{2,10},{6,14},... | collective-permute-start | bytes 1572872 | tf_op jit(solution)/shard_map/ppermute | solution.py:243
  136.6 20.2 %collective-permute-start.8 = (bf16[1,512,512]{2,1,0:T(8,128)(2,1)S(1)}, bf16[1,512,512]{2,1,0:T(8,128)(2,1)S(1)}, u32[]{:S(2)}, u32[]{:S(2)}) collective-permute-start(bf16[1,512,512]{2,1,0:T(8,128)(2,1)S(1)} %fusion.137.refs_4_.refs_7_), channel_id=1, source_target_pairs={{0,8},{4,12},{8,0},{12,4},{1,9},{5,13},{9,1},{13,5},{2,10},{6,14},... | collective-permute-start | bytes 1572872 | tf_op jit(solution)/shard_map/ppermute | solution.py:243
  157.9 8.7 %collective-permute-start.9 = (bf16[2,512,512]{2,1,0:T(8,128)(2,1)}, bf16[2,512,512]{2,1,0:T(8,128)(2,1)}, u32[]{:S(2)}, u32[]{:S(2)}) collective-permute-start(bf16[2,512,512]{2,1,0:T(8,128)(2,1)} %maximum_add_fusion.9), channel_id=1, source_target_pairs={{0,4},{4,0},{8,12},{12,8},{1,5},{5,1},{9,13},{13,9},{2,6},{6,2},{1... | collective-permute-start | bytes 3145736 | tf_op jit(solution)/shard_map/ppermute | solution.py:243
  163.6 26.6 %collective-permute-start.10 = (bf16[128,2048]{1,0:T(8,128)(2,1)}, bf16[128,2048]{1,0:T(8,128)(2,1)}, u32[]{:S(2)}, u32[]{:S(2)}) collective-permute-start(bf16[128,2048]{1,0:T(8,128)(2,1)} %pad_maximum_fusion.18), channel_id=1, source_target_pairs={{0,2},{1,3},{2,0},{3,1},{4,6},{5,7},{6,4},{7,5},{8,10},{9,11},{10,... | collective-permute-start | bytes 1572872 | tf_op jit(solution)/shard_map/ppermute | solution.py:243
  190.3 218.8 %reduce-scatter.7.cloned.1.call-start = ((), (), s32[]{:S(2)}) async-start(), calls=%async_computation.7 | async-start | bytes 9437184 | tf_op jit(solution)/shard_map/reduce_scatter | solution.py:382
  192.1 13.9 %collective-permute-start.11 = (bf16[256,1024]{1,0:T(8,128)(2,1)S(1)}, bf16[256,1024]{1,0:T(8,128)(2,1)S(1)}, u32[]{:S(2)}, u32[]{:S(2)}) collective-permute-start(bf16[256,1024]{1,0:T(8,128)(2,1)S(1)} %fusion.129), channel_id=1, source_target_pairs={{0,1},{1,0},{2,3},{3,2},{4,5},{5,4},{6,7},{7,6},{8,9},{9,8},{10,11... | collective-permute-start | bytes 1572872 | tf_op jit(solution)/shard_map/ppermute | solution.py:243
  213.4 7.6 %collective-permute-start.15 = (bf16[2,1024]{1,0:T(2,128)(2,1)S(1)}, bf16[2,1024]{1,0:T(2,128)(2,1)S(1)}, u32[]{:S(2)}, u32[]{:S(2)}) collective-permute-start(bf16[2,1024]{1,0:T(2,128)(2,1)S(1)} %get-tuple-element.299), channel_id=1, source_target_pairs={{1,0},{4,1},{5,4},{8,5},{9,8},{12,9},{13,12},{3,2},{6,3},{7,6},{10... | collective-permute-start | bytes 12296 | tf_op jit(solution)/shard_map/ppermute | solution.py:446
  225.6 14.4 %collective-permute-start.16 = (bf16[256,1024]{1,0:T(8,128)(2,1)S(1)}, bf16[256,1024]{1,0:T(8,128)(2,1)S(1)}, u32[]{:S(2)}, u32[]{:S(2)}) collective-permute-start(bf16[256,1024]{1,0:T(8,128)(2,1)S(1)} %multiply_convert_fusion.10), channel_id=1, source_target_pairs={{0,1},{1,0},{2,3},{3,2},{4,5},{5,4},{6,7},{7,6},{8,9},{9,8},{10,11... | collective-permute-start | bytes 1572872 | tf_op jit(solution)/shard_map/ppermute | solution.py:243
  248.3 13.6 %collective-permute-start.17 = (bf16[256,1024]{1,0:T(8,128)(2,1)S(1)}, bf16[256,1024]{1,0:T(8,128)(2,1)S(1)}, u32[]{:S(2)}, u32[]{:S(2)}) collective-permute-start(bf16[256,1024]{1,0:T(8,128)(2,1)S(1)} %fusion.111), channel_id=1, source_target_pairs={{0,1},{1,0},{2,3},{3,2},{4,5},{5,4},{6,7},{7,6},{8,9},{9,8},{10,11... | collective-permute-start | bytes 1572872 | tf_op jit(solution)/shard_map/ppermute | solution.py:243
  264.6 12.7 %collective-permute-start.18 = (bf16[256,1024]{1,0:T(8,128)(2,1)S(1)}, bf16[256,1024]{1,0:T(8,128)(2,1)S(1)}, u32[]{:S(2)}, u32[]{:S(2)}) collective-permute-start(bf16[256,1024]{1,0:T(8,128)(2,1)S(1)} %multiply_convert_fusion.5), channel_id=1, source_target_pairs={{0,1},{1,0},{2,3},{3,2},{4,5},{5,4},{6,7},{7,6},{8,9},{9,8},{10,11... | collective-permute-start | bytes 1572872 | tf_op jit(solution)/shard_map/ppermute | solution.py:243
  281.5 17.0 %collective-permute-start.19 = (bf16[256,1024]{1,0:T(8,128)(2,1)}, bf16[256,1024]{1,0:T(8,128)(2,1)}, u32[]{:S(2)}, u32[]{:S(2)}) collective-permute-start(bf16[256,1024]{1,0:T(8,128)(2,1)} %fusion.122), channel_id=1, source_target_pairs={{0,1},{1,0},{2,3},{3,2},{4,5},{5,4},{6,7},{7,6},{8,9},{9,8},{10,11... | collective-permute-start | bytes 1572872 | tf_op jit(solution)/shard_map/ppermute | solution.py:243
  302.4 168.7 %reduce-scatter.9.cloned.1.call-start = ((), (), s32[]{:S(2)}) async-start(), calls=%async_computation.8 | async-start | bytes 7077888 | tf_op jit(solution)/shard_map/reduce_scatter | solution.py:382
  313.7 7.6 %collective-permute-start.21 = (bf16[2,1024]{1,0:T(2,128)(2,1)S(1)}, bf16[2,1024]{1,0:T(2,128)(2,1)S(1)}, u32[]{:S(2)}, u32[]{:S(2)}) collective-permute-start(bf16[2,1024]{1,0:T(2,128)(2,1)S(1)} %get-tuple-element.297), channel_id=1, source_target_pairs={{0,1},{1,4},{4,5},{5,8},{8,9},{9,12},{12,13},{2,3},{3,6},{6,7},{7,... | collective-permute-start | bytes 12296 | tf_op jit(solution)/shard_map/ppermute | solution.py:445
  329.2 13.2 %collective-permute-start.22 = (bf16[256,1024]{1,0:T(8,128)(2,1)S(1)}, bf16[256,1024]{1,0:T(8,128)(2,1)}, u32[]{:S(2)}, u32[]{:S(2)}) collective-permute-start(bf16[256,1024]{1,0:T(8,128)(2,1)S(1)} %get-tuple-element.260), channel_id=1, source_target_pairs={{0,1},{1,0},{2,3},{3,2},{4,5},{5,4},{6,7},{7,6},{8,9},{9,8},{10,11... | collective-permute-start | bytes 1572872 | tf_op jit(solution)/shard_map/ppermute | solution.py:243
  363.7 25.6 %collective-permute-start.25 = (bf16[256,1024]{1,0:T(8,128)(2,1)S(1)}, bf16[256,1024]{1,0:T(8,128)(2,1)S(1)}, u32[]{:S(2)}, u32[]{:S(2)}) collective-permute-start(bf16[256,1024]{1,0:T(8,128)(2,1)S(1)} %fusion.210), channel_id=1, source_target_pairs={{0,1},{1,0},{2,3},{3,2},{4,5},{5,4},{6,7},{7,6},{8,9},{9,8},{10,11... | collective-permute-start | bytes 1572872 | tf_op jit(solution)/shard_map/ppermute | solution.py:243
  364.0 25.3 %collective-permute-start.26 = (bf16[256,1024]{1,0:T(8,128)(2,1)S(1)}, bf16[256,1024]{1,0:T(8,128)(2,1)S(1)}, u32[]{:S(2)}, u32[]{:S(2)}) collective-permute-start(bf16[256,1024]{1,0:T(8,128)(2,1)S(1)} %fusion.210), channel_id=1, source_target_pairs={{0,2},{1,3},{2,0},{3,1},{4,6},{5,7},{6,4},{7,5},{8,10},{9,11},{10,... | collective-permute-start | bytes 1572872 | tf_op jit(solution)/shard_map/ppermute | solution.py:243
  367.4 18.1 %collective-permute-start.24 = (bf16[1,512,512]{2,1,0:T(8,128)(2,1)S(1)}, bf16[1,512,512]{2,1,0:T(8,128)(2,1)S(1)}, u32[]{:S(2)}, u32[]{:S(2)}) collective-permute-start(bf16[1,512,512]{2,1,0:T(8,128)(2,1)S(1)} %slice.442), channel_id=1, source_target_pairs={{0,8},{4,12},{8,0},{12,4},{1,9},{5,13},{9,1},{13,5},{2,10},{6,14},... | collective-permute-start | bytes 1572872 | tf_op jit(solution)/shard_map/ppermute | solution.py:243
  394.1 14.0 %collective-permute-start.28 = (bf16[1,512,512]{2,1,0:T(8,128)(2,1)S(1)}, bf16[1,512,512]{2,1,0:T(8,128)(2,1)S(1)}, u32[]{:S(2)}, u32[]{:S(2)}) collective-permute-start(bf16[1,512,512]{2,1,0:T(8,128)(2,1)S(1)} %slice.444), channel_id=1, source_target_pairs={{0,8},{4,12},{8,0},{12,4},{1,9},{5,13},{9,1},{13,5},{2,10},{6,14},... | collective-permute-start | bytes 1572872 | tf_op jit(solution)/shard_map/ppermute | solution.py:243
  409.1 128.6 %reduce-scatter.11.cloned.1.call-start = ((), (), s32[]{:S(2)}) async-start(), calls=%async_computation.9 | async-start | bytes 4718592 | tf_op jit(solution)/shard_map/reduce_scatter | solution.py:382
  409.4 32.4 %collective-permute-start.31 = (bf16[256,1024]{1,0:T(8,128)(2,1)}, bf16[256,1024]{1,0:T(8,128)(2,1)}, u32[]{:S(2)}, u32[]{:S(2)}) collective-permute-start(bf16[256,1024]{1,0:T(8,128)(2,1)} %copy-done.75), channel_id=1, source_target_pairs={{0,1},{1,0},{2,3},{3,2},{4,5},{5,4},{6,7},{7,6},{8,9},{9,8},{10,11... | collective-permute-start | bytes 1572872 | tf_op jit(solution)/shard_map/ppermute | solution.py:243
  416.9 23.3 %collective-permute-start.29 = (bf16[256,1024]{1,0:T(8,128)(2,1)}, bf16[256,1024]{1,0:T(8,128)(2,1)}, u32[]{:S(2)}, u32[]{:S(2)}) collective-permute-start(bf16[256,1024]{1,0:T(8,128)(2,1)} %fusion.108), channel_id=1, source_target_pairs={{0,1},{1,0},{2,3},{3,2},{4,5},{5,4},{6,7},{7,6},{8,9},{9,8},{10,11... | collective-permute-start | bytes 1572872 | tf_op jit(solution)/shard_map/ppermute | solution.py:243
  425.5 16.3 %collective-permute-start.30 = (bf16[128,1024]{1,0:T(8,128)(2,1)S(1)}, bf16[128,1024]{1,0:T(8,128)(2,1)}, u32[]{:S(2)}, u32[]{:S(2)}) collective-permute-start(bf16[128,1024]{1,0:T(8,128)(2,1)S(1)} %slice.369), channel_id=1, source_target_pairs={{0,2},{1,3},{2,0},{3,1},{4,6},{5,7},{6,4},{7,5},{8,10},{9,11},{10,... | collective-permute-start | bytes 786440 | tf_op jit(solution)/shard_map/ppermute | solution.py:243
  444.4 23.7 %collective-permute-start.32 = (bf16[256,1024]{1,0:T(8,128)(2,1)}, bf16[256,1024]{1,0:T(8,128)(2,1)S(1)}, u32[]{:S(2)}, u32[]{:S(2)}) collective-permute-start(bf16[256,1024]{1,0:T(8,128)(2,1)} %get-tuple-element.94), channel_id=1, source_target_pairs={{0,1},{1,0},{2,3},{3,2},{4,5},{5,4},{6,7},{7,6},{8,9},{9,8},{10,11... | collective-permute-start | bytes 1572872 | tf_op jit(solution)/shard_map/ppermute | solution.py:243
  445.5 25.2 %collective-permute-start.33 = (bf16[256,1024]{1,0:T(8,128)(2,1)}, bf16[256,1024]{1,0:T(8,128)(2,1)}, u32[]{:S(2)}, u32[]{:S(2)}) collective-permute-start(bf16[256,1024]{1,0:T(8,128)(2,1)} %get-tuple-element.94), channel_id=1, source_target_pairs={{0,2},{1,3},{2,0},{3,1},{4,6},{5,7},{6,4},{7,5},{8,10},{9,11},{10,... | collective-permute-start | bytes 1572872 | tf_op jit(solution)/shard_map/ppermute | solution.py:243
  470.7 35.0 %collective-permute-start.35 = (bf16[256,1024]{1,0:T(8,128)(2,1)}, bf16[256,1024]{1,0:T(8,128)(2,1)}, u32[]{:S(2)}, u32[]{:S(2)}) collective-permute-start(bf16[256,1024]{1,0:T(8,128)(2,1)} %collective-permute-done.33), channel_id=1, source_target_pairs={{0,1},{1,0},{2,3},{3,2},{4,5},{5,4},{6,7},{7,6},{8,9},{9,8},{10,11... | collective-permute-start | bytes 1572872 | tf_op jit(solution)/shard_map/ppermute | solution.py:243
  471.1 177.5 %reduce-scatter.13.cloned.1.call-start = ((), (), s32[]{:S(2)}) async-start(), calls=%async_computation.10 | async-start | bytes 4718592
  478.1 20.1 %collective-permute-start.36 = (bf16[64,3072]{1,0:T(8,128)(2,1)S(1)}, bf16[64,3072]{1,0:T(8,128)(2,1)S(1)}, u32[]{:S(2)}, u32[]{:S(2)}) collective-permute-start(bf16[64,3072]{1,0:T(8,128)(2,1)S(1)} %constant_dynamic-slice_fusion.3), channel_id=1, source_target_pairs={{0,2},{1,3},{2,0},{3,1},{4,6},{5,7},{6,4},{7,5},{8,10},{9,11},{10,... | collective-permute-start | bytes 1179656 | tf_op jit(solution)/shard_map/ppermute | solution.py:243
  498.4 7.3 %collective-permute-start.37 = (bf16[32,3072]{1,0:T(8,128)(2,1)S(1)}, bf16[32,3072]{1,0:T(8,128)(2,1)S(1)}, u32[]{:S(2)}, u32[]{:S(2)}) collective-permute-start(bf16[32,3072]{1,0:T(8,128)(2,1)S(1)} %constant_dynamic-slice_fusion.2), channel_id=1, source_target_pairs={{0,1},{1,0},{2,3},{3,2},{4,5},{5,4},{6,7},{7,6},{8,9},{9,8},{10,11... | collective-permute-start | bytes 589832 | tf_op jit(solution)/shard_map/ppermute | solution.py:243
  500.5 43.9 %collective-permute-start.34 = (bf16[256,1024]{1,0:T(8,128)(2,1)}, bf16[256,1024]{1,0:T(8,128)(2,1)}, u32[]{:S(2)}, u32[]{:S(2)}) collective-permute-start(bf16[256,1024]{1,0:T(8,128)(2,1)} %convolution_convert_fusion.6), channel_id=1, source_target_pairs={{0,1},{1,0},{2,3},{3,2},{4,5},{5,4},{6,7},{7,6},{8,9},{9,8},{10,11... | collective-permute-start | bytes 1572872 | tf_op jit(solution)/shard_map/ppermute | solution.py:243
  508.5 18.3 %collective-permute-start.38 = (bf16[256,1024]{1,0:T(8,128)(2,1)S(1)}, bf16[256,1024]{1,0:T(8,128)(2,1)S(1)}, u32[]{:S(2)}, u32[]{:S(2)}) collective-permute-start(bf16[256,1024]{1,0:T(8,128)(2,1)S(1)} %get-tuple-element.341), channel_id=1, source_target_pairs={{0,1},{1,0},{2,3},{3,2},{4,5},{5,4},{6,7},{7,6},{8,9},{9,8},{10,11... | collective-permute-start | bytes 1572872 | tf_op jit(solution)/shard_map/ppermute | solution.py:243
  528.4 26.1 %collective-permute-start.39 = (bf16[256,1024]{1,0:T(8,128)(2,1)}, bf16[256,1024]{1,0:T(8,128)(2,1)}, u32[]{:S(2)}, u32[]{:S(2)}) collective-permute-start(bf16[256,1024]{1,0:T(8,128)(2,1)} %add_convert_fusion.2), channel_id=1, source_target_pairs={{0,2},{1,3},{2,0},{3,1},{4,6},{5,7},{6,4},{7,5},{8,10},{9,11},{10,... | collective-permute-start | bytes 1572872 | tf_op jit(solution)/shard_map/ppermute | solution.py:243
  559.8 24.3 %collective-permute-start.40 = (bf16[256,1024]{1,0:T(8,128)(2,1)}, bf16[256,1024]{1,0:T(8,128)(2,1)}, u32[]{:S(2)}, u32[]{:S(2)}) collective-permute-start(bf16[256,1024]{1,0:T(8,128)(2,1)} %fusion.143), channel_id=1, source_target_pairs={{0,1},{1,0},{2,3},{3,2},{4,5},{5,4},{6,7},{7,6},{8,9},{9,8},{10,11... | collective-permute-start | bytes 1572872 | tf_op jit(solution)/shard_map/ppermute | solution.py:243
  560.5 26.8 %collective-permute-start.41 = (bf16[256,1024]{1,0:T(8,128)(2,1)}, bf16[256,1024]{1,0:T(8,128)(2,1)}, u32[]{:S(2)}, u32[]{:S(2)}) collective-permute-start(bf16[256,1024]{1,0:T(8,128)(2,1)} %fusion.143), channel_id=1, source_target_pairs={{0,2},{1,3},{2,0},{3,1},{4,6},{5,7},{6,4},{7,5},{8,10},{9,11},{10,... | collective-permute-start | bytes 1572872 | tf_op jit(solution)/shard_map/ppermute | solution.py:243
  600.6 32.0 %collective-permute-start.42 = (bf16[256,1024]{1,0:T(8,128)(2,1)}, bf16[256,1024]{1,0:T(8,128)(2,1)}, u32[]{:S(2)}, u32[]{:S(2)}) collective-permute-start(bf16[256,1024]{1,0:T(8,128)(2,1)} %collective-permute-done.41), channel_id=1, source_target_pairs={{0,1},{1,0},{2,3},{3,2},{4,5},{5,4},{6,7},{7,6},{8,9},{9,8},{10,11... | collective-permute-start | bytes 1572872 | tf_op jit(solution)/shard_map/ppermute | solution.py:243
  601.0 19.7 %collective-permute-start.46 = (f32[90,128]{1,0:T(8,128)S(1)}, f32[90,128]{1,0:T(8,128)S(1)}, u32[]{:S(2)}, u32[]{:S(2)}) collective-permute-start(f32[90,128]{1,0:T(8,128)S(1)} %add.648), channel_id=1, source_target_pairs={{0,1},{1,0},{2,3},{3,2},{4,5},{5,4},{6,7},{7,6},{8,9},{9,8},{10,11... | collective-permute-start | bytes 138248 | tf_op jit(solution)/shard_map/ppermute | solution.py:243
  603.7 24.5 %collective-permute-start.49 = (bf16[128,1024]{1,0:T(8,128)(2,1)S(1)}, bf16[128,1024]{1,0:T(8,128)(2,1)}, u32[]{:S(2)}, u32[]{:S(2)}) collective-permute-start(bf16[128,1024]{1,0:T(8,128)(2,1)S(1)} %slice_add_fusion), channel_id=1, source_target_pairs={{0,2},{1,3},{2,0},{3,1},{4,6},{5,7},{6,4},{7,5},{8,10},{9,11},{10,... | collective-permute-start | bytes 786440 | tf_op jit(solution)/shard_map/ppermute | solution.py:243
  634.1 12.0 %collective-permute-start.48 = (bf16[128,1024]{1,0:T(8,128)(2,1)S(1)}, bf16[128,1024]{1,0:T(8,128)(2,1)S(1)}, u32[]{:S(2)}, u32[]{:S(2)}) collective-permute-start(bf16[128,1024]{1,0:T(8,128)(2,1)S(1)} %pad_maximum_fusion.20), channel_id=1, source_target_pairs={{0,2},{1,3},{2,0},{3,1},{4,6},{5,7},{6,4},{7,5},{8,10},{9,11},{10,... | collective-permute-start | bytes 786440 | tf_op jit(solution)/shard_map/ppermute | solution.py:243
  (140 other events, 946.5 us)
Sparse Core Ops, SparseCore 0:
  33.2 27.6 all-gather.3
  64.7 45.9 all-gather.5
  190.3 33.9 all-gather.7
  302.5 69.7 reduce-scatter.6
  409.2 61.8 reduce-scatter.8
  474.3 51.1 reduce-scatter.10
  544.5 49.5 reduce-scatter.12

commit v4 on v3

--- a/solution.py
+++ b/solution.py
@@ -31,7 +31,7 @@
         in_specs=[pl.BlockSpec((1, 1, width), lambda h: (h, 0, 0))],
         out_specs=pl.BlockSpec((1, tiles, TILE, TILE), lambda h: (h, 0, 0, 0)),
         out_shape=jax.ShapeDtypeStruct((heads, tiles, TILE, TILE), jnp.float32),
-        cost_estimate=pl.CostEstimate(flops=heads*TILE*TILE, transcendentals=0, bytes_accessed=heads*TILE*TILE),
+        cost_estimate=pl.CostEstimate(flops=TILE, transcendentals=0, bytes_accessed=TILE),
     )(window[:, None])
 
 def offset_sums_kernel(when_ref, tiles_ref, out_ref, wide):
@@ -59,7 +59,7 @@
         out_specs=pl.BlockSpec((1, 1, width), lambda h: (h, 0, 0)),
         out_shape=jax.ShapeDtypeStruct((heads, 1, width), jnp.float32),
         scratch_shapes=[pltpu.VMEM((TILE, width), jnp.float32)],
-        cost_estimate=pl.CostEstimate(flops=heads*TILE*TILE, transcendentals=0, bytes_accessed=heads*TILE*TILE),
+        cost_estimate=pl.CostEstimate(flops=TILE, transcendentals=0, bytes_accessed=TILE),
     )(mark(when)[None], tile_grads)[:, 0]
 
 def columns_of(head, per_shard):
@@ -295,7 +295,7 @@
 
 
 def sum_everyone(array):
-    for axis in ("seq", "dp", "heads"):
+    for axis in ("heads", "dp", "seq"):
         for bit in bits(lax.axis_size(axis)):
             array = array + swap(array, axis, bit)
     return array
@@ -508,15 +508,12 @@
     return (gradient + part, grads, small)
 
 
-def fold_heads(both):
-    for bit in reversed(bits(lax.axis_size("heads"))):
-        both = both.astype(jnp.bfloat16)
-        half = both.shape[0] // 2
-        here = bit_of("heads", bit) * half
-        kept = lax.dynamic_slice_in_dim(both, here, half, 0)
-        sent = lax.dynamic_slice_in_dim(both, half - here, half, 0)
-        both = kept.astype(jnp.float32) + swap(sent, "heads", bit).astype(jnp.float32)
-    return both
+def fold_step(both, bit):
+    here = bit_of("heads", bit)
+    kept = lax.dynamic_index_in_dim(both, here, both.ndim - 3, keepdims=False)
+    sent = lax.dynamic_index_in_dim(both, 1 - here, both.ndim - 3, keepdims=False)
+    came = swap(sent.astype(jnp.bfloat16), "heads", bit)
+    return kept.astype(jnp.float32) + came.astype(jnp.float32)
 
 
 def on_device(
@@ -560,7 +557,8 @@
     own_qkv = jnp.concatenate([query_weight, key_weight, value_weight], axis=1)
     q_cols, out_cols, n_qkv = query_weight.shape[1], output_weight.shape[0], own_qkv.shape[1]
     output_piece = lax.dynamic_slice_in_dim(output_weight, group_at * part, part, 1).T
-    attn_piece = far_swap(jnp.concatenate([own_rows(own_qkv), output_piece], axis=1))
+    attn_piece = [own_rows(w) for w in (query_weight, key_weight, value_weight)]
+    attn_piece = far_swap(jnp.concatenate(attn_piece + [output_piece], axis=1))
     small_piece = jnp.concatenate([depthwise, conv_gain[None], depth_gain[None]], axis=0).T
     small_piece = jnp.pad(small_piece, ((0, 0), (0, 128 - small_piece.shape[1])))
     conv_piece = jnp.concatenate([pointwise_in, pointwise_out, small_piece], axis=1)
@@ -587,7 +585,7 @@
         ffn1_pre.append(pres)
         ffn1_act.append(acts)
         ffn1_partial.append(partials)
-    attn_piece = later(attn_piece, ffn1_act[0][0])
+    attn_piece = later(attn_piece, ffn1_partial[1][-1])
     far_attn = gather_all(attn_piece)
     far_qkv, far_output = far_attn[:, :n_qkv], far_attn[:, n_qkv:]
     for bit in bits(n_heads):
@@ -597,9 +595,9 @@
             [jnp.where(lower, conv_piece, other), jnp.where(lower, other, conv_piece)], axis=0
         )
         if bit < len(bits(n_heads)) - 1:
-            conv_piece = later(conv_piece, ffn1_act[1][-1])
+            conv_piece = later(conv_piece, ffn1_partial[1][-1])
     summed = reduce_parts(ffn1_partial[1])
-    conv_all = gather_all(later(conv_piece, summed))
+    conv_all = gather_all(later(conv_piece, ffn1_partial[1][0]))
     pw_in, pw_out = conv_all[:, : 2 * width], conv_all[:, 2 * width : 3 * width]
     small_all = conv_all[:, 3 * width : 3 * width + KERNEL + 2].T
     conv_weights = (pw_in, pw_out, small_all[:KERNEL], small_all[KERNEL], small_all[KERNEL + 1])
@@ -620,15 +618,18 @@
         [seq_at.astype(jnp.int32)[None], jnp.stack([starts, ends], axis=1).reshape(-1)]
     )
     reversed_buckets = jnp.pad(bucket_of[::-1], (0, 1))
-    window = lax.dynamic_slice_in_dim(reversed_buckets, seq_at * local, (n_q + n_k) * TILE, 0)
+    window = lax.dynamic_slice_in_dim(reversed_buckets, seq_at * local + mark(summed), (n_q + n_k) * TILE, 0)
     levels = lax.broadcasted_iota(jnp.int32, (position_table.shape[1], window.shape[0]), 0)
     onehot = (levels == window[None, :]).astype(jnp.float32)
     tables = jnp.concatenate([position_table, far_swap(position_table)], axis=0)
     biases = jnp.dot(tables, onehot, precision=HIGHEST) * LOG2E
     per_shard = q_cols // HEAD_DIM
     tiles = [bias_tiles(biases[:per_shard]), bias_tiles(biases[per_shard:])]
-    far_part = far_swap(summed.astype(bf16))
-    far_part, tiles[0], tiles[1], scalars = tie(far_part, tiles[0], tiles[1], scalars)
+    summed = later(later(summed.astype(bf16), ffn1_partial[0][0]), ffn1_partial[0][-1])
+    far_part = far_swap(summed)
+    far_part, tiles[0], tiles[1], scalars, own_qkv = tie(
+        far_part, tiles[0], tiles[1], scalars, own_qkv
+    )
     stream_one = stream_zero + 0.5 * (
         reduce_parts(ffn1_partial[0]) + far_part.astype(jnp.float32)
     )
@@ -637,8 +638,6 @@
     low = reorder(gather_parts(attn_out.astype(bf16)))
     hidden = ffn2_in.shape[1]
     ffn2_pieces = [own_rows(ffn2_in, mark(low)), own_rows(ffn2_out, mark(low))]
-    if hidden == width:
-        ffn2_pieces = [jnp.concatenate(ffn2_pieces, axis=1)]
     ffn2_pieces = [far_swap(piece) for piece in ffn2_pieces]
     seq_bits = bits(lax.axis_size("seq"))
     both_kv = [plain(low, qkv[:, q_cols:]).astype(bf16)[None] for qkv in (own_qkv, far_qkv)]
@@ -657,9 +656,11 @@
             scalars, queries[shard], tiles[shard], query_ids[None], my_ids[:, None],
             pieces[shard], per_shard,
         )
+        mixture, ffn2_pieces[shard] = tie(mixture, ffn2_pieces[shard])
         mixtures.append(mixture)
         log_totals.append(log_total)
-    mixtures[1], ffn2_pieces = tie(mixtures[1], ffn2_pieces)
+    if hidden == width:
+        ffn2_pieces = [jnp.concatenate(ffn2_pieces, axis=1)]
     far_ffn2 = [gather_all(piece) for piece in ffn2_pieces]
     if hidden == width:
         far_ffn2 = [far_ffn2[0][:, :hidden], far_ffn2[0][:, hidden:]]
@@ -685,6 +686,7 @@
 
     normed_grad, ffn2_grads = ffn_backward(grad_four, ffn2_state, ffn2_weights)
     ffn2_grads = scatter_groups(ffn2_grads)
+    ffn2_out_g, ffn2_in_g = ffn2_grads[:, : 2 * hidden], ffn2_grads[:, 2 * hidden :]
     stream_part, ffn2_gain_grad = norm_backward(normed_grad, ffn2_hat, ffn2_inverse, ffn2_gain)
     grad_three = grad_four + stream_part
     grad_two, conv_grads, conv_small = conv_backward(
@@ -721,10 +723,11 @@
         kv_grads.append(kv_grad[0])
         all_tile_grads.append(tile_grads)
     layer_far = gather_parts(layer_far)
-    ffn2_grads, conv_grads, kv_grads[1] = tie(ffn2_grads, conv_grads, kv_grads[1])
+    ffn2_out_came = far_swap(ffn2_out_g[:, hidden:])
+    ffn2_in_g, conv_grads, kv_grads[1], ffn2_out_came, layer_far = tie(
+        ffn2_in_g, conv_grads, kv_grads[1], ffn2_out_came, layer_far
+    )
     conv_grads = scatter_groups(conv_grads)
-    n_hid = 2 * hidden
-    ffn2_out_came = far_columns(ffn2_grads, [(hidden, n_hid)])
     qkv_grads = [jnp.concatenate(pair, axis=1) for pair in zip(q_grads, kv_grads)]
     grad_parts = [cut_parts(grads) for grads in qkv_grads]
     partials = [against(own, own_qkv) + against(far, far_qkv) for own, far in zip(*grad_parts)]
@@ -737,9 +740,7 @@
         ],
         axis=1,
     )
-    normed_grad, attn_grads, ffn2_out_came, layer_far = tie(
-        normed_grad, attn_grads, ffn2_out_came, layer_far
-    )
+    normed_grad, attn_grads = tie(normed_grad, attn_grads)
     stream_part, attn_gain_grad = norm_backward(normed_grad, attn_hat, attn_inverse, attn_gain)
     grad_one = grad_two + stream_part
 
@@ -748,8 +749,6 @@
     branches = [near, gather_parts(far)]
     attn_grads, conv_grads, branches[0][-1] = tie(attn_grads, conv_grads, branches[0][-1])
     attn_grads = scatter_groups(attn_grads)
-    conv_grads = fold_heads(conv_grads)
-    branches[1][-1], conv_grads = tie(branches[1][-1], conv_grads)
     pre_lows, partials = [], []
     for f in (0, 1):
         pre_lows.append(
@@ -777,9 +776,16 @@
     )
     ffn1_grads, attn_grads = tie(ffn1_grads, attn_grads)
     ffn1_grads = scatter_groups(ffn1_grads).astype(jnp.float32)
-    far_part = far_swap(reduce_parts(partials[1]).astype(bf16)).astype(jnp.float32)
+    partials[0][-1] = later(partials[0][-1], last_sent)
+    ffn2_in_came = far_swap(later(ffn2_in_g[:, hidden:], branches[1][0]))
+    far_sum, ffn2_in_came = tie(reduce_parts(partials[1]).astype(bf16), ffn2_in_came)
+    head_bits = bits(n_heads)
+    conv_grads = conv_grads.reshape((2,) * len(head_bits) + (-1, 3 * width))
+    for bit in head_bits[:-1]:
+        conv_grads = fold_step(later(conv_grads, branches[1][0]), bit)
+    far_part, conv_grads = tie(far_swap(far_sum), conv_grads)
     near_sum = reduce_parts(partials[0])
-    normed_grad = near_sum + far_part
+    normed_grad = near_sum + far_part.astype(jnp.float32)
     stream_part, ffn1_gain_grad = norm_backward(normed_grad, *ffn1_norm, ffn1_gain)
     grad_zero = grad_one + stream_part
 
@@ -787,10 +793,10 @@
     near, far = tie(gather_parts(low), far_swap(low))
     spread_grad = near, gather_parts(far)
 
-    (f2_out_g,) = add_far(ffn2_grads, ffn2_out_came, [(0, hidden)])
-    ffn2_in_came = far_columns(later(ffn2_grads, spread_grad[1][0]), [(n_hid + hidden, 2 * n_hid)])
-    (f2_in_g,) = add_far(ffn2_grads, ffn2_in_came, [(n_hid, n_hid + hidden)])
+    (f2_out_g,) = add_far(ffn2_out_g, ffn2_out_came, [(0, hidden)])
+    (f2_in_g,) = add_far(ffn2_in_g, ffn2_in_came, [(0, hidden)])
     n_out = 2 * out_cols
+    conv_grads = fold_step(later(conv_grads, spread_grad[1][0]), head_bits[-1])
     attn_came = far_columns(later(attn_grads, spread_grad[1][0]), [(out_cols, n_out), (n_out + n_qkv, n_out + 2 * n_qkv)])
     o_g, qkv_g = add_far(attn_grads, attn_came, [(0, out_cols), (n_out, n_out + n_qkv)])
 

time: 671 us -> 634 us (0.945)
  waiting for transfers between devices: 231 us -> 192 us
  starting transfers between devices: 65 us -> 74.2 us
  matrix products: 111 us -> 104 us
  Pallas kernels: 68.7 us -> 61.9 us
    ppermute x46 -> x47, waiting for transfers between devices: 229 us -> 185 us  [swap(): return lax.ppermute(array, axis, [(i, i ^ 1 << bit) for i in range(count)])]
    ppermute x46 -> x47, starting transfers between devices: 52.8 us -> 63.3 us  [swap(): return lax.ppermute(array, axis, [(i, i ^ 1 << bit) for i in range(count)])]
    unnamed x274 -> x283, local copies, waits for them, and re-layouts: 27.6 us -> 25.1 us
  transfers between devices with their start and end apart: 57 -> 58, of which waited for: 28 -> 28; matrix products, arithmetic and copies ran while one was open for 34% -> 34% of each run, Pallas kernels for 10% -> 10%
where the time goes in v4:
time: 634 us; the launch traced here: 625 us
  waiting for transfers between devices  192 us (30%)
  matrix products  104 us (16%)
  other arithmetic  88.2 us (14%)
  starting transfers between devices  74.2 us (12%)
  local copies, waits for them, and re-layouts  67.1 us (11%)
  Pallas kernels  61.9 us (10%)
  between operations  36.4 us (6%)
    ppermute x47, waiting for transfers between devices, swap(): return lax.ppermute(array, axis, [(i, i ^ 1 << bit) for i in range(count)])  185 us
    ppermute x47, starting transfers between devices, swap(): return lax.ppermute(array, axis, [(i, i ^ 1 << bit) for i in range(count)])  63.3 us
    dot_general x25, matrix products, plain(): return jnp.dot(left, right, preferred_element_type=jnp.float32)  46.8 us
    dot_general x25, matrix products, against(): lax.dot_general(left, right, (((1,), (1,)), ((), ())), preferred_element_...  32.4 us
    pallas_call x2, Pallas kernels, attend_back(): pl.pallas_call(fn, grid_spec=pltpu.PrefetchScalarGridSpec(num_scalar_pref...  25.5 us
    unnamed x283, local copies, waits for them, and re-layouts  25.1 us
    dot_general x8, matrix products, outer(): lax.dot_general(left, right, (((0,), (0,)), ((), ())), preferred_element_...  23.6 us
    pallas_call x2, Pallas kernels, attend(): pl.pallas_call(fn, grid_spec=pltpu.PrefetchScalarGridSpec(num_scalar_pref...  21.7 us
  transfers between devices with their start and end apart: 58, of which 28 were waited for; matrix products, arithmetic and copies ran while one was open for 34% of the time, Pallas kernels for 10%

profile of v4, /device:TPU:0, one launch (start us, length us, event | category | flops | bytes accessed | tf_op | source)
XLA Modules:
  0.0 624.6 jit_solution(13322803144577272672)
XLA Ops:
  16.8 3.1 collective-permute-start
  29.7 3.0 multiply_convert_fusion.15
  36.4 2.9 multiply_convert_fusion.18
  40.2 3.6 fusion.260
  52.1 3.7 add_add_fusion
  57.7 7.4 %collective-permute-done.14 = bf16[64,3200]{1,0:T(8,128)(2,1)} collective-permute-done((bf16[64,3200]{1,0:T(8,128)(2,1)S(1)}, bf16[64,3200]{1,0:T(8,128)(2,1)}, u32[]{:S(2)}, u32[]{:S(2)}) %collective-permute-start.14) | collective-permute-done | bytes 409632 | tf_op jit(solution)/shard_map/ppermute | solution.py:243
  82.3 3.5 shard_map.365.refs_1_
  85.7 3.4 shard_map.366.refs_1_
  89.2 14.0 %collective-permute-done.1 = bf16[256,1024]{1,0:T(8,128)(2,1)S(1)} collective-permute-done((bf16[256,1024]{1,0:T(8,128)(2,1)}, bf16[256,1024]{1,0:T(8,128)(2,1)S(1)}, u32[]{:S(2)}, u32[]{:S(2)}) %collective-permute-start.1) | collective-permute-done | bytes 524320 | tf_op jit(solution)/shard_map/ppermute | solution.py:243
  107.4 13.5 %collective-permute-done.4 = bf16[256,1024]{1,0:T(8,128)(2,1)} collective-permute-done((bf16[256,1024]{1,0:T(8,128)(2,1)}, bf16[256,1024]{1,0:T(8,128)(2,1)}, u32[]{:S(2)}, u32[]{:S(2)}) %collective-permute-start.4) | collective-permute-done | bytes 524320 | tf_op jit(solution)/shard_map/ppermute | solution.py:243
  128.9 6.8 %collective-permute-done.5.refs_5_.refs_8_ = bf16[1,512,512]{2,1,0:T(8,128)(2,1)} collective-permute-done((bf16[1,512,512]{2,1,0:T(8,128)(2,1)S(1)}, bf16[1,512,512]{2,1,0:T(8,128)(2,1)}, u32[]{:S(2)}, u32[]{:S(2)}) %collective-permute-start.5) | collective-permute-done | bytes 524320 | tf_op jit(solution)/shard_map/ppermute | solution.py:243
  146.8 10.8 %shard_map.367 = (bf16[512,256]{1,0:T(8,128)(2,1)}, f32[2,1,512]{2,1,0:T(1,128)}) custom-call(s32[5]{0:T(128)} %pad_add_fusion.1.scal, bf16[512,256]{1,0:T(8,128)(2,1)} %convolution_convert_fusion.11.refs_0_, f32[2,9,256,256]{3,2,1,0:T(8,128)} %shard_map.365.refs_1_, s32[1,512]{1,0:T(1,128)} %get-tuple-element.281.refs_2_, s32[2048,1]{1,0:T(8,128)} %copy.111.refs_3_, ...), custom_call_target="tpu_custom_call" | custom-call | flops 1073741824 | bytes 4718592 | tf_op jit(solution)/shard_map/pallas_call | solution.py:131
  163.1 4.8 collective-permute-start.11
  170.1 10.8 %shard_map.368 = (bf16[512,256]{1,0:T(8,128)(2,1)}, f32[2,1,512]{2,1,0:T(1,128)}) custom-call(s32[5]{0:T(128)} %pad_add_fusion.1.scal, bf16[512,256]{1,0:T(8,128)(2,1)} %convolution_convert_fusion.10.refs_0_, f32[2,9,256,256]{3,2,1,0:T(8,128)} %shard_map.366.refs_1_, s32[1,512]{1,0:T(1,128)} %get-tuple-element.281.refs_2_, s32[2048,1]{1,0:T(8,128)} %copy.111.refs_3_, ...), custom_call_target="tpu_custom_call" | custom-call | flops 1073741824 | bytes 4718592 | tf_op jit(solution)/shard_map/pallas_call | solution.py:131
  186.9 11.5 %collective-permute-done.12 = bf16[256,1024]{1,0:T(8,128)(2,1)S(1)} collective-permute-done((bf16[256,1024]{1,0:T(8,128)(2,1)S(1)}, bf16[256,1024]{1,0:T(8,128)(2,1)S(1)}, u32[]{:S(2)}, u32[]{:S(2)}) %collective-permute-start.12) | collective-permute-done | bytes 524320 | tf_op jit(solution)/shard_map/ppermute | solution.py:243
  201.5 3.9 fusion.2
  206.9 5.0 collective-permute-start.15
  222.2 10.8 %collective-permute-done.17 = bf16[256,1024]{1,0:T(8,128)(2,1)S(1)} collective-permute-done((bf16[256,1024]{1,0:T(8,128)(2,1)S(1)}, bf16[256,1024]{1,0:T(8,128)(2,1)S(1)}, u32[]{:S(2)}, u32[]{:S(2)}) %collective-permute-start.17) | collective-permute-done | bytes 524320 | tf_op jit(solution)/shard_map/ppermute | solution.py:243
  244.6 10.3 %collective-permute-done.18 = bf16[256,1024]{1,0:T(8,128)(2,1)S(1)} collective-permute-done((bf16[256,1024]{1,0:T(8,128)(2,1)S(1)}, bf16[256,1024]{1,0:T(8,128)(2,1)S(1)}, u32[]{:S(2)}, u32[]{:S(2)}) %collective-permute-start.18) | collective-permute-done | bytes 524320 | tf_op jit(solution)/shard_map/ppermute | solution.py:243
  263.8 6.6 %collective-permute-done.19 = bf16[256,1024]{1,0:T(8,128)(2,1)S(1)} collective-permute-done((bf16[256,1024]{1,0:T(8,128)(2,1)S(1)}, bf16[256,1024]{1,0:T(8,128)(2,1)S(1)}, u32[]{:S(2)}, u32[]{:S(2)}) %collective-permute-start.19) | collective-permute-done | bytes 524320 | tf_op jit(solution)/shard_map/ppermute | solution.py:243
  276.2 4.4 convolution_convert_fusion.3
  280.6 4.4 convolution_convert_fusion.2
  285.0 7.9 %pad_maximum_fusion = bf16[1024,4096]{1,0:T(8,128)(2,1)} fusion(bf16[1024,2048]{1,0:T(8,128)(2,1)} %convolution_convert_fusion.2, bf16[1024,2048]{1,0:T(8,128)(2,1)} %convolution_convert_fusion.3), kind=kLoop, calls=%fused_computation | loop fusion | flops 16777216 | bytes 16777216 | tf_op jit(solution)/shard_map/concatenate | solution.py:417
  293.0 3.9 convert_add_fusion.2
  301.4 3.1 multiply_reduce_fusion
  322.6 4.8 pad_maximum_fusion.1
  327.4 6.7 %collective-permute-done.23 = bf16[256,1024]{1,0:T(8,128)(2,1)} collective-permute-done((bf16[256,1024]{1,0:T(8,128)(2,1)S(1)}, bf16[256,1024]{1,0:T(8,128)(2,1)}, u32[]{:S(2)}, u32[]{:S(2)}) %collective-permute-start.23) | collective-permute-done | bytes 524320 | tf_op jit(solution)/shard_map/ppermute | solution.py:243
  337.1 12.8 %shard_map.369 = (bf16[512,256]{1,0:T(8,128)(2,1)S(1)}, bf16[4,512,512]{2,1,0:T(8,128)(2,1)}, f32[2,9,256,256]{3,2,1,0:T(8,128)}) custom-call(s32[5]{0:T(128)S(1)} %copy-done.13, bf16[512,256]{1,0:T(8,128)(2,1)S(1)} %copy-done.11, f32[2,9,256,256]{3,2,1,0:T(8,128)} %shard_map.365.refs_1_, s32[1,512]{1,0:T(1,128)S(1)} %copy-done.12, s32[2048,1]{1,0:T(8,128)S(1)} %copy-done.1, ...), custom_call_target="tpu_custom_call" | custom-call | flops 2684354560 | bytes 9437184 | tf_op jit(solution)/shard_map/pallas_call | solution.py:209
  355.3 5.8 collective-permute-start.27
  365.1 12.7 %shard_map.370 = (bf16[512,256]{1,0:T(8,128)(2,1)S(1)}, bf16[4,512,512]{2,1,0:T(8,128)(2,1)}, f32[2,9,256,256]{3,2,1,0:T(8,128)}) custom-call(s32[5]{0:T(128)S(1)} %broadcast_add_fusion.4.scal, bf16[512,256]{1,0:T(8,128)(2,1)S(1)} %copy-done.10, f32[2,9,256,256]{3,2,1,0:T(8,128)} %shard_map.366.refs_1_, s32[1,512]{1,0:T(1,128)S(1)} %copy-done.12, ...), custom_call_target="tpu_custom_call" | custom-call | flops 2684354560 | bytes 9437184 | tf_op jit(solution)/shard_map/pallas_call | solution.py:209
  378.9 5.4 collective-permute-done.27
  395.4 9.4 %collective-permute-done.29 = bf16[1,512,512]{2,1,0:T(8,128)(2,1)} collective-permute-done((bf16[1,512,512]{2,1,0:T(8,128)(2,1)}, bf16[1,512,512]{2,1,0:T(8,128)(2,1)}, u32[]{:S(2)}, u32[]{:S(2)}) %collective-permute-start.29) | collective-permute-done | bytes 524320 | tf_op jit(solution)/shard_map/ppermute | solution.py:243
  426.0 3.4 convolution_convert_fusion
  442.8 16.8 %collective-permute-done.33 = bf16[256,1024]{1,0:T(8,128)(2,1)S(1)} collective-permute-done((bf16[256,1024]{1,0:T(8,128)(2,1)S(1)}, bf16[256,1024]{1,0:T(8,128)(2,1)S(1)}, u32[]{:S(2)}, u32[]{:S(2)}) %collective-permute-start.33) | collective-permute-done | bytes 524320 | tf_op jit(solution)/shard_map/ppermute | solution.py:243
  467.8 5.0 reduce-scatter.9.cloned.1.call-done
  473.1 5.2 collective-permute-done.35
  488.0 5.9 collective-permute-done.37
  501.7 3.6 fusion.49
  507.8 10.2 %collective-permute-done.40 = bf16[2,32,3072]{2,1,0:T(8,128)(2,1)S(1)} collective-permute-done((bf16[2,32,3072]{2,1,0:T(8,128)(2,1)S(1)}, bf16[2,32,3072]{2,1,0:T(8,128)(2,1)S(1)}, u32[]{:S(2)}, u32[]{:S(2)}) %collective-permute-start.40) | collective-permute-done | bytes 393248 | tf_op jit(solution)/shard_map/ppermute | solution.py:243
  519.1 6.5 %collective-permute-done.36 = bf16[256,1024]{1,0:T(8,128)(2,1)S(1)} collective-permute-done((bf16[256,1024]{1,0:T(8,128)(2,1)S(1)}, bf16[256,1024]{1,0:T(8,128)(2,1)S(1)}, u32[]{:S(2)}, u32[]{:S(2)}) %collective-permute-start.36) | collective-permute-done | bytes 524320 | tf_op jit(solution)/shard_map/ppermute | solution.py:243
  527.5 6.7 %copy.119 = bf16[1024,2048]{1,0:T(8,128)(2,1)} copy(bf16[1024,2048]{0,1:T(8,128)(2,1)} %pad_maximum_fusion.3) | data formatting | bytes 8388608
  545.7 4.0 shard_map.371
  549.7 3.8 shard_map.372
  555.0 6.6 %collective-permute-done.41 = bf16[256,1024]{1,0:T(8,128)(2,1)} collective-permute-done((bf16[256,1024]{1,0:T(8,128)(2,1)}, bf16[256,1024]{1,0:T(8,128)(2,1)}, u32[]{:S(2)}, u32[]{:S(2)}) %collective-permute-start.41) | collective-permute-done | bytes 524320 | tf_op jit(solution)/shard_map/ppermute | solution.py:243
  572.3 8.4 %collective-permute-done.45 = f32[90,128]{1,0:T(8,128)S(1)} collective-permute-done((f32[90,128]{1,0:T(8,128)S(1)}, f32[90,128]{1,0:T(8,128)S(1)}, u32[]{:S(2)}, u32[]{:S(2)}) %collective-permute-start.45) | collective-permute-done | bytes 46112 | tf_op jit(solution)/shard_map/ppermute | solution.py:243
  582.2 3.5 collective-permute-start.50
  588.1 3.5 collective-permute-done.50
  600.8 8.9 %collective-permute-done.49 = bf16[128,1024]{1,0:T(8,128)(2,1)S(1)} collective-permute-done((bf16[128,1024]{1,0:T(8,128)(2,1)S(1)}, bf16[128,1024]{1,0:T(8,128)(2,1)S(1)}, u32[]{:S(2)}, u32[]{:S(2)}) %collective-permute-start.49) | collective-permute-done | bytes 262176 | tf_op jit(solution)/shard_map/ppermute | solution.py:243
  (616 shorter events, 265.2 us)
Async XLA Ops:
  7.2 117.6 %all-gather.4.cloned.1.call-start = ((), (), s32[]{:S(2)}) async-start(), calls=%async_computation.4 | async-start | bytes 2359296 | tf_op jit(solution)/shard_map/all_gather | solution.py:251
  16.8 35.3 %collective-permute-start = (bf16[256,1024]{1,0:T(8,128)(2,1)}, bf16[256,1024]{1,0:T(8,128)(2,1)}, u32[]{:S(2)}, u32[]{:S(2)}) collective-permute-start(bf16[256,1024]{1,0:T(8,128)(2,1)} %get-tuple-element.335), channel_id=1, source_target_pairs={{0,1},{1,0},{2,3},{3,2},{4,5},{5,4},{6,7},{7,6},{8,9},{9,8},{10,11... | collective-permute-start | bytes 1572872 | tf_op jit(solution)/shard_map/ppermute | solution.py:243
  25.0 14.4 %collective-permute-start.6 = (bf16[128,1024]{0,1:T(8,128)(2,1)}, bf16[128,1024]{0,1:T(8,128)(2,1)S(1)}, u32[]{:S(2)}, u32[]{:S(2)}) collective-permute-start(bf16[128,1024]{0,1:T(8,128)(2,1)} %pad_maximum_fusion.20), channel_id=1, source_target_pairs={{0,2},{1,3},{2,0},{3,1},{4,6},{5,7},{6,4},{7,5},{8,10},{9,11},{10,... | collective-permute-start | bytes 786440 | tf_op jit(solution)/shard_map/ppermute | solution.py:243
  29.2 14.6 %collective-permute-start.13 = (bf16[32,3200]{1,0:T(8,128)(2,1)}, bf16[32,3200]{1,0:T(8,128)(2,1)}, u32[]{:S(2)}, u32[]{:S(2)}) collective-permute-start(bf16[32,3200]{1,0:T(8,128)(2,1)} %fusion.210), channel_id=1, source_target_pairs={{0,1},{1,0},{2,3},{3,2},{4,5},{5,4},{6,7},{7,6},{8,9},{9,8},{10,11... | collective-permute-start | bytes 614408 | tf_op jit(solution)/shard_map/ppermute | solution.py:243
  40.1 160.0 %all-gather.6.cloned.1.call-start = ((), (), s32[]{:S(2)}) async-start(), calls=%async_computation.5 | async-start | bytes 7372800 | tf_op jit(solution)/shard_map/all_gather | solution.py:251
  44.9 20.2 %collective-permute-start.14 = (bf16[64,3200]{1,0:T(8,128)(2,1)S(1)}, bf16[64,3200]{1,0:T(8,128)(2,1)}, u32[]{:S(2)}, u32[]{:S(2)}) collective-permute-start(bf16[64,3200]{1,0:T(8,128)(2,1)S(1)} %maximum_add_fusion.11), channel_id=1, source_target_pairs={{0,2},{1,3},{2,0},{3,1},{4,6},{5,7},{6,4},{7,5},{8,10},{9,11},{10,... | collective-permute-start | bytes 1228808 | tf_op jit(solution)/shard_map/ppermute | solution.py:243
  67.3 169.9 %all-gather.8.cloned.1.call-start = ((), (), s32[]{:S(2)}) async-start(), calls=%async_computation.6 | async-start | bytes 4718592 | tf_op jit(solution)/shard_map/all_gather | solution.py:251
  67.5 13.3 %collective-permute-start.2 = (f32[2,32]{1,0:T(2,128)}, f32[2,32]{1,0:T(2,128)S(1)}, u32[]{:S(2)}, u32[]{:S(2)}) collective-permute-start(f32[2,32]{1,0:T(2,128)} %param.33), channel_id=1, source_target_pairs={{0,2},{1,3},{2,0},{3,1},{4,6},{5,7},{6,4},{7,5},{8,10},{9,11},{10,... | collective-permute-start | bytes 776 | tf_op jit(solution)/shard_map/ppermute | solution.py:243
  67.6 36.4 %collective-permute-start.3 = (bf16[256,1024]{1,0:T(8,128)(2,1)}, bf16[256,1024]{1,0:T(8,128)(2,1)}, u32[]{:S(2)}, u32[]{:S(2)}) collective-permute-start(bf16[256,1024]{1,0:T(8,128)(2,1)} %get-tuple-element.338), channel_id=1, source_target_pairs={{0,1},{1,0},{2,3},{3,2},{4,5},{5,4},{6,7},{7,6},{8,9},{9,8},{10,11... | collective-permute-start | bytes 1572872 | tf_op jit(solution)/shard_map/ppermute | solution.py:243
  77.7 25.5 %collective-permute-start.1 = (bf16[256,1024]{1,0:T(8,128)(2,1)}, bf16[256,1024]{1,0:T(8,128)(2,1)S(1)}, u32[]{:S(2)}, u32[]{:S(2)}) collective-permute-start(bf16[256,1024]{1,0:T(8,128)(2,1)} %get-tuple-element.282), channel_id=1, source_target_pairs={{0,2},{1,3},{2,0},{3,1},{4,6},{5,7},{6,4},{7,5},{8,10},{9,11},{10,... | collective-permute-start | bytes 1572872 | tf_op jit(solution)/shard_map/ppermute | solution.py:243
  107.4 13.5 %collective-permute-start.4 = (bf16[256,1024]{1,0:T(8,128)(2,1)}, bf16[256,1024]{1,0:T(8,128)(2,1)}, u32[]{:S(2)}, u32[]{:S(2)}) collective-permute-start(bf16[256,1024]{1,0:T(8,128)(2,1)} %multiply_convert_fusion.14), channel_id=1, source_target_pairs={{0,1},{1,0},{2,3},{3,2},{4,5},{5,4},{6,7},{7,6},{8,9},{9,8},{10,11... | collective-permute-start | bytes 1572872 | tf_op jit(solution)/shard_map/ppermute | solution.py:243
  123.3 12.4 %collective-permute-start.5 = (bf16[1,512,512]{2,1,0:T(8,128)(2,1)S(1)}, bf16[1,512,512]{2,1,0:T(8,128)(2,1)}, u32[]{:S(2)}, u32[]{:S(2)}) collective-permute-start(bf16[1,512,512]{2,1,0:T(8,128)(2,1)S(1)} %fusion.117.refs_4_.refs_7_), channel_id=1, source_target_pairs={{0,8},{4,12},{8,0},{12,4},{1,9},{5,13},{9,1},{13,5},{2,10},{6,14},... | collective-permute-start | bytes 1572872 | tf_op jit(solution)/shard_map/ppermute | solution.py:243
  137.8 9.0 %collective-permute-start.7 = (bf16[2,512,512]{2,1,0:T(8,128)(2,1)}, bf16[2,512,512]{2,1,0:T(8,128)(2,1)}, u32[]{:S(2)}, u32[]{:S(2)}) collective-permute-start(bf16[2,512,512]{2,1,0:T(8,128)(2,1)} %maximum_add_fusion.8), channel_id=1, source_target_pairs={{0,4},{4,0},{8,12},{12,8},{1,5},{5,1},{9,13},{13,9},{2,6},{6,2},{1... | collective-permute-start | bytes 3145736 | tf_op jit(solution)/shard_map/ppermute | solution.py:243
  137.8 24.0 %collective-permute-start.9 = (bf16[1,512,512]{2,1,0:T(8,128)(2,1)S(1)}, bf16[1,512,512]{2,1,0:T(8,128)(2,1)S(1)}, u32[]{:S(2)}, u32[]{:S(2)}) collective-permute-start(bf16[1,512,512]{2,1,0:T(8,128)(2,1)S(1)} %fusion.118.refs_4_.refs_7_), channel_id=1, source_target_pairs={{0,8},{4,12},{8,0},{12,4},{1,9},{5,13},{9,1},{13,5},{2,10},{6,14},... | collective-permute-start | bytes 1572872 | tf_op jit(solution)/shard_map/ppermute | solution.py:243
  144.2 15.1 %collective-permute-start.8 = (bf16[128,1024]{1,0:T(8,128)(2,1)S(1)}, bf16[128,1024]{1,0:T(8,128)(2,1)}, u32[]{:S(2)}, u32[]{:S(2)}) collective-permute-start(bf16[128,1024]{1,0:T(8,128)(2,1)S(1)} %constant_dynamic-slice_fusion.3), channel_id=1, source_target_pairs={{0,2},{1,3},{2,0},{3,1},{4,6},{5,7},{6,4},{7,5},{8,10},{9,11},{10,... | collective-permute-start | bytes 786440 | tf_op jit(solution)/shard_map/ppermute | solution.py:243
  163.1 17.9 %collective-permute-start.11 = (bf16[128,1024]{1,0:T(8,128)(2,1)S(1)}, bf16[128,1024]{1,0:T(8,128)(2,1)S(1)}, u32[]{:S(2)}, u32[]{:S(2)}) collective-permute-start(bf16[128,1024]{1,0:T(8,128)(2,1)S(1)} %constant_dynamic-slice_fusion.2), channel_id=1, source_target_pairs={{0,2},{1,3},{2,0},{3,1},{4,6},{5,7},{6,4},{7,5},{8,10},{9,11},{10,... | collective-permute-start | bytes 786440 | tf_op jit(solution)/shard_map/ppermute | solution.py:243
  182.9 208.7 %reduce-scatter.7.cloned.1.call-start = ((), (), s32[]{:S(2)}) async-start(), calls=%async_computation.7 | async-start | bytes 9437184 | tf_op jit(solution)/shard_map/reduce_scatter | solution.py:382
  184.8 13.6 %collective-permute-start.12 = (bf16[256,1024]{1,0:T(8,128)(2,1)S(1)}, bf16[256,1024]{1,0:T(8,128)(2,1)S(1)}, u32[]{:S(2)}, u32[]{:S(2)}) collective-permute-start(bf16[256,1024]{1,0:T(8,128)(2,1)S(1)} %fusion.110), channel_id=1, source_target_pairs={{0,1},{1,0},{2,3},{3,2},{4,5},{5,4},{6,7},{7,6},{8,9},{9,8},{10,11... | collective-permute-start | bytes 1572872 | tf_op jit(solution)/shard_map/ppermute | solution.py:243
  218.4 14.6 %collective-permute-start.17 = (bf16[256,1024]{1,0:T(8,128)(2,1)S(1)}, bf16[256,1024]{1,0:T(8,128)(2,1)S(1)}, u32[]{:S(2)}, u32[]{:S(2)}) collective-permute-start(bf16[256,1024]{1,0:T(8,128)(2,1)S(1)} %multiply_convert_fusion.10), channel_id=1, source_target_pairs={{0,1},{1,0},{2,3},{3,2},{4,5},{5,4},{6,7},{7,6},{8,9},{9,8},{10,11... | collective-permute-start | bytes 1572872 | tf_op jit(solution)/shard_map/ppermute | solution.py:243
  241.2 13.7 %collective-permute-start.18 = (bf16[256,1024]{1,0:T(8,128)(2,1)S(1)}, bf16[256,1024]{1,0:T(8,128)(2,1)S(1)}, u32[]{:S(2)}, u32[]{:S(2)}) collective-permute-start(bf16[256,1024]{1,0:T(8,128)(2,1)S(1)} %fusion.91), channel_id=1, source_target_pairs={{0,1},{1,0},{2,3},{3,2},{4,5},{5,4},{6,7},{7,6},{8,9},{9,8},{10,11... | collective-permute-start | bytes 1572872 | tf_op jit(solution)/shard_map/ppermute | solution.py:243
  257.6 12.8 %collective-permute-start.19 = (bf16[256,1024]{1,0:T(8,128)(2,1)S(1)}, bf16[256,1024]{1,0:T(8,128)(2,1)S(1)}, u32[]{:S(2)}, u32[]{:S(2)}) collective-permute-start(bf16[256,1024]{1,0:T(8,128)(2,1)S(1)} %multiply_convert_fusion.5), channel_id=1, source_target_pairs={{0,1},{1,0},{2,3},{3,2},{4,5},{5,4},{6,7},{7,6},{8,9},{9,8},{10,11... | collective-permute-start | bytes 1572872 | tf_op jit(solution)/shard_map/ppermute | solution.py:243
  274.6 18.4 %collective-permute-start.20 = (bf16[256,1024]{1,0:T(8,128)(2,1)}, bf16[256,1024]{1,0:T(8,128)(2,1)}, u32[]{:S(2)}, u32[]{:S(2)}) collective-permute-start(bf16[256,1024]{1,0:T(8,128)(2,1)} %fusion.102), channel_id=1, source_target_pairs={{0,1},{1,0},{2,3},{3,2},{4,5},{5,4},{6,7},{7,6},{8,9},{9,8},{10,11... | collective-permute-start | bytes 1572872 | tf_op jit(solution)/shard_map/ppermute | solution.py:243
  296.9 175.9 %reduce-scatter.9.cloned.1.call-start = ((), (), s32[]{:S(2)}) async-start(), calls=%async_computation.8 | async-start | bytes 7077888 | tf_op jit(solution)/shard_map/reduce_scatter | solution.py:382
  320.4 13.6 %collective-permute-start.23 = (bf16[256,1024]{1,0:T(8,128)(2,1)S(1)}, bf16[256,1024]{1,0:T(8,128)(2,1)}, u32[]{:S(2)}, u32[]{:S(2)}) collective-permute-start(bf16[256,1024]{1,0:T(8,128)(2,1)S(1)} %get-tuple-element.270), channel_id=1, source_target_pairs={{0,1},{1,0},{2,3},{3,2},{4,5},{5,4},{6,7},{7,6},{8,9},{9,8},{10,11... | collective-permute-start | bytes 1572872 | tf_op jit(solution)/shard_map/ppermute | solution.py:243
  351.3 9.8 %collective-permute-start.24 = (bf16[2,512,512]{2,1,0:T(8,128)(2,1)S(1)}, bf16[2,512,512]{2,1,0:T(8,128)(2,1)S(1)}, u32[]{:S(2)}, u32[]{:S(2)}) collective-permute-start(bf16[2,512,512]{2,1,0:T(8,128)(2,1)S(1)} %slice.384), channel_id=1, source_target_pairs={{0,4},{4,0},{8,12},{12,8},{1,5},{5,1},{9,13},{13,9},{2,6},{6,2},{1... | collective-permute-start | bytes 3145736 | tf_op jit(solution)/shard_map/ppermute | solution.py:243
  353.5 25.4 %collective-permute-start.26 = (bf16[256,1024]{1,0:T(8,128)(2,1)S(1)}, bf16[256,1024]{1,0:T(8,128)(2,1)S(1)}, u32[]{:S(2)}, u32[]{:S(2)}) collective-permute-start(bf16[256,1024]{1,0:T(8,128)(2,1)S(1)} %fusion.189), channel_id=1, source_target_pairs={{0,1},{1,0},{2,3},{3,2},{4,5},{5,4},{6,7},{7,6},{8,9},{9,8},{10,11... | collective-permute-start | bytes 1572872 | tf_op jit(solution)/shard_map/ppermute | solution.py:243
  355.3 29.0 %collective-permute-start.27 = (bf16[256,1024]{1,0:T(8,128)(2,1)S(1)}, bf16[256,1024]{1,0:T(8,128)(2,1)}, u32[]{:S(2)}, u32[]{:S(2)}) collective-permute-start(bf16[256,1024]{1,0:T(8,128)(2,1)S(1)} %fusion.189), channel_id=1, source_target_pairs={{0,2},{1,3},{2,0},{3,1},{4,6},{5,7},{6,4},{7,5},{8,10},{9,11},{10,... | collective-permute-start | bytes 1572872 | tf_op jit(solution)/shard_map/ppermute | solution.py:243
  361.5 16.4 %collective-permute-start.25 = (bf16[1,512,512]{2,1,0:T(8,128)(2,1)S(1)}, bf16[1,512,512]{2,1,0:T(8,128)(2,1)S(1)}, u32[]{:S(2)}, u32[]{:S(2)}) collective-permute-start(bf16[1,512,512]{2,1,0:T(8,128)(2,1)S(1)} %slice.472), channel_id=1, source_target_pairs={{0,8},{4,12},{8,0},{12,4},{1,9},{5,13},{9,1},{13,5},{2,10},{6,14},... | collective-permute-start | bytes 1572872 | tf_op jit(solution)/shard_map/ppermute | solution.py:243
  390.5 14.3 %collective-permute-start.29 = (bf16[1,512,512]{2,1,0:T(8,128)(2,1)}, bf16[1,512,512]{2,1,0:T(8,128)(2,1)}, u32[]{:S(2)}, u32[]{:S(2)}) collective-permute-start(bf16[1,512,512]{2,1,0:T(8,128)(2,1)} %slice.475), channel_id=1, source_target_pairs={{0,8},{4,12},{8,0},{12,4},{1,9},{5,13},{9,1},{13,5},{2,10},{6,14},... | collective-permute-start | bytes 1572872 | tf_op jit(solution)/shard_map/ppermute | solution.py:243
  390.5 19.9 %collective-permute-start.31 = (bf16[256,1024]{1,0:T(8,128)(2,1)}, bf16[256,1024]{1,0:T(8,128)(2,1)}, u32[]{:S(2)}, u32[]{:S(2)}) collective-permute-start(bf16[256,1024]{1,0:T(8,128)(2,1)} %collective-permute-done.27), channel_id=1, source_target_pairs={{0,1},{1,0},{2,3},{3,2},{4,5},{5,4},{6,7},{7,6},{8,9},{9,8},{10,11... | collective-permute-start | bytes 1572872 | tf_op jit(solution)/shard_map/ppermute | solution.py:243
  392.6 17.8 %collective-permute-start.30 = (bf16[128,1024]{1,0:T(8,128)(2,1)S(1)}, bf16[128,1024]{1,0:T(8,128)(2,1)S(1)}, u32[]{:S(2)}, u32[]{:S(2)}) collective-permute-start(bf16[128,1024]{1,0:T(8,128)(2,1)S(1)} %slice.476), channel_id=1, source_target_pairs={{0,2},{1,3},{2,0},{3,1},{4,6},{5,7},{6,4},{7,5},{8,10},{9,11},{10,... | collective-permute-start | bytes 786440 | tf_op jit(solution)/shard_map/ppermute | solution.py:243
  410.4 117.0 %reduce-scatter.11.cloned.1.call-start = ((), (), s32[]{:S(2)}) async-start(), calls=%async_computation.9 | async-start | bytes 4718592 | tf_op jit(solution)/shard_map/reduce_scatter | solution.py:382
  416.1 15.7 %collective-permute-start.32 = (bf16[256,1024]{1,0:T(8,128)(2,1)}, bf16[256,1024]{1,0:T(8,128)(2,1)}, u32[]{:S(2)}, u32[]{:S(2)}) collective-permute-start(bf16[256,1024]{1,0:T(8,128)(2,1)} %fusion.90), channel_id=1, source_target_pairs={{0,1},{1,0},{2,3},{3,2},{4,5},{5,4},{6,7},{7,6},{8,9},{9,8},{10,11... | collective-permute-start | bytes 1572872 | tf_op jit(solution)/shard_map/ppermute | solution.py:243
  435.5 24.1 %collective-permute-start.33 = (bf16[256,1024]{1,0:T(8,128)(2,1)S(1)}, bf16[256,1024]{1,0:T(8,128)(2,1)S(1)}, u32[]{:S(2)}, u32[]{:S(2)}) collective-permute-start(bf16[256,1024]{1,0:T(8,128)(2,1)S(1)} %get-tuple-element.101), channel_id=1, source_target_pairs={{0,1},{1,0},{2,3},{3,2},{4,5},{5,4},{6,7},{7,6},{8,9},{9,8},{10,11... | collective-permute-start | bytes 1572872 | tf_op jit(solution)/shard_map/ppermute | solution.py:243
  435.9 23.7 %collective-permute-start.34 = (bf16[256,1024]{1,0:T(8,128)(2,1)S(1)}, bf16[256,1024]{1,0:T(8,128)(2,1)}, u32[]{:S(2)}, u32[]{:S(2)}) collective-permute-start(bf16[256,1024]{1,0:T(8,128)(2,1)S(1)} %get-tuple-element.101), channel_id=1, source_target_pairs={{0,2},{1,3},{2,0},{3,1},{4,6},{5,7},{6,4},{7,5},{8,10},{9,11},{10,... | collective-permute-start | bytes 1572872 | tf_op jit(solution)/shard_map/ppermute | solution.py:243
  459.7 18.6 %collective-permute-start.35 = (bf16[256,1024]{1,0:T(8,128)(2,1)}, bf16[256,1024]{1,0:T(8,128)(2,1)}, u32[]{:S(2)}, u32[]{:S(2)}) collective-permute-start(bf16[256,1024]{1,0:T(8,128)(2,1)} %collective-permute-done.34), channel_id=1, source_target_pairs={{0,1},{1,0},{2,3},{3,2},{4,5},{5,4},{6,7},{7,6},{8,9},{9,8},{10,11... | collective-permute-start | bytes 1572872 | tf_op jit(solution)/shard_map/ppermute | solution.py:243
  464.1 30.6 %collective-permute-start.38 = (bf16[128,1024]{1,0:T(8,128)(2,1)S(1)}, bf16[128,1024]{1,0:T(8,128)(2,1)S(1)}, u32[]{:S(2)}, u32[]{:S(2)}) collective-permute-start(bf16[128,1024]{1,0:T(8,128)(2,1)S(1)} %slice_add_fusion), channel_id=1, source_target_pairs={{0,2},{1,3},{2,0},{3,1},{4,6},{5,7},{6,4},{7,5},{8,10},{9,11},{10,... | collective-permute-start | bytes 786440 | tf_op jit(solution)/shard_map/ppermute | solution.py:243
  472.8 139.4 %reduce-scatter.13.cloned.1.call-start = ((), (), s32[]{:S(2)}) async-start(), calls=%async_computation.10 | async-start | bytes 4718592
  482.0 11.9 %collective-permute-start.37 = (bf16[256,1024]{1,0:T(8,128)(2,1)S(1)}, bf16[256,1024]{1,0:T(8,128)(2,1)S(1)}, u32[]{:S(2)}, u32[]{:S(2)}) collective-permute-start(bf16[256,1024]{1,0:T(8,128)(2,1)S(1)} %get-tuple-element.354), channel_id=1, source_target_pairs={{0,1},{1,0},{2,3},{3,2},{4,5},{5,4},{6,7},{7,6},{8,9},{9,8},{10,11... | collective-permute-start | bytes 1572872 | tf_op jit(solution)/shard_map/ppermute | solution.py:243
  494.7 24.4 %collective-permute-start.39 = (bf16[256,1024]{1,0:T(8,128)(2,1)S(1)}, bf16[256,1024]{1,0:T(8,128)(2,1)S(1)}, u32[]{:S(2)}, u32[]{:S(2)}) collective-permute-start(bf16[256,1024]{1,0:T(8,128)(2,1)S(1)} %add_convert_fusion.2), channel_id=1, source_target_pairs={{0,2},{1,3},{2,0},{3,1},{4,6},{5,7},{6,4},{7,5},{8,10},{9,11},{10,... | collective-permute-start | bytes 1572872 | tf_op jit(solution)/shard_map/ppermute | solution.py:243
  494.9 23.2 %collective-permute-start.40 = (bf16[2,32,3072]{2,1,0:T(8,128)(2,1)S(1)}, bf16[2,32,3072]{2,1,0:T(8,128)(2,1)S(1)}, u32[]{:S(2)}, u32[]{:S(2)}) collective-permute-start(bf16[2,32,3072]{2,1,0:T(8,128)(2,1)S(1)} %dynamic-slice_bitcast_fusion), channel_id=1, source_target_pairs={{0,1},{1,0},{2,3},{3,2},{4,5},{5,4},{6,7},{7,6},{8,9},{9,8},{10,11... | collective-permute-start | bytes 1179656 | tf_op jit(solution)/shard_map/ppermute | solution.py:243
  498.0 27.6 %collective-permute-start.36 = (bf16[256,1024]{1,0:T(8,128)(2,1)S(1)}, bf16[256,1024]{1,0:T(8,128)(2,1)S(1)}, u32[]{:S(2)}, u32[]{:S(2)}) collective-permute-start(bf16[256,1024]{1,0:T(8,128)(2,1)S(1)} %fusion.107), channel_id=1, source_target_pairs={{0,1},{1,0},{2,3},{3,2},{4,5},{5,4},{6,7},{7,6},{8,9},{9,8},{10,11... | collective-permute-start | bytes 1572872 | tf_op jit(solution)/shard_map/ppermute | solution.py:243
  537.0 24.6 %collective-permute-start.41 = (bf16[256,1024]{1,0:T(8,128)(2,1)}, bf16[256,1024]{1,0:T(8,128)(2,1)}, u32[]{:S(2)}, u32[]{:S(2)}) collective-permute-start(bf16[256,1024]{1,0:T(8,128)(2,1)} %fusion.124), channel_id=1, source_target_pairs={{0,1},{1,0},{2,3},{3,2},{4,5},{5,4},{6,7},{7,6},{8,9},{9,8},{10,11... | collective-permute-start | bytes 1572872 | tf_op jit(solution)/shard_map/ppermute | solution.py:243
  538.3 25.7 %collective-permute-start.42 = (bf16[256,1024]{1,0:T(8,128)(2,1)}, bf16[256,1024]{1,0:T(8,128)(2,1)}, u32[]{:S(2)}, u32[]{:S(2)}) collective-permute-start(bf16[256,1024]{1,0:T(8,128)(2,1)} %fusion.124), channel_id=1, source_target_pairs={{0,2},{1,3},{2,0},{3,1},{4,6},{5,7},{6,4},{7,5},{8,10},{9,11},{10,... | collective-permute-start | bytes 1572872 | tf_op jit(solution)/shard_map/ppermute | solution.py:243
  568.7 26.7 %collective-permute-start.43 = (bf16[256,1024]{1,0:T(8,128)(2,1)}, bf16[256,1024]{1,0:T(8,128)(2,1)}, u32[]{:S(2)}, u32[]{:S(2)}) collective-permute-start(bf16[256,1024]{1,0:T(8,128)(2,1)} %collective-permute-done.42), channel_id=1, source_target_pairs={{0,1},{1,0},{2,3},{3,2},{4,5},{5,4},{6,7},{7,6},{8,9},{9,8},{10,11... | collective-permute-start | bytes 1572872 | tf_op jit(solution)/shard_map/ppermute | solution.py:243
  571.7 9.0 %collective-permute-start.45 = (f32[90,128]{1,0:T(8,128)S(1)}, f32[90,128]{1,0:T(8,128)S(1)}, u32[]{:S(2)}, u32[]{:S(2)}) collective-permute-start(f32[90,128]{1,0:T(8,128)S(1)} %fusion.246), channel_id=1, source_target_pairs={{0,2},{1,3},{2,0},{3,1},{4,6},{5,7},{6,4},{7,5},{8,10},{9,11},{10,... | collective-permute-start | bytes 138248 | tf_op jit(solution)/shard_map/ppermute | solution.py:243
  582.2 9.3 %collective-permute-start.50 = (bf16[32,3072]{1,0:T(8,128)(2,1)S(1)}, bf16[32,3072]{1,0:T(8,128)(2,1)S(1)}, u32[]{:S(2)}, u32[]{:S(2)}) collective-permute-start(bf16[32,3072]{1,0:T(8,128)(2,1)S(1)} %fusion.211), channel_id=1, source_target_pairs={{0,2},{1,3},{2,0},{3,1},{4,6},{5,7},{6,4},{7,5},{8,10},{9,11},{10,... | collective-permute-start | bytes 589832 | tf_op jit(solution)/shard_map/ppermute | solution.py:243
  596.9 12.9 %collective-permute-start.49 = (bf16[128,1024]{1,0:T(8,128)(2,1)S(1)}, bf16[128,1024]{1,0:T(8,128)(2,1)S(1)}, u32[]{:S(2)}, u32[]{:S(2)}) collective-permute-start(bf16[128,1024]{1,0:T(8,128)(2,1)S(1)} %pad_maximum_fusion.21), channel_id=1, source_target_pairs={{0,2},{1,3},{2,0},{3,1},{4,6},{5,7},{6,4},{7,5},{8,10},{9,11},{10,... | collective-permute-start | bytes 786440 | tf_op jit(solution)/shard_map/ppermute | solution.py:243
  (145 other events, 953.2 us)
Sparse Core Ops, SparseCore 0:
  40.2 27.9 all-gather.3
  70.2 46.4 all-gather.5
  183.0 40.1 all-gather.7
  297.0 73.4 reduce-scatter.6
  410.5 62.2 reduce-scatter.8
  476.0 51.1 reduce-scatter.10
  534.4 51.5 reduce-scatter.12

commit v5 on v4

--- a/solution.py
+++ b/solution.py
@@ -3,6 +3,7 @@
 import jax.numpy as jnp
 from jax import lax
 from jax.experimental import pallas as pl
+from jax.experimental.layout import Layout, with_layout_constraint
 from jax.experimental.pallas import tpu as pltpu
 from jax.sharding import PartitionSpec as P
 
@@ -294,8 +295,8 @@
     return sigmoid * (1.0 + values * (1.0 - sigmoid))
 
 
-def sum_everyone(array):
-    for axis in ("heads", "dp", "seq"):
+def sum_over(array, axes):
+    for axis in axes:
         for bit in bits(lax.axis_size(axis)):
             array = array + swap(array, axis, bit)
     return array
@@ -383,7 +384,8 @@
 
 
 def grad_of(left, right):
-    return outer(left, right).astype(jnp.bfloat16)
+    grads = outer(left, right).astype(jnp.bfloat16)
+    return with_layout_constraint(grads, Layout(major_to_minor=(0, 1)))
 
 
 def ffn_forward(low_own, weights):
@@ -554,8 +556,8 @@
     group_at = lax.axis_index(("dp", "seq"))
     part = width // groups
 
-    own_qkv = jnp.concatenate([query_weight, key_weight, value_weight], axis=1)
-    q_cols, out_cols, n_qkv = query_weight.shape[1], output_weight.shape[0], own_qkv.shape[1]
+    q_cols, out_cols = query_weight.shape[1], output_weight.shape[0]
+    n_qkv = 3 * q_cols
     output_piece = lax.dynamic_slice_in_dim(output_weight, group_at * part, part, 1).T
     attn_piece = [own_rows(w) for w in (query_weight, key_weight, value_weight)]
     attn_piece = far_swap(jnp.concatenate(attn_piece + [output_piece], axis=1))
@@ -597,26 +599,8 @@
         if bit < len(bits(n_heads)) - 1:
             conv_piece = later(conv_piece, ffn1_partial[1][-1])
     summed = reduce_parts(ffn1_partial[1])
-    conv_all = gather_all(later(conv_piece, ffn1_partial[1][0]))
-    pw_in, pw_out = conv_all[:, : 2 * width], conv_all[:, 2 * width : 3 * width]
-    small_all = conv_all[:, 3 * width : 3 * width + KERNEL + 2].T
-    conv_weights = (pw_in, pw_out, small_all[:KERNEL], small_all[KERNEL], small_all[KERNEL + 1])
+    near_first = ffn1_partial[0][:-1] + [later(ffn1_partial[0][-1], summed)]
     n_q, n_k = local // TILE, length // TILE
-    my_ids = lax.dynamic_index_in_dim(segment_ids, my_row, 0, keepdims=False)
-    reach = KERNEL // 2
-    ids_pad = jnp.pad(my_ids, (reach, reach), constant_values=-1)
-    query_ids = lax.dynamic_slice_in_dim(my_ids, seq_at * local, local, 0)
-    window_ids = lax.dynamic_slice_in_dim(
-        ids_pad, seq_at * local + mine * block, block + 2 * reach, 0
-    )
-    low_ids = query_ids.reshape(n_q, TILE)[:, 0]
-    top_ids = query_ids.reshape(n_q, TILE)[:, TILE - 1]
-    starts = jnp.sum((my_ids[None] < low_ids[:, None]).astype(jnp.int32), axis=1) // TILE
-    ends = jnp.sum((my_ids[None] <= top_ids[:, None]).astype(jnp.int32), axis=1)
-    ends = (ends + TILE - 1) // TILE
-    scalars = jnp.concatenate(
-        [seq_at.astype(jnp.int32)[None], jnp.stack([starts, ends], axis=1).reshape(-1)]
-    )
     reversed_buckets = jnp.pad(bucket_of[::-1], (0, 1))
     window = lax.dynamic_slice_in_dim(reversed_buckets, seq_at * local + mark(summed), (n_q + n_k) * TILE, 0)
     levels = lax.broadcasted_iota(jnp.int32, (position_table.shape[1], window.shape[0]), 0)
@@ -627,11 +611,32 @@
     tiles = [bias_tiles(biases[:per_shard]), bias_tiles(biases[per_shard:])]
     summed = later(later(summed.astype(bf16), ffn1_partial[0][0]), ffn1_partial[0][-1])
     far_part = far_swap(summed)
-    far_part, tiles[0], tiles[1], scalars, own_qkv = tie(
-        far_part, tiles[0], tiles[1], scalars, own_qkv
+    far_part, tiles[0], tiles[1], near_part = tie(
+        far_part, tiles[0], tiles[1], reduce_parts(near_first)
     )
     stream_one = stream_zero + 0.5 * (
-        reduce_parts(ffn1_partial[0]) + far_part.astype(jnp.float32)
+        near_part + far_part.astype(jnp.float32)
+    )
+
+    conv_all = gather_all(later(conv_piece, far_part))
+    pw_in, pw_out = conv_all[:, : 2 * width], conv_all[:, 2 * width : 3 * width]
+    small_all = conv_all[:, 3 * width : 3 * width + KERNEL + 2].T
+    conv_weights = (pw_in, pw_out, small_all[:KERNEL], small_all[KERNEL], small_all[KERNEL + 1])
+
+    my_ids = lax.dynamic_index_in_dim(segment_ids, my_row + mark(far_part), 0, keepdims=False)
+    reach = KERNEL // 2
+    ids_pad = jnp.pad(my_ids, (reach, reach), constant_values=-1)
+    query_ids = lax.dynamic_slice_in_dim(my_ids, seq_at * local, local, 0)
+    window_ids = lax.dynamic_slice_in_dim(
+        ids_pad, seq_at * local + mine * block, block + 2 * reach, 0
+    )
+    low_ids = query_ids.reshape(n_q, TILE)[:, 0]
+    top_ids = query_ids.reshape(n_q, TILE)[:, TILE - 1]
+    starts = jnp.sum((my_ids[None] < low_ids[:, None]).astype(jnp.int32), axis=1) // TILE
+    ends = jnp.sum((my_ids[None] <= top_ids[:, None]).astype(jnp.int32), axis=1)
+    ends = (ends + TILE - 1) // TILE
+    scalars = jnp.concatenate(
+        [seq_at.astype(jnp.int32)[None], jnp.stack([starts, ends], axis=1).reshape(-1)]
     )
 
     attn_out, attn_hat, attn_inverse = norm_forward(stream_one, attn_gain)
@@ -640,6 +645,9 @@
     ffn2_pieces = [own_rows(ffn2_in, mark(low)), own_rows(ffn2_out, mark(low))]
     ffn2_pieces = [far_swap(piece) for piece in ffn2_pieces]
     seq_bits = bits(lax.axis_size("seq"))
+    own_qkv = jnp.concatenate(
+        [later(query_weight, far_part), key_weight, value_weight], axis=1
+    )
     both_kv = [plain(low, qkv[:, q_cols:]).astype(bf16)[None] for qkv in (own_qkv, far_qkv)]
     pieces, queries, mixtures, log_totals = [], [], [], []
     for shard in (0, 1):
@@ -796,9 +804,8 @@
     (f2_out_g,) = add_far(ffn2_out_g, ffn2_out_came, [(0, hidden)])
     (f2_in_g,) = add_far(ffn2_in_g, ffn2_in_came, [(0, hidden)])
     n_out = 2 * out_cols
-    conv_grads = fold_step(later(conv_grads, spread_grad[1][0]), head_bits[-1])
-    attn_came = far_columns(later(attn_grads, spread_grad[1][0]), [(out_cols, n_out), (n_out + n_qkv, n_out + 2 * n_qkv)])
-    o_g, qkv_g = add_far(attn_grads, attn_came, [(0, out_cols), (n_out, n_out + n_qkv)])
+    conv_grads = fold_step(later(conv_grads, spread_grad[0][-1]), head_bits[-1])
+    attn_came = far_columns(later(attn_grads, spread_grad[0][-1]), [(out_cols, n_out), (n_out + n_qkv, n_out + 2 * n_qkv)])
 
     all_heads = jnp.zeros((n_heads * per_shard, position_table.shape[1]), jnp.float32)
     all_heads = lax.dynamic_update_slice_in_dim(all_heads, table_grads[0], place * per_shard, 0)
@@ -807,8 +814,12 @@
     )
     gains = [ffn1_gain_grad, attn_gain_grad, ffn2_gain_grad, final_gain_grad] + conv_small
     small = jnp.concatenate([jnp.stack(gains).reshape(-1), all_heads.reshape(-1)])
-    small = later(small.reshape(-1, 128), spread_grad[1][0])
-    small = sum_everyone(small).reshape(-1)
+    small = later(small.reshape(-1, 128), spread_grad[0][-1])
+    small, attn_came, conv_grads, spread_grad[1][-1] = tie(
+        sum_over(small, ("dp", "seq")), attn_came, conv_grads, spread_grad[1][-1]
+    )
+    small = sum_over(small, ("heads",)).reshape(-1)
+    o_g, qkv_g = add_far(attn_grads, attn_came, [(0, out_cols), (n_out, n_out + n_qkv)])
     gains_all = small[: len(gains) * width].reshape(len(gains), width)
     table_all = small[len(gains) * width :].reshape(all_heads.shape)
     table_mine = lax.dynamic_slice_in_dim(table_all, place * per_shard, per_shard, 0)

time: 634 us -> 637 us (level)
  waiting for transfers between devices: 192 us -> 205 us
  starting transfers between devices: 74.2 us -> 64.4 us
  other arithmetic: 88.2 us -> 94.6 us
    ppermute x47, waiting for transfers between devices: 185 us -> 200 us  [swap(): return lax.ppermute(array, axis, [(i, i ^ 1 << bit) for i in range(count)])]
    ppermute x47, starting transfers between devices: 63.3 us -> 52.7 us  [swap(): return lax.ppermute(array, axis, [(i, i ^ 1 << bit) for i in range(count)])]
    unnamed x283 -> x299, local copies, waits for them, and re-layouts: 25.1 us -> 24.2 us
  transfers between devices with their start and end apart: 58 -> 58, of which waited for: 28 -> 32; matrix products, arithmetic and copies ran while one was open for 34% -> 35% of each run, Pallas kernels for 10% -> 10%
where the time goes in v5:
time: 637 us; the launch traced here: 626 us
  waiting for transfers between devices  205 us (32%)
  matrix products  101 us (16%)
  other arithmetic  94.6 us (15%)
  starting transfers between devices  64.4 us (10%)
  local copies, waits for them, and re-layouts  62.7 us (10%)
  Pallas kernels  61.9 us (10%)
  between operations  36.4 us (6%)
    ppermute x47, waiting for transfers between devices, swap(): return lax.ppermute(array, axis, [(i, i ^ 1 << bit) for i in range(count)])  200 us
    ppermute x47, starting transfers between devices, swap(): return lax.ppermute(array, axis, [(i, i ^ 1 << bit) for i in range(count)])  52.7 us
    dot_general x25, matrix products, plain(): return jnp.dot(left, right, preferred_element_type=jnp.float32)  42.5 us
    dot_general x25, matrix products, against(): lax.dot_general(left, right, (((1,), (1,)), ((), ())), preferred_element_...  34.9 us
    pallas_call x2, Pallas kernels, attend_back(): pl.pallas_call(fn, grid_spec=pltpu.PrefetchScalarGridSpec(num_scalar_pref...  25.5 us
    unnamed x299, local copies, waits for them, and re-layouts  24.2 us
    pallas_call x2, Pallas kernels, attend(): pl.pallas_call(fn, grid_spec=pltpu.PrefetchScalarGridSpec(num_scalar_pref...  21.9 us
    dot_general x8, matrix products, outer(): lax.dot_general(left, right, (((0,), (0,)), ((), ())), preferred_element_...  21.5 us
  transfers between devices with their start and end apart: 58, of which 32 were waited for; matrix products, arithmetic and copies ran while one was open for 35% of the time, Pallas kernels for 10%

profile of v5, /device:TPU:0, one launch (start us, length us, event | category | flops | bytes accessed | tf_op | source)
XLA Modules:
  0.0 626.1 jit_solution(16312648024084819319)
XLA Ops:
  17.4 3.1 collective-permute-start
  45.2 2.9 multiply_convert_fusion.18
  51.8 3.0 collective-permute-start.14
  54.8 3.4 add_add_fusion
  63.5 3.5 shard_map.365.refs_1_
  67.0 3.4 shard_map.366.refs_1_
  73.8 10.7 %collective-permute-done.14 = bf16[64,3200]{1,0:T(8,128)(2,1)} collective-permute-done((bf16[64,3200]{1,0:T(8,128)(2,1)S(1)}, bf16[64,3200]{1,0:T(8,128)(2,1)}, u32[]{:S(2)}, u32[]{:S(2)}) %collective-permute-start.14) | collective-permute-done | bytes 409632 | tf_op jit(solution)/shard_map/ppermute | solution.py:244
  86.5 14.0 %collective-permute-done.3 = bf16[256,1024]{1,0:T(8,128)(2,1)S(1)} collective-permute-done((bf16[256,1024]{1,0:T(8,128)(2,1)S(1)}, bf16[256,1024]{1,0:T(8,128)(2,1)S(1)}, u32[]{:S(2)}, u32[]{:S(2)}) %collective-permute-start.3) | collective-permute-done | bytes 524320 | tf_op jit(solution)/shard_map/ppermute | solution.py:244
  112.3 9.6 %collective-permute-done.4 = bf16[256,1024]{1,0:T(8,128)(2,1)} collective-permute-done((bf16[256,1024]{1,0:T(8,128)(2,1)}, bf16[256,1024]{1,0:T(8,128)(2,1)}, u32[]{:S(2)}, u32[]{:S(2)}) %collective-permute-start.4) | collective-permute-done | bytes 524320 | tf_op jit(solution)/shard_map/ppermute | solution.py:244
  130.1 11.6 %collective-permute-done.5.refs_5_.refs_8_ = bf16[1,512,512]{2,1,0:T(8,128)(2,1)} collective-permute-done((bf16[1,512,512]{2,1,0:T(8,128)(2,1)S(1)}, bf16[1,512,512]{2,1,0:T(8,128)(2,1)}, u32[]{:S(2)}, u32[]{:S(2)}) %collective-permute-start.5) | collective-permute-done | bytes 524320 | tf_op jit(solution)/shard_map/ppermute | solution.py:244
  157.1 10.9 %shard_map.367 = (bf16[512,256]{1,0:T(8,128)(2,1)}, f32[2,1,512]{2,1,0:T(1,128)}) custom-call(s32[5]{0:T(128)} %pad_add_fusion.1.scal, bf16[512,256]{1,0:T(8,128)(2,1)} %convolution_convert_fusion.11.refs_0_, f32[2,9,256,256]{3,2,1,0:T(8,128)} %shard_map.365.refs_1_, s32[1,512]{1,0:T(1,128)} %get-tuple-element.267.refs_2_, s32[2048,1]{1,0:T(8,128)} %copy.88.refs_3_, ...), custom_call_target="tpu_custom_call" | custom-call | flops 1073741824 | bytes 4718592 | tf_op jit(solution)/shard_map/pallas_call | solution.py:132
  173.1 3.3 collective-permute-start.11
  178.7 11.0 %shard_map.368 = (bf16[512,256]{1,0:T(8,128)(2,1)}, f32[2,1,512]{2,1,0:T(1,128)}) custom-call(s32[5]{0:T(128)} %pad_add_fusion.1.scal, bf16[512,256]{1,0:T(8,128)(2,1)} %convolution_convert_fusion.10.refs_0_, f32[2,9,256,256]{3,2,1,0:T(8,128)} %shard_map.366.refs_1_, s32[1,512]{1,0:T(1,128)} %get-tuple-element.267.refs_2_, s32[2048,1]{1,0:T(8,128)} %copy.88.refs_3_, ...), custom_call_target="tpu_custom_call" | custom-call | flops 1073741824 | bytes 4718592 | tf_op jit(solution)/shard_map/pallas_call | solution.py:132
  196.8 10.3 %collective-permute-done.12 = bf16[256,1024]{1,0:T(8,128)(2,1)S(1)} collective-permute-done((bf16[256,1024]{1,0:T(8,128)(2,1)S(1)}, bf16[256,1024]{1,0:T(8,128)(2,1)S(1)}, u32[]{:S(2)}, u32[]{:S(2)}) %collective-permute-start.12) | collective-permute-done | bytes 524320 | tf_op jit(solution)/shard_map/ppermute | solution.py:244
  210.2 3.9 fusion.2
  215.7 5.0 collective-permute-start.15
  230.3 10.6 %collective-permute-done.17 = bf16[256,1024]{1,0:T(8,128)(2,1)S(1)} collective-permute-done((bf16[256,1024]{1,0:T(8,128)(2,1)S(1)}, bf16[256,1024]{1,0:T(8,128)(2,1)S(1)}, u32[]{:S(2)}, u32[]{:S(2)}) %collective-permute-start.17) | collective-permute-done | bytes 524320 | tf_op jit(solution)/shard_map/ppermute | solution.py:244
  252.8 10.6 %collective-permute-done.18 = bf16[256,1024]{1,0:T(8,128)(2,1)S(1)} collective-permute-done((bf16[256,1024]{1,0:T(8,128)(2,1)S(1)}, bf16[256,1024]{1,0:T(8,128)(2,1)S(1)}, u32[]{:S(2)}, u32[]{:S(2)}) %collective-permute-start.18) | collective-permute-done | bytes 524320 | tf_op jit(solution)/shard_map/ppermute | solution.py:244
  272.0 7.4 %collective-permute-done.19 = bf16[256,1024]{1,0:T(8,128)(2,1)S(1)} collective-permute-done((bf16[256,1024]{1,0:T(8,128)(2,1)S(1)}, bf16[256,1024]{1,0:T(8,128)(2,1)S(1)}, u32[]{:S(2)}, u32[]{:S(2)}) %collective-permute-start.19) | collective-permute-done | bytes 524320 | tf_op jit(solution)/shard_map/ppermute | solution.py:244
  284.5 4.3 convolution_convert_fusion.3
  288.9 4.4 convolution_convert_fusion.2
  293.3 7.9 %pad_maximum_fusion = bf16[1024,4096]{1,0:T(8,128)(2,1)} fusion(bf16[1024,2048]{1,0:T(8,128)(2,1)} %convolution_convert_fusion.2, bf16[1024,2048]{1,0:T(8,128)(2,1)} %convolution_convert_fusion.3), kind=kLoop, calls=%fused_computation | loop fusion | flops 16777216 | bytes 16777216 | tf_op jit(solution)/shard_map/concatenate | solution.py:419
  301.2 3.9 convert_add_fusion.2
  309.6 3.6 multiply_reduce_fusion
  333.2 4.8 pad_maximum_fusion.1
  338.0 6.8 %collective-permute-done.23 = bf16[256,1024]{1,0:T(8,128)(2,1)} collective-permute-done((bf16[256,1024]{1,0:T(8,128)(2,1)S(1)}, bf16[256,1024]{1,0:T(8,128)(2,1)}, u32[]{:S(2)}, u32[]{:S(2)}) %collective-permute-start.23) | collective-permute-done | bytes 524320 | tf_op jit(solution)/shard_map/ppermute | solution.py:244
  347.7 12.8 %shard_map.369 = (bf16[512,256]{1,0:T(8,128)(2,1)S(1)}, bf16[4,512,512]{2,1,0:T(8,128)(2,1)}, f32[2,9,256,256]{3,2,1,0:T(8,128)}) custom-call(s32[5]{0:T(128)S(1)} %copy-done.13, bf16[512,256]{1,0:T(8,128)(2,1)S(1)} %copy-done.11, f32[2,9,256,256]{3,2,1,0:T(8,128)} %shard_map.365.refs_1_, s32[1,512]{1,0:T(1,128)S(1)} %copy-done.12, s32[2048,1]{1,0:T(8,128)S(1)} %copy-done.1, ...), custom_call_target="tpu_custom_call" | custom-call | flops 2684354560 | bytes 9437184 | tf_op jit(solution)/shard_map/pallas_call | solution.py:210
  366.2 4.1 collective-permute-start.27
  374.4 12.7 %shard_map.370 = (bf16[512,256]{1,0:T(8,128)(2,1)S(1)}, bf16[4,512,512]{2,1,0:T(8,128)(2,1)}, f32[2,9,256,256]{3,2,1,0:T(8,128)}) custom-call(s32[5]{0:T(128)S(1)} %broadcast_add_fusion.5.scal, bf16[512,256]{1,0:T(8,128)(2,1)S(1)} %copy-done.10, f32[2,9,256,256]{3,2,1,0:T(8,128)} %shard_map.366.refs_1_, s32[1,512]{1,0:T(1,128)S(1)} %copy-done.12, ...), custom_call_target="tpu_custom_call" | custom-call | flops 2684354560 | bytes 9437184 | tf_op jit(solution)/shard_map/pallas_call | solution.py:210
  390.6 3.0 collective-permute-done.27
  404.6 9.6 %collective-permute-done.29 = bf16[1,512,512]{2,1,0:T(8,128)(2,1)} collective-permute-done((bf16[1,512,512]{2,1,0:T(8,128)(2,1)}, bf16[1,512,512]{2,1,0:T(8,128)(2,1)}, u32[]{:S(2)}, u32[]{:S(2)}) %collective-permute-start.29) | collective-permute-done | bytes 524320 | tf_op jit(solution)/shard_map/ppermute | solution.py:244
  417.2 4.1 collective-permute-done.31
  436.4 3.4 convolution_convert_fusion
  454.1 15.6 %collective-permute-done.33 = bf16[256,1024]{1,0:T(8,128)(2,1)S(1)} collective-permute-done((bf16[256,1024]{1,0:T(8,128)(2,1)S(1)}, bf16[256,1024]{1,0:T(8,128)(2,1)S(1)}, u32[]{:S(2)}, u32[]{:S(2)}) %collective-permute-start.33) | collective-permute-done | bytes 524320 | tf_op jit(solution)/shard_map/ppermute | solution.py:244
  469.7 4.0 collective-permute-done.34
  477.8 3.3 reduce-scatter.7.cloned.1.call-done
  481.3 8.4 %collective-permute-done.35 = bf16[256,1024]{1,0:T(8,128)(2,1)S(1)} collective-permute-done((bf16[256,1024]{1,0:T(8,128)(2,1)S(1)}, bf16[256,1024]{1,0:T(8,128)(2,1)S(1)}, u32[]{:S(2)}, u32[]{:S(2)}) %collective-permute-start.35) | collective-permute-done | bytes 524320 | tf_op jit(solution)/shard_map/ppermute | solution.py:244
  489.8 3.0 fusion.116
  498.7 5.9 collective-permute-done.37
  521.7 10.4 %collective-permute-done.40 = bf16[2,32,3072]{2,1,0:T(8,128)(2,1)S(1)} collective-permute-done((bf16[2,32,3072]{2,1,0:T(8,128)(2,1)}, bf16[2,32,3072]{2,1,0:T(8,128)(2,1)S(1)}, u32[]{:S(2)}, u32[]{:S(2)}) %collective-permute-start.40) | collective-permute-done | bytes 393248 | tf_op jit(solution)/shard_map/ppermute | solution.py:244
  534.0 5.5 collective-permute-done.36
  539.6 3.0 fusion.128
  553.5 3.8 shard_map.371
  557.4 3.8 shard_map.372
  563.4 4.1 collective-permute-done.41
  571.8 4.9 collective-permute-done.43
  582.7 8.5 %collective-permute-done.47 = bf16[32,3072]{1,0:T(8,128)(2,1)S(1)} collective-permute-done((bf16[32,3072]{1,0:T(8,128)(2,1)S(1)}, bf16[32,3072]{1,0:T(8,128)(2,1)S(1)}, u32[]{:S(2)}, u32[]{:S(2)}) %collective-permute-start.47) | collective-permute-done | bytes 196640 | tf_op jit(solution)/shard_map/ppermute | solution.py:244
  591.3 12.7 %collective-permute-done.48 = bf16[256,1024]{1,0:T(8,128)(2,1)S(1)} collective-permute-done((bf16[256,1024]{1,0:T(8,128)(2,1)S(1)}, bf16[256,1024]{1,0:T(8,128)(2,1)S(1)}, u32[]{:S(2)}, u32[]{:S(2)}) %collective-permute-start.48) | collective-permute-done | bytes 524320 | tf_op jit(solution)/shard_map/ppermute | solution.py:244
  (635 shorter events, 269.3 us)
Async XLA Ops:
  7.2 118.7 %all-gather.4.cloned.1.call-start = ((), (), s32[]{:S(2)}) async-start(), calls=%async_computation.4 | async-start | bytes 2359296 | tf_op jit(solution)/shard_map/all_gather | solution.py:252
  17.4 37.4 %collective-permute-start = (bf16[256,1024]{1,0:T(8,128)(2,1)}, bf16[256,1024]{1,0:T(8,128)(2,1)}, u32[]{:S(2)}, u32[]{:S(2)}) collective-permute-start(bf16[256,1024]{1,0:T(8,128)(2,1)} %get-tuple-element.321), channel_id=1, source_target_pairs={{0,1},{1,0},{2,3},{3,2},{4,5},{5,4},{6,7},{7,6},{8,9},{9,8},{10,11... | collective-permute-start | bytes 1572872 | tf_op jit(solution)/shard_map/ppermute | solution.py:244
  20.4 40.3 %collective-permute-start.2 = (f32[2,32]{1,0:T(2,128)}, f32[2,32]{1,0:T(2,128)}, u32[]{:S(2)}, u32[]{:S(2)}) collective-permute-start(f32[2,32]{1,0:T(2,128)} %param.33), channel_id=1, source_target_pairs={{0,2},{1,3},{2,0},{3,1},{4,6},{5,7},{6,4},{7,5},{8,10},{9,11},{10,... | collective-permute-start | bytes 776 | tf_op jit(solution)/shard_map/ppermute | solution.py:244
  28.1 21.7 %collective-permute-start.6 = (bf16[128,1024]{0,1:T(8,128)(2,1)}, bf16[128,1024]{0,1:T(8,128)(2,1)S(1)}, u32[]{:S(2)}, u32[]{:S(2)}) collective-permute-start(bf16[128,1024]{0,1:T(8,128)(2,1)} %pad_maximum_fusion.22), channel_id=1, source_target_pairs={{0,2},{1,3},{2,0},{3,1},{4,6},{5,7},{6,4},{7,5},{8,10},{9,11},{10,... | collective-permute-start | bytes 786440 | tf_op jit(solution)/shard_map/ppermute | solution.py:244
  30.1 18.0 %collective-permute-start.13 = (bf16[32,3200]{1,0:T(8,128)(2,1)}, bf16[32,3200]{1,0:T(8,128)(2,1)}, u32[]{:S(2)}, u32[]{:S(2)}) collective-permute-start(bf16[32,3200]{1,0:T(8,128)(2,1)} %fusion.221), channel_id=1, source_target_pairs={{0,1},{1,0},{2,3},{3,2},{4,5},{5,4},{6,7},{7,6},{8,9},{9,8},{10,11... | collective-permute-start | bytes 614408 | tf_op jit(solution)/shard_map/ppermute | solution.py:244
  50.6 158.2 %all-gather.6.cloned.1.call-start = ((), (), s32[]{:S(2)}) async-start(), calls=%async_computation.5 | async-start | bytes 7372800 | tf_op jit(solution)/shard_map/all_gather | solution.py:252
  51.8 32.7 %collective-permute-start.14 = (bf16[64,3200]{1,0:T(8,128)(2,1)S(1)}, bf16[64,3200]{1,0:T(8,128)(2,1)}, u32[]{:S(2)}, u32[]{:S(2)}) collective-permute-start(bf16[64,3200]{1,0:T(8,128)(2,1)S(1)} %maximum_add_fusion.11), channel_id=1, source_target_pairs={{0,2},{1,3},{2,0},{3,1},{4,6},{5,7},{6,4},{7,5},{8,10},{9,11},{10,... | collective-permute-start | bytes 1228808 | tf_op jit(solution)/shard_map/ppermute | solution.py:244
  63.5 38.0 %collective-permute-start.1 = (bf16[256,1024]{1,0:T(8,128)(2,1)}, bf16[256,1024]{1,0:T(8,128)(2,1)}, u32[]{:S(2)}, u32[]{:S(2)}) collective-permute-start(bf16[256,1024]{1,0:T(8,128)(2,1)} %get-tuple-element.268), channel_id=1, source_target_pairs={{0,2},{1,3},{2,0},{3,1},{4,6},{5,7},{6,4},{7,5},{8,10},{9,11},{10,... | collective-permute-start | bytes 1572872 | tf_op jit(solution)/shard_map/ppermute | solution.py:244
  71.8 28.6 %collective-permute-start.3 = (bf16[256,1024]{1,0:T(8,128)(2,1)S(1)}, bf16[256,1024]{1,0:T(8,128)(2,1)S(1)}, u32[]{:S(2)}, u32[]{:S(2)}) collective-permute-start(bf16[256,1024]{1,0:T(8,128)(2,1)S(1)} %add_convert_fusion.5), channel_id=1, source_target_pairs={{0,1},{1,0},{2,3},{3,2},{4,5},{5,4},{6,7},{7,6},{8,9},{9,8},{10,11... | collective-permute-start | bytes 1572872 | tf_op jit(solution)/shard_map/ppermute | solution.py:244
  106.1 139.0 %all-gather.8.cloned.1.call-start = ((), (), s32[]{:S(2)}) async-start(), calls=%async_computation.6 | async-start | bytes 4718592 | tf_op jit(solution)/shard_map/all_gather | solution.py:252
  110.2 11.7 %collective-permute-start.4 = (bf16[256,1024]{1,0:T(8,128)(2,1)}, bf16[256,1024]{1,0:T(8,128)(2,1)}, u32[]{:S(2)}, u32[]{:S(2)}) collective-permute-start(bf16[256,1024]{1,0:T(8,128)(2,1)} %multiply_convert_fusion.14), channel_id=1, source_target_pairs={{0,1},{1,0},{2,3},{3,2},{4,5},{5,4},{6,7},{7,6},{8,9},{9,8},{10,11... | collective-permute-start | bytes 1572872 | tf_op jit(solution)/shard_map/ppermute | solution.py:244
  124.3 17.4 %collective-permute-start.5 = (bf16[1,512,512]{2,1,0:T(8,128)(2,1)S(1)}, bf16[1,512,512]{2,1,0:T(8,128)(2,1)}, u32[]{:S(2)}, u32[]{:S(2)}) collective-permute-start(bf16[1,512,512]{2,1,0:T(8,128)(2,1)S(1)} %fusion.125.refs_4_.refs_7_), channel_id=1, source_target_pairs={{0,8},{4,12},{8,0},{12,4},{1,9},{5,13},{9,1},{13,5},{2,10},{6,14},... | collective-permute-start | bytes 1572872 | tf_op jit(solution)/shard_map/ppermute | solution.py:244
  143.8 13.3 %collective-permute-start.7 = (bf16[2,512,512]{2,1,0:T(8,128)(2,1)}, bf16[2,512,512]{2,1,0:T(8,128)(2,1)}, u32[]{:S(2)}, u32[]{:S(2)}) collective-permute-start(bf16[2,512,512]{2,1,0:T(8,128)(2,1)} %maximum_add_fusion.8), channel_id=1, source_target_pairs={{0,4},{4,0},{8,12},{12,8},{1,5},{5,1},{9,13},{13,9},{2,6},{6,2},{1... | collective-permute-start | bytes 3145736 | tf_op jit(solution)/shard_map/ppermute | solution.py:244
  147.3 24.7 %collective-permute-start.9 = (bf16[1,512,512]{2,1,0:T(8,128)(2,1)S(1)}, bf16[1,512,512]{2,1,0:T(8,128)(2,1)S(1)}, u32[]{:S(2)}, u32[]{:S(2)}) collective-permute-start(bf16[1,512,512]{2,1,0:T(8,128)(2,1)S(1)} %fusion.126.refs_4_.refs_7_), channel_id=1, source_target_pairs={{0,8},{4,12},{8,0},{12,4},{1,9},{5,13},{9,1},{13,5},{2,10},{6,14},... | collective-permute-start | bytes 1572872 | tf_op jit(solution)/shard_map/ppermute | solution.py:244
  151.8 16.2 %collective-permute-start.8 = (bf16[128,1024]{1,0:T(8,128)(2,1)S(1)}, bf16[128,1024]{1,0:T(8,128)(2,1)}, u32[]{:S(2)}, u32[]{:S(2)}) collective-permute-start(bf16[128,1024]{1,0:T(8,128)(2,1)S(1)} %constant_dynamic-slice_fusion.3), channel_id=1, source_target_pairs={{0,2},{1,3},{2,0},{3,1},{4,6},{5,7},{6,4},{7,5},{8,10},{9,11},{10,... | collective-permute-start | bytes 786440 | tf_op jit(solution)/shard_map/ppermute | solution.py:244
  173.1 16.6 %collective-permute-start.11 = (bf16[128,1024]{1,0:T(8,128)(2,1)S(1)}, bf16[128,1024]{1,0:T(8,128)(2,1)S(1)}, u32[]{:S(2)}, u32[]{:S(2)}) collective-permute-start(bf16[128,1024]{1,0:T(8,128)(2,1)S(1)} %constant_dynamic-slice_fusion.2), channel_id=1, source_target_pairs={{0,2},{1,3},{2,0},{3,1},{4,6},{5,7},{6,4},{7,5},{8,10},{9,11},{10,... | collective-permute-start | bytes 786440 | tf_op jit(solution)/shard_map/ppermute | solution.py:244
  191.7 210.0 %reduce-scatter.5.cloned.1.call-start = ((), (), s32[]{:S(2)}) async-start(), calls=%async_computation.7 | async-start | bytes 9437184 | tf_op jit(solution)/shard_map/reduce_scatter | solution.py:383
  193.5 13.6 %collective-permute-start.12 = (bf16[256,1024]{1,0:T(8,128)(2,1)S(1)}, bf16[256,1024]{1,0:T(8,128)(2,1)S(1)}, u32[]{:S(2)}, u32[]{:S(2)}) collective-permute-start(bf16[256,1024]{1,0:T(8,128)(2,1)S(1)} %fusion.118), channel_id=1, source_target_pairs={{0,1},{1,0},{2,3},{3,2},{4,5},{5,4},{6,7},{7,6},{8,9},{9,8},{10,11... | collective-permute-start | bytes 1572872 | tf_op jit(solution)/shard_map/ppermute | solution.py:244
  214.4 7.6 %collective-permute-start.16 = (bf16[2,1024]{1,0:T(2,128)(2,1)S(1)}, bf16[2,1024]{1,0:T(2,128)(2,1)S(1)}, u32[]{:S(2)}, u32[]{:S(2)}) collective-permute-start(bf16[2,1024]{1,0:T(2,128)(2,1)S(1)} %get-tuple-element.295), channel_id=1, source_target_pairs={{1,0},{4,1},{5,4},{8,5},{9,8},{12,9},{13,12},{3,2},{6,3},{7,6},{10... | collective-permute-start | bytes 12296 | tf_op jit(solution)/shard_map/ppermute | solution.py:448
  226.6 14.3 %collective-permute-start.17 = (bf16[256,1024]{1,0:T(8,128)(2,1)S(1)}, bf16[256,1024]{1,0:T(8,128)(2,1)S(1)}, u32[]{:S(2)}, u32[]{:S(2)}) collective-permute-start(bf16[256,1024]{1,0:T(8,128)(2,1)S(1)} %multiply_convert_fusion.10), channel_id=1, source_target_pairs={{0,1},{1,0},{2,3},{3,2},{4,5},{5,4},{6,7},{7,6},{8,9},{9,8},{10,11... | collective-permute-start | bytes 1572872 | tf_op jit(solution)/shard_map/ppermute | solution.py:244
  249.1 14.3 %collective-permute-start.18 = (bf16[256,1024]{1,0:T(8,128)(2,1)S(1)}, bf16[256,1024]{1,0:T(8,128)(2,1)S(1)}, u32[]{:S(2)}, u32[]{:S(2)}) collective-permute-start(bf16[256,1024]{1,0:T(8,128)(2,1)S(1)} %fusion.99), channel_id=1, source_target_pairs={{0,1},{1,0},{2,3},{3,2},{4,5},{5,4},{6,7},{7,6},{8,9},{9,8},{10,11... | collective-permute-start | bytes 1572872 | tf_op jit(solution)/shard_map/ppermute | solution.py:244
  266.0 13.4 %collective-permute-start.19 = (bf16[256,1024]{1,0:T(8,128)(2,1)S(1)}, bf16[256,1024]{1,0:T(8,128)(2,1)S(1)}, u32[]{:S(2)}, u32[]{:S(2)}) collective-permute-start(bf16[256,1024]{1,0:T(8,128)(2,1)S(1)} %multiply_convert_fusion.5), channel_id=1, source_target_pairs={{0,1},{1,0},{2,3},{3,2},{4,5},{5,4},{6,7},{7,6},{8,9},{9,8},{10,11... | collective-permute-start | bytes 1572872 | tf_op jit(solution)/shard_map/ppermute | solution.py:244
  283.6 17.6 %collective-permute-start.20 = (bf16[256,1024]{1,0:T(8,128)(2,1)}, bf16[256,1024]{1,0:T(8,128)(2,1)}, u32[]{:S(2)}, u32[]{:S(2)}) collective-permute-start(bf16[256,1024]{1,0:T(8,128)(2,1)} %fusion.110), channel_id=1, source_target_pairs={{0,1},{1,0},{2,3},{3,2},{4,5},{5,4},{6,7},{7,6},{8,9},{9,8},{10,11... | collective-permute-start | bytes 1572872 | tf_op jit(solution)/shard_map/ppermute | solution.py:244
  305.1 176.0 %reduce-scatter.7.cloned.1.call-start = ((), (), s32[]{:S(2)}) async-start(), calls=%async_computation.8 | async-start | bytes 7077888 | tf_op jit(solution)/shard_map/reduce_scatter | solution.py:383
  331.0 13.8 %collective-permute-start.23 = (bf16[256,1024]{1,0:T(8,128)(2,1)S(1)}, bf16[256,1024]{1,0:T(8,128)(2,1)}, u32[]{:S(2)}, u32[]{:S(2)}) collective-permute-start(bf16[256,1024]{1,0:T(8,128)(2,1)S(1)} %get-tuple-element.256), channel_id=1, source_target_pairs={{0,1},{1,0},{2,3},{3,2},{4,5},{5,4},{6,7},{7,6},{8,9},{9,8},{10,11... | collective-permute-start | bytes 1572872 | tf_op jit(solution)/shard_map/ppermute | solution.py:244
  362.0 8.4 %collective-permute-start.24 = (bf16[2,512,512]{2,1,0:T(8,128)(2,1)S(1)}, bf16[2,512,512]{2,1,0:T(8,128)(2,1)S(1)}, u32[]{:S(2)}, u32[]{:S(2)}) collective-permute-start(bf16[2,512,512]{2,1,0:T(8,128)(2,1)S(1)} %slice.381), channel_id=1, source_target_pairs={{0,4},{4,0},{8,12},{12,8},{1,5},{5,1},{9,13},{13,9},{2,6},{6,2},{1... | collective-permute-start | bytes 3145736 | tf_op jit(solution)/shard_map/ppermute | solution.py:244
  365.6 24.9 %collective-permute-start.26 = (bf16[256,1024]{1,0:T(8,128)(2,1)S(1)}, bf16[256,1024]{1,0:T(8,128)(2,1)S(1)}, u32[]{:S(2)}, u32[]{:S(2)}) collective-permute-start(bf16[256,1024]{1,0:T(8,128)(2,1)S(1)} %fusion.201), channel_id=1, source_target_pairs={{0,1},{1,0},{2,3},{3,2},{4,5},{5,4},{6,7},{7,6},{8,9},{9,8},{10,11... | collective-permute-start | bytes 1572872 | tf_op jit(solution)/shard_map/ppermute | solution.py:244
  366.2 27.3 %collective-permute-start.27 = (bf16[256,1024]{1,0:T(8,128)(2,1)S(1)}, bf16[256,1024]{1,0:T(8,128)(2,1)}, u32[]{:S(2)}, u32[]{:S(2)}) collective-permute-start(bf16[256,1024]{1,0:T(8,128)(2,1)S(1)} %fusion.201), channel_id=1, source_target_pairs={{0,2},{1,3},{2,0},{3,1},{4,6},{5,7},{6,4},{7,5},{8,10},{9,11},{10,... | collective-permute-start | bytes 1572872 | tf_op jit(solution)/shard_map/ppermute | solution.py:244
  370.8 16.4 %collective-permute-start.25 = (bf16[1,512,512]{2,1,0:T(8,128)(2,1)S(1)}, bf16[1,512,512]{2,1,0:T(8,128)(2,1)S(1)}, u32[]{:S(2)}, u32[]{:S(2)}) collective-permute-start(bf16[1,512,512]{2,1,0:T(8,128)(2,1)S(1)} %slice.468), channel_id=1, source_target_pairs={{0,8},{4,12},{8,0},{12,4},{1,9},{5,13},{9,1},{13,5},{2,10},{6,14},... | collective-permute-start | bytes 1572872 | tf_op jit(solution)/shard_map/ppermute | solution.py:244
  399.7 14.4 %collective-permute-start.29 = (bf16[1,512,512]{2,1,0:T(8,128)(2,1)}, bf16[1,512,512]{2,1,0:T(8,128)(2,1)}, u32[]{:S(2)}, u32[]{:S(2)}) collective-permute-start(bf16[1,512,512]{2,1,0:T(8,128)(2,1)} %slice.471), channel_id=1, source_target_pairs={{0,8},{4,12},{8,0},{12,4},{1,9},{5,13},{9,1},{13,5},{2,10},{6,14},... | collective-permute-start | bytes 1572872 | tf_op jit(solution)/shard_map/ppermute | solution.py:244
  401.7 19.6 %collective-permute-start.31 = (bf16[256,1024]{1,0:T(8,128)(2,1)}, bf16[256,1024]{1,0:T(8,128)(2,1)}, u32[]{:S(2)}, u32[]{:S(2)}) collective-permute-start(bf16[256,1024]{1,0:T(8,128)(2,1)} %collective-permute-done.27), channel_id=1, source_target_pairs={{0,1},{1,0},{2,3},{3,2},{4,5},{5,4},{6,7},{7,6},{8,9},{9,8},{10,11... | collective-permute-start | bytes 1572872 | tf_op jit(solution)/shard_map/ppermute | solution.py:244
  402.7 18.6 %collective-permute-start.30 = (bf16[128,1024]{1,0:T(8,128)(2,1)S(1)}, bf16[128,1024]{1,0:T(8,128)(2,1)S(1)}, u32[]{:S(2)}, u32[]{:S(2)}) collective-permute-start(bf16[128,1024]{1,0:T(8,128)(2,1)S(1)} %slice.472), channel_id=1, source_target_pairs={{0,2},{1,3},{2,0},{3,1},{4,6},{5,7},{6,4},{7,5},{8,10},{9,11},{10,... | collective-permute-start | bytes 786440 | tf_op jit(solution)/shard_map/ppermute | solution.py:244
  421.3 121.3 %reduce-scatter.9.cloned.1.call-start = ((), (), s32[]{:S(2)}) async-start(), calls=%async_computation.9 | async-start | bytes 4718592 | tf_op jit(solution)/shard_map/reduce_scatter | solution.py:383
  429.1 14.1 %collective-permute-start.32 = (bf16[256,1024]{1,0:T(8,128)(2,1)}, bf16[256,1024]{1,0:T(8,128)(2,1)}, u32[]{:S(2)}, u32[]{:S(2)}) collective-permute-start(bf16[256,1024]{1,0:T(8,128)(2,1)} %fusion.96), channel_id=1, source_target_pairs={{0,1},{1,0},{2,3},{3,2},{4,5},{5,4},{6,7},{7,6},{8,9},{9,8},{10,11... | collective-permute-start | bytes 1572872 | tf_op jit(solution)/shard_map/ppermute | solution.py:244
  447.8 22.0 %collective-permute-start.33 = (bf16[256,1024]{1,0:T(8,128)(2,1)S(1)}, bf16[256,1024]{1,0:T(8,128)(2,1)S(1)}, u32[]{:S(2)}, u32[]{:S(2)}) collective-permute-start(bf16[256,1024]{1,0:T(8,128)(2,1)S(1)} %get-tuple-element.103), channel_id=1, source_target_pairs={{0,1},{1,0},{2,3},{3,2},{4,5},{5,4},{6,7},{7,6},{8,9},{9,8},{10,11... | collective-permute-start | bytes 1572872 | tf_op jit(solution)/shard_map/ppermute | solution.py:244
  449.8 23.9 %collective-permute-start.34 = (bf16[256,1024]{1,0:T(8,128)(2,1)S(1)}, bf16[256,1024]{1,0:T(8,128)(2,1)S(1)}, u32[]{:S(2)}, u32[]{:S(2)}) collective-permute-start(bf16[256,1024]{1,0:T(8,128)(2,1)S(1)} %get-tuple-element.103), channel_id=1, source_target_pairs={{0,2},{1,3},{2,0},{3,1},{4,6},{5,7},{6,4},{7,5},{8,10},{9,11},{10,... | collective-permute-start | bytes 1572872 | tf_op jit(solution)/shard_map/ppermute | solution.py:244
  473.7 16.0 %collective-permute-start.35 = (bf16[256,1024]{1,0:T(8,128)(2,1)S(1)}, bf16[256,1024]{1,0:T(8,128)(2,1)S(1)}, u32[]{:S(2)}, u32[]{:S(2)}) collective-permute-start(bf16[256,1024]{1,0:T(8,128)(2,1)S(1)} %collective-permute-done.34), channel_id=1, source_target_pairs={{0,1},{1,0},{2,3},{3,2},{4,5},{5,4},{6,7},{7,6},{8,9},{9,8},{10,11... | collective-permute-start | bytes 1572872 | tf_op jit(solution)/shard_map/ppermute | solution.py:244
  475.6 30.5 %collective-permute-start.38 = (bf16[128,1024]{1,0:T(8,128)(2,1)S(1)}, bf16[128,1024]{1,0:T(8,128)(2,1)}, u32[]{:S(2)}, u32[]{:S(2)}) collective-permute-start(bf16[128,1024]{1,0:T(8,128)(2,1)S(1)} %slice_add_fusion), channel_id=1, source_target_pairs={{0,2},{1,3},{2,0},{3,1},{4,6},{5,7},{6,4},{7,5},{8,10},{9,11},{10,... | collective-permute-start | bytes 786440 | tf_op jit(solution)/shard_map/ppermute | solution.py:244
  481.1 134.8 %reduce-scatter.11.cloned.1.call-start = ((), (), s32[]{:S(2)}) async-start(), calls=%async_computation.10 | async-start | bytes 4718592 | tf_op jit(solution)/shard_map/reduce_scatter | solution.py:383
  493.5 11.1 %collective-permute-start.37 = (bf16[256,1024]{1,0:T(8,128)(2,1)S(1)}, bf16[256,1024]{1,0:T(8,128)(2,1)S(1)}, u32[]{:S(2)}, u32[]{:S(2)}) collective-permute-start(bf16[256,1024]{1,0:T(8,128)(2,1)S(1)} %get-tuple-element.337), channel_id=1, source_target_pairs={{0,1},{1,0},{2,3},{3,2},{4,5},{5,4},{6,7},{7,6},{8,9},{9,8},{10,11... | collective-permute-start | bytes 1572872 | tf_op jit(solution)/shard_map/ppermute | solution.py:244
  506.2 27.9 %collective-permute-start.39 = (bf16[256,1024]{1,0:T(8,128)(2,1)}, bf16[256,1024]{1,0:T(8,128)(2,1)}, u32[]{:S(2)}, u32[]{:S(2)}) collective-permute-start(bf16[256,1024]{1,0:T(8,128)(2,1)} %add_convert_fusion.2), channel_id=1, source_target_pairs={{0,2},{1,3},{2,0},{3,1},{4,6},{5,7},{6,4},{7,5},{8,10},{9,11},{10,... | collective-permute-start | bytes 1572872 | tf_op jit(solution)/shard_map/ppermute | solution.py:244
  509.6 22.4 %collective-permute-start.40 = (bf16[2,32,3072]{2,1,0:T(8,128)(2,1)}, bf16[2,32,3072]{2,1,0:T(8,128)(2,1)S(1)}, u32[]{:S(2)}, u32[]{:S(2)}) collective-permute-start(bf16[2,32,3072]{2,1,0:T(8,128)(2,1)} %dynamic-slice_bitcast_fusion), channel_id=1, source_target_pairs={{0,1},{1,0},{2,3},{3,2},{4,5},{5,4},{6,7},{7,6},{8,9},{9,8},{10,11... | collective-permute-start | bytes 1179656 | tf_op jit(solution)/shard_map/ppermute | solution.py:244
  513.9 25.6 %collective-permute-start.36 = (bf16[256,1024]{1,0:T(8,128)(2,1)}, bf16[256,1024]{1,0:T(8,128)(2,1)}, u32[]{:S(2)}, u32[]{:S(2)}) collective-permute-start(bf16[256,1024]{1,0:T(8,128)(2,1)} %fusion.115), channel_id=1, source_target_pairs={{0,1},{1,0},{2,3},{3,2},{4,5},{5,4},{6,7},{7,6},{8,9},{9,8},{10,11... | collective-permute-start | bytes 1572872 | tf_op jit(solution)/shard_map/ppermute | solution.py:244
  546.4 21.2 %collective-permute-start.41 = (bf16[256,1024]{1,0:T(8,128)(2,1)}, bf16[256,1024]{1,0:T(8,128)(2,1)}, u32[]{:S(2)}, u32[]{:S(2)}) collective-permute-start(bf16[256,1024]{1,0:T(8,128)(2,1)} %fusion.132), channel_id=1, source_target_pairs={{0,1},{1,0},{2,3},{3,2},{4,5},{5,4},{6,7},{7,6},{8,9},{9,8},{10,11... | collective-permute-start | bytes 1572872 | tf_op jit(solution)/shard_map/ppermute | solution.py:244
  546.4 22.5 %collective-permute-start.42 = (bf16[256,1024]{1,0:T(8,128)(2,1)}, bf16[256,1024]{1,0:T(8,128)(2,1)S(1)}, u32[]{:S(2)}, u32[]{:S(2)}) collective-permute-start(bf16[256,1024]{1,0:T(8,128)(2,1)} %fusion.132), channel_id=1, source_target_pairs={{0,2},{1,3},{2,0},{3,1},{4,6},{5,7},{6,4},{7,5},{8,10},{9,11},{10,... | collective-permute-start | bytes 1572872 | tf_op jit(solution)/shard_map/ppermute | solution.py:244
  579.5 11.8 %collective-permute-start.47 = (bf16[32,3072]{1,0:T(8,128)(2,1)S(1)}, bf16[32,3072]{1,0:T(8,128)(2,1)S(1)}, u32[]{:S(2)}, u32[]{:S(2)}) collective-permute-start(bf16[32,3072]{1,0:T(8,128)(2,1)S(1)} %fusion.222), channel_id=1, source_target_pairs={{0,2},{1,3},{2,0},{3,1},{4,6},{5,7},{6,4},{7,5},{8,10},{9,11},{10,... | collective-permute-start | bytes 589832 | tf_op jit(solution)/shard_map/ppermute | solution.py:244
  579.8 24.1 %collective-permute-start.48 = (bf16[256,1024]{1,0:T(8,128)(2,1)S(1)}, bf16[256,1024]{1,0:T(8,128)(2,1)S(1)}, u32[]{:S(2)}, u32[]{:S(2)}) collective-permute-start(bf16[256,1024]{1,0:T(8,128)(2,1)S(1)} %collective-permute-done.42), channel_id=1, source_target_pairs={{0,1},{1,0},{2,3},{3,2},{4,5},{5,4},{6,7},{7,6},{8,9},{9,8},{10,11... | collective-permute-start | bytes 1572872 | tf_op jit(solution)/shard_map/ppermute | solution.py:244
  582.3 21.6 %collective-permute-start.46 = (bf16[128,1024]{1,0:T(8,128)(2,1)S(1)}, bf16[128,1024]{1,0:T(8,128)(2,1)S(1)}, u32[]{:S(2)}, u32[]{:S(2)}) collective-permute-start(bf16[128,1024]{1,0:T(8,128)(2,1)S(1)} %pad_maximum_fusion.23), channel_id=1, source_target_pairs={{0,2},{1,3},{2,0},{3,1},{4,6},{5,7},{6,4},{7,5},{8,10},{9,11},{10,... | collective-permute-start | bytes 786440 | tf_op jit(solution)/shard_map/ppermute | solution.py:244
  (154 other events, 932.1 us)
Sparse Core Ops, SparseCore 0:
  50.7 29.6 all-gather.3
  106.2 66.6 all-gather.5
  191.8 37.6 all-gather.7
  305.2 74.4 reduce-scatter.4
  421.4 59.6 reduce-scatter.6
  484.9 51.1 reduce-scatter.8
  542.7 50.0 reduce-scatter.10

commit v6 on v5

--- a/solution.py
+++ b/solution.py
@@ -598,7 +598,7 @@
         )
         if bit < len(bits(n_heads)) - 1:
             conv_piece = later(conv_piece, ffn1_partial[1][-1])
-    summed = reduce_parts(ffn1_partial[1])
+    summed, conv_piece = tie(reduce_parts(ffn1_partial[1]), conv_piece)
     near_first = ffn1_partial[0][:-1] + [later(ffn1_partial[0][-1], summed)]
     n_q, n_k = local // TILE, length // TILE
     reversed_buckets = jnp.pad(bucket_of[::-1], (0, 1))
@@ -618,11 +618,6 @@
         near_part + far_part.astype(jnp.float32)
     )
 
-    conv_all = gather_all(later(conv_piece, far_part))
-    pw_in, pw_out = conv_all[:, : 2 * width], conv_all[:, 2 * width : 3 * width]
-    small_all = conv_all[:, 3 * width : 3 * width + KERNEL + 2].T
-    conv_weights = (pw_in, pw_out, small_all[:KERNEL], small_all[KERNEL], small_all[KERNEL + 1])
-
     my_ids = lax.dynamic_index_in_dim(segment_ids, my_row + mark(far_part), 0, keepdims=False)
     reach = KERNEL // 2
     ids_pad = jnp.pad(my_ids, (reach, reach), constant_values=-1)
@@ -641,6 +636,10 @@
 
     attn_out, attn_hat, attn_inverse = norm_forward(stream_one, attn_gain)
     low = reorder(gather_parts(attn_out.astype(bf16)))
+    conv_all = gather_all(later(conv_piece, far_part))
+    pw_in, pw_out = conv_all[:, : 2 * width], conv_all[:, 2 * width : 3 * width]
+    small_all = conv_all[:, 3 * width : 3 * width + KERNEL + 2].T
+    conv_weights = (pw_in, pw_out, small_all[:KERNEL], small_all[KERNEL], small_all[KERNEL + 1])
     hidden = ffn2_in.shape[1]
     ffn2_pieces = [own_rows(ffn2_in, mark(low)), own_rows(ffn2_out, mark(low))]
     ffn2_pieces = [far_swap(piece) for piece in ffn2_pieces]
@@ -815,9 +814,7 @@
     gains = [ffn1_gain_grad, attn_gain_grad, ffn2_gain_grad, final_gain_grad] + conv_small
     small = jnp.concatenate([jnp.stack(gains).reshape(-1), all_heads.reshape(-1)])
     small = later(small.reshape(-1, 128), spread_grad[0][-1])
-    small, attn_came, conv_grads, spread_grad[1][-1] = tie(
-        sum_over(small, ("dp", "seq")), attn_came, conv_grads, spread_grad[1][-1]
-    )
+    small, attn_came = tie(sum_over(small, ("dp", "seq")), attn_came)
     small = sum_over(small, ("heads",)).reshape(-1)
     o_g, qkv_g = add_far(attn_grads, attn_came, [(0, out_cols), (n_out, n_out + n_qkv)])
     gains_all = small[: len(gains) * width].reshape(len(gains), width)

time: 637 us -> 665 us (1.044)
  waiting for transfers between devices: 205 us -> 225 us
  Pallas kernels: 61.9 us -> 69.1 us
    ppermute x47, waiting for transfers between devices: 200 us -> 221 us  [swap(): return lax.ppermute(array, axis, [(i, i ^ 1 << bit) for i in range(count)])]
    unnamed x299 -> x295, local copies, waits for them, and re-layouts: 24.2 us -> 20.3 us
  transfers between devices with their start and end apart: 58 -> 58, of which waited for: 32 -> 33; matrix products, arithmetic and copies ran while one was open for 35% -> 33% of each run, Pallas kernels for 10% -> 11%
where the time goes in v6:
time: 665 us; the launch traced here: 654 us
  waiting for transfers between devices  225 us (34%)
  matrix products  107 us (16%)
  other arithmetic  90.3 us (14%)
  Pallas kernels  69.1 us (10%)
  starting transfers between devices  69 us (10%)
  local copies, waits for them, and re-layouts  57.7 us (9%)
  between operations  36.4 us (5%)
    ppermute x47, waiting for transfers between devices, swap(): return lax.ppermute(array, axis, [(i, i ^ 1 << bit) for i in range(count)])  221 us
    ppermute x47, starting transfers between devices, swap(): return lax.ppermute(array, axis, [(i, i ^ 1 << bit) for i in range(count)])  58.1 us
    dot_general x25, matrix products, plain(): return jnp.dot(left, right, preferred_element_type=jnp.float32)  48.2 us
    dot_general x25, matrix products, against(): lax.dot_general(left, right, (((1,), (1,)), ((), ())), preferred_element_...  35 us
    pallas_call x2, Pallas kernels, attend_back(): pl.pallas_call(fn, grid_spec=pltpu.PrefetchScalarGridSpec(num_scalar_pref...  29.1 us
    pallas_call x2, Pallas kernels, attend(): pl.pallas_call(fn, grid_spec=pltpu.PrefetchScalarGridSpec(num_scalar_pref...  25.3 us
    dot_general x8, matrix products, outer(): lax.dot_general(left, right, (((0,), (0,)), ((), ())), preferred_element_...  21.5 us
    unnamed x295, local copies, waits for them, and re-layouts  20.3 us
  transfers between devices with their start and end apart: 58, of which 33 were waited for; matrix products, arithmetic and copies ran while one was open for 33% of the time, Pallas kernels for 11%

profile of v6, /device:TPU:0, one launch (start us, length us, event | category | flops | bytes accessed | tf_op | source)
XLA Modules:
  0.0 654.3 jit_solution(13774304537851018279)
XLA Ops:
  16.8 3.1 collective-permute-start
  20.7 3.0 collective-permute-start.4
  37.2 5.0 collective-permute-done.1
  49.4 14.3 %collective-permute-done.2 = bf16[64,3200]{1,0:T(8,128)(2,1)} collective-permute-done((bf16[64,3200]{1,0:T(8,128)(2,1)S(1)}, bf16[64,3200]{1,0:T(8,128)(2,1)}, u32[]{:S(2)}, u32[]{:S(2)}) %collective-permute-start.2) | collective-permute-done | bytes 409632 | tf_op jit(solution)/shard_map/ppermute | solution.py:244
  67.6 3.7 add_convert_fusion.5
  76.8 7.8 %collective-permute-done.5 = bf16[256,1024]{1,0:T(8,128)(2,1)} collective-permute-done((bf16[256,1024]{1,0:T(8,128)(2,1)}, bf16[256,1024]{1,0:T(8,128)(2,1)}, u32[]{:S(2)}, u32[]{:S(2)}) %collective-permute-start.5) | collective-permute-done | bytes 524320 | tf_op jit(solution)/shard_map/ppermute | solution.py:244
  84.5 3.5 convert_add_fusion.3
  94.1 3.4 shard_map.365.refs_1_
  97.6 3.6 shard_map.366.refs_1_
  101.1 14.7 %collective-permute-done.3 = bf16[256,1024]{1,0:T(8,128)(2,1)S(1)} collective-permute-done((bf16[256,1024]{1,0:T(8,128)(2,1)}, bf16[256,1024]{1,0:T(8,128)(2,1)S(1)}, u32[]{:S(2)}, u32[]{:S(2)}) %collective-permute-start.3) | collective-permute-done | bytes 524320 | tf_op jit(solution)/shard_map/ppermute | solution.py:244
  125.0 10.4 %collective-permute-done.6 = bf16[256,1024]{1,0:T(8,128)(2,1)} collective-permute-done((bf16[256,1024]{1,0:T(8,128)(2,1)}, bf16[256,1024]{1,0:T(8,128)(2,1)}, u32[]{:S(2)}, u32[]{:S(2)}) %collective-permute-start.6) | collective-permute-done | bytes 524320 | tf_op jit(solution)/shard_map/ppermute | solution.py:244
  143.8 12.5 %collective-permute-done.7.refs_5_.refs_8_ = bf16[1,512,512]{2,1,0:T(8,128)(2,1)} collective-permute-done((bf16[1,512,512]{2,1,0:T(8,128)(2,1)S(1)}, bf16[1,512,512]{2,1,0:T(8,128)(2,1)}, u32[]{:S(2)}, u32[]{:S(2)}) %collective-permute-start.7) | collective-permute-done | bytes 524320 | tf_op jit(solution)/shard_map/ppermute | solution.py:244
  167.9 4.9 collective-permute-start.10
  175.3 12.6 %shard_map.367 = (bf16[512,256]{1,0:T(8,128)(2,1)}, f32[2,1,512]{2,1,0:T(1,128)}) custom-call(s32[5]{0:T(128)} %pad_add_fusion.1.scal, bf16[512,256]{1,0:T(8,128)(2,1)} %convolution_convert_fusion.11.refs_0_, f32[2,9,256,256]{3,2,1,0:T(8,128)} %shard_map.365.refs_1_, s32[1,512]{1,0:T(1,128)} %get-tuple-element.267.refs_2_, s32[2048,1]{1,0:T(8,128)} %copy.88.refs_3_, ...), custom_call_target="tpu_custom_call" | custom-call | flops 1073741824 | bytes 4718592 | tf_op jit(solution)/shard_map/pallas_call | solution.py:132
  195.8 12.7 %shard_map.368 = (bf16[512,256]{1,0:T(8,128)(2,1)}, f32[2,1,512]{2,1,0:T(1,128)}) custom-call(s32[5]{0:T(128)} %pad_add_fusion.1.scal, bf16[512,256]{1,0:T(8,128)(2,1)} %convolution_convert_fusion.10.refs_0_, f32[2,9,256,256]{3,2,1,0:T(8,128)} %shard_map.366.refs_1_, s32[1,512]{1,0:T(1,128)} %get-tuple-element.267.refs_2_, s32[2048,1]{1,0:T(8,128)} %copy.88.refs_3_, ...), custom_call_target="tpu_custom_call" | custom-call | flops 1073741824 | bytes 4718592 | tf_op jit(solution)/shard_map/pallas_call | solution.py:132
  215.6 10.8 %collective-permute-done.14 = bf16[256,1024]{1,0:T(8,128)(2,1)S(1)} collective-permute-done((bf16[256,1024]{1,0:T(8,128)(2,1)S(1)}, bf16[256,1024]{1,0:T(8,128)(2,1)S(1)}, u32[]{:S(2)}, u32[]{:S(2)}) %collective-permute-start.14) | collective-permute-done | bytes 524320 | tf_op jit(solution)/shard_map/ppermute | solution.py:244
  229.4 3.9 fusion.2
  234.9 5.0 collective-permute-start.15
  250.2 10.5 %collective-permute-done.17 = bf16[256,1024]{1,0:T(8,128)(2,1)S(1)} collective-permute-done((bf16[256,1024]{1,0:T(8,128)(2,1)S(1)}, bf16[256,1024]{1,0:T(8,128)(2,1)S(1)}, u32[]{:S(2)}, u32[]{:S(2)}) %collective-permute-start.17) | collective-permute-done | bytes 524320 | tf_op jit(solution)/shard_map/ppermute | solution.py:244
  272.4 10.9 %collective-permute-done.18 = bf16[256,1024]{1,0:T(8,128)(2,1)S(1)} collective-permute-done((bf16[256,1024]{1,0:T(8,128)(2,1)S(1)}, bf16[256,1024]{1,0:T(8,128)(2,1)S(1)}, u32[]{:S(2)}, u32[]{:S(2)}) %collective-permute-start.18) | collective-permute-done | bytes 524320 | tf_op jit(solution)/shard_map/ppermute | solution.py:244
  292.2 7.2 %collective-permute-done.19 = bf16[256,1024]{1,0:T(8,128)(2,1)S(1)} collective-permute-done((bf16[256,1024]{1,0:T(8,128)(2,1)S(1)}, bf16[256,1024]{1,0:T(8,128)(2,1)S(1)}, u32[]{:S(2)}, u32[]{:S(2)}) %collective-permute-start.19) | collective-permute-done | bytes 524320 | tf_op jit(solution)/shard_map/ppermute | solution.py:244
  305.3 4.3 convolution_convert_fusion.3
  309.7 4.4 convolution_convert_fusion.2
  314.1 7.9 %pad_maximum_fusion = bf16[1024,4096]{1,0:T(8,128)(2,1)} fusion(bf16[1024,2048]{1,0:T(8,128)(2,1)} %convolution_convert_fusion.2, bf16[1024,2048]{1,0:T(8,128)(2,1)} %convolution_convert_fusion.3), kind=kLoop, calls=%fused_computation | loop fusion | flops 16777216 | bytes 16777216 | tf_op jit(solution)/shard_map/concatenate | solution.py:419
  322.0 3.9 convert_add_fusion.2
  330.4 3.7 multiply_reduce_fusion
  353.3 4.8 pad_maximum_fusion.1
  358.1 5.8 collective-permute-done.23
  367.0 14.6 %shard_map.369 = (bf16[512,256]{1,0:T(8,128)(2,1)S(1)}, bf16[4,512,512]{2,1,0:T(8,128)(2,1)}, f32[2,9,256,256]{3,2,1,0:T(8,128)}) custom-call(s32[5]{0:T(128)S(1)} %copy-done.13, bf16[512,256]{1,0:T(8,128)(2,1)S(1)} %copy-done.11, f32[2,9,256,256]{3,2,1,0:T(8,128)} %shard_map.365.refs_1_, s32[1,512]{1,0:T(1,128)S(1)} %copy-done.12, s32[2048,1]{1,0:T(8,128)S(1)} %copy-done.1, ...), custom_call_target="tpu_custom_call" | custom-call | flops 2684354560 | bytes 9437184 | tf_op jit(solution)/shard_map/pallas_call | solution.py:210
  386.5 4.2 collective-permute-start.25
  394.1 14.6 %shard_map.370 = (bf16[512,256]{1,0:T(8,128)(2,1)S(1)}, bf16[4,512,512]{2,1,0:T(8,128)(2,1)}, f32[2,9,256,256]{3,2,1,0:T(8,128)}) custom-call(s32[5]{0:T(128)S(1)} %broadcast_add_fusion.6.scal, bf16[512,256]{1,0:T(8,128)(2,1)S(1)} %copy-done.10, f32[2,9,256,256]{3,2,1,0:T(8,128)} %shard_map.366.refs_1_, s32[1,512]{1,0:T(1,128)S(1)} %copy-done.12, ...), custom_call_target="tpu_custom_call" | custom-call | flops 2684354560 | bytes 9437184 | tf_op jit(solution)/shard_map/pallas_call | solution.py:210
  425.7 7.0 %collective-permute-done.29 = bf16[1,512,512]{2,1,0:T(8,128)(2,1)} collective-permute-done((bf16[1,512,512]{2,1,0:T(8,128)(2,1)}, bf16[1,512,512]{2,1,0:T(8,128)(2,1)}, u32[]{:S(2)}, u32[]{:S(2)}) %collective-permute-start.29) | collective-permute-done | bytes 524320 | tf_op jit(solution)/shard_map/ppermute | solution.py:244
  435.7 4.0 collective-permute-done.31
  457.2 3.4 convolution_convert_fusion
  474.2 17.9 %collective-permute-done.33 = bf16[256,1024]{1,0:T(8,128)(2,1)S(1)} collective-permute-done((bf16[256,1024]{1,0:T(8,128)(2,1)S(1)}, bf16[256,1024]{1,0:T(8,128)(2,1)S(1)}, u32[]{:S(2)}, u32[]{:S(2)}) %collective-permute-start.33) | collective-permute-done | bytes 524320 | tf_op jit(solution)/shard_map/ppermute | solution.py:244
  502.0 8.6 %collective-permute-done.35 = bf16[256,1024]{1,0:T(8,128)(2,1)S(1)} collective-permute-done((bf16[256,1024]{1,0:T(8,128)(2,1)S(1)}, bf16[256,1024]{1,0:T(8,128)(2,1)S(1)}, u32[]{:S(2)}, u32[]{:S(2)}) %collective-permute-start.35) | collective-permute-done | bytes 524320 | tf_op jit(solution)/shard_map/ppermute | solution.py:244
  519.6 6.9 %collective-permute-done.37 = bf16[256,1024]{1,0:T(8,128)(2,1)S(1)} collective-permute-done((bf16[256,1024]{1,0:T(8,128)(2,1)S(1)}, bf16[256,1024]{1,0:T(8,128)(2,1)S(1)}, u32[]{:S(2)}, u32[]{:S(2)}) %collective-permute-start.37) | collective-permute-done | bytes 524320 | tf_op jit(solution)/shard_map/ppermute | solution.py:244
  541.8 11.2 %collective-permute-done.40 = bf16[2,32,3072]{2,1,0:T(8,128)(2,1)S(1)} collective-permute-done((bf16[2,32,3072]{2,1,0:T(8,128)(2,1)}, bf16[2,32,3072]{2,1,0:T(8,128)(2,1)S(1)}, u32[]{:S(2)}, u32[]{:S(2)}) %collective-permute-start.40) | collective-permute-done | bytes 393248 | tf_op jit(solution)/shard_map/ppermute | solution.py:244
  555.1 5.6 collective-permute-done.36
  574.3 3.8 shard_map.371
  578.3 3.8 shard_map.372
  584.3 4.2 collective-permute-done.41
  592.9 4.9 collective-permute-done.44
  603.3 6.6 %collective-permute-done.50 = bf16[32,3072]{1,0:T(8,128)(2,1)S(1)} collective-permute-done((bf16[32,3072]{1,0:T(8,128)(2,1)S(1)}, bf16[32,3072]{1,0:T(8,128)(2,1)S(1)}, u32[]{:S(2)}, u32[]{:S(2)}) %collective-permute-start.50) | collective-permute-done | bytes 196640 | tf_op jit(solution)/shard_map/ppermute | solution.py:244
  611.3 7.3 %collective-permute-done.43 = bf16[256,1024]{1,0:T(8,128)(2,1)S(1)} collective-permute-done((bf16[256,1024]{1,0:T(8,128)(2,1)S(1)}, bf16[256,1024]{1,0:T(8,128)(2,1)S(1)}, u32[]{:S(2)}, u32[]{:S(2)}) %collective-permute-start.43) | collective-permute-done | bytes 524320 | tf_op jit(solution)/shard_map/ppermute | solution.py:244
  622.0 10.4 %collective-permute-done.47 = bf16[128,1024]{1,0:T(8,128)(2,1)S(1)} collective-permute-done((bf16[128,1024]{1,0:T(8,128)(2,1)S(1)}, bf16[128,1024]{1,0:T(8,128)(2,1)S(1)}, u32[]{:S(2)}, u32[]{:S(2)}) %collective-permute-start.47) | collective-permute-done | bytes 262176 | tf_op jit(solution)/shard_map/ppermute | solution.py:244
  633.2 3.3 collective-permute-done.48
  637.6 4.0 collective-permute-done.49
  (631 shorter events, 273.2 us)
Async XLA Ops:
  7.2 132.4 %all-gather.4.cloned.1.call-start = ((), (), s32[]{:S(2)}) async-start(), calls=%async_computation.4 | async-start | bytes 2359296 | tf_op jit(solution)/shard_map/all_gather | solution.py:252
  16.8 30.1 %collective-permute-start = (bf16[256,1024]{1,0:T(8,128)(2,1)}, bf16[256,1024]{1,0:T(8,128)(2,1)}, u32[]{:S(2)}, u32[]{:S(2)}) collective-permute-start(bf16[256,1024]{1,0:T(8,128)(2,1)} %get-tuple-element.315), channel_id=1, source_target_pairs={{0,1},{1,0},{2,3},{3,2},{4,5},{5,4},{6,7},{7,6},{8,9},{9,8},{10,11... | collective-permute-start | bytes 1572872 | tf_op jit(solution)/shard_map/ppermute | solution.py:244
  20.7 21.4 %collective-permute-start.1 = (bf16[32,3200]{1,0:T(8,128)(2,1)}, bf16[32,3200]{1,0:T(8,128)(2,1)}, u32[]{:S(2)}, u32[]{:S(2)}) collective-permute-start(bf16[32,3200]{1,0:T(8,128)(2,1)} %fusion.221), channel_id=1, source_target_pairs={{0,1},{1,0},{2,3},{3,2},{4,5},{5,4},{6,7},{7,6},{8,9},{9,8},{10,11... | collective-permute-start | bytes 614408 | tf_op jit(solution)/shard_map/ppermute | solution.py:244
  20.7 55.1 %collective-permute-start.4 = (f32[2,32]{1,0:T(2,128)}, f32[2,32]{1,0:T(2,128)}, u32[]{:S(2)}, u32[]{:S(2)}) collective-permute-start(f32[2,32]{1,0:T(2,128)} %param.33), channel_id=1, source_target_pairs={{0,2},{1,3},{2,0},{3,1},{4,6},{5,7},{6,4},{7,5},{8,10},{9,11},{10,... | collective-permute-start | bytes 776 | tf_op jit(solution)/shard_map/ppermute | solution.py:244
  29.5 15.6 %collective-permute-start.8 = (bf16[128,1024]{0,1:T(8,128)(2,1)}, bf16[128,1024]{0,1:T(8,128)(2,1)}, u32[]{:S(2)}, u32[]{:S(2)}) collective-permute-start(bf16[128,1024]{0,1:T(8,128)(2,1)} %pad_maximum_fusion.23), channel_id=1, source_target_pairs={{0,2},{1,3},{2,0},{3,1},{4,6},{5,7},{6,4},{7,5},{8,10},{9,11},{10,... | collective-permute-start | bytes 786440 | tf_op jit(solution)/shard_map/ppermute | solution.py:244
  43.2 20.5 %collective-permute-start.2 = (bf16[64,3200]{1,0:T(8,128)(2,1)S(1)}, bf16[64,3200]{1,0:T(8,128)(2,1)}, u32[]{:S(2)}, u32[]{:S(2)}) collective-permute-start(bf16[64,3200]{1,0:T(8,128)(2,1)S(1)} %maximum_add_fusion.10), channel_id=1, source_target_pairs={{0,2},{1,3},{2,0},{3,1},{4,6},{5,7},{6,4},{7,5},{8,10},{9,11},{10,... | collective-permute-start | bytes 1228808 | tf_op jit(solution)/shard_map/ppermute | solution.py:244
  46.8 181.2 %all-gather.6.cloned.1.call-start = ((), (), s32[]{:S(2)}) async-start(), calls=%async_computation.5 | async-start | bytes 7372800 | tf_op jit(solution)/shard_map/all_gather | solution.py:252
  71.2 13.3 %collective-permute-start.5 = (bf16[256,1024]{1,0:T(8,128)(2,1)}, bf16[256,1024]{1,0:T(8,128)(2,1)}, u32[]{:S(2)}, u32[]{:S(2)}) collective-permute-start(bf16[256,1024]{1,0:T(8,128)(2,1)} %get-tuple-element.321), channel_id=1, source_target_pairs={{0,1},{1,0},{2,3},{3,2},{4,5},{5,4},{6,7},{7,6},{8,9},{9,8},{10,11... | collective-permute-start | bytes 1572872 | tf_op jit(solution)/shard_map/ppermute | solution.py:244
  90.7 25.1 %collective-permute-start.3 = (bf16[256,1024]{1,0:T(8,128)(2,1)}, bf16[256,1024]{1,0:T(8,128)(2,1)S(1)}, u32[]{:S(2)}, u32[]{:S(2)}) collective-permute-start(bf16[256,1024]{1,0:T(8,128)(2,1)} %add_add_fusion), channel_id=1, source_target_pairs={{0,2},{1,3},{2,0},{3,1},{4,6},{5,7},{6,4},{7,5},{8,10},{9,11},{10,... | collective-permute-start | bytes 1572872 | tf_op jit(solution)/shard_map/ppermute | solution.py:244
  118.7 146.2 %all-gather.8.cloned.1.call-start = ((), (), s32[]{:S(2)}) async-start(), calls=%async_computation.6 | async-start | bytes 4718592 | tf_op jit(solution)/shard_map/all_gather | solution.py:252
  122.2 13.3 %collective-permute-start.6 = (bf16[256,1024]{1,0:T(8,128)(2,1)}, bf16[256,1024]{1,0:T(8,128)(2,1)}, u32[]{:S(2)}, u32[]{:S(2)}) collective-permute-start(bf16[256,1024]{1,0:T(8,128)(2,1)} %multiply_convert_fusion.14), channel_id=1, source_target_pairs={{0,1},{1,0},{2,3},{3,2},{4,5},{5,4},{6,7},{7,6},{8,9},{9,8},{10,11... | collective-permute-start | bytes 1572872 | tf_op jit(solution)/shard_map/ppermute | solution.py:244
  137.8 18.5 %collective-permute-start.7 = (bf16[1,512,512]{2,1,0:T(8,128)(2,1)S(1)}, bf16[1,512,512]{2,1,0:T(8,128)(2,1)}, u32[]{:S(2)}, u32[]{:S(2)}) collective-permute-start(bf16[1,512,512]{2,1,0:T(8,128)(2,1)S(1)} %fusion.125.refs_4_.refs_7_), channel_id=1, source_target_pairs={{0,8},{4,12},{8,0},{12,4},{1,9},{5,13},{9,1},{13,5},{2,10},{6,14},... | collective-permute-start | bytes 1572872 | tf_op jit(solution)/shard_map/ppermute | solution.py:244
  158.4 16.9 %collective-permute-start.9 = (bf16[2,512,512]{2,1,0:T(8,128)(2,1)}, bf16[2,512,512]{2,1,0:T(8,128)(2,1)}, u32[]{:S(2)}, u32[]{:S(2)}) collective-permute-start(bf16[2,512,512]{2,1,0:T(8,128)(2,1)} %maximum_add_fusion.8), channel_id=1, source_target_pairs={{0,4},{4,0},{8,12},{12,8},{1,5},{5,1},{9,13},{13,9},{2,6},{6,2},{1... | collective-permute-start | bytes 3145736 | tf_op jit(solution)/shard_map/ppermute | solution.py:244
  162.0 28.6 %collective-permute-start.11 = (bf16[1,512,512]{2,1,0:T(8,128)(2,1)S(1)}, bf16[1,512,512]{2,1,0:T(8,128)(2,1)S(1)}, u32[]{:S(2)}, u32[]{:S(2)}) collective-permute-start(bf16[1,512,512]{2,1,0:T(8,128)(2,1)S(1)} %fusion.126.refs_4_.refs_7_), channel_id=1, source_target_pairs={{0,8},{4,12},{8,0},{12,4},{1,9},{5,13},{9,1},{13,5},{2,10},{6,14},... | collective-permute-start | bytes 1572872 | tf_op jit(solution)/shard_map/ppermute | solution.py:244
  167.9 20.0 %collective-permute-start.10 = (bf16[128,1024]{1,0:T(8,128)(2,1)S(1)}, bf16[128,1024]{1,0:T(8,128)(2,1)}, u32[]{:S(2)}, u32[]{:S(2)}) collective-permute-start(bf16[128,1024]{1,0:T(8,128)(2,1)S(1)} %constant_dynamic-slice_fusion.3), channel_id=1, source_target_pairs={{0,2},{1,3},{2,0},{3,1},{4,6},{5,7},{6,4},{7,5},{8,10},{9,11},{10,... | collective-permute-start | bytes 786440 | tf_op jit(solution)/shard_map/ppermute | solution.py:244
  193.4 15.1 %collective-permute-start.13 = (bf16[128,1024]{1,0:T(8,128)(2,1)S(1)}, bf16[128,1024]{1,0:T(8,128)(2,1)S(1)}, u32[]{:S(2)}, u32[]{:S(2)}) collective-permute-start(bf16[128,1024]{1,0:T(8,128)(2,1)S(1)} %constant_dynamic-slice_fusion.2), channel_id=1, source_target_pairs={{0,2},{1,3},{2,0},{3,1},{4,6},{5,7},{6,4},{7,5},{8,10},{9,11},{10,... | collective-permute-start | bytes 786440 | tf_op jit(solution)/shard_map/ppermute | solution.py:244
  210.4 211.4 %reduce-scatter.5.cloned.1.call-start = ((), (), s32[]{:S(2)}) async-start(), calls=%async_computation.7 | async-start | bytes 9437184 | tf_op jit(solution)/shard_map/reduce_scatter | solution.py:383
  212.3 14.1 %collective-permute-start.14 = (bf16[256,1024]{1,0:T(8,128)(2,1)S(1)}, bf16[256,1024]{1,0:T(8,128)(2,1)S(1)}, u32[]{:S(2)}, u32[]{:S(2)}) collective-permute-start(bf16[256,1024]{1,0:T(8,128)(2,1)S(1)} %fusion.118), channel_id=1, source_target_pairs={{0,1},{1,0},{2,3},{3,2},{4,5},{5,4},{6,7},{7,6},{8,9},{9,8},{10,11... | collective-permute-start | bytes 1572872 | tf_op jit(solution)/shard_map/ppermute | solution.py:244
  233.6 7.6 %collective-permute-start.16 = (bf16[2,1024]{1,0:T(2,128)(2,1)S(1)}, bf16[2,1024]{1,0:T(2,128)(2,1)S(1)}, u32[]{:S(2)}, u32[]{:S(2)}) collective-permute-start(bf16[2,1024]{1,0:T(2,128)(2,1)S(1)} %get-tuple-element.293), channel_id=1, source_target_pairs={{1,0},{4,1},{5,4},{8,5},{9,8},{12,9},{13,12},{3,2},{6,3},{7,6},{10... | collective-permute-start | bytes 12296 | tf_op jit(solution)/shard_map/ppermute | solution.py:448
  234.9 6.4 collective-permute-start.15
  246.5 14.3 %collective-permute-start.17 = (bf16[256,1024]{1,0:T(8,128)(2,1)S(1)}, bf16[256,1024]{1,0:T(8,128)(2,1)S(1)}, u32[]{:S(2)}, u32[]{:S(2)}) collective-permute-start(bf16[256,1024]{1,0:T(8,128)(2,1)S(1)} %multiply_convert_fusion.10), channel_id=1, source_target_pairs={{0,1},{1,0},{2,3},{3,2},{4,5},{5,4},{6,7},{7,6},{8,9},{9,8},{10,11... | collective-permute-start | bytes 1572872 | tf_op jit(solution)/shard_map/ppermute | solution.py:244
  269.0 14.4 %collective-permute-start.18 = (bf16[256,1024]{1,0:T(8,128)(2,1)S(1)}, bf16[256,1024]{1,0:T(8,128)(2,1)S(1)}, u32[]{:S(2)}, u32[]{:S(2)}) collective-permute-start(bf16[256,1024]{1,0:T(8,128)(2,1)S(1)} %fusion.99), channel_id=1, source_target_pairs={{0,1},{1,0},{2,3},{3,2},{4,5},{5,4},{6,7},{7,6},{8,9},{9,8},{10,11... | collective-permute-start | bytes 1572872 | tf_op jit(solution)/shard_map/ppermute | solution.py:244
  286.0 13.5 %collective-permute-start.19 = (bf16[256,1024]{1,0:T(8,128)(2,1)S(1)}, bf16[256,1024]{1,0:T(8,128)(2,1)S(1)}, u32[]{:S(2)}, u32[]{:S(2)}) collective-permute-start(bf16[256,1024]{1,0:T(8,128)(2,1)S(1)} %multiply_convert_fusion.5), channel_id=1, source_target_pairs={{0,1},{1,0},{2,3},{3,2},{4,5},{5,4},{6,7},{7,6},{8,9},{9,8},{10,11... | collective-permute-start | bytes 1572872 | tf_op jit(solution)/shard_map/ppermute | solution.py:244
  303.6 18.3 %collective-permute-start.20 = (bf16[256,1024]{1,0:T(8,128)(2,1)}, bf16[256,1024]{1,0:T(8,128)(2,1)}, u32[]{:S(2)}, u32[]{:S(2)}) collective-permute-start(bf16[256,1024]{1,0:T(8,128)(2,1)} %fusion.110), channel_id=1, source_target_pairs={{0,1},{1,0},{2,3},{3,2},{4,5},{5,4},{6,7},{7,6},{8,9},{9,8},{10,11... | collective-permute-start | bytes 1572872 | tf_op jit(solution)/shard_map/ppermute | solution.py:244
  325.9 175.9 %reduce-scatter.7.cloned.1.call-start = ((), (), s32[]{:S(2)}) async-start(), calls=%async_computation.8 | async-start | bytes 7077888 | tf_op jit(solution)/shard_map/reduce_scatter | solution.py:383
  351.1 12.8 %collective-permute-start.23 = (bf16[256,1024]{1,0:T(8,128)(2,1)S(1)}, bf16[256,1024]{1,0:T(8,128)(2,1)}, u32[]{:S(2)}, u32[]{:S(2)}) collective-permute-start(bf16[256,1024]{1,0:T(8,128)(2,1)S(1)} %get-tuple-element.256), channel_id=1, source_target_pairs={{0,1},{1,0},{2,3},{3,2},{4,5},{5,4},{6,7},{7,6},{8,9},{9,8},{10,11... | collective-permute-start | bytes 1572872 | tf_op jit(solution)/shard_map/ppermute | solution.py:244
  385.5 24.1 %collective-permute-start.26 = (bf16[256,1024]{1,0:T(8,128)(2,1)S(1)}, bf16[256,1024]{1,0:T(8,128)(2,1)S(1)}, u32[]{:S(2)}, u32[]{:S(2)}) collective-permute-start(bf16[256,1024]{1,0:T(8,128)(2,1)S(1)} %fusion.201), channel_id=1, source_target_pairs={{0,1},{1,0},{2,3},{3,2},{4,5},{5,4},{6,7},{7,6},{8,9},{9,8},{10,11... | collective-permute-start | bytes 1572872 | tf_op jit(solution)/shard_map/ppermute | solution.py:244
  385.6 26.7 %collective-permute-start.27 = (bf16[256,1024]{1,0:T(8,128)(2,1)S(1)}, bf16[256,1024]{1,0:T(8,128)(2,1)}, u32[]{:S(2)}, u32[]{:S(2)}) collective-permute-start(bf16[256,1024]{1,0:T(8,128)(2,1)S(1)} %fusion.201), channel_id=1, source_target_pairs={{0,2},{1,3},{2,0},{3,1},{4,6},{5,7},{6,4},{7,5},{8,10},{9,11},{10,... | collective-permute-start | bytes 1572872 | tf_op jit(solution)/shard_map/ppermute | solution.py:244
  386.5 22.2 %collective-permute-start.25 = (bf16[1,512,512]{2,1,0:T(8,128)(2,1)S(1)}, bf16[1,512,512]{2,1,0:T(8,128)(2,1)S(1)}, u32[]{:S(2)}, u32[]{:S(2)}) collective-permute-start(bf16[1,512,512]{2,1,0:T(8,128)(2,1)S(1)} %slice.467), channel_id=1, source_target_pairs={{0,8},{4,12},{8,0},{12,4},{1,9},{5,13},{9,1},{13,5},{2,10},{6,14},... | collective-permute-start | bytes 1572872 | tf_op jit(solution)/shard_map/ppermute | solution.py:244
  418.4 14.3 %collective-permute-start.29 = (bf16[1,512,512]{2,1,0:T(8,128)(2,1)}, bf16[1,512,512]{2,1,0:T(8,128)(2,1)}, u32[]{:S(2)}, u32[]{:S(2)}) collective-permute-start(bf16[1,512,512]{2,1,0:T(8,128)(2,1)} %slice.470), channel_id=1, source_target_pairs={{0,8},{4,12},{8,0},{12,4},{1,9},{5,13},{9,1},{13,5},{2,10},{6,14},... | collective-permute-start | bytes 1572872 | tf_op jit(solution)/shard_map/ppermute | solution.py:244
  419.7 20.1 %collective-permute-start.31 = (bf16[256,1024]{1,0:T(8,128)(2,1)}, bf16[256,1024]{1,0:T(8,128)(2,1)}, u32[]{:S(2)}, u32[]{:S(2)}) collective-permute-start(bf16[256,1024]{1,0:T(8,128)(2,1)} %collective-permute-done.27), channel_id=1, source_target_pairs={{0,1},{1,0},{2,3},{3,2},{4,5},{5,4},{6,7},{7,6},{8,9},{9,8},{10,11... | collective-permute-start | bytes 1572872 | tf_op jit(solution)/shard_map/ppermute | solution.py:244
  422.9 16.8 %collective-permute-start.30 = (bf16[128,1024]{1,0:T(8,128)(2,1)S(1)}, bf16[128,1024]{1,0:T(8,128)(2,1)S(1)}, u32[]{:S(2)}, u32[]{:S(2)}) collective-permute-start(bf16[128,1024]{1,0:T(8,128)(2,1)S(1)} %slice.471), channel_id=1, source_target_pairs={{0,2},{1,3},{2,0},{3,1},{4,6},{5,7},{6,4},{7,5},{8,10},{9,11},{10,... | collective-permute-start | bytes 786440 | tf_op jit(solution)/shard_map/ppermute | solution.py:244
  439.8 123.9 %reduce-scatter.9.cloned.1.call-start = ((), (), s32[]{:S(2)}) async-start(), calls=%async_computation.9 | async-start | bytes 4718592 | tf_op jit(solution)/shard_map/reduce_scatter | solution.py:383
  447.1 16.8 %collective-permute-start.32 = (bf16[256,1024]{1,0:T(8,128)(2,1)}, bf16[256,1024]{1,0:T(8,128)(2,1)}, u32[]{:S(2)}, u32[]{:S(2)}) collective-permute-start(bf16[256,1024]{1,0:T(8,128)(2,1)} %fusion.96), channel_id=1, source_target_pairs={{0,1},{1,0},{2,3},{3,2},{4,5},{5,4},{6,7},{7,6},{8,9},{9,8},{10,11... | collective-permute-start | bytes 1572872 | tf_op jit(solution)/shard_map/ppermute | solution.py:244
  468.6 23.5 %collective-permute-start.33 = (bf16[256,1024]{1,0:T(8,128)(2,1)S(1)}, bf16[256,1024]{1,0:T(8,128)(2,1)S(1)}, u32[]{:S(2)}, u32[]{:S(2)}) collective-permute-start(bf16[256,1024]{1,0:T(8,128)(2,1)S(1)} %get-tuple-element.105), channel_id=1, source_target_pairs={{0,1},{1,0},{2,3},{3,2},{4,5},{5,4},{6,7},{7,6},{8,9},{9,8},{10,11... | collective-permute-start | bytes 1572872 | tf_op jit(solution)/shard_map/ppermute | solution.py:244
  468.6 23.5 %collective-permute-start.34 = (bf16[256,1024]{1,0:T(8,128)(2,1)S(1)}, bf16[256,1024]{1,0:T(8,128)(2,1)S(1)}, u32[]{:S(2)}, u32[]{:S(2)}) collective-permute-start(bf16[256,1024]{1,0:T(8,128)(2,1)S(1)} %get-tuple-element.105), channel_id=1, source_target_pairs={{0,2},{1,3},{2,0},{3,1},{4,6},{5,7},{6,4},{7,5},{8,10},{9,11},{10,... | collective-permute-start | bytes 1572872 | tf_op jit(solution)/shard_map/ppermute | solution.py:244
  492.1 18.5 %collective-permute-start.35 = (bf16[256,1024]{1,0:T(8,128)(2,1)S(1)}, bf16[256,1024]{1,0:T(8,128)(2,1)S(1)}, u32[]{:S(2)}, u32[]{:S(2)}) collective-permute-start(bf16[256,1024]{1,0:T(8,128)(2,1)S(1)} %collective-permute-done.34), channel_id=1, source_target_pairs={{0,1},{1,0},{2,3},{3,2},{4,5},{5,4},{6,7},{7,6},{8,9},{9,8},{10,11... | collective-permute-start | bytes 1572872 | tf_op jit(solution)/shard_map/ppermute | solution.py:244
  495.5 32.5 %collective-permute-start.38 = (bf16[128,1024]{1,0:T(8,128)(2,1)S(1)}, bf16[128,1024]{1,0:T(8,128)(2,1)}, u32[]{:S(2)}, u32[]{:S(2)}) collective-permute-start(bf16[128,1024]{1,0:T(8,128)(2,1)S(1)} %slice_add_fusion), channel_id=1, source_target_pairs={{0,2},{1,3},{2,0},{3,1},{4,6},{5,7},{6,4},{7,5},{8,10},{9,11},{10,... | collective-permute-start | bytes 786440 | tf_op jit(solution)/shard_map/ppermute | solution.py:244
  501.8 142.3 %reduce-scatter.11.cloned.1.call-start = ((), (), s32[]{:S(2)}) async-start(), calls=%async_computation.10 | async-start | bytes 4718592 | tf_op jit(solution)/shard_map/reduce_scatter | solution.py:383
  514.4 12.0 %collective-permute-start.37 = (bf16[256,1024]{1,0:T(8,128)(2,1)S(1)}, bf16[256,1024]{1,0:T(8,128)(2,1)S(1)}, u32[]{:S(2)}, u32[]{:S(2)}) collective-permute-start(bf16[256,1024]{1,0:T(8,128)(2,1)S(1)} %get-tuple-element.339), channel_id=1, source_target_pairs={{0,1},{1,0},{2,3},{3,2},{4,5},{5,4},{6,7},{7,6},{8,9},{9,8},{10,11... | collective-permute-start | bytes 1572872 | tf_op jit(solution)/shard_map/ppermute | solution.py:244
  528.0 27.1 %collective-permute-start.39 = (bf16[256,1024]{1,0:T(8,128)(2,1)}, bf16[256,1024]{1,0:T(8,128)(2,1)}, u32[]{:S(2)}, u32[]{:S(2)}) collective-permute-start(bf16[256,1024]{1,0:T(8,128)(2,1)} %add_convert_fusion.2), channel_id=1, source_target_pairs={{0,2},{1,3},{2,0},{3,1},{4,6},{5,7},{6,4},{7,5},{8,10},{9,11},{10,... | collective-permute-start | bytes 1572872 | tf_op jit(solution)/shard_map/ppermute | solution.py:244
  529.8 23.3 %collective-permute-start.40 = (bf16[2,32,3072]{2,1,0:T(8,128)(2,1)}, bf16[2,32,3072]{2,1,0:T(8,128)(2,1)S(1)}, u32[]{:S(2)}, u32[]{:S(2)}) collective-permute-start(bf16[2,32,3072]{2,1,0:T(8,128)(2,1)} %dynamic-slice_bitcast_fusion), channel_id=1, source_target_pairs={{0,1},{1,0},{2,3},{3,2},{4,5},{5,4},{6,7},{7,6},{8,9},{9,8},{10,11... | collective-permute-start | bytes 1179656 | tf_op jit(solution)/shard_map/ppermute | solution.py:244
  532.8 27.9 %collective-permute-start.36 = (bf16[256,1024]{1,0:T(8,128)(2,1)}, bf16[256,1024]{1,0:T(8,128)(2,1)}, u32[]{:S(2)}, u32[]{:S(2)}) collective-permute-start(bf16[256,1024]{1,0:T(8,128)(2,1)} %fusion.115), channel_id=1, source_target_pairs={{0,1},{1,0},{2,3},{3,2},{4,5},{5,4},{6,7},{7,6},{8,9},{9,8},{10,11... | collective-permute-start | bytes 1572872 | tf_op jit(solution)/shard_map/ppermute | solution.py:244
  567.5 21.0 %collective-permute-start.41 = (bf16[256,1024]{1,0:T(8,128)(2,1)}, bf16[256,1024]{1,0:T(8,128)(2,1)}, u32[]{:S(2)}, u32[]{:S(2)}) collective-permute-start(bf16[256,1024]{1,0:T(8,128)(2,1)} %fusion.132), channel_id=1, source_target_pairs={{0,1},{1,0},{2,3},{3,2},{4,5},{5,4},{6,7},{7,6},{8,9},{9,8},{10,11... | collective-permute-start | bytes 1572872 | tf_op jit(solution)/shard_map/ppermute | solution.py:244
  567.5 22.6 %collective-permute-start.42 = (bf16[256,1024]{1,0:T(8,128)(2,1)}, bf16[256,1024]{1,0:T(8,128)(2,1)S(1)}, u32[]{:S(2)}, u32[]{:S(2)}) collective-permute-start(bf16[256,1024]{1,0:T(8,128)(2,1)} %fusion.132), channel_id=1, source_target_pairs={{0,2},{1,3},{2,0},{3,1},{4,6},{5,7},{6,4},{7,5},{8,10},{9,11},{10,... | collective-permute-start | bytes 1572872 | tf_op jit(solution)/shard_map/ppermute | solution.py:244
  597.9 12.0 %collective-permute-start.50 = (bf16[32,3072]{1,0:T(8,128)(2,1)S(1)}, bf16[32,3072]{1,0:T(8,128)(2,1)S(1)}, u32[]{:S(2)}, u32[]{:S(2)}) collective-permute-start(bf16[32,3072]{1,0:T(8,128)(2,1)S(1)} %fusion.222), channel_id=1, source_target_pairs={{0,2},{1,3},{2,0},{3,1},{4,6},{5,7},{6,4},{7,5},{8,10},{9,11},{10,... | collective-permute-start | bytes 589832 | tf_op jit(solution)/shard_map/ppermute | solution.py:244
  600.5 18.1 %collective-permute-start.43 = (bf16[256,1024]{1,0:T(8,128)(2,1)S(1)}, bf16[256,1024]{1,0:T(8,128)(2,1)S(1)}, u32[]{:S(2)}, u32[]{:S(2)}) collective-permute-start(bf16[256,1024]{1,0:T(8,128)(2,1)S(1)} %collective-permute-done.42), channel_id=1, source_target_pairs={{0,1},{1,0},{2,3},{3,2},{4,5},{5,4},{6,7},{7,6},{8,9},{9,8},{10,11... | collective-permute-start | bytes 1572872 | tf_op jit(solution)/shard_map/ppermute | solution.py:244
  618.9 13.5 %collective-permute-start.47 = (bf16[128,1024]{1,0:T(8,128)(2,1)S(1)}, bf16[128,1024]{1,0:T(8,128)(2,1)S(1)}, u32[]{:S(2)}, u32[]{:S(2)}) collective-permute-start(bf16[128,1024]{1,0:T(8,128)(2,1)S(1)} %pad_maximum_fusion.24), channel_id=1, source_target_pairs={{0,2},{1,3},{2,0},{3,1},{4,6},{5,7},{6,4},{7,5},{8,10},{9,11},{10,... | collective-permute-start | bytes 786440 | tf_op jit(solution)/shard_map/ppermute | solution.py:244
  (152 other events, 904.1 us)
Sparse Core Ops, SparseCore 0:
  47.0 28.2 all-gather.3
  118.8 54.3 all-gather.5
  210.6 39.7 all-gather.7
  326.0 74.8 reduce-scatter.4
  439.9 61.8 reduce-scatter.6
  505.6 51.1 reduce-scatter.8
  563.9 49.6 reduce-scatter.10

commit v7 on v4

--- a/solution.py
+++ b/solution.py
@@ -3,6 +3,7 @@
 import jax.numpy as jnp
 from jax import lax
 from jax.experimental import pallas as pl
+from jax.experimental.layout import Layout, with_layout_constraint
 from jax.experimental.pallas import tpu as pltpu
 from jax.sharding import PartitionSpec as P
 
@@ -383,7 +384,8 @@
 
 
 def grad_of(left, right):
-    return outer(left, right).astype(jnp.bfloat16)
+    grads = outer(left, right).astype(jnp.bfloat16)
+    return with_layout_constraint(grads, Layout(major_to_minor=(0, 1)))
 
 
 def ffn_forward(low_own, weights):

time: 634 us -> 628 us (level)
  local copies, waits for them, and re-layouts: 67.1 us -> 57.4 us
    unnamed x283 -> x311, local copies, waits for them, and re-layouts: 25.1 us -> 18.1 us
  transfers between devices with their start and end apart: 58 -> 58, of which waited for: 28 -> 30; matrix products, arithmetic and copies ran while one was open for 34% -> 34% of each run, Pallas kernels for 10% -> 10%
where the time goes in v7:
time: 628 us; the launch traced here: 617 us
  waiting for transfers between devices  194 us (31%)
  matrix products  103 us (16%)
  other arithmetic  91.7 us (15%)
  starting transfers between devices  73.2 us (12%)
  Pallas kernels  62 us (10%)
  local copies, waits for them, and re-layouts  57.4 us (9%)
  between operations  36.5 us (6%)
    ppermute x47, waiting for transfers between devices, swap(): return lax.ppermute(array, axis, [(i, i ^ 1 << bit) for i in range(count)])  181 us
    ppermute x47, starting transfers between devices, swap(): return lax.ppermute(array, axis, [(i, i ^ 1 << bit) for i in range(count)])  60.8 us
    dot_general x25, matrix products, plain(): return jnp.dot(left, right, preferred_element_type=jnp.float32)  46.9 us
    dot_general x25, matrix products, against(): lax.dot_general(left, right, (((1,), (1,)), ((), ())), preferred_element_...  34.7 us
    pallas_call x2, Pallas kernels, attend_back(): pl.pallas_call(fn, grid_spec=pltpu.PrefetchScalarGridSpec(num_scalar_pref...  25.6 us
    pallas_call x2, Pallas kernels, attend(): pl.pallas_call(fn, grid_spec=pltpu.PrefetchScalarGridSpec(num_scalar_pref...  21.6 us
    dot_general x8, matrix products, outer(): lax.dot_general(left, right, (((0,), (0,)), ((), ())), preferred_element_...  19.9 us
    unnamed x311, local copies, waits for them, and re-layouts  18.1 us
  transfers between devices with their start and end apart: 58, of which 30 were waited for; matrix products, arithmetic and copies ran while one was open for 34% of the time, Pallas kernels for 10%

profile of v7, /device:TPU:0, one launch (start us, length us, event | category | flops | bytes accessed | tf_op | source)
XLA Modules:
  0.0 617.4 jit_solution(12732488466702393)
XLA Ops:
  16.8 3.1 collective-permute-start
  29.7 3.0 multiply_convert_fusion.15
  36.4 3.0 multiply_convert_fusion.18
  40.2 3.6 fusion.260
  52.1 3.8 add_add_fusion
  57.7 7.4 %collective-permute-done.14 = bf16[64,3200]{1,0:T(8,128)(2,1)} collective-permute-done((bf16[64,3200]{1,0:T(8,128)(2,1)S(1)}, bf16[64,3200]{1,0:T(8,128)(2,1)}, u32[]{:S(2)}, u32[]{:S(2)}) %collective-permute-start.14) | collective-permute-done | bytes 409632 | tf_op jit(solution)/shard_map/ppermute | solution.py:244
  82.3 3.4 shard_map.365.refs_1_
  85.7 3.5 shard_map.366.refs_1_
  89.2 14.0 %collective-permute-done.1 = bf16[256,1024]{1,0:T(8,128)(2,1)S(1)} collective-permute-done((bf16[256,1024]{1,0:T(8,128)(2,1)}, bf16[256,1024]{1,0:T(8,128)(2,1)S(1)}, u32[]{:S(2)}, u32[]{:S(2)}) %collective-permute-start.1) | collective-permute-done | bytes 524320 | tf_op jit(solution)/shard_map/ppermute | solution.py:244
  107.4 13.5 %collective-permute-done.4 = bf16[256,1024]{1,0:T(8,128)(2,1)} collective-permute-done((bf16[256,1024]{1,0:T(8,128)(2,1)}, bf16[256,1024]{1,0:T(8,128)(2,1)}, u32[]{:S(2)}, u32[]{:S(2)}) %collective-permute-start.4) | collective-permute-done | bytes 524320 | tf_op jit(solution)/shard_map/ppermute | solution.py:244
  128.9 6.8 %collective-permute-done.5.refs_5_.refs_8_ = bf16[1,512,512]{2,1,0:T(8,128)(2,1)} collective-permute-done((bf16[1,512,512]{2,1,0:T(8,128)(2,1)S(1)}, bf16[1,512,512]{2,1,0:T(8,128)(2,1)}, u32[]{:S(2)}, u32[]{:S(2)}) %collective-permute-start.5) | collective-permute-done | bytes 524320 | tf_op jit(solution)/shard_map/ppermute | solution.py:244
  146.7 10.8 %shard_map.367 = (bf16[512,256]{1,0:T(8,128)(2,1)}, f32[2,1,512]{2,1,0:T(1,128)}) custom-call(s32[5]{0:T(128)} %pad_add_fusion.1.scal, bf16[512,256]{1,0:T(8,128)(2,1)} %convolution_convert_fusion.11.refs_0_, f32[2,9,256,256]{3,2,1,0:T(8,128)} %shard_map.365.refs_1_, s32[1,512]{1,0:T(1,128)} %get-tuple-element.261.refs_2_, s32[2048,1]{1,0:T(8,128)} %copy.88.refs_3_, ...), custom_call_target="tpu_custom_call" | custom-call | flops 1073741824 | bytes 4718592 | tf_op jit(solution)/shard_map/pallas_call | solution.py:132
  163.1 3.1 collective-permute-start.11
  168.4 10.8 %shard_map.368 = (bf16[512,256]{1,0:T(8,128)(2,1)}, f32[2,1,512]{2,1,0:T(1,128)}) custom-call(s32[5]{0:T(128)} %pad_add_fusion.1.scal, bf16[512,256]{1,0:T(8,128)(2,1)} %convolution_convert_fusion.10.refs_0_, f32[2,9,256,256]{3,2,1,0:T(8,128)} %shard_map.366.refs_1_, s32[1,512]{1,0:T(1,128)} %get-tuple-element.261.refs_2_, s32[2048,1]{1,0:T(8,128)} %copy.88.refs_3_, ...), custom_call_target="tpu_custom_call" | custom-call | flops 1073741824 | bytes 4718592 | tf_op jit(solution)/shard_map/pallas_call | solution.py:132
  185.1 12.0 %collective-permute-done.12 = bf16[256,1024]{1,0:T(8,128)(2,1)S(1)} collective-permute-done((bf16[256,1024]{1,0:T(8,128)(2,1)S(1)}, bf16[256,1024]{1,0:T(8,128)(2,1)S(1)}, u32[]{:S(2)}, u32[]{:S(2)}) %collective-permute-start.12) | collective-permute-done | bytes 524320 | tf_op jit(solution)/shard_map/ppermute | solution.py:244
  200.2 3.9 fusion.2
  205.7 5.0 collective-permute-start.15
  221.0 10.4 %collective-permute-done.17 = bf16[256,1024]{1,0:T(8,128)(2,1)S(1)} collective-permute-done((bf16[256,1024]{1,0:T(8,128)(2,1)S(1)}, bf16[256,1024]{1,0:T(8,128)(2,1)S(1)}, u32[]{:S(2)}, u32[]{:S(2)}) %collective-permute-start.17) | collective-permute-done | bytes 524320 | tf_op jit(solution)/shard_map/ppermute | solution.py:244
  242.1 10.8 %collective-permute-done.18 = bf16[256,1024]{1,0:T(8,128)(2,1)S(1)} collective-permute-done((bf16[256,1024]{1,0:T(8,128)(2,1)S(1)}, bf16[256,1024]{1,0:T(8,128)(2,1)S(1)}, u32[]{:S(2)}, u32[]{:S(2)}) %collective-permute-start.18) | collective-permute-done | bytes 524320 | tf_op jit(solution)/shard_map/ppermute | solution.py:244
  260.3 7.6 %collective-permute-done.19 = bf16[256,1024]{1,0:T(8,128)(2,1)S(1)} collective-permute-done((bf16[256,1024]{1,0:T(8,128)(2,1)S(1)}, bf16[256,1024]{1,0:T(8,128)(2,1)S(1)}, u32[]{:S(2)}, u32[]{:S(2)}) %collective-permute-start.19) | collective-permute-done | bytes 524320 | tf_op jit(solution)/shard_map/ppermute | solution.py:244
  272.4 4.3 convolution_convert_fusion.3
  276.7 4.4 convolution_convert_fusion.2
  281.2 7.9 %pad_maximum_fusion = bf16[1024,4096]{1,0:T(8,128)(2,1)} fusion(bf16[1024,2048]{1,0:T(8,128)(2,1)} %convolution_convert_fusion.2, bf16[1024,2048]{1,0:T(8,128)(2,1)} %convolution_convert_fusion.3), kind=kLoop, calls=%fused_computation | loop fusion | flops 16777216 | bytes 16777216 | tf_op jit(solution)/shard_map/concatenate | solution.py:419
  289.1 3.9 convert_add_fusion.2
  297.5 3.5 multiply_reduce_fusion
  303.5 3.6 collective-permute-start.22
  321.7 4.7 pad_maximum_fusion.1
  326.5 5.9 collective-permute-done.23
  335.4 12.8 %shard_map.369 = (bf16[512,256]{1,0:T(8,128)(2,1)S(1)}, bf16[4,512,512]{2,1,0:T(8,128)(2,1)}, f32[2,9,256,256]{3,2,1,0:T(8,128)}) custom-call(s32[5]{0:T(128)S(1)} %copy-done.13, bf16[512,256]{1,0:T(8,128)(2,1)S(1)} %copy-done.11, f32[2,9,256,256]{3,2,1,0:T(8,128)} %shard_map.365.refs_1_, s32[1,512]{1,0:T(1,128)S(1)} %copy-done.12, s32[2048,1]{1,0:T(8,128)S(1)} %copy-done.1, ...), custom_call_target="tpu_custom_call" | custom-call | flops 2684354560 | bytes 9437184 | tf_op jit(solution)/shard_map/pallas_call | solution.py:210
  352.6 3.5 collective-permute-start.27
  360.0 12.8 %shard_map.370 = (bf16[512,256]{1,0:T(8,128)(2,1)S(1)}, bf16[4,512,512]{2,1,0:T(8,128)(2,1)}, f32[2,9,256,256]{3,2,1,0:T(8,128)}) custom-call(s32[5]{0:T(128)S(1)} %broadcast_add_fusion.4.scal, bf16[512,256]{1,0:T(8,128)(2,1)S(1)} %copy-done.10, f32[2,9,256,256]{3,2,1,0:T(8,128)} %shard_map.366.refs_1_, s32[1,512]{1,0:T(1,128)S(1)} %copy-done.12, ...), custom_call_target="tpu_custom_call" | custom-call | flops 2684354560 | bytes 9437184 | tf_op jit(solution)/shard_map/pallas_call | solution.py:210
  372.8 3.6 collective-permute-done.25
  391.3 7.1 %collective-permute-done.29 = bf16[1,512,512]{2,1,0:T(8,128)(2,1)} collective-permute-done((bf16[1,512,512]{2,1,0:T(8,128)(2,1)}, bf16[1,512,512]{2,1,0:T(8,128)(2,1)}, u32[]{:S(2)}, u32[]{:S(2)}) %collective-permute-start.29) | collective-permute-done | bytes 524320 | tf_op jit(solution)/shard_map/ppermute | solution.py:244
  401.4 4.2 collective-permute-done.31
  438.5 14.2 %collective-permute-done.33 = bf16[256,1024]{1,0:T(8,128)(2,1)S(1)} collective-permute-done((bf16[256,1024]{1,0:T(8,128)(2,1)S(1)}, bf16[256,1024]{1,0:T(8,128)(2,1)S(1)}, u32[]{:S(2)}, u32[]{:S(2)}) %collective-permute-start.33) | collective-permute-done | bytes 524320 | tf_op jit(solution)/shard_map/ppermute | solution.py:244
  452.7 3.5 collective-permute-done.34
  461.7 10.5 %reduce-scatter.7.cloned.1.call-done = bf16[128,3072]{1,0:T(8,128)(2,1)} async-done(((bf16[1024,3072]{1,0:T(8,128)(2,1)}), bf16[128,3072]{1,0:T(8,128)(2,1)}) %reduce-scatter.7.cloned.1.call-update) | async-done | bytes 786448 | tf_op jit(solution)/shard_map/reduce_scatter | solution.py:383
  481.3 8.4 %collective-permute-done.37 = bf16[256,1024]{1,0:T(8,128)(2,1)S(1)} collective-permute-done((bf16[256,1024]{1,0:T(8,128)(2,1)S(1)}, bf16[256,1024]{1,0:T(8,128)(2,1)S(1)}, u32[]{:S(2)}, u32[]{:S(2)}) %collective-permute-start.37) | collective-permute-done | bytes 524320 | tf_op jit(solution)/shard_map/ppermute | solution.py:244
  507.6 10.3 %collective-permute-done.40 = bf16[2,32,3072]{2,1,0:T(8,128)(2,1)S(1)} collective-permute-done((bf16[2,32,3072]{2,1,0:T(8,128)(2,1)}, bf16[2,32,3072]{2,1,0:T(8,128)(2,1)S(1)}, u32[]{:S(2)}, u32[]{:S(2)}) %collective-permute-start.40) | collective-permute-done | bytes 393248 | tf_op jit(solution)/shard_map/ppermute | solution.py:244
  519.9 6.9 %collective-permute-done.36 = bf16[256,1024]{1,0:T(8,128)(2,1)} collective-permute-done((bf16[256,1024]{1,0:T(8,128)(2,1)}, bf16[256,1024]{1,0:T(8,128)(2,1)}, u32[]{:S(2)}, u32[]{:S(2)}) %collective-permute-start.36) | collective-permute-done | bytes 524320 | tf_op jit(solution)/shard_map/ppermute | solution.py:244
  526.8 3.0 fusion.125
  541.8 4.0 shard_map.371
  546.0 3.8 shard_map.372
  552.0 4.5 collective-permute-done.41
  566.0 8.6 %collective-permute-done.45 = f32[90,128]{1,0:T(8,128)S(1)} collective-permute-done((f32[90,128]{1,0:T(8,128)S(1)}, f32[90,128]{1,0:T(8,128)S(1)}, u32[]{:S(2)}, u32[]{:S(2)}) %collective-permute-start.45) | collective-permute-done | bytes 46112 | tf_op jit(solution)/shard_map/ppermute | solution.py:244
  574.8 3.5 collective-permute-start.50
  589.9 3.1 collective-permute-start.49
  595.8 8.8 %collective-permute-done.49 = bf16[128,1024]{1,0:T(8,128)(2,1)S(1)} collective-permute-done((bf16[128,1024]{1,0:T(8,128)(2,1)S(1)}, bf16[128,1024]{1,0:T(8,128)(2,1)S(1)}, u32[]{:S(2)}, u32[]{:S(2)}) %collective-permute-start.49) | collective-permute-done | bytes 262176 | tf_op jit(solution)/shard_map/ppermute | solution.py:244
  (643 shorter events, 266.1 us)
Async XLA Ops:
  7.2 117.6 %all-gather.4.cloned.1.call-start = ((), (), s32[]{:S(2)}) async-start(), calls=%async_computation.4 | async-start | bytes 2359296 | tf_op jit(solution)/shard_map/all_gather | solution.py:252
  16.8 35.3 %collective-permute-start = (bf16[256,1024]{1,0:T(8,128)(2,1)}, bf16[256,1024]{1,0:T(8,128)(2,1)}, u32[]{:S(2)}, u32[]{:S(2)}) collective-permute-start(bf16[256,1024]{1,0:T(8,128)(2,1)} %get-tuple-element.315), channel_id=1, source_target_pairs={{0,1},{1,0},{2,3},{3,2},{4,5},{5,4},{6,7},{7,6},{8,9},{9,8},{10,11... | collective-permute-start | bytes 1572872 | tf_op jit(solution)/shard_map/ppermute | solution.py:244
  25.0 14.4 %collective-permute-start.6 = (bf16[128,1024]{0,1:T(8,128)(2,1)}, bf16[128,1024]{0,1:T(8,128)(2,1)S(1)}, u32[]{:S(2)}, u32[]{:S(2)}) collective-permute-start(bf16[128,1024]{0,1:T(8,128)(2,1)} %pad_maximum_fusion.20), channel_id=1, source_target_pairs={{0,2},{1,3},{2,0},{3,1},{4,6},{5,7},{6,4},{7,5},{8,10},{9,11},{10,... | collective-permute-start | bytes 786440 | tf_op jit(solution)/shard_map/ppermute | solution.py:244
  29.2 14.6 %collective-permute-start.13 = (bf16[32,3200]{1,0:T(8,128)(2,1)}, bf16[32,3200]{1,0:T(8,128)(2,1)}, u32[]{:S(2)}, u32[]{:S(2)}) collective-permute-start(bf16[32,3200]{1,0:T(8,128)(2,1)} %fusion.210), channel_id=1, source_target_pairs={{0,1},{1,0},{2,3},{3,2},{4,5},{5,4},{6,7},{7,6},{8,9},{9,8},{10,11... | collective-permute-start | bytes 614408 | tf_op jit(solution)/shard_map/ppermute | solution.py:244
  40.1 158.8 %all-gather.6.cloned.1.call-start = ((), (), s32[]{:S(2)}) async-start(), calls=%async_computation.5 | async-start | bytes 7372800 | tf_op jit(solution)/shard_map/all_gather | solution.py:252
  44.9 20.2 %collective-permute-start.14 = (bf16[64,3200]{1,0:T(8,128)(2,1)S(1)}, bf16[64,3200]{1,0:T(8,128)(2,1)}, u32[]{:S(2)}, u32[]{:S(2)}) collective-permute-start(bf16[64,3200]{1,0:T(8,128)(2,1)S(1)} %maximum_add_fusion.11), channel_id=1, source_target_pairs={{0,2},{1,3},{2,0},{3,1},{4,6},{5,7},{6,4},{7,5},{8,10},{9,11},{10,... | collective-permute-start | bytes 1228808 | tf_op jit(solution)/shard_map/ppermute | solution.py:244
  67.3 168.3 %all-gather.8.cloned.1.call-start = ((), (), s32[]{:S(2)}) async-start(), calls=%async_computation.6 | async-start | bytes 4718592 | tf_op jit(solution)/shard_map/all_gather | solution.py:252
  67.5 13.3 %collective-permute-start.2 = (f32[2,32]{1,0:T(2,128)}, f32[2,32]{1,0:T(2,128)S(1)}, u32[]{:S(2)}, u32[]{:S(2)}) collective-permute-start(f32[2,32]{1,0:T(2,128)} %param.33), channel_id=1, source_target_pairs={{0,2},{1,3},{2,0},{3,1},{4,6},{5,7},{6,4},{7,5},{8,10},{9,11},{10,... | collective-permute-start | bytes 776 | tf_op jit(solution)/shard_map/ppermute | solution.py:244
  67.6 36.4 %collective-permute-start.3 = (bf16[256,1024]{1,0:T(8,128)(2,1)}, bf16[256,1024]{1,0:T(8,128)(2,1)}, u32[]{:S(2)}, u32[]{:S(2)}) collective-permute-start(bf16[256,1024]{1,0:T(8,128)(2,1)} %get-tuple-element.318), channel_id=1, source_target_pairs={{0,1},{1,0},{2,3},{3,2},{4,5},{5,4},{6,7},{7,6},{8,9},{9,8},{10,11... | collective-permute-start | bytes 1572872 | tf_op jit(solution)/shard_map/ppermute | solution.py:244
  77.7 25.5 %collective-permute-start.1 = (bf16[256,1024]{1,0:T(8,128)(2,1)}, bf16[256,1024]{1,0:T(8,128)(2,1)S(1)}, u32[]{:S(2)}, u32[]{:S(2)}) collective-permute-start(bf16[256,1024]{1,0:T(8,128)(2,1)} %get-tuple-element.262), channel_id=1, source_target_pairs={{0,2},{1,3},{2,0},{3,1},{4,6},{5,7},{6,4},{7,5},{8,10},{9,11},{10,... | collective-permute-start | bytes 1572872 | tf_op jit(solution)/shard_map/ppermute | solution.py:244
  107.4 13.5 %collective-permute-start.4 = (bf16[256,1024]{1,0:T(8,128)(2,1)}, bf16[256,1024]{1,0:T(8,128)(2,1)}, u32[]{:S(2)}, u32[]{:S(2)}) collective-permute-start(bf16[256,1024]{1,0:T(8,128)(2,1)} %multiply_convert_fusion.14), channel_id=1, source_target_pairs={{0,1},{1,0},{2,3},{3,2},{4,5},{5,4},{6,7},{7,6},{8,9},{9,8},{10,11... | collective-permute-start | bytes 1572872 | tf_op jit(solution)/shard_map/ppermute | solution.py:244
  123.3 12.4 %collective-permute-start.5 = (bf16[1,512,512]{2,1,0:T(8,128)(2,1)S(1)}, bf16[1,512,512]{2,1,0:T(8,128)(2,1)}, u32[]{:S(2)}, u32[]{:S(2)}) collective-permute-start(bf16[1,512,512]{2,1,0:T(8,128)(2,1)S(1)} %fusion.117.refs_4_.refs_7_), channel_id=1, source_target_pairs={{0,8},{4,12},{8,0},{12,4},{1,9},{5,13},{9,1},{13,5},{2,10},{6,14},... | collective-permute-start | bytes 1572872 | tf_op jit(solution)/shard_map/ppermute | solution.py:244
  137.8 8.9 %collective-permute-start.7 = (bf16[2,512,512]{2,1,0:T(8,128)(2,1)}, bf16[2,512,512]{2,1,0:T(8,128)(2,1)}, u32[]{:S(2)}, u32[]{:S(2)}) collective-permute-start(bf16[2,512,512]{2,1,0:T(8,128)(2,1)} %maximum_add_fusion.8), channel_id=1, source_target_pairs={{0,4},{4,0},{8,12},{12,8},{1,5},{5,1},{9,13},{13,9},{2,6},{6,2},{1... | collective-permute-start | bytes 3145736 | tf_op jit(solution)/shard_map/ppermute | solution.py:244
  137.8 23.9 %collective-permute-start.9 = (bf16[1,512,512]{2,1,0:T(8,128)(2,1)S(1)}, bf16[1,512,512]{2,1,0:T(8,128)(2,1)S(1)}, u32[]{:S(2)}, u32[]{:S(2)}) collective-permute-start(bf16[1,512,512]{2,1,0:T(8,128)(2,1)S(1)} %fusion.118.refs_4_.refs_7_), channel_id=1, source_target_pairs={{0,8},{4,12},{8,0},{12,4},{1,9},{5,13},{9,1},{13,5},{2,10},{6,14},... | collective-permute-start | bytes 1572872 | tf_op jit(solution)/shard_map/ppermute | solution.py:244
  144.2 15.1 %collective-permute-start.8 = (bf16[128,1024]{1,0:T(8,128)(2,1)S(1)}, bf16[128,1024]{1,0:T(8,128)(2,1)}, u32[]{:S(2)}, u32[]{:S(2)}) collective-permute-start(bf16[128,1024]{1,0:T(8,128)(2,1)S(1)} %constant_dynamic-slice_fusion.3), channel_id=1, source_target_pairs={{0,2},{1,3},{2,0},{3,1},{4,6},{5,7},{6,4},{7,5},{8,10},{9,11},{10,... | collective-permute-start | bytes 786440 | tf_op jit(solution)/shard_map/ppermute | solution.py:244
  163.1 16.2 %collective-permute-start.11 = (bf16[128,1024]{1,0:T(8,128)(2,1)S(1)}, bf16[128,1024]{1,0:T(8,128)(2,1)S(1)}, u32[]{:S(2)}, u32[]{:S(2)}) collective-permute-start(bf16[128,1024]{1,0:T(8,128)(2,1)S(1)} %constant_dynamic-slice_fusion.2), channel_id=1, source_target_pairs={{0,2},{1,3},{2,0},{3,1},{4,6},{5,7},{6,4},{7,5},{8,10},{9,11},{10,... | collective-permute-start | bytes 786440 | tf_op jit(solution)/shard_map/ppermute | solution.py:244
  181.2 206.3 %reduce-scatter.5.cloned.1.call-start = ((), (), s32[]{:S(2)}) async-start(), calls=%async_computation.7 | async-start | bytes 9437184 | tf_op jit(solution)/shard_map/reduce_scatter | solution.py:383
  183.0 14.1 %collective-permute-start.12 = (bf16[256,1024]{1,0:T(8,128)(2,1)S(1)}, bf16[256,1024]{1,0:T(8,128)(2,1)S(1)}, u32[]{:S(2)}, u32[]{:S(2)}) collective-permute-start(bf16[256,1024]{1,0:T(8,128)(2,1)S(1)} %fusion.110), channel_id=1, source_target_pairs={{0,1},{1,0},{2,3},{3,2},{4,5},{5,4},{6,7},{7,6},{8,9},{9,8},{10,11... | collective-permute-start | bytes 1572872 | tf_op jit(solution)/shard_map/ppermute | solution.py:244
  204.4 7.6 %collective-permute-start.16 = (bf16[2,1024]{1,0:T(2,128)(2,1)S(1)}, bf16[2,1024]{1,0:T(2,128)(2,1)S(1)}, u32[]{:S(2)}, u32[]{:S(2)}) collective-permute-start(bf16[2,1024]{1,0:T(2,128)(2,1)S(1)} %get-tuple-element.289), channel_id=1, source_target_pairs={{1,0},{4,1},{5,4},{8,5},{9,8},{12,9},{13,12},{3,2},{6,3},{7,6},{10... | collective-permute-start | bytes 12296 | tf_op jit(solution)/shard_map/ppermute | solution.py:448
  217.3 14.1 %collective-permute-start.17 = (bf16[256,1024]{1,0:T(8,128)(2,1)S(1)}, bf16[256,1024]{1,0:T(8,128)(2,1)S(1)}, u32[]{:S(2)}, u32[]{:S(2)}) collective-permute-start(bf16[256,1024]{1,0:T(8,128)(2,1)S(1)} %multiply_convert_fusion.10), channel_id=1, source_target_pairs={{0,1},{1,0},{2,3},{3,2},{4,5},{5,4},{6,7},{7,6},{8,9},{9,8},{10,11... | collective-permute-start | bytes 1572872 | tf_op jit(solution)/shard_map/ppermute | solution.py:244
  239.6 13.2 %collective-permute-start.18 = (bf16[256,1024]{1,0:T(8,128)(2,1)S(1)}, bf16[256,1024]{1,0:T(8,128)(2,1)S(1)}, u32[]{:S(2)}, u32[]{:S(2)}) collective-permute-start(bf16[256,1024]{1,0:T(8,128)(2,1)S(1)} %fusion.91), channel_id=1, source_target_pairs={{0,1},{1,0},{2,3},{3,2},{4,5},{5,4},{6,7},{7,6},{8,9},{9,8},{10,11... | collective-permute-start | bytes 1572872 | tf_op jit(solution)/shard_map/ppermute | solution.py:244
  255.5 12.4 %collective-permute-start.19 = (bf16[256,1024]{1,0:T(8,128)(2,1)S(1)}, bf16[256,1024]{1,0:T(8,128)(2,1)S(1)}, u32[]{:S(2)}, u32[]{:S(2)}) collective-permute-start(bf16[256,1024]{1,0:T(8,128)(2,1)S(1)} %multiply_convert_fusion.5), channel_id=1, source_target_pairs={{0,1},{1,0},{2,3},{3,2},{4,5},{5,4},{6,7},{7,6},{8,9},{9,8},{10,11... | collective-permute-start | bytes 1572872 | tf_op jit(solution)/shard_map/ppermute | solution.py:244
  272.1 17.0 %collective-permute-start.20 = (bf16[256,1024]{1,0:T(8,128)(2,1)}, bf16[256,1024]{1,0:T(8,128)(2,1)}, u32[]{:S(2)}, u32[]{:S(2)}) collective-permute-start(bf16[256,1024]{1,0:T(8,128)(2,1)} %fusion.102), channel_id=1, source_target_pairs={{0,1},{1,0},{2,3},{3,2},{4,5},{5,4},{6,7},{7,6},{8,9},{9,8},{10,11... | collective-permute-start | bytes 1572872 | tf_op jit(solution)/shard_map/ppermute | solution.py:244
  293.0 179.2 %reduce-scatter.7.cloned.1.call-start = ((), (), s32[]{:S(2)}) async-start(), calls=%async_computation.8 | async-start | bytes 7077888 | tf_op jit(solution)/shard_map/reduce_scatter | solution.py:383
  319.5 12.8 %collective-permute-start.23 = (bf16[256,1024]{1,0:T(8,128)(2,1)S(1)}, bf16[256,1024]{1,0:T(8,128)(2,1)}, u32[]{:S(2)}, u32[]{:S(2)}) collective-permute-start(bf16[256,1024]{1,0:T(8,128)(2,1)S(1)} %get-tuple-element.250), channel_id=1, source_target_pairs={{0,1},{1,0},{2,3},{3,2},{4,5},{5,4},{6,7},{7,6},{8,9},{9,8},{10,11... | collective-permute-start | bytes 1572872 | tf_op jit(solution)/shard_map/ppermute | solution.py:244
  351.8 25.6 %collective-permute-start.26 = (bf16[256,1024]{1,0:T(8,128)(2,1)S(1)}, bf16[256,1024]{1,0:T(8,128)(2,1)S(1)}, u32[]{:S(2)}, u32[]{:S(2)}) collective-permute-start(bf16[256,1024]{1,0:T(8,128)(2,1)S(1)} %fusion.189), channel_id=1, source_target_pairs={{0,1},{1,0},{2,3},{3,2},{4,5},{5,4},{6,7},{7,6},{8,9},{9,8},{10,11... | collective-permute-start | bytes 1572872 | tf_op jit(solution)/shard_map/ppermute | solution.py:244
  352.6 24.8 %collective-permute-start.27 = (bf16[256,1024]{1,0:T(8,128)(2,1)S(1)}, bf16[256,1024]{1,0:T(8,128)(2,1)}, u32[]{:S(2)}, u32[]{:S(2)}) collective-permute-start(bf16[256,1024]{1,0:T(8,128)(2,1)S(1)} %fusion.189), channel_id=1, source_target_pairs={{0,2},{1,3},{2,0},{3,1},{4,6},{5,7},{6,4},{7,5},{8,10},{9,11},{10,... | collective-permute-start | bytes 1572872 | tf_op jit(solution)/shard_map/ppermute | solution.py:244
  356.5 20.0 %collective-permute-start.25 = (bf16[1,512,512]{2,1,0:T(8,128)(2,1)S(1)}, bf16[1,512,512]{2,1,0:T(8,128)(2,1)S(1)}, u32[]{:S(2)}, u32[]{:S(2)}) collective-permute-start(bf16[1,512,512]{2,1,0:T(8,128)(2,1)S(1)} %slice.472), channel_id=1, source_target_pairs={{0,8},{4,12},{8,0},{12,4},{1,9},{5,13},{9,1},{13,5},{2,10},{6,14},... | collective-permute-start | bytes 1572872 | tf_op jit(solution)/shard_map/ppermute | solution.py:244
  383.8 14.6 %collective-permute-start.29 = (bf16[1,512,512]{2,1,0:T(8,128)(2,1)}, bf16[1,512,512]{2,1,0:T(8,128)(2,1)}, u32[]{:S(2)}, u32[]{:S(2)}) collective-permute-start(bf16[1,512,512]{2,1,0:T(8,128)(2,1)} %slice.475), channel_id=1, source_target_pairs={{0,8},{4,12},{8,0},{12,4},{1,9},{5,13},{9,1},{13,5},{2,10},{6,14},... | collective-permute-start | bytes 1572872 | tf_op jit(solution)/shard_map/ppermute | solution.py:244
  385.8 19.8 %collective-permute-start.31 = (bf16[256,1024]{1,0:T(8,128)(2,1)}, bf16[256,1024]{1,0:T(8,128)(2,1)}, u32[]{:S(2)}, u32[]{:S(2)}) collective-permute-start(bf16[256,1024]{1,0:T(8,128)(2,1)} %collective-permute-done.27), channel_id=1, source_target_pairs={{0,1},{1,0},{2,3},{3,2},{4,5},{5,4},{6,7},{7,6},{8,9},{9,8},{10,11... | collective-permute-start | bytes 1572872 | tf_op jit(solution)/shard_map/ppermute | solution.py:244
  388.5 17.1 %collective-permute-start.30 = (bf16[128,1024]{1,0:T(8,128)(2,1)S(1)}, bf16[128,1024]{1,0:T(8,128)(2,1)S(1)}, u32[]{:S(2)}, u32[]{:S(2)}) collective-permute-start(bf16[128,1024]{1,0:T(8,128)(2,1)S(1)} %slice.476), channel_id=1, source_target_pairs={{0,2},{1,3},{2,0},{3,1},{4,6},{5,7},{6,4},{7,5},{8,10},{9,11},{10,... | collective-permute-start | bytes 786440 | tf_op jit(solution)/shard_map/ppermute | solution.py:244
  405.6 124.2 %reduce-scatter.9.cloned.1.call-start = ((), (), s32[]{:S(2)}) async-start(), calls=%async_computation.9 | async-start | bytes 4718592 | tf_op jit(solution)/shard_map/reduce_scatter | solution.py:383
  411.3 14.5 %collective-permute-start.32 = (bf16[256,1024]{1,0:T(8,128)(2,1)}, bf16[256,1024]{1,0:T(8,128)(2,1)}, u32[]{:S(2)}, u32[]{:S(2)}) collective-permute-start(bf16[256,1024]{1,0:T(8,128)(2,1)} %fusion.90), channel_id=1, source_target_pairs={{0,1},{1,0},{2,3},{3,2},{4,5},{5,4},{6,7},{7,6},{8,9},{9,8},{10,11... | collective-permute-start | bytes 1572872 | tf_op jit(solution)/shard_map/ppermute | solution.py:244
  429.9 22.8 %collective-permute-start.33 = (bf16[256,1024]{1,0:T(8,128)(2,1)S(1)}, bf16[256,1024]{1,0:T(8,128)(2,1)S(1)}, u32[]{:S(2)}, u32[]{:S(2)}) collective-permute-start(bf16[256,1024]{1,0:T(8,128)(2,1)S(1)} %get-tuple-element.101), channel_id=1, source_target_pairs={{0,1},{1,0},{2,3},{3,2},{4,5},{5,4},{6,7},{7,6},{8,9},{9,8},{10,11... | collective-permute-start | bytes 1572872 | tf_op jit(solution)/shard_map/ppermute | solution.py:244
  431.7 24.5 %collective-permute-start.34 = (bf16[256,1024]{1,0:T(8,128)(2,1)S(1)}, bf16[256,1024]{1,0:T(8,128)(2,1)S(1)}, u32[]{:S(2)}, u32[]{:S(2)}) collective-permute-start(bf16[256,1024]{1,0:T(8,128)(2,1)S(1)} %get-tuple-element.101), channel_id=1, source_target_pairs={{0,2},{1,3},{2,0},{3,1},{4,6},{5,7},{6,4},{7,5},{8,10},{9,11},{10,... | collective-permute-start | bytes 1572872 | tf_op jit(solution)/shard_map/ppermute | solution.py:244
  456.2 16.2 %collective-permute-start.35 = (bf16[256,1024]{1,0:T(8,128)(2,1)S(1)}, bf16[256,1024]{1,0:T(8,128)(2,1)S(1)}, u32[]{:S(2)}, u32[]{:S(2)}) collective-permute-start(bf16[256,1024]{1,0:T(8,128)(2,1)S(1)} %collective-permute-done.34), channel_id=1, source_target_pairs={{0,1},{1,0},{2,3},{3,2},{4,5},{5,4},{6,7},{7,6},{8,9},{9,8},{10,11... | collective-permute-start | bytes 1572872 | tf_op jit(solution)/shard_map/ppermute | solution.py:244
  458.1 33.1 %collective-permute-start.38 = (bf16[128,1024]{1,0:T(8,128)(2,1)S(1)}, bf16[128,1024]{1,0:T(8,128)(2,1)}, u32[]{:S(2)}, u32[]{:S(2)}) collective-permute-start(bf16[128,1024]{1,0:T(8,128)(2,1)S(1)} %slice_add_fusion), channel_id=1, source_target_pairs={{0,2},{1,3},{2,0},{3,1},{4,6},{5,7},{6,4},{7,5},{8,10},{9,11},{10,... | collective-permute-start | bytes 786440 | tf_op jit(solution)/shard_map/ppermute | solution.py:244
  472.2 135.0 %reduce-scatter.11.cloned.1.call-start = ((), (), s32[]{:S(2)}) async-start(), calls=%async_computation.10 | async-start | bytes 4718592 | tf_op jit(solution)/shard_map/reduce_scatter | solution.py:383
  476.2 13.5 %collective-permute-start.37 = (bf16[256,1024]{1,0:T(8,128)(2,1)S(1)}, bf16[256,1024]{1,0:T(8,128)(2,1)S(1)}, u32[]{:S(2)}, u32[]{:S(2)}) collective-permute-start(bf16[256,1024]{1,0:T(8,128)(2,1)S(1)} %get-tuple-element.334), channel_id=1, source_target_pairs={{0,1},{1,0},{2,3},{3,2},{4,5},{5,4},{6,7},{7,6},{8,9},{9,8},{10,11... | collective-permute-start | bytes 1572872 | tf_op jit(solution)/shard_map/ppermute | solution.py:244
  491.3 28.6 %collective-permute-start.39 = (bf16[256,1024]{1,0:T(8,128)(2,1)}, bf16[256,1024]{1,0:T(8,128)(2,1)}, u32[]{:S(2)}, u32[]{:S(2)}) collective-permute-start(bf16[256,1024]{1,0:T(8,128)(2,1)} %add_convert_fusion.2), channel_id=1, source_target_pairs={{0,2},{1,3},{2,0},{3,1},{4,6},{5,7},{6,4},{7,5},{8,10},{9,11},{10,... | collective-permute-start | bytes 1572872 | tf_op jit(solution)/shard_map/ppermute | solution.py:244
  495.5 22.4 %collective-permute-start.40 = (bf16[2,32,3072]{2,1,0:T(8,128)(2,1)}, bf16[2,32,3072]{2,1,0:T(8,128)(2,1)S(1)}, u32[]{:S(2)}, u32[]{:S(2)}) collective-permute-start(bf16[2,32,3072]{2,1,0:T(8,128)(2,1)} %dynamic-slice_bitcast_fusion), channel_id=1, source_target_pairs={{0,1},{1,0},{2,3},{3,2},{4,5},{5,4},{6,7},{7,6},{8,9},{9,8},{10,11... | collective-permute-start | bytes 1179656 | tf_op jit(solution)/shard_map/ppermute | solution.py:244
  499.6 27.2 %collective-permute-start.36 = (bf16[256,1024]{1,0:T(8,128)(2,1)}, bf16[256,1024]{1,0:T(8,128)(2,1)}, u32[]{:S(2)}, u32[]{:S(2)}) collective-permute-start(bf16[256,1024]{1,0:T(8,128)(2,1)} %fusion.107), channel_id=1, source_target_pairs={{0,1},{1,0},{2,3},{3,2},{4,5},{5,4},{6,7},{7,6},{8,9},{9,8},{10,11... | collective-permute-start | bytes 1572872 | tf_op jit(solution)/shard_map/ppermute | solution.py:244
  533.7 22.8 %collective-permute-start.41 = (bf16[256,1024]{1,0:T(8,128)(2,1)}, bf16[256,1024]{1,0:T(8,128)(2,1)}, u32[]{:S(2)}, u32[]{:S(2)}) collective-permute-start(bf16[256,1024]{1,0:T(8,128)(2,1)} %fusion.124), channel_id=1, source_target_pairs={{0,1},{1,0},{2,3},{3,2},{4,5},{5,4},{6,7},{7,6},{8,9},{9,8},{10,11... | collective-permute-start | bytes 1572872 | tf_op jit(solution)/shard_map/ppermute | solution.py:244
  533.7 24.1 %collective-permute-start.42 = (bf16[256,1024]{1,0:T(8,128)(2,1)}, bf16[256,1024]{1,0:T(8,128)(2,1)}, u32[]{:S(2)}, u32[]{:S(2)}) collective-permute-start(bf16[256,1024]{1,0:T(8,128)(2,1)} %fusion.124), channel_id=1, source_target_pairs={{0,2},{1,3},{2,0},{3,1},{4,6},{5,7},{6,4},{7,5},{8,10},{9,11},{10,... | collective-permute-start | bytes 1572872 | tf_op jit(solution)/shard_map/ppermute | solution.py:244
  562.4 26.0 %collective-permute-start.43 = (bf16[256,1024]{1,0:T(8,128)(2,1)}, bf16[256,1024]{1,0:T(8,128)(2,1)}, u32[]{:S(2)}, u32[]{:S(2)}) collective-permute-start(bf16[256,1024]{1,0:T(8,128)(2,1)} %collective-permute-done.42), channel_id=1, source_target_pairs={{0,1},{1,0},{2,3},{3,2},{4,5},{5,4},{6,7},{7,6},{8,9},{9,8},{10,11... | collective-permute-start | bytes 1572872 | tf_op jit(solution)/shard_map/ppermute | solution.py:244
  565.0 9.6 %collective-permute-start.45 = (f32[90,128]{1,0:T(8,128)S(1)}, f32[90,128]{1,0:T(8,128)S(1)}, u32[]{:S(2)}, u32[]{:S(2)}) collective-permute-start(f32[90,128]{1,0:T(8,128)S(1)} %fusion.246), channel_id=1, source_target_pairs={{0,2},{1,3},{2,0},{3,1},{4,6},{5,7},{6,4},{7,5},{8,10},{9,11},{10,... | collective-permute-start | bytes 138248 | tf_op jit(solution)/shard_map/ppermute | solution.py:244
  574.8 9.7 %collective-permute-start.50 = (bf16[32,3072]{1,0:T(8,128)(2,1)S(1)}, bf16[32,3072]{1,0:T(8,128)(2,1)S(1)}, u32[]{:S(2)}, u32[]{:S(2)}) collective-permute-start(bf16[32,3072]{1,0:T(8,128)(2,1)S(1)} %fusion.211), channel_id=1, source_target_pairs={{0,2},{1,3},{2,0},{3,1},{4,6},{5,7},{6,4},{7,5},{8,10},{9,11},{10,... | collective-permute-start | bytes 589832 | tf_op jit(solution)/shard_map/ppermute | solution.py:244
  589.9 14.8 %collective-permute-start.49 = (bf16[128,1024]{1,0:T(8,128)(2,1)S(1)}, bf16[128,1024]{1,0:T(8,128)(2,1)S(1)}, u32[]{:S(2)}, u32[]{:S(2)}) collective-permute-start(bf16[128,1024]{1,0:T(8,128)(2,1)S(1)} %pad_maximum_fusion.21), channel_id=1, source_target_pairs={{0,2},{1,3},{2,0},{3,1},{4,6},{5,7},{6,4},{7,5},{8,10},{9,11},{10,... | collective-permute-start | bytes 786440 | tf_op jit(solution)/shard_map/ppermute | solution.py:244
  (160 other events, 974.7 us)
Sparse Core Ops, SparseCore 0:
  40.2 27.9 all-gather.3
  70.1 46.5 all-gather.5
  181.3 39.5 all-gather.7
  293.1 79.5 reduce-scatter.4
  405.8 66.3 reduce-scatter.6
  476.0 51.1 reduce-scatter.8
  530.5 51.6 reduce-scatter.10
